TPU v7x, 256 devices: a whole 4x4x8 slice. The times are simulated.
256 devices in a mesh: ka: 8 (over y, x_hi), rows: 32 (over x_lo, z, core).
Axes of the slice: x: 4 (x_hi: 2, x_lo: 2; x = x_hi * 2 + x_lo), y: 4, z: 8, core: 2. Of those that a mesh axis runs over, the one named last changes fastest.
Arguments:
- drive: float32 [131072, 256], P(('ka', 'rows')), may hold values from -6 to 6
- relax: float32 [131072], P(('ka', 'rows')), may hold values from 0.2 to 1
- blocks: bfloat16 [65536, 4096], P(('ka', 'rows')), may hold values from -0.09375 to 0.09375
- row_block: int32 [65536], P(('ka', 'rows')), may hold values from -1 to 2047, as said below
- col_block: int32 [65536], P(('ka', 'rows')), may hold values from -1 to 2047, as said below
Outputs:
- distribution: float32 [131072, 256], P(('ka', 'rows'))
Inputs may be any that keep to these rules, and one draw needn't show every extreme that they name: `row_block`: the slots form groups of 256 in order, one group for each block of 8 row blocks (the row blocks of one device); a group's live slots come first and name row blocks of that group's own 8; -1 marks an empty slot. Every group has at least 85 live slots and some group is full in every draw. `col_block`: with the state blocks numbered (ka index * 32 + rows index) * 8 + block, a live slot's column block has the ka index of its row block or the next one modulo 8, and a rows index that differs from its row block's rows index by at most one, modulo 32; no pair of row and column blocks is named twice; -1 exactly where row_block is -1.
All inputs are finite; a program needn't handle non-finite values.
Results may differ from a plain program's by a relative error of at most 0.0015.
Values may be sent and summed in bfloat16 or wider, within the bound.
No kernel may reach another device: no remote copies, remote signals or barrier semaphores. Data moves between devices by JAX's collectives and lax.ppermute only.
A program may use at most 128 MiB of HBM per device.

v0:
```python
import jax
import jax.numpy as jnp
from jax import lax
from jax.sharding import PartitionSpec as P

STATES_PER_BLOCK = 64
ITERS = 2


def shifted(value, axis, steps):
    count = lax.axis_size(axis)
    pairs = [(source, (source + steps) % count) for source in range(count)]
    return lax.ppermute(value, axis, pairs)


def padded(array, sides, width):
    for axis, dim in sides:
        size, length = (lax.axis_size(axis), array.shape[dim])
        up = [(i, (i + 1) % size) for i in range(size)]
        down = [(j, i) for i, j in up]
        last = lax.slice_in_dim(array, length - width, length, axis=dim)
        first = lax.slice_in_dim(array, 0, width, axis=dim)
        before = lax.ppermute(last, axis, up)
        after = lax.ppermute(first, axis, down)
        array = jnp.concatenate([before, array, after], axis=dim)
    return array


def dense_band(kernel_items, position, block_count, block_side):
    band_count = 6 * block_count
    spare = block_count * band_count
    filled = (
        jnp.zeros((spare + 1, block_side, block_side), kernel_items.dtype)
        .at[position]
        .set(kernel_items)[:spare]
    )
    filled = filled.reshape(block_count, band_count, block_side, block_side).transpose(0, 2, 1, 3)
    return filled.reshape(block_count * block_side, band_count * block_side)


def local(drive, relax, blocks, row_block, col_block):
    rows_here = drive.shape[0]
    channel_count = drive.shape[1]
    block_side = STATES_PER_BLOCK
    block_count = rows_here // block_side
    band_count = 6 * block_count
    slot_total = blocks.shape[0]
    ka_count = lax.axis_size("ka")
    row_count = lax.axis_size("rows")
    ka_place = lax.axis_index("ka")
    row_place = lax.axis_index("rows")
    live_slot = row_block >= 0
    row_start = (ka_place * row_count + row_place) * block_count
    row_slot = jnp.where(live_slot, row_block - row_start, 0)
    column = jnp.where(live_slot, col_block, 0)
    target_ka = column // (row_count * block_count)
    target_row = column // block_count % row_count
    target_block = column % block_count
    ka_step = (target_ka - ka_place + ka_count) % ka_count
    row_step = (target_row - row_place + 1 + row_count) % row_count
    band_slot = (ka_step * 3 + row_step) * block_count + target_block
    position = jnp.where(live_slot, row_slot * band_count + band_slot, block_count * band_count)
    forward_matrix = dense_band(
        blocks.reshape(slot_total, block_side, block_side), position, block_count, block_side
    )
    state_field = drive
    for sweep_index in range(ITERS):
        wire_field = state_field.astype(jnp.bfloat16)
        next_field = shifted(wire_field, "ka", -1)
        paired = jnp.stack([wire_field, next_field])
        band_field = padded(paired, (("rows", 1),), rows_here)
        band_flat = band_field.reshape(band_count * block_side, channel_count)
        acc_rows = jnp.dot(forward_matrix, band_flat, preferred_element_type=jnp.float32)
        acc_band = lax.dot_general(
            forward_matrix, wire_field, (((0,), (0,)), ((), ())), preferred_element_type=jnp.float32
        )
        mirrored = acc_band.reshape(2, 3, rows_here, channel_count)
        collected = mirrored[:, 1]
        for block_offset in (-1, 1):
            collected = collected + shifted(mirrored[:, block_offset + 1], "rows", block_offset)
        returned = collected[0] + shifted(collected[1], "ka", 1)
        state_field = drive + relax[:, None] * (acc_rows + returned)
    return state_field


def solution(mesh):
    return jax.shard_map(
        local,
        mesh=mesh,
        in_specs=(
            P(("ka", "rows"), None),
            P(("ka", "rows")),
            P(("ka", "rows"), None),
            P(("ka", "rows")),
            P(("ka", "rows")),
        ),
        out_specs=P(("ka", "rows"), None),
        check_vma=False,
    )
```

profile of v0, /device:TPU:1, one launch (start us, length us, event | category | flops | bytes accessed | tf_op | source)
XLA Modules:
  0.0 173.1 jit_solution(10165639616082554986)
XLA Ops:
  0.0 3.3 %copy.19 = bf16[256,4096]{0,1:T(8,128)(2,1)S(1)} copy(bf16[256,4096]{1,0:T(8,128)(2,1)} %param.7) | data formatting | bytes 4194304 | tf_op args[2]
  3.3 6.7 %copy.20 = bf16[256,64,64]{2,1,0:T(8,128)(2,1)} copy(bf16[256,64,64]{0,2,1:T(8,128)(2,1)S(1)} %bitcast.66) | data formatting | bytes 4194304 | tf_op jit(solution)/shard_map/reshape | solution.py:64
  10.0 4.3 %broadcast_in_dim.14 = bf16[385,64,64]{2,1,0:T(8,128)(2,1)} broadcast(bf16[]{:T(256)} %constant.67.clone.1), dimensions={} | broadcast | bytes 3153922 | tf_op jit(solution)/shard_map/broadcast_in_dim | solution.py:33
  14.3 34.7 %scatter_fusion = bf16[385,64,64]{2,1,0:T(8,128)(2,1)} fusion(bf16[385,64,64]{2,1,0:T(8,128)(2,1)} %broadcast_in_dim.14, s32[256]{0:T(256)S(1)} %compare_select_fusion, bf16[256,64,64]{2,1,0:T(8,128)(2,1)} %copy.20), kind=kCustom, calls=%fused_computation | custom fusion | bytes 6292480 | tf_op jit(solution)/shard_map/scatter | solution.py:35
  49.0 4.3 %slice.44 = bf16[384,64,64]{2,1,0:T(8,128)(2,1)S(1)} slice(bf16[385,64,64]{2,1,0:T(8,128)(2,1)} %scatter_fusion), slice={[0:384], [0:64], [0:64]} | slice | bytes 6291456 | tf_op jit(solution)/shard_map/slice | solution.py:33
  53.3 6.9 %copy.22 = bf16[8,64,48,64]{3,2,1,0:T(8,128)(2,1)} copy(bf16[8,64,48,64]{3,1,2,0:T(8,128)(2,1)S(1)} %bitcast.65) | data formatting | bytes 6291456 | tf_op jit(solution)/shard_map/transpose | solution.py:37
  60.2 7.5 %reshape.22 = bf16[512,3072]{1,0:T(8,128)(2,1)S(1)} reshape(bf16[8,64,48,64]{3,2,1,0:T(8,128)(2,1)} %copy.22) | data formatting | bytes 6291456 | tf_op jit(solution)/shard_map/reshape | solution.py:38
  67.8 2.8 %copy.23 = bf16[3072,512]{1,0:T(8,128)(2,1)} copy(bf16[3072,512]{0,1:T(8,128)(2,1)S(1)} %bitcast.62) | data formatting | bytes 6291456 | tf_op jit(solution)/shard_map/dot_general | solution.py:74
  70.6 1.1 convert_element_type.6
  71.7 2.9 %fusion.2 = f32[2,3,512,256]{3,2,0,1:T(8,128)S(1)} fusion(bf16[2,3,512,512]{3,2,1,0:T(8,128)(2,1)} %bitcast.63, bf16[512,256]{1,0:T(8,128)(2,1)S(1)} %convert_element_type.6), kind=kOutput, calls=%fused_computation.3 | convolution fusion | flops 805306368 | bytes 6553600 | tf_op jit(solution)/shard_map/dot_general | solution.py:74
  74.7 2.7 %collective-permute-start.3 = (f32[2,512,256]{2,1,0:T(8,128)S(1)}, f32[2,512,256]{2,1,0:T(8,128)S(1)}, u32[]{:S(2)}, u32[]{:S(2)}) collective-permute-start(f32[2,512,256]{2,1,0:T(8,128)S(1)} %get-tuple-element.7), channel_id=1, source_target_pairs={{0,31},{1,0},{2,1},{3,2},{4,3},{5,4},{6,5},{7,6},{8,7},{9,8},{10,9... | collective-permute-start | bytes 3145736 | tf_op jit(solution)/shard_map/ppermute | solution.py:13
  77.3 0.9 collective-permute-start.4
  78.2 4.2 %collective-permute-start = (bf16[512,256]{1,0:T(8,128)(2,1)S(1)}, bf16[512,256]{1,0:T(8,128)(2,1)S(1)}, u32[]{:S(2)}, u32[]{:S(2)}) collective-permute-start(bf16[512,256]{1,0:T(8,128)(2,1)S(1)} %convert_element_type.6), channel_id=1, source_target_pairs={{0,224},{32,0},{64,32},{96,64},{128,96},{160,128},{192,160},{224,1... | collective-permute-start | bytes 786440 | tf_op jit(solution)/shard_map/ppermute | solution.py:13
  82.5 14.9 %collective-permute-done = bf16[512,256]{1,0:T(8,128)(2,1)S(1)} collective-permute-done((bf16[512,256]{1,0:T(8,128)(2,1)S(1)}, bf16[512,256]{1,0:T(8,128)(2,1)S(1)}, u32[]{:S(2)}, u32[]{:S(2)}) %collective-permute-start) | collective-permute-done | bytes 262176 | tf_op jit(solution)/shard_map/ppermute | solution.py:13
  97.6 4.1 %collective-permute-start.2 = (bf16[2,512,256]{2,1,0:T(8,128)(2,1)S(1)}, bf16[2,512,256]{2,1,0:T(8,128)(2,1)S(1)}, u32[]{:S(2)}, u32[]{:S(2)}) collective-permute-start(bf16[2,512,256]{2,1,0:T(8,128)(2,1)S(1)} %pad_maximum_fusion.2), channel_id=1, source_target_pairs={{1,0},{2,1},{3,2},{4,3},{5,4},{6,5},{7,6},{8,7},{9,8},{10,9},{11,1... | collective-permute-start | bytes 1572872 | tf_op jit(solution)/shard_map/ppermute | solution.py:24
  101.7 0.2 fusion.12
  102.0 2.4 %collective-permute-start.5 = (f32[512,256]{1,0:T(8,128)S(1)}, f32[512,256]{1,0:T(8,128)S(1)}, u32[]{:S(2)}, u32[]{:S(2)}) collective-permute-start(f32[512,256]{1,0:T(8,128)S(1)} %slice_bitcast_fusion.8), channel_id=1, source_target_pairs={{0,32},{32,64},{64,96},{96,128},{128,160},{160,192},{192,224},{224... | collective-permute-start | bytes 1572872 | tf_op jit(solution)/shard_map/ppermute | solution.py:13
  104.4 2.2 %collective-permute-done.2 = bf16[2,512,256]{2,1,0:T(8,128)(2,1)S(1)} collective-permute-done((bf16[2,512,256]{2,1,0:T(8,128)(2,1)S(1)}, bf16[2,512,256]{2,1,0:T(8,128)(2,1)S(1)}, u32[]{:S(2)}, u32[]{:S(2)}) %collective-permute-start.2) | collective-permute-done | bytes 524320 | tf_op jit(solution)/shard_map/ppermute | solution.py:24
  106.6 15.3 %collective-permute-done.5 = f32[512,256]{1,0:T(8,128)S(1)} collective-permute-done((f32[512,256]{1,0:T(8,128)S(1)}, f32[512,256]{1,0:T(8,128)S(1)}, u32[]{:S(2)}, u32[]{:S(2)}) %collective-permute-start.5) | collective-permute-done | bytes 524320 | tf_op jit(solution)/shard_map/ppermute | solution.py:13
  121.9 1.0 fusion.8
  122.9 0.9 copy-done
  123.8 1.0 fusion
  125.0 3.8 %collective-permute-start.9 = (f32[2,512,256]{2,1,0:T(8,128)S(1)}, f32[2,512,256]{2,1,0:T(8,128)S(1)}, u32[]{:S(2)}, u32[]{:S(2)}) collective-permute-start(f32[2,512,256]{2,1,0:T(8,128)S(1)} %get-tuple-element.5), channel_id=1, source_target_pairs={{0,31},{1,0},{2,1},{3,2},{4,3},{5,4},{6,5},{7,6},{8,7},{9,8},{10,9... | collective-permute-start | bytes 3145736 | tf_op jit(solution)/shard_map/ppermute | solution.py:13
  128.8 2.5 %collective-permute-start.6 = (bf16[512,256]{1,0:T(8,128)(2,1)S(1)}, bf16[512,256]{1,0:T(8,128)(2,1)S(1)}, u32[]{:S(2)}, u32[]{:S(2)}) collective-permute-start(bf16[512,256]{1,0:T(8,128)(2,1)S(1)} %fusion.8), channel_id=1, source_target_pairs={{0,224},{32,0},{64,32},{96,64},{128,96},{160,128},{192,160},{224,1... | collective-permute-start | bytes 786440 | tf_op jit(solution)/shard_map/ppermute | solution.py:13
  131.3 18.0 %collective-permute-done.6 = bf16[512,256]{1,0:T(8,128)(2,1)S(1)} collective-permute-done((bf16[512,256]{1,0:T(8,128)(2,1)S(1)}, bf16[512,256]{1,0:T(8,128)(2,1)S(1)}, u32[]{:S(2)}, u32[]{:S(2)}) %collective-permute-start.6) | collective-permute-done | bytes 262176 | tf_op jit(solution)/shard_map/ppermute | solution.py:13
  149.4 1.1 collective-permute-start.8
  150.5 0.2 fusion.10
  150.7 0.8 collective-permute-start.11
  151.6 3.9 %collective-permute-done.7 = bf16[2,512,256]{2,1,0:T(8,128)(2,1)S(1)} collective-permute-done((bf16[2,512,256]{2,1,0:T(8,128)(2,1)S(1)}, bf16[2,512,256]{2,1,0:T(8,128)(2,1)S(1)}, u32[]{:S(2)}, u32[]{:S(2)}) %collective-permute-start.7) | collective-permute-done | bytes 524320 | tf_op jit(solution)/shard_map/ppermute | solution.py:23
  155.5 2.9 %collective-permute-done.8 = bf16[2,512,256]{2,1,0:T(8,128)(2,1)S(1)} collective-permute-done((bf16[2,512,256]{2,1,0:T(8,128)(2,1)S(1)}, bf16[2,512,256]{2,1,0:T(8,128)(2,1)S(1)}, u32[]{:S(2)}, u32[]{:S(2)}) %collective-permute-start.8) | collective-permute-done | bytes 524320 | tf_op jit(solution)/shard_map/ppermute | solution.py:24
  158.5 12.8 %collective-permute-done.11 = f32[512,256]{1,0:T(8,128)S(1)} collective-permute-done((f32[512,256]{1,0:T(8,128)S(1)}, f32[512,256]{1,0:T(8,128)S(1)}, u32[]{:S(2)}, u32[]{:S(2)}) %collective-permute-start.11) | collective-permute-done | bytes 524320 | tf_op jit(solution)/shard_map/ppermute | solution.py:13
  171.2 1.8 %fusion.5 = f32[512,256]{1,0:T(8,128)} fusion(f32[512,256]{1,0:T(8,128)S(1)} %copy-done.1, bf16[512,3072]{1,0:T(8,128)(2,1)S(1)} %reshape.22, bf16[3072,256]{1,0:T(8,128)(2,1)S(1)} %bitcast.68, f32[512,256]{1,0:T(8,128)S(1)} %collective-permute-done.11, f32[2,512,256]{2,1,0:T(8,128)S(1)} %fusion.10, f32[512]{0:T(512)S(1)} %copy-done.2), kind=kOutput, calls=%fused_computation.9 | convolution fusion | flops 805830656 | bytes 6817792 | tf_op jit(solution)/shard_map/dot_general | solution.py:73
  (27 shorter events, 1.0 us)
Async XLA Ops:
  3.3 6.7 %copy-start.3 = (s32[256]{0:T(256)S(1)}, s32[256]{0:T(256)}, u32[]{:S(2)}) copy-start(s32[256]{0:T(256)} %param.9) | copy-start | bytes 3076
  3.3 6.7 %copy-start.4 = (s32[256]{0:T(256)S(1)}, s32[256]{0:T(256)}, u32[]{:S(2)}) copy-start(s32[256]{0:T(256)} %param.8) | copy-start | bytes 3076
  74.5 8.0 %copy-start.1 = (f32[512,256]{1,0:T(8,128)S(1)}, f32[512,256]{1,0:T(8,128)}, u32[]{:S(2)}) copy-start(f32[512,256]{1,0:T(8,128)} %param.5) | copy-start | bytes 1572868
  74.7 27.0 %collective-permute-start.3 = (f32[2,512,256]{2,1,0:T(8,128)S(1)}, f32[2,512,256]{2,1,0:T(8,128)S(1)}, u32[]{:S(2)}, u32[]{:S(2)}) collective-permute-start(f32[2,512,256]{2,1,0:T(8,128)S(1)} %get-tuple-element.7), channel_id=1, source_target_pairs={{0,31},{1,0},{2,1},{3,2},{4,3},{5,4},{6,5},{7,6},{8,7},{9,8},{10,9... | collective-permute-start | bytes 3145736 | tf_op jit(solution)/shard_map/ppermute | solution.py:13
  77.3 24.3 %collective-permute-start.4 = (f32[2,512,256]{2,1,0:T(8,128)S(1)}, f32[2,512,256]{2,1,0:T(8,128)S(1)}, u32[]{:S(2)}, u32[]{:S(2)}) collective-permute-start(f32[2,512,256]{2,1,0:T(8,128)S(1)} %get-tuple-element.8), channel_id=1, source_target_pairs={{0,1},{1,2},{2,3},{3,4},{4,5},{5,6},{6,7},{7,8},{8,9},{9,10},{10,1... | collective-permute-start | bytes 3145736 | tf_op jit(solution)/shard_map/ppermute | solution.py:13
  78.2 19.2 %collective-permute-start = (bf16[512,256]{1,0:T(8,128)(2,1)S(1)}, bf16[512,256]{1,0:T(8,128)(2,1)S(1)}, u32[]{:S(2)}, u32[]{:S(2)}) collective-permute-start(bf16[512,256]{1,0:T(8,128)(2,1)S(1)} %convert_element_type.6), channel_id=1, source_target_pairs={{0,224},{32,0},{64,32},{96,64},{128,96},{160,128},{192,160},{224,1... | collective-permute-start | bytes 786440 | tf_op jit(solution)/shard_map/ppermute | solution.py:13
  97.5 6.9 %collective-permute-start.1 = (bf16[2,512,256]{2,1,0:T(8,128)(2,1)S(1)}, bf16[2,512,256]{2,1,0:T(8,128)(2,1)S(1)}, u32[]{:S(2)}, u32[]{:S(2)}) collective-permute-start(bf16[2,512,256]{2,1,0:T(8,128)(2,1)S(1)} %pad_maximum_fusion.2), channel_id=1, source_target_pairs={{0,1},{1,2},{2,3},{3,4},{4,5},{5,6},{6,7},{7,8},{8,9},{9,10},{10,1... | collective-permute-start | bytes 1572872 | tf_op jit(solution)/shard_map/ppermute | solution.py:23
  97.6 9.0 %collective-permute-start.2 = (bf16[2,512,256]{2,1,0:T(8,128)(2,1)S(1)}, bf16[2,512,256]{2,1,0:T(8,128)(2,1)S(1)}, u32[]{:S(2)}, u32[]{:S(2)}) collective-permute-start(bf16[2,512,256]{2,1,0:T(8,128)(2,1)S(1)} %pad_maximum_fusion.2), channel_id=1, source_target_pairs={{1,0},{2,1},{3,2},{4,3},{5,4},{6,5},{7,6},{8,7},{9,8},{10,9},{11,1... | collective-permute-start | bytes 1572872 | tf_op jit(solution)/shard_map/ppermute | solution.py:24
  101.9 20.0 %copy-start.2 = (f32[512]{0:T(512)S(1)}, f32[512]{0:T(512)}, u32[]{:S(2)}) copy-start(f32[512]{0:T(512)} %param.6) | copy-start | bytes 6148
  102.0 20.0 %collective-permute-start.5 = (f32[512,256]{1,0:T(8,128)S(1)}, f32[512,256]{1,0:T(8,128)S(1)}, u32[]{:S(2)}, u32[]{:S(2)}) collective-permute-start(f32[512,256]{1,0:T(8,128)S(1)} %slice_bitcast_fusion.8), channel_id=1, source_target_pairs={{0,32},{32,64},{64,96},{96,128},{128,160},{160,192},{192,224},{224... | collective-permute-start | bytes 1572872 | tf_op jit(solution)/shard_map/ppermute | solution.py:13
  121.9 1.9 %copy-start = (bf16[3072,512]{1,0:T(8,128)(2,1)S(1)}, bf16[3072,512]{1,0:T(8,128)(2,1)}, u32[]{:S(2)}) copy-start(bf16[3072,512]{1,0:T(8,128)(2,1)} %copy.23) | copy-start | bytes 9437188
  124.9 25.5 %collective-permute-start.10 = (f32[2,512,256]{2,1,0:T(8,128)S(1)}, f32[2,512,256]{2,1,0:T(8,128)S(1)}, u32[]{:S(2)}, u32[]{:S(2)}) collective-permute-start(f32[2,512,256]{2,1,0:T(8,128)S(1)} %get-tuple-element.6), channel_id=1, source_target_pairs={{0,1},{1,2},{2,3},{3,4},{4,5},{5,6},{6,7},{7,8},{8,9},{9,10},{10,1... | collective-permute-start | bytes 3145736 | tf_op jit(solution)/shard_map/ppermute | solution.py:13
  125.0 25.5 %collective-permute-start.9 = (f32[2,512,256]{2,1,0:T(8,128)S(1)}, f32[2,512,256]{2,1,0:T(8,128)S(1)}, u32[]{:S(2)}, u32[]{:S(2)}) collective-permute-start(f32[2,512,256]{2,1,0:T(8,128)S(1)} %get-tuple-element.5), channel_id=1, source_target_pairs={{0,31},{1,0},{2,1},{3,2},{4,3},{5,4},{6,5},{7,6},{8,7},{9,8},{10,9... | collective-permute-start | bytes 3145736 | tf_op jit(solution)/shard_map/ppermute | solution.py:13
  128.8 20.5 %collective-permute-start.6 = (bf16[512,256]{1,0:T(8,128)(2,1)S(1)}, bf16[512,256]{1,0:T(8,128)(2,1)S(1)}, u32[]{:S(2)}, u32[]{:S(2)}) collective-permute-start(bf16[512,256]{1,0:T(8,128)(2,1)S(1)} %fusion.8), channel_id=1, source_target_pairs={{0,224},{32,0},{64,32},{96,64},{128,96},{160,128},{192,160},{224,1... | collective-permute-start | bytes 786440 | tf_op jit(solution)/shard_map/ppermute | solution.py:13
  149.3 6.2 %collective-permute-start.7 = (bf16[2,512,256]{2,1,0:T(8,128)(2,1)S(1)}, bf16[2,512,256]{2,1,0:T(8,128)(2,1)S(1)}, u32[]{:S(2)}, u32[]{:S(2)}) collective-permute-start(bf16[2,512,256]{2,1,0:T(8,128)(2,1)S(1)} %pad_maximum_fusion.3), channel_id=1, source_target_pairs={{0,1},{1,2},{2,3},{3,4},{4,5},{5,6},{6,7},{7,8},{8,9},{9,10},{10,1... | collective-permute-start | bytes 1572872 | tf_op jit(solution)/shard_map/ppermute | solution.py:23
  149.4 9.0 %collective-permute-start.8 = (bf16[2,512,256]{2,1,0:T(8,128)(2,1)S(1)}, bf16[2,512,256]{2,1,0:T(8,128)(2,1)S(1)}, u32[]{:S(2)}, u32[]{:S(2)}) collective-permute-start(bf16[2,512,256]{2,1,0:T(8,128)(2,1)S(1)} %pad_maximum_fusion.3), channel_id=1, source_target_pairs={{1,0},{2,1},{3,2},{4,3},{5,4},{6,5},{7,6},{8,7},{9,8},{10,9},{11,1... | collective-permute-start | bytes 1572872 | tf_op jit(solution)/shard_map/ppermute | solution.py:24
  150.7 20.5 %collective-permute-start.11 = (f32[512,256]{1,0:T(8,128)S(1)}, f32[512,256]{1,0:T(8,128)S(1)}, u32[]{:S(2)}, u32[]{:S(2)}) collective-permute-start(f32[512,256]{1,0:T(8,128)S(1)} %slice_bitcast_fusion.6), channel_id=1, source_target_pairs={{0,32},{32,64},{64,96},{96,128},{128,160},{160,192},{192,224},{224... | collective-permute-start | bytes 1572872 | tf_op jit(solution)/shard_map/ppermute | solution.py:13
where the time goes:
time: 175 us; the launch traced here: 173 us
  local copies, waits for them, and re-layouts  71.7 us (41%)
  waiting for transfers between devices  69.9 us (40%)
  starting transfers between devices  22.8 us (13%)
  matrix products  6.66 us (4%)
  other arithmetic  1.84 us (1%)
    ppermute x8, waiting for transfers between devices, shifted(): return lax.ppermute(value, axis, pairs)  60.9 us
    scatter x1, local copies, waits for them, and re-layouts, dense_band(): filled = jnp.zeros((spare + 1, block_side, block_side), kernel_items.dtyp...  34.7 us
    ppermute x8, starting transfers between devices, shifted(): return lax.ppermute(value, axis, pairs)  17.4 us
    reshape x1, local copies, waits for them, and re-layouts, dense_band(): return filled.reshape(block_count * block_side, band_count * block_side)  7.51 us
    transpose x1, local copies, waits for them, and re-layouts, dense_band(): filled.reshape(block_count, band_count, block_side, block_side)  6.92 us
    reshape x1, local copies, waits for them, and re-layouts, local(): blocks.reshape(slot_total, block_side, block_side)  6.67 us
    ppermute x2, starting transfers between devices, padded(): after = lax.ppermute(first, axis, down)  5.21 us
    ppermute x2, waiting for transfers between devices, padded(): after = lax.ppermute(first, axis, down)  5.02 us
  transfers between devices with their start and end apart: 12, of which 7 were waited for; matrix products, arithmetic and copies ran while one was open for 0% of the time, Pallas kernels for 0%

commit v1 on v0

v1 whole, which is shorter than its diff:
```python
import functools

import jax
import jax.numpy as jnp
from jax import lax
from jax.experimental import pallas as pl
from jax.experimental.pallas import tpu as pltpu
from jax.sharding import PartitionSpec as P

SIDE = 64
LANES = 128
ITERS = 2
TN = (((0,), (0,)), ((), ()))


def shifted(value, axis, steps):
    count = lax.axis_size(axis)
    pairs = [(source, (source + steps) % count) for source in range(count)]
    return lax.ppermute(value, axis, pairs)


def log2(n):
    assert n & (n - 1) == 0
    return n.bit_length() - 1


def call(kernel, outs, flops, *args, scratch=()):
    nbytes = sum(a.size * a.dtype.itemsize for a in args)
    return pl.pallas_call(
        kernel,
        out_shape=outs,
        in_specs=[pl.BlockSpec(memory_space=pltpu.VMEM)] * len(args),
        out_specs=jax.tree.map(lambda _: pl.BlockSpec(memory_space=pltpu.VMEM), outs),
        scratch_shapes=list(scratch),
        cost_estimate=pl.CostEstimate(flops=flops, transcendentals=0, bytes_accessed=nbytes),
        compiler_params=pltpu.CompilerParams(vmem_limit_bytes=40 << 20),
    )(*args)


def to_interleaved(value, dst_ref, scratch_ref, count):
    for g in range(value.shape[1] // LANES):
        lanes = slice(g * LANES, (g + 1) * LANES)
        scratch_ref[g] = value[:, lanes]
        for t in range(SIDE // 2):
            pair = [scratch_ref[g, pl.ds(2 * t + h, count, stride=SIDE), :] for h in range(2)]
            dst_ref[2 * t * count : (2 * t + 2) * count, lanes] = jnp.concatenate(pair, axis=0).astype(jnp.bfloat16)


def split_transposed(matrix, field, left_ref, middle_ref, right_ref):
    rows = left_ref.shape[0]
    for k, ref in enumerate((left_ref, middle_ref, right_ref)):
        part = lax.dot_general(matrix[:, k * rows : (k + 1) * rows], field, TN, preferred_element_type=jnp.float32)
        ref[...] = part.astype(ref.dtype)


def build_body(half, sizes, blocks_ref, row_ref, col_ref, drive_ref, matrix_ref, field_ref, left_ref, middle_ref, right_ref, scratch_ref):
    count, row_devs, ka_devs = sizes
    bits, row_bits = log2(count), log2(row_devs)
    row = row_ref[...]
    col = col_ref[...]
    ka_step = ((col >> (bits + row_bits)) - (row >> (bits + row_bits))) & (ka_devs - 1)
    row_step = (((col >> bits) & (row_devs - 1)) - ((row >> bits) & (row_devs - 1)) + 1) & (row_devs - 1)
    band = row_step * count + (col & (count - 1))
    groups = 3 * count // 2
    place = ((band & 1) * groups + (band >> 1)) * count + (row & (count - 1))
    place = jnp.where((row >= 0) & (ka_step == half), place, -1)
    slots = blocks_ref.shape[0]
    total = 2 * groups * count
    chosen = lax.broadcasted_iota(jnp.int32, (total, slots), 0) == place
    chosen = jnp.where(chosen, 1.0, 0.0).astype(jnp.bfloat16)
    low = lax.broadcasted_iota(jnp.int32, (groups * count, 2 * SIDE), 1) < SIDE
    for u in range(SIDE // 4):
        found = jnp.dot(chosen, blocks_ref[:, u * 4 * SIDE : (u + 1) * 4 * SIDE], preferred_element_type=jnp.float32)
        for w in range(2):
            t = 2 * u + w
            even = found[: groups * count, w * 2 * SIDE : (w + 1) * 2 * SIDE]
            odd = found[groups * count :, w * 2 * SIDE : (w + 1) * 2 * SIDE]
            first = jnp.where(low, even, pltpu.roll(odd, SIDE, 1))
            second = jnp.where(low, pltpu.roll(even, SIDE, 1), odd)
            for q in range(groups):
                pair = [v[q * count : (q + 1) * count, :] for v in (first, second)]
                matrix_ref[2 * t * count : (2 * t + 2) * count, 2 * q * SIDE : (2 * q + 2) * SIDE] = jnp.concatenate(
                    pair, axis=0
                ).astype(jnp.bfloat16)
    to_interleaved(drive_ref[...], field_ref, scratch_ref, count)
    split_transposed(matrix_ref[...], field_ref[...], left_ref, middle_ref, right_ref)


def forward_body(count, cross_ref, own_ref, *refs):
    fields = refs[:6]
    middle_ref, left_ref, right_ref, out_ref, scratch_ref = refs[6:]
    rows = out_ref.shape[0]
    acc = None
    for k in range(3):
        for matrix, field in ((own_ref, fields[k]), (cross_ref, fields[3 + k])):
            part = jnp.dot(matrix[:, k * rows : (k + 1) * rows], field[...], preferred_element_type=jnp.float32)
            acc = part if acc is None else acc + part
    for g in range(acc.shape[1] // LANES):
        lanes = slice(g * LANES, (g + 1) * LANES)
        scratch_ref[g] = acc[:, lanes]
        for b in range(count):
            here = slice(b * SIDE, (b + 1) * SIDE)
            extra = middle_ref[here, lanes] + left_ref[here, lanes].astype(jnp.float32) + right_ref[here, lanes].astype(jnp.float32)
            out_ref[here, lanes] = scratch_ref[g, pl.ds(b, SIDE, stride=count), :] + extra


def update_body(count, drive_ref, relax_ref, forward_ref, received_ref, cross_ref, wire_ref, field_ref, left_ref, middle_ref, right_ref, scratch_ref):
    field = drive_ref[...] + relax_ref[...] * (forward_ref[...] + received_ref[...].astype(jnp.float32))
    wire_ref[...] = field.astype(jnp.bfloat16)
    to_interleaved(field, field_ref, scratch_ref, count)
    split_transposed(cross_ref[...], field_ref[...], left_ref, middle_ref, right_ref)


def transposed_body(matrix_ref, field_ref, left_ref, middle_ref, right_ref):
    split_transposed(matrix_ref[...], field_ref[...], left_ref, middle_ref, right_ref)


def final_body(drive_ref, relax_ref, forward_ref, received_ref, out_ref):
    out_ref[...] = drive_ref[...] + relax_ref[...] * (forward_ref[...] + received_ref[...].astype(jnp.float32))


def halo(value):
    return shifted(value, "rows", 1), shifted(value, "rows", -1)


def local(drive, relax, blocks, row_block, col_block):
    rows, channels = drive.shape
    count = rows // SIDE
    sizes = (count, lax.axis_size("rows"), lax.axis_size("ka"))
    bf16, f32 = jnp.bfloat16, jnp.float32
    small = jax.ShapeDtypeStruct((rows, channels), bf16)
    wide = jax.ShapeDtypeStruct((rows, channels), f32)
    matrix = jax.ShapeDtypeStruct((rows, 3 * rows), bf16)
    staging = pltpu.VMEM((channels // LANES, rows, LANES), f32)
    row2 = row_block.reshape(1, -1)
    col2 = col_block.reshape(1, -1)
    relax2 = relax.reshape(-1, 1)
    work = 2 * rows * rows * 3 * channels
    wire = drive.astype(bf16)
    cross, field, left, middle, right = call(
        functools.partial(build_body, 1, sizes), (matrix, small, small, wide, small), 2 * work, blocks, row2, col2, drive,
        scratch=[staging],
    )
    own, _, own_left, own_middle, own_right = call(
        functools.partial(build_body, 0, sizes), (matrix, small, small, wide, small), 2 * work, blocks, row2, col2, drive,
        scratch=[staging],
    )
    for sweep in range(ITERS):
        down = shifted(wire, "ka", -1)
        before, after = halo(wire)
        got = middle + shifted(left, "rows", -1).astype(f32) + shifted(right, "rows", 1).astype(f32)
        received = shifted(got.astype(bf16), "ka", 1)
        own_after = shifted(own_left, "rows", -1)
        own_before = shifted(own_right, "rows", 1)
        down_before, down_after = halo(down)
        forward = call(
            functools.partial(forward_body, count), wide, 2 * work,
            cross, own, before, wire, after, down_before, down, down_after, own_middle, own_after, own_before,
            scratch=[staging],
        )
        if sweep + 1 == ITERS:
            return call(final_body, wide, 0, drive, relax2, forward, received)
        wire, field, left, middle, right = call(
            functools.partial(update_body, count), (small, small, small, wide, small), work,
            drive, relax2, forward, received, cross, scratch=[staging],
        )
        own_left, own_middle, own_right = call(transposed_body, (small, wide, small), work, own, field)


def solution(mesh):
    spread = P(("ka", "rows"))
    wide = P(("ka", "rows"), None)
    return jax.shard_map(
        local, mesh=mesh, in_specs=(wide, spread, wide, spread, spread), out_specs=wide, check_vma=False
    )
```

time: 175 us -> 82.9 us (0.47)
  the two profiles are of different devices: /device:TPU:1 before, /device:TPU:2 now
where the time goes in v1:
time: 82.9 us; the launch traced here: 82.6 us
  starting transfers between devices  43.5 us (52%)
  waiting for transfers between devices  18.8 us (23%)
  Pallas kernels  10.6 us (13%)
  local copies, waits for them, and re-layouts  7.81 us (9%)
  other arithmetic  1.6 us (2%)
    ppermute x20, starting transfers between devices, shifted(): return lax.ppermute(value, axis, pairs)  43.5 us
    ppermute x20, waiting for transfers between devices, shifted(): return lax.ppermute(value, axis, pairs)  18.8 us
    pallas_call x7, Pallas kernels, call(): pl.pallas_call(kernel, out_shape=outs, in_specs=[pl.BlockSpec(memory_spac...  10.6 us
    unnamed x24, local copies, waits for them, and re-layouts  7.66 us
  transfers between devices with their start and end apart: 20, of which 6 were waited for; matrix products, arithmetic and copies ran while one was open for 2% of the time, Pallas kernels for 7%

profile of v1, /device:TPU:2, one launch (start us, length us, event | category | flops | bytes accessed | tf_op | source)
XLA Modules:
  0.0 82.6 jit_solution(5634529629922047342)
XLA Ops:
  0.0 1.0 %copy-done = f32[512,256]{1,0:T(8,128)S(1)} copy-done((f32[512,256]{1,0:T(8,128)S(1)}, f32[512,256]{1,0:T(8,128)}, u32[]{:S(2)}) %copy-start) | copy-done | bytes 524312
  1.0 1.6 %copy-done.8 = bf16[256,4096]{1,0:T(8,128)(2,1)S(1)} copy-done((bf16[256,4096]{1,0:T(8,128)(2,1)S(1)}, bf16[256,4096]{1,0:T(8,128)(2,1)}, u32[]{:S(2)}) %copy-start.8) | copy-done | bytes 2097176
  4.0 1.8 %shard_map.56 = (bf16[512,1536]{1,0:T(8,128)(2,1)S(1)}, bf16[512,256]{1,0:T(8,128)(2,1)}, bf16[512,256]{1,0:T(8,128)(2,1)S(1)}, f32[512,256]{1,0:T(8,128)S(1)}, bf16[512,256]{1,0:T(8,128)(2,1)S(1)}) custom-call(bf16[256,4096]{1,0:T(8,128)(2,1)S(1)} %copy-done.8, s32[1,256]{1,0:T(1,128)S(1)} %bitcast.3, s32[1,256]{1,0:T(1,128)S(1)} %bitcast.5, ...), custom_call_target="tpu_custom_call" | custom-call | flops 805306368 | bytes 2623488 | tf_op jit(solution)/shard_map/pallas_call | solution.py:29
  5.8 5.3 %collective-permute-start.5 = (bf16[512,256]{1,0:T(8,128)(2,1)S(1)}, bf16[512,256]{1,0:T(8,128)(2,1)S(1)}, u32[]{:S(2)}, u32[]{:S(2)}) collective-permute-start(bf16[512,256]{1,0:T(8,128)(2,1)S(1)} %get-tuple-element.24), channel_id=1, source_target_pairs={{0,31},{1,0},{2,1},{3,2},{4,3},{5,4},{6,5},{7,6},{8,7},{9,8},{10,9... | collective-permute-start | bytes 786440 | tf_op jit(solution)/shard_map/ppermute | solution.py:19
  11.1 0.7 convert_element_type.21.refs_1_
  11.8 4.9 %collective-permute-start.2 = (bf16[512,256]{1,0:T(8,128)(2,1)}, bf16[512,256]{1,0:T(8,128)(2,1)}, u32[]{:S(2)}, u32[]{:S(2)}) collective-permute-start(bf16[512,256]{1,0:T(8,128)(2,1)} %convert_element_type.21.refs_1_), channel_id=1, source_target_pairs={{0,224},{32,0},{64,32},{96,64},{128,96},{160,128},{192,160},{224,1... | collective-permute-start | bytes 786440 | tf_op jit(solution)/shard_map/ppermute | solution.py:19
  16.7 1.8 %shard_map.55 = (bf16[512,1536]{1,0:T(8,128)(2,1)S(1)}, bf16[512,256]{1,0:T(8,128)(2,1)}, bf16[512,256]{1,0:T(8,128)(2,1)S(1)}, f32[512,256]{1,0:T(8,128)S(1)}, bf16[512,256]{1,0:T(8,128)(2,1)S(1)}) custom-call(bf16[256,4096]{1,0:T(8,128)(2,1)S(1)} %copy-done.8, s32[1,256]{1,0:T(1,128)S(1)} %bitcast.4, s32[1,256]{1,0:T(1,128)S(1)} %bitcast.6, ...), custom_call_target="tpu_custom_call" | custom-call | flops 805306368 | bytes 2623488 | tf_op jit(solution)/shard_map/pallas_call | solution.py:29
  18.5 1.0 %collective-permute-start.7 = (bf16[512,256]{1,0:T(8,128)(2,1)S(1)}, bf16[512,256]{1,0:T(8,128)(2,1)S(1)}, u32[]{:S(2)}, u32[]{:S(2)}) collective-permute-start(bf16[512,256]{1,0:T(8,128)(2,1)S(1)} %get-tuple-element.27), channel_id=1, source_target_pairs={{0,31},{1,0},{2,1},{3,2},{4,3},{5,4},{6,5},{7,6},{8,7},{9,8},{10,9... | collective-permute-start | bytes 786440 | tf_op jit(solution)/shard_map/ppermute | solution.py:19
  19.6 1.3 %collective-permute-done.2.refs_4_ = bf16[512,256]{1,0:T(8,128)(2,1)} collective-permute-done((bf16[512,256]{1,0:T(8,128)(2,1)}, bf16[512,256]{1,0:T(8,128)(2,1)}, u32[]{:S(2)}, u32[]{:S(2)}) %collective-permute-start.2) | collective-permute-done | bytes 262176 | tf_op jit(solution)/shard_map/ppermute | solution.py:19
  20.9 6.5 %collective-permute-start.1 = (bf16[512,256]{1,0:T(8,128)(2,1)}, bf16[512,256]{1,0:T(8,128)(2,1)}, u32[]{:S(2)}, u32[]{:S(2)}) collective-permute-start(bf16[512,256]{1,0:T(8,128)(2,1)} %convert_element_type.21.refs_1_), channel_id=1, source_target_pairs={{0,31},{1,0},{2,1},{3,2},{4,3},{5,4},{6,5},{7,6},{8,7},{9,8},{10,9... | collective-permute-start | bytes 786440 | tf_op jit(solution)/shard_map/ppermute | solution.py:19
  27.4 3.8 %collective-permute-start.4 = (bf16[512,256]{1,0:T(8,128)(2,1)}, bf16[512,256]{1,0:T(8,128)(2,1)}, u32[]{:S(2)}, u32[]{:S(2)}) collective-permute-start(bf16[512,256]{1,0:T(8,128)(2,1)} %collective-permute-done.2.refs_4_), channel_id=1, source_target_pairs={{0,31},{1,0},{2,1},{3,2},{4,3},{5,4},{6,5},{7,6},{8,7},{9,8},{10,9... | collective-permute-start | bytes 786440 | tf_op jit(solution)/shard_map/ppermute | solution.py:19
  31.2 0.8 add_convert_fusion.1
  32.0 0.7 copy-done.6
  32.7 3.8 %collective-permute-start.9 = (bf16[512,256]{1,0:T(8,128)(2,1)}, bf16[512,256]{1,0:T(8,128)(2,1)}, u32[]{:S(2)}, u32[]{:S(2)}) collective-permute-start(bf16[512,256]{1,0:T(8,128)(2,1)} %add_convert_fusion.1), channel_id=1, source_target_pairs={{0,32},{32,64},{64,96},{96,128},{128,160},{160,192},{192,224},{224... | collective-permute-start | bytes 786440 | tf_op jit(solution)/shard_map/ppermute | solution.py:19
  36.7 1.0 %copy-done.3 = f32[512,256]{1,0:T(8,128)S(1)} copy-done((f32[512,256]{1,0:T(8,128)S(1)}, f32[512,256]{1,0:T(8,128)}, u32[]{:S(2)}) %copy-start.3) | copy-done | bytes 524312
  37.8 0.9 %copy-done.5 = bf16[512,256]{1,0:T(8,128)(2,1)S(1)} copy-done((bf16[512,256]{1,0:T(8,128)(2,1)S(1)}, bf16[512,256]{1,0:T(8,128)(2,1)}, u32[]{:S(2)}) %copy-start.5) | copy-done | bytes 262168
  38.7 0.9 %copy-done.7 = bf16[512,256]{1,0:T(8,128)(2,1)S(1)} copy-done((bf16[512,256]{1,0:T(8,128)(2,1)S(1)}, bf16[512,256]{1,0:T(8,128)(2,1)}, u32[]{:S(2)}) %copy-start.7) | copy-done | bytes 262168
  39.7 2.4 %shard_map.57.forward_ref = f32[512,256]{1,0:T(8,128)S(1)} custom-call(bf16[512,1536]{1,0:T(8,128)(2,1)S(1)} %get-tuple-element.21.cross_ref, bf16[512,1536]{1,0:T(8,128)(2,1)S(1)} %get-tuple-element.22.own_ref.matrix_ref, bf16[512,256]{1,0:T(8,128)(2,1)} %collective-permute-done.refs_0_, bf16[512,256]{1,0:T(8,128)(2,1)} %convert_element_type.21.refs_1_, ...), custom_call_target="tpu_custom_call" | custom-call | flops 805306368 | bytes 5767168 | tf_op jit(solution)/shard_map/pallas_call | solution.py:29
  42.1 0.9 %collective-permute-done.9.received_ref = bf16[512,256]{1,0:T(8,128)(2,1)} collective-permute-done((bf16[512,256]{1,0:T(8,128)(2,1)}, bf16[512,256]{1,0:T(8,128)(2,1)}, u32[]{:S(2)}, u32[]{:S(2)}) %collective-permute-start.9) | collective-permute-done | bytes 262176 | tf_op jit(solution)/shard_map/ppermute | solution.py:19
  43.0 2.0 %shard_map.58 = (bf16[512,256]{1,0:T(8,128)(2,1)S(1)}, bf16[512,256]{1,0:T(8,128)(2,1)S(1)}, bf16[512,256]{1,0:T(8,128)(2,1)S(1)}, f32[512,256]{1,0:T(8,128)S(1)}, bf16[512,256]{1,0:T(8,128)(2,1)S(1)}) custom-call(f32[512,256]{1,0:T(8,128)S(1)} %copy-done.1, f32[512,1]{1,0:T(8,128)S(1)} %copy.7.relax_ref, f32[512,256]{1,0:T(8,128)S(1)} %shard_map.57.forward_ref, ...), custom_call_target="tpu_custom_call" | custom-call | flops 402653184 | bytes 2885632 | tf_op jit(solution)/shard_map/pallas_call | solution.py:29
  45.1 4.2 %collective-permute-start.17 = (bf16[512,256]{1,0:T(8,128)(2,1)S(1)}, bf16[512,256]{1,0:T(8,128)(2,1)S(1)}, u32[]{:S(2)}, u32[]{:S(2)}) collective-permute-start(bf16[512,256]{1,0:T(8,128)(2,1)S(1)} %get-tuple-element.35), channel_id=1, source_target_pairs={{0,31},{1,0},{2,1},{3,2},{4,3},{5,4},{6,5},{7,6},{8,7},{9,8},{10,9... | collective-permute-start | bytes 786440 | tf_op jit(solution)/shard_map/ppermute | solution.py:19
  49.9 2.2 %collective-permute-start.12 = (bf16[512,256]{1,0:T(8,128)(2,1)S(1)}, bf16[512,256]{1,0:T(8,128)(2,1)S(1)}, u32[]{:S(2)}, u32[]{:S(2)}) collective-permute-start(bf16[512,256]{1,0:T(8,128)(2,1)S(1)} %get-tuple-element.29.refs_1_), channel_id=1, source_target_pairs={{0,224},{32,0},{64,32},{96,64},{128,96},{160,128},{192,160},{224,1... | collective-permute-start | bytes 786440 | tf_op jit(solution)/shard_map/ppermute | solution.py:19
  52.2 4.2 %collective-permute-start.15 = (bf16[512,256]{1,0:T(8,128)(2,1)S(1)}, bf16[512,256]{1,0:T(8,128)(2,1)S(1)}, u32[]{:S(2)}, u32[]{:S(2)}) collective-permute-start(bf16[512,256]{1,0:T(8,128)(2,1)S(1)} %get-tuple-element.32), channel_id=1, source_target_pairs={{0,31},{1,0},{2,1},{3,2},{4,3},{5,4},{6,5},{7,6},{8,7},{9,8},{10,9... | collective-permute-start | bytes 786440 | tf_op jit(solution)/shard_map/ppermute | solution.py:19
  56.3 1.0 %collective-permute-done.18 = bf16[512,256]{1,0:T(8,128)(2,1)S(1)} collective-permute-done((bf16[512,256]{1,0:T(8,128)(2,1)S(1)}, bf16[512,256]{1,0:T(8,128)(2,1)S(1)}, u32[]{:S(2)}, u32[]{:S(2)}) %collective-permute-start.18) | collective-permute-done | bytes 262176 | tf_op jit(solution)/shard_map/ppermute | solution.py:19
  57.3 3.0 %collective-permute-start.11 = (bf16[512,256]{1,0:T(8,128)(2,1)S(1)}, bf16[512,256]{1,0:T(8,128)(2,1)S(1)}, u32[]{:S(2)}, u32[]{:S(2)}) collective-permute-start(bf16[512,256]{1,0:T(8,128)(2,1)S(1)} %get-tuple-element.29.refs_1_), channel_id=1, source_target_pairs={{0,31},{1,0},{2,1},{3,2},{4,3},{5,4},{6,5},{7,6},{8,7},{9,8},{10,9... | collective-permute-start | bytes 786440 | tf_op jit(solution)/shard_map/ppermute | solution.py:19
  60.3 6.0 %collective-permute-done.12.refs_4_ = bf16[512,256]{1,0:T(8,128)(2,1)S(1)} collective-permute-done((bf16[512,256]{1,0:T(8,128)(2,1)S(1)}, bf16[512,256]{1,0:T(8,128)(2,1)S(1)}, u32[]{:S(2)}, u32[]{:S(2)}) %collective-permute-start.12) | collective-permute-done | bytes 262176 | tf_op jit(solution)/shard_map/ppermute | solution.py:19
  66.3 3.9 %collective-permute-start.14 = (bf16[512,256]{1,0:T(8,128)(2,1)S(1)}, bf16[512,256]{1,0:T(8,128)(2,1)S(1)}, u32[]{:S(2)}, u32[]{:S(2)}) collective-permute-start(bf16[512,256]{1,0:T(8,128)(2,1)S(1)} %collective-permute-done.12.refs_4_), channel_id=1, source_target_pairs={{0,31},{1,0},{2,1},{3,2},{4,3},{5,4},{6,5},{7,6},{8,7},{9,8},{10,9... | collective-permute-start | bytes 786440 | tf_op jit(solution)/shard_map/ppermute | solution.py:19
  70.3 0.8 collective-permute-start.19
  71.0 3.2 %collective-permute-done.13.refs_3_ = bf16[512,256]{1,0:T(8,128)(2,1)S(1)} collective-permute-done((bf16[512,256]{1,0:T(8,128)(2,1)S(1)}, bf16[512,256]{1,0:T(8,128)(2,1)S(1)}, u32[]{:S(2)}, u32[]{:S(2)}) %collective-permute-start.13) | collective-permute-done | bytes 262176 | tf_op jit(solution)/shard_map/ppermute | solution.py:19
  74.2 1.0 %shard_map.60.forward_ref = f32[512,256]{1,0:T(8,128)S(1)} custom-call(bf16[512,1536]{1,0:T(8,128)(2,1)S(1)} %get-tuple-element.21.cross_ref, bf16[512,1536]{1,0:T(8,128)(2,1)S(1)} %get-tuple-element.22.own_ref.matrix_ref, bf16[512,256]{1,0:T(8,128)(2,1)S(1)} %collective-permute-done.10.refs_0_, bf16[512,256]{1,0:T(8,128)(2,1)S(1)} %get-tuple-element.29.refs_1_, ...), custom_call_target="tpu_custom_call" | custom-call | flops 805306368 | bytes 5767168 | tf_op jit(solution)/shard_map/pallas_call | solution.py:29
  75.2 6.4 %collective-permute-done.19.received_ref = bf16[512,256]{1,0:T(8,128)(2,1)S(1)} collective-permute-done((bf16[512,256]{1,0:T(8,128)(2,1)S(1)}, bf16[512,256]{1,0:T(8,128)(2,1)S(1)}, u32[]{:S(2)}, u32[]{:S(2)}) %collective-permute-start.19) | collective-permute-done | bytes 262176 | tf_op jit(solution)/shard_map/ppermute | solution.py:19
  81.6 0.9 %shard_map.61 = f32[512,256]{1,0:T(8,128)} custom-call(f32[512,256]{1,0:T(8,128)S(1)} %copy-done.1, f32[512,1]{1,0:T(8,128)S(1)} %copy.7.relax_ref, f32[512,256]{1,0:T(8,128)S(1)} %shard_map.60.forward_ref, bf16[512,256]{1,0:T(8,128)(2,1)S(1)} %collective-permute-done.19.received_ref), custom_call_target="tpu_custom_call" | custom-call | bytes 1312768 | tf_op jit(solution)/shard_map/pallas_call | solution.py:29
  (43 shorter events, 2.4 us)
Async XLA Ops:
  0.0 1.0 %copy-start = (f32[512,256]{1,0:T(8,128)S(1)}, f32[512,256]{1,0:T(8,128)}, u32[]{:S(2)}) copy-start(f32[512,256]{1,0:T(8,128)} %drive_ref.7) | copy-start | bytes 1572868
  1.0 1.6 %copy-start.8 = (bf16[256,4096]{1,0:T(8,128)(2,1)S(1)}, bf16[256,4096]{1,0:T(8,128)(2,1)}, u32[]{:S(2)}) copy-start(bf16[256,4096]{1,0:T(8,128)(2,1)} %blocks_ref.3) | copy-start | bytes 6291460
  2.6 0.7 copy-start.9
  3.3 0.7 copy-start.10
  5.8 6.0 %copy-start.2 = (f32[512,256]{1,0:T(8,128)}, f32[512,256]{1,0:T(8,128)S(1)}, u32[]{:S(2)}) copy-start(f32[512,256]{1,0:T(8,128)S(1)} %get-tuple-element.23.refs_6_) | copy-start | bytes 1572868
  5.8 13.7 %collective-permute-start.5 = (bf16[512,256]{1,0:T(8,128)(2,1)S(1)}, bf16[512,256]{1,0:T(8,128)(2,1)S(1)}, u32[]{:S(2)}, u32[]{:S(2)}) collective-permute-start(bf16[512,256]{1,0:T(8,128)(2,1)S(1)} %get-tuple-element.24), channel_id=1, source_target_pairs={{0,31},{1,0},{2,1},{3,2},{4,3},{5,4},{6,5},{7,6},{8,7},{9,8},{10,9... | collective-permute-start | bytes 786440 | tf_op jit(solution)/shard_map/ppermute | solution.py:19
  11.8 24.7 %copy-start.11 = (f32[512]{0:T(512)S(1)}, f32[512]{0:T(512)}, u32[]{:S(2)}) copy-start(f32[512]{0:T(512)} %param.6) | copy-start | bytes 6148
  11.8 9.1 %collective-permute-start.2 = (bf16[512,256]{1,0:T(8,128)(2,1)}, bf16[512,256]{1,0:T(8,128)(2,1)}, u32[]{:S(2)}, u32[]{:S(2)}) collective-permute-start(bf16[512,256]{1,0:T(8,128)(2,1)} %convert_element_type.21.refs_1_), channel_id=1, source_target_pairs={{0,224},{32,0},{64,32},{96,64},{128,96},{160,128},{192,160},{224,1... | collective-permute-start | bytes 786440 | tf_op jit(solution)/shard_map/ppermute | solution.py:19
  18.5 8.9 %collective-permute-start.7 = (bf16[512,256]{1,0:T(8,128)(2,1)S(1)}, bf16[512,256]{1,0:T(8,128)(2,1)S(1)}, u32[]{:S(2)}, u32[]{:S(2)}) collective-permute-start(bf16[512,256]{1,0:T(8,128)(2,1)S(1)} %get-tuple-element.27), channel_id=1, source_target_pairs={{0,31},{1,0},{2,1},{3,2},{4,3},{5,4},{6,5},{7,6},{8,7},{9,8},{10,9... | collective-permute-start | bytes 786440 | tf_op jit(solution)/shard_map/ppermute | solution.py:19
  19.5 7.9 %collective-permute-start.8 = (bf16[512,256]{1,0:T(8,128)(2,1)S(1)}, bf16[512,256]{1,0:T(8,128)(2,1)S(1)}, u32[]{:S(2)}, u32[]{:S(2)}) collective-permute-start(bf16[512,256]{1,0:T(8,128)(2,1)S(1)} %get-tuple-element.28), channel_id=1, source_target_pairs={{0,1},{1,2},{2,3},{3,4},{4,5},{5,6},{6,7},{7,8},{8,9},{9,10},{10,1... | collective-permute-start | bytes 786440 | tf_op jit(solution)/shard_map/ppermute | solution.py:19
  19.5 12.5 %collective-permute-start.6 = (bf16[512,256]{1,0:T(8,128)(2,1)S(1)}, bf16[512,256]{1,0:T(8,128)(2,1)S(1)}, u32[]{:S(2)}, u32[]{:S(2)}) collective-permute-start(bf16[512,256]{1,0:T(8,128)(2,1)S(1)} %get-tuple-element.25), channel_id=1, source_target_pairs={{0,1},{1,2},{2,3},{3,4},{4,5},{5,6},{6,7},{7,8},{8,9},{9,10},{10,1... | collective-permute-start | bytes 786440 | tf_op jit(solution)/shard_map/ppermute | solution.py:19
  19.5 17.0 %copy-start.4 = (bf16[512,256]{1,0:T(8,128)(2,1)}, bf16[512,256]{1,0:T(8,128)(2,1)S(1)}, u32[]{:S(2)}) copy-start(bf16[512,256]{1,0:T(8,128)(2,1)S(1)} %collective-permute-done.5.refs_7_) | copy-start | bytes 786436
  19.5 17.2 %collective-permute-start = (bf16[512,256]{1,0:T(8,128)(2,1)}, bf16[512,256]{1,0:T(8,128)(2,1)}, u32[]{:S(2)}, u32[]{:S(2)}) collective-permute-start(bf16[512,256]{1,0:T(8,128)(2,1)} %convert_element_type.21.refs_1_), channel_id=1, source_target_pairs={{0,1},{1,2},{2,3},{3,4},{4,5},{5,6},{6,7},{7,8},{8,9},{9,10},{10,1... | collective-permute-start | bytes 786440 | tf_op jit(solution)/shard_map/ppermute | solution.py:19
  20.9 15.8 %collective-permute-start.1 = (bf16[512,256]{1,0:T(8,128)(2,1)}, bf16[512,256]{1,0:T(8,128)(2,1)}, u32[]{:S(2)}, u32[]{:S(2)}) collective-permute-start(bf16[512,256]{1,0:T(8,128)(2,1)} %convert_element_type.21.refs_1_), channel_id=1, source_target_pairs={{0,31},{1,0},{2,1},{3,2},{4,3},{5,4},{6,5},{7,6},{8,7},{9,8},{10,9... | collective-permute-start | bytes 786440 | tf_op jit(solution)/shard_map/ppermute | solution.py:19
  27.4 9.4 %collective-permute-start.3 = (bf16[512,256]{1,0:T(8,128)(2,1)}, bf16[512,256]{1,0:T(8,128)(2,1)}, u32[]{:S(2)}, u32[]{:S(2)}) collective-permute-start(bf16[512,256]{1,0:T(8,128)(2,1)} %collective-permute-done.2.refs_4_), channel_id=1, source_target_pairs={{0,1},{1,2},{2,3},{3,4},{4,5},{5,6},{6,7},{7,8},{8,9},{9,10},{10,1... | collective-permute-start | bytes 786440 | tf_op jit(solution)/shard_map/ppermute | solution.py:19
  27.4 9.3 %collective-permute-start.4 = (bf16[512,256]{1,0:T(8,128)(2,1)}, bf16[512,256]{1,0:T(8,128)(2,1)}, u32[]{:S(2)}, u32[]{:S(2)}) collective-permute-start(bf16[512,256]{1,0:T(8,128)(2,1)} %collective-permute-done.2.refs_4_), channel_id=1, source_target_pairs={{0,31},{1,0},{2,1},{3,2},{4,3},{5,4},{6,5},{7,6},{8,7},{9,8},{10,9... | collective-permute-start | bytes 786440 | tf_op jit(solution)/shard_map/ppermute | solution.py:19
  32.0 0.7 copy-start.6
  32.7 10.3 %collective-permute-start.9 = (bf16[512,256]{1,0:T(8,128)(2,1)}, bf16[512,256]{1,0:T(8,128)(2,1)}, u32[]{:S(2)}, u32[]{:S(2)}) collective-permute-start(bf16[512,256]{1,0:T(8,128)(2,1)} %add_convert_fusion.1), channel_id=1, source_target_pairs={{0,32},{32,64},{64,96},{96,128},{128,160},{160,192},{192,224},{224... | collective-permute-start | bytes 786440 | tf_op jit(solution)/shard_map/ppermute | solution.py:19
  36.7 1.0 %copy-start.3 = (f32[512,256]{1,0:T(8,128)S(1)}, f32[512,256]{1,0:T(8,128)}, u32[]{:S(2)}) copy-start(f32[512,256]{1,0:T(8,128)} %copy-done.2) | copy-start | bytes 1572868
  37.8 0.9 %copy-start.5 = (bf16[512,256]{1,0:T(8,128)(2,1)S(1)}, bf16[512,256]{1,0:T(8,128)(2,1)}, u32[]{:S(2)}) copy-start(bf16[512,256]{1,0:T(8,128)(2,1)} %copy-done.4) | copy-start | bytes 786436
  38.7 0.9 %copy-start.7 = (bf16[512,256]{1,0:T(8,128)(2,1)S(1)}, bf16[512,256]{1,0:T(8,128)(2,1)}, u32[]{:S(2)}) copy-start(bf16[512,256]{1,0:T(8,128)(2,1)} %copy-done.6) | copy-start | bytes 786436
  39.7 3.4 %copy-start.1 = (f32[512,256]{1,0:T(8,128)S(1)}, f32[512,256]{1,0:T(8,128)}, u32[]{:S(2)}) copy-start(f32[512,256]{1,0:T(8,128)} %drive_ref.7) | copy-start | bytes 1572868
  45.1 11.2 %collective-permute-start.17 = (bf16[512,256]{1,0:T(8,128)(2,1)S(1)}, bf16[512,256]{1,0:T(8,128)(2,1)S(1)}, u32[]{:S(2)}, u32[]{:S(2)}) collective-permute-start(bf16[512,256]{1,0:T(8,128)(2,1)S(1)} %get-tuple-element.35), channel_id=1, source_target_pairs={{0,31},{1,0},{2,1},{3,2},{4,3},{5,4},{6,5},{7,6},{8,7},{9,8},{10,9... | collective-permute-start | bytes 786440 | tf_op jit(solution)/shard_map/ppermute | solution.py:19
  49.3 8.0 %collective-permute-start.18 = (bf16[512,256]{1,0:T(8,128)(2,1)S(1)}, bf16[512,256]{1,0:T(8,128)(2,1)S(1)}, u32[]{:S(2)}, u32[]{:S(2)}) collective-permute-start(bf16[512,256]{1,0:T(8,128)(2,1)S(1)} %get-tuple-element.36), channel_id=1, source_target_pairs={{0,1},{1,2},{2,3},{3,4},{4,5},{5,6},{6,7},{7,8},{8,9},{9,10},{10,1... | collective-permute-start | bytes 786440 | tf_op jit(solution)/shard_map/ppermute | solution.py:19
  49.9 16.4 %collective-permute-start.12 = (bf16[512,256]{1,0:T(8,128)(2,1)S(1)}, bf16[512,256]{1,0:T(8,128)(2,1)S(1)}, u32[]{:S(2)}, u32[]{:S(2)}) collective-permute-start(bf16[512,256]{1,0:T(8,128)(2,1)S(1)} %get-tuple-element.29.refs_1_), channel_id=1, source_target_pairs={{0,224},{32,0},{64,32},{96,64},{128,96},{160,128},{192,160},{224,1... | collective-permute-start | bytes 786440 | tf_op jit(solution)/shard_map/ppermute | solution.py:19
  52.2 14.2 %collective-permute-start.15 = (bf16[512,256]{1,0:T(8,128)(2,1)S(1)}, bf16[512,256]{1,0:T(8,128)(2,1)S(1)}, u32[]{:S(2)}, u32[]{:S(2)}) collective-permute-start(bf16[512,256]{1,0:T(8,128)(2,1)S(1)} %get-tuple-element.32), channel_id=1, source_target_pairs={{0,31},{1,0},{2,1},{3,2},{4,3},{5,4},{6,5},{7,6},{8,7},{9,8},{10,9... | collective-permute-start | bytes 786440 | tf_op jit(solution)/shard_map/ppermute | solution.py:19
  56.3 13.9 %collective-permute-start.16 = (bf16[512,256]{1,0:T(8,128)(2,1)S(1)}, bf16[512,256]{1,0:T(8,128)(2,1)S(1)}, u32[]{:S(2)}, u32[]{:S(2)}) collective-permute-start(bf16[512,256]{1,0:T(8,128)(2,1)S(1)} %get-tuple-element.33), channel_id=1, source_target_pairs={{0,1},{1,2},{2,3},{3,4},{4,5},{5,6},{6,7},{7,8},{8,9},{9,10},{10,1... | collective-permute-start | bytes 786440 | tf_op jit(solution)/shard_map/ppermute | solution.py:19
  56.3 14.7 %collective-permute-start.10 = (bf16[512,256]{1,0:T(8,128)(2,1)S(1)}, bf16[512,256]{1,0:T(8,128)(2,1)S(1)}, u32[]{:S(2)}, u32[]{:S(2)}) collective-permute-start(bf16[512,256]{1,0:T(8,128)(2,1)S(1)} %get-tuple-element.29.refs_1_), channel_id=1, source_target_pairs={{0,1},{1,2},{2,3},{3,4},{4,5},{5,6},{6,7},{7,8},{8,9},{9,10},{10,1... | collective-permute-start | bytes 786440 | tf_op jit(solution)/shard_map/ppermute | solution.py:19
  57.3 13.7 %collective-permute-start.11 = (bf16[512,256]{1,0:T(8,128)(2,1)S(1)}, bf16[512,256]{1,0:T(8,128)(2,1)S(1)}, u32[]{:S(2)}, u32[]{:S(2)}) collective-permute-start(bf16[512,256]{1,0:T(8,128)(2,1)S(1)} %get-tuple-element.29.refs_1_), channel_id=1, source_target_pairs={{0,31},{1,0},{2,1},{3,2},{4,3},{5,4},{6,5},{7,6},{8,7},{9,8},{10,9... | collective-permute-start | bytes 786440 | tf_op jit(solution)/shard_map/ppermute | solution.py:19
  66.3 7.9 %collective-permute-start.13 = (bf16[512,256]{1,0:T(8,128)(2,1)S(1)}, bf16[512,256]{1,0:T(8,128)(2,1)S(1)}, u32[]{:S(2)}, u32[]{:S(2)}) collective-permute-start(bf16[512,256]{1,0:T(8,128)(2,1)S(1)} %collective-permute-done.12.refs_4_), channel_id=1, source_target_pairs={{0,1},{1,2},{2,3},{3,4},{4,5},{5,6},{6,7},{7,8},{8,9},{9,10},{10,1... | collective-permute-start | bytes 786440 | tf_op jit(solution)/shard_map/ppermute | solution.py:19
  66.3 7.9 %collective-permute-start.14 = (bf16[512,256]{1,0:T(8,128)(2,1)S(1)}, bf16[512,256]{1,0:T(8,128)(2,1)S(1)}, u32[]{:S(2)}, u32[]{:S(2)}) collective-permute-start(bf16[512,256]{1,0:T(8,128)(2,1)S(1)} %collective-permute-done.12.refs_4_), channel_id=1, source_target_pairs={{0,31},{1,0},{2,1},{3,2},{4,3},{5,4},{6,5},{7,6},{8,7},{9,8},{10,9... | collective-permute-start | bytes 786440 | tf_op jit(solution)/shard_map/ppermute | solution.py:19
  70.3 11.4 %collective-permute-start.19 = (bf16[512,256]{1,0:T(8,128)(2,1)S(1)}, bf16[512,256]{1,0:T(8,128)(2,1)S(1)}, u32[]{:S(2)}, u32[]{:S(2)}) collective-permute-start(bf16[512,256]{1,0:T(8,128)(2,1)S(1)} %add_convert_fusion), channel_id=1, source_target_pairs={{0,32},{32,64},{64,96},{96,128},{128,160},{160,192},{192,224},{224... | collective-permute-start | bytes 786440 | tf_op jit(solution)/shard_map/ppermute | solution.py:19

commit v2 on v1

v2 whole, which is shorter than its diff:
```python
import functools

import jax
import jax.numpy as jnp
from jax import lax
from jax.experimental import pallas as pl
from jax.experimental.pallas import tpu as pltpu
from jax.sharding import PartitionSpec as P

SIDE = 64
LANES = 128
ITERS = 2
PIECES = 4
BF16, F32 = jnp.bfloat16, jnp.float32
VMEM = pl.BlockSpec(memory_space=pltpu.VMEM)
HBM = pl.BlockSpec(memory_space=pltpu.HBM)


def log2(n):
    assert n & (n - 1) == 0
    return n.bit_length() - 1


def shifted(value, axis, steps):
    count = lax.axis_size(axis)
    return lax.ppermute(value, axis, [(source, (source + steps) % count) for source in range(count)])


def mate(value):
    return lax.ppermute(value, "rows", [(i, i ^ 1) for i in range(lax.axis_size("rows"))])


def far(value):
    count = lax.axis_size("rows")
    return lax.ppermute(value, "rows", [(i, (i + 1 if i & 1 else i - 1) % count) for i in range(count)])


def call(kernel, outs, flops, args, specs=None, scratch=()):
    if specs:
        args = [pltpu.with_memory_space_constraint(a, pltpu.HBM) for a in args]
    nbytes = sum(a.size * a.dtype.itemsize for a in args)
    return pl.pallas_call(
        kernel,
        out_shape=outs,
        in_specs=specs or [VMEM] * len(args),
        out_specs=jax.tree.map(lambda _: VMEM, outs),
        scratch_shapes=list(scratch),
        cost_estimate=pl.CostEstimate(flops=flops, transcendentals=0, bytes_accessed=nbytes),
        compiler_params=pltpu.CompilerParams(vmem_limit_bytes=5 << 20),
    )(*args)


def dot(a, b):
    return jnp.dot(a, b, preferred_element_type=F32)


def dot_t(a, b):
    return lax.dot_general(a, b, (((0,), (0,)), ((), ())), preferred_element_type=F32)


def interleave(value, scratch_ref, dst_ref):
    count = value.shape[0] // SIDE
    for g in range(value.shape[1] // LANES):
        lanes = slice(g * LANES, (g + 1) * LANES)
        scratch_ref[g] = value[:, lanes]
        for t in range(SIDE // 2):
            pair = [scratch_ref[g, pl.ds(2 * t + h, count, stride=SIDE), :] for h in range(2)]
            dst_ref[2 * t * count : (2 * t + 2) * count, lanes] = jnp.concatenate(pair, axis=0).astype(BF16)


def restored(value, scratch_ref):
    count = value.shape[0] // SIDE
    columns = []
    for g in range(value.shape[1] // LANES):
        scratch_ref[g] = value[:, g * LANES : (g + 1) * LANES]
        columns.append(jnp.concatenate([scratch_ref[g, pl.ds(b, SIDE, stride=count), :] for b in range(count)], axis=0))
    return jnp.concatenate(columns, axis=1)


def build(half, sizes, blocks_hbm, row_hbm, col_hbm, blocks, ids, sems, stores):
    count, row_devs, ka_devs = sizes
    bits, row_bits = log2(count), log2(row_devs)
    copies = [pltpu.make_async_copy(h, ids.at[k : k + 1], sems.at[k]) for k, h in enumerate((row_hbm, col_hbm))]
    width = blocks.shape[1] // PIECES
    for k in range(PIECES):
        lanes = pl.ds(k * width, width)
        copies.append(pltpu.make_async_copy(blocks_hbm.at[:, lanes], blocks.at[:, lanes], sems.at[2 + k]))
    for copy in copies:
        copy.start()
    copies[0].wait()
    copies[1].wait()
    row = ids[0:1, :]
    col = ids[1:2, :]
    row_place = (row >> bits) & (row_devs - 1)
    ka_step = ((col >> (bits + row_bits)) - (row >> (bits + row_bits))) & (ka_devs - 1)
    row_step = (((col >> bits) & (row_devs - 1)) - row_place + 1) & (row_devs - 1)
    is_mate = (row_step >> 1) == ((row_place & 1) ^ 1)
    group = jnp.where(row_step == 1, 0, jnp.where(is_mate, 1, 2))
    band = group * count + (col & (count - 1))
    pairs = 3 * count // 2
    place = ((band & 1) * pairs + (band >> 1)) * count + (row & (count - 1))
    place = jnp.where((row >= 0) & (ka_step == half), place, -1)
    slots = blocks.shape[0]
    chosen = lax.broadcasted_iota(jnp.int32, (2 * pairs * count, slots), 0) == place
    chosen = jnp.where(chosen, 1.0, 0.0).astype(BF16)
    low = lax.broadcasted_iota(jnp.int32, (pairs * count, LANES), 1) < SIDE
    for u in range(SIDE // 4):
        if u % (SIDE // 4 // PIECES) == 0:
            copies[2 + u // (SIDE // 4 // PIECES)].wait()
        found = dot(chosen, blocks[:, u * 2 * LANES : (u + 1) * 2 * LANES])
        for w in range(2):
            t = 2 * u + w
            even = found[: pairs * count, w * LANES : (w + 1) * LANES]
            odd = found[pairs * count :, w * LANES : (w + 1) * LANES]
            first = jnp.where(low, even, pltpu.roll(odd, SIDE, 1))
            second = jnp.where(low, pltpu.roll(even, SIDE, 1), odd)
            for q in range(pairs):
                pair = [v[q * count : (q + 1) * count, :] for v in (first, second)]
                tile = jnp.concatenate(pair, axis=0).astype(BF16)
                per = pairs // 3
                lanes = slice((q % per) * LANES, (q % per + 1) * LANES)
                stores[q // per][2 * t * count : (2 * t + 2) * count, lanes] = tile


def emit(cross, wire, perm_ref, wire_ref, self_ref, mate_ref, far_ref):
    perm = perm_ref[...]
    wire_ref[...] = wire
    self_ref[...] = dot_t(cross[0][...], perm)
    for k, ref in ((2, far_ref), (1, mate_ref)):
        ref[0] = dot_t(cross[k][...], perm).astype(BF16)
        ref[1] = wire


def first_body(sizes, blocks_hbm, row_hbm, col_hbm, drive_hbm, relax_hbm, *refs):
    cross, (perm_ref, wire_ref, self_ref, mate_ref, far_ref, spread_ref) = refs[:3], refs[3:9]
    blocks, ids, drive, relax, scratch, sems = refs[9:]
    later = [
        pltpu.make_async_copy(drive_hbm, drive, sems.at[2 + PIECES]),
        pltpu.make_async_copy(relax_hbm, relax, sems.at[3 + PIECES]),
    ]
    for copy in later:
        copy.start()
    build(1, sizes, blocks_hbm, row_hbm, col_hbm, blocks, ids, sems, cross)
    for copy in later:
        copy.wait()
    spread_ref[...] = jnp.broadcast_to(relax[...], (LANES, relax.shape[1])).T
    field = drive[...]
    interleave(field, scratch, perm_ref)
    emit(cross, field.astype(BF16), perm_ref, wire_ref, self_ref, mate_ref, far_ref)


def second_body(sizes, blocks_hbm, row_hbm, col_hbm, *refs):
    build(0, sizes, blocks_hbm, row_hbm, col_hbm, *refs[3:], refs[:3])


def own_body(*refs):
    mats, sent, (wire_ref, perm_ref, mate_ref, far_ref) = refs[:3], refs[3:5], refs[5:9]
    out_ref, scratch, other = refs[9:]
    total = dot_t(mats[0][...], perm_ref[...])
    straight = dot(mats[0][...], wire_ref[...])
    for k, ref in ((0, mate_ref), (1, far_ref)):
        wire = ref[1]
        interleave(wire.astype(F32), scratch, other)
        straight += dot(mats[k + 1][...], wire)
        total += dot_t(sent[k][...], other[...])
    out_ref[...] = total + restored(straight, scratch)


def new_field(cross, nexts, own_ref, received_ref, drive_ref, relax_ref, scratch):
    straight = dot(cross[0][...], nexts[0][...])
    straight += dot(cross[1][...], nexts[1][...])
    straight += dot(cross[2][...], nexts[2][...])
    product = own_ref[...] + received_ref[...].astype(F32) + restored(straight, scratch)
    scale = jnp.concatenate([relax_ref[...]] * (product.shape[1] // LANES), axis=1)
    return drive_ref[...] + scale * product


def update_body(*refs):
    cross, nexts, rest = refs[:3], refs[3:6], refs[6:10]
    perm_ref, wire_ref, self_ref, mate_ref, far_ref, scratch = refs[10:]
    field = new_field(cross, nexts, *rest, scratch)
    interleave(field, scratch, perm_ref)
    emit(cross, field.astype(BF16), perm_ref, wire_ref, self_ref, mate_ref, far_ref)


def final_body(*refs):
    refs[10][...] = new_field(refs[:3], refs[3:6], *refs[6:10], refs[11])


def local(drive, relax, blocks, row_block, col_block):
    rows, channels = drive.shape
    slots = blocks.shape[0]
    sizes = (rows // SIDE, lax.axis_size("rows"), lax.axis_size("ka"))
    small = jax.ShapeDtypeStruct((rows, channels), BF16)
    double = jax.ShapeDtypeStruct((2, rows, channels), BF16)
    wide = jax.ShapeDtypeStruct((rows, channels), F32)
    matrices = (jax.ShapeDtypeStruct((rows, rows), BF16),) * 3
    emitted = (small, small, wide, double, double)
    staging = pltpu.VMEM((channels // LANES, rows, LANES), F32)
    fetch = [pltpu.VMEM(blocks.shape, BF16), pltpu.VMEM((2, slots), jnp.int32)]
    row2 = row_block.reshape(1, -1)
    col2 = col_block.reshape(1, -1)
    relax2 = relax.reshape(1, -1)
    work = 2 * rows * rows * channels
    spread = jax.ShapeDtypeStruct((rows, LANES), F32)
    *cross, perm, wire, partial, to_mate, to_far, relax3 = call(
        functools.partial(first_body, sizes), (*matrices, *emitted, spread), 9 * work,
        [blocks, row2, col2, drive, relax2], [HBM] * 5,
        fetch + [pltpu.VMEM(drive.shape, F32), pltpu.VMEM((1, rows), F32), staging, pltpu.SemaphoreType.DMA((4 + PIECES,))],
    )
    own = None
    for sweep in range(ITERS):
        down = shifted(wire, "ka", -1)
        from_far = far(to_far)
        from_mate = mate(to_mate)
        if own is None:
            own = call(
                functools.partial(second_body, sizes), matrices, 6 * work, [blocks, row2, col2], [HBM] * 3,
                fetch + [pltpu.SemaphoreType.DMA((2 + PIECES,))],
            )
            sent = [mate(own[1]), far(own[2])]
        got = partial + from_mate[0].astype(F32) + from_far[0].astype(F32)
        received = shifted(got.astype(BF16), "ka", 1)
        nexts = [down, mate(down), far(down)]
        own_product = call(
            own_body, wide, 9 * work, [*own, *sent, wire, perm, from_mate, from_far],
            scratch=[staging, pltpu.VMEM((rows, channels), BF16)],
        )
        args = [*cross, *nexts, own_product, received, drive, relax3]
        if sweep + 1 == ITERS:
            return call(final_body, wide, 3 * work, args, scratch=[staging])
        perm, wire, partial, to_mate, to_far = call(update_body, emitted, 6 * work, args, scratch=[staging])


def solution(mesh):
    spread = P(("ka", "rows"))
    wide = P(("ka", "rows"), None)
    return jax.shard_map(
        local, mesh=mesh, in_specs=(wide, spread, wide, spread, spread), out_specs=wide, check_vma=False
    )
```

time: 82.9 us -> 82.8 us (level)
  the two profiles are of different devices: /device:TPU:2 before, /device:TPU:1 now
where the time goes in v2:
time: 82.8 us; the launch traced here: 82.7 us
  starting transfers between devices  35.2 us (43%)
  waiting for transfers between devices  34.3 us (41%)
  Pallas kernels  12.9 us (16%)
    ppermute x4, waiting for transfers between devices, shifted(): lax.ppermute(value, axis, [(source, (source + steps) % count) for source...  34.2 us
    ppermute x5, starting transfers between devices, mate(): lax.ppermute(value, 'rows', [(i, i ^ 1) for i in range(lax.axis_size('row...  23.3 us
    pallas_call x6, Pallas kernels, call(): pl.pallas_call(kernel, out_shape=outs, in_specs=specs or [VMEM] * len(arg...  12.9 us
    ppermute x4, starting transfers between devices, shifted(): lax.ppermute(value, axis, [(source, (source + steps) % count) for source...  11.1 us
  transfers between devices with their start and end apart: 14, of which 4 were waited for; matrix products, arithmetic and copies ran while one was open for 0% of the time, Pallas kernels for 7%

profile of v2, /device:TPU:1, one launch (start us, length us, event | category | flops | bytes accessed | tf_op | source)
XLA Modules:
  0.0 82.7 jit_solution(8160733612299195232)
XLA Ops:
  0.0 3.7 %shard_map.55 = (bf16[512,512]{1,0:T(8,128)(2,1)S(1)}, bf16[512,512]{1,0:T(8,128)(2,1)S(1)}, bf16[512,512]{1,0:T(8,128)(2,1)S(1)}, bf16[512,256]{1,0:T(8,128)(2,...) custom-call(bf16[256,4096]{1,0:T(8,128)(2,1)} %blocks_hbm.3, ...), custom_call_target="tpu_custom_call" | custom-call | flops 1207959552 | bytes 2625536 | tf_op jit(solution)/shard_map/pallas_call | solution.py:42
  3.7 3.3 %collective-permute-start.5 = (bf16[2,512,256]{2,1,0:T(8,128)(2,1)S(1)}, bf16[2,512,256]{2,1,0:T(8,128)(2,1)S(1)}, u32[]{:S(2)}, u32[]{:S(2)}) collective-permute-start(bf16[2,512,256]{2,1,0:T(8,128)(2,1)S(1)} %get-tuple-element.30), channel_id=1, source_target_pairs={{0,1},{1,0},{2,3},{3,2},{4,5},{5,4},{6,7},{7,6},{8,9},{9,8},{10,11... | collective-permute-start | bytes 1572872 | tf_op jit(solution)/shard_map/ppermute | solution.py:30
  7.1 0.0 collective-permute-start.6
  7.1 5.1 %collective-permute-start = (bf16[512,256]{1,0:T(8,128)(2,1)S(1)}, bf16[512,256]{1,0:T(8,128)(2,1)S(1)}, u32[]{:S(2)}, u32[]{:S(2)}) collective-permute-start(bf16[512,256]{1,0:T(8,128)(2,1)S(1)} %get-tuple-element.25.refs_5_), channel_id=1, source_target_pairs={{0,224},{32,0},{64,32},{96,64},{128,96},{160,128},{192,160},{224,1... | collective-permute-start | bytes 786440 | tf_op jit(solution)/shard_map/ppermute | solution.py:26
  12.2 2.5 %shard_map.56 = (bf16[512,512]{1,0:T(8,128)(2,1)S(1)}, bf16[512,512]{1,0:T(8,128)(2,1)S(1)}, bf16[512,512]{1,0:T(8,128)(2,1)S(1)}) custom-call(bf16[256,4096]{1,0:T(8,128)(2,1)} %blocks_hbm.3, s32[1,256]{1,0:T(1,128)} %bitcast.25, s32[1,256]{1,0:T(1,128)} %bitcast.27), custom_call_target="tpu_custom_call" | custom-call | flops 805306368 | bytes 2099200 | tf_op jit(solution)/shard_map/pallas_call | solution.py:42
  14.7 5.3 %collective-permute-start.3 = (bf16[512,512]{1,0:T(8,128)(2,1)S(1)}, bf16[512,512]{1,0:T(8,128)(2,1)S(1)}, u32[]{:S(2)}, u32[]{:S(2)}) collective-permute-start(bf16[512,512]{1,0:T(8,128)(2,1)S(1)} %get-tuple-element.27.refs_1_), channel_id=1, source_target_pairs={{0,1},{1,0},{2,3},{3,2},{4,5},{5,4},{6,7},{7,6},{8,9},{9,8},{10,11... | collective-permute-start | bytes 1572872 | tf_op jit(solution)/shard_map/ppermute | solution.py:30
  20.0 0.0 collective-permute-start.4
  20.0 0.9 %collective-permute-done.refs_3_ = bf16[512,256]{1,0:T(8,128)(2,1)S(1)} collective-permute-done((bf16[512,256]{1,0:T(8,128)(2,1)S(1)}, bf16[512,256]{1,0:T(8,128)(2,1)S(1)}, u32[]{:S(2)}, u32[]{:S(2)}) %collective-permute-start) | collective-permute-done | bytes 262176 | tf_op jit(solution)/shard_map/ppermute | solution.py:26
  21.0 0.8 collective-permute-start.2
  21.8 0.0 collective-permute-done.5.refs_7_
  21.8 10.7 %collective-permute-start.1 = (bf16[512,256]{1,0:T(8,128)(2,1)S(1)}, bf16[512,256]{1,0:T(8,128)(2,1)S(1)}, u32[]{:S(2)}, u32[]{:S(2)}) collective-permute-start(bf16[512,256]{1,0:T(8,128)(2,1)S(1)} %collective-permute-done.refs_3_), channel_id=1, source_target_pairs={{0,1},{1,0},{2,3},{3,2},{4,5},{5,4},{6,7},{7,6},{8,9},{9,8},{10,11... | collective-permute-start | bytes 786440 | tf_op jit(solution)/shard_map/ppermute | solution.py:30
  32.4 0.0 collective-permute-done.6.refs_8_
  32.5 0.1 fusion.1
  32.5 2.9 %collective-permute-start.7 = (bf16[512,256]{1,0:T(8,128)(2,1)S(1)}, bf16[512,256]{1,0:T(8,128)(2,1)S(1)}, u32[]{:S(2)}, u32[]{:S(2)}) collective-permute-start(bf16[512,256]{1,0:T(8,128)(2,1)S(1)} %fusion.1), channel_id=1, source_target_pairs={{0,32},{32,64},{64,96},{96,128},{128,160},{160,192},{192,224},{224... | collective-permute-start | bytes 786440 | tf_op jit(solution)/shard_map/ppermute | solution.py:26
  35.5 0.0 collective-permute-done.3.refs_3_
  35.5 1.4 %shard_map.57.refs_6_ = f32[512,256]{1,0:T(8,128)S(1)} custom-call(bf16[512,512]{1,0:T(8,128)(2,1)S(1)} %get-tuple-element.26.refs_0_, bf16[512,512]{1,0:T(8,128)(2,1)S(1)} %get-tuple-element.27.refs_1_, bf16[512,512]{1,0:T(8,128)(2,1)S(1)} %get-tuple-element.28.refs_2_, bf16[512,512]{1,0:T(8,128)(2,1)S(1)} %collective-permute-done.3.refs_3_, ...), custom_call_target="tpu_custom_call" | custom-call | flops 1207959552 | bytes 4194304 | tf_op jit(solution)/shard_map/pallas_call | solution.py:42
  36.9 0.0 collective-permute-done.1.refs_4_
  36.9 10.3 %collective-permute-done.7.refs_7_ = bf16[512,256]{1,0:T(8,128)(2,1)S(1)} collective-permute-done((bf16[512,256]{1,0:T(8,128)(2,1)S(1)}, bf16[512,256]{1,0:T(8,128)(2,1)S(1)}, u32[]{:S(2)}, u32[]{:S(2)}) %collective-permute-start.7) | collective-permute-done | bytes 262176 | tf_op jit(solution)/shard_map/ppermute | solution.py:26
  47.3 2.3 %shard_map.58 = (bf16[512,256]{1,0:T(8,128)(2,1)S(1)}, bf16[512,256]{1,0:T(8,128)(2,1)S(1)}, f32[512,256]{1,0:T(8,128)S(1)}, bf16[2,512,256]{2,1,0:T(8,128)(2,1)S(1)}, bf16[2,512,256]{2,1,0:T(8,128)(2,1)S(1)}) custom-call(bf16[512,512]{1,0:T(8,128)(2,1)S(1)} %get-tuple-element.22.refs_0_, bf16[512,512]{1,0:T(8,128)(2,1)S(1)} %get-tuple-element.23.refs_1_, ...), custom_call_target="tpu_custom_call" | custom-call | flops 805306368 | bytes 3932160 | tf_op jit(solution)/shard_map/pallas_call | solution.py:42
  49.6 0.5 collective-permute-start.11
  50.1 0.0 collective-permute-start.12
  50.1 1.6 %collective-permute-start.8 = (bf16[512,256]{1,0:T(8,128)(2,1)S(1)}, bf16[512,256]{1,0:T(8,128)(2,1)S(1)}, u32[]{:S(2)}, u32[]{:S(2)}) collective-permute-start(bf16[512,256]{1,0:T(8,128)(2,1)S(1)} %get-tuple-element.34.refs_5_), channel_id=1, source_target_pairs={{0,224},{32,0},{64,32},{96,64},{128,96},{160,128},{192,160},{224,1... | collective-permute-start | bytes 786440 | tf_op jit(solution)/shard_map/ppermute | solution.py:26
  51.7 11.4 %collective-permute-done.8.refs_3_ = bf16[512,256]{1,0:T(8,128)(2,1)S(1)} collective-permute-done((bf16[512,256]{1,0:T(8,128)(2,1)S(1)}, bf16[512,256]{1,0:T(8,128)(2,1)S(1)}, u32[]{:S(2)}, u32[]{:S(2)}) %collective-permute-start.8) | collective-permute-done | bytes 262176 | tf_op jit(solution)/shard_map/ppermute | solution.py:26
  63.1 3.4 %collective-permute-start.9 = (bf16[512,256]{1,0:T(8,128)(2,1)S(1)}, bf16[512,256]{1,0:T(8,128)(2,1)S(1)}, u32[]{:S(2)}, u32[]{:S(2)}) collective-permute-start(bf16[512,256]{1,0:T(8,128)(2,1)S(1)} %collective-permute-done.8.refs_3_), channel_id=1, source_target_pairs={{0,1},{1,0},{2,3},{3,2},{4,5},{5,4},{6,7},{7,6},{8,9},{9,8},{10,11... | collective-permute-start | bytes 786440 | tf_op jit(solution)/shard_map/ppermute | solution.py:30
  66.5 0.0 collective-permute-done.11.refs_7_
  66.5 0.0 collective-permute-done.12.refs_8_
  66.5 0.1 fusion
  66.6 1.5 %collective-permute-start.13 = (bf16[512,256]{1,0:T(8,128)(2,1)S(1)}, bf16[512,256]{1,0:T(8,128)(2,1)S(1)}, u32[]{:S(2)}, u32[]{:S(2)}) collective-permute-start(bf16[512,256]{1,0:T(8,128)(2,1)S(1)} %fusion), channel_id=1, source_target_pairs={{0,32},{32,64},{64,96},{96,128},{128,160},{160,192},{192,224},{224... | collective-permute-start | bytes 786440 | tf_op jit(solution)/shard_map/ppermute | solution.py:26
  68.1 1.4 %shard_map.59.refs_6_ = f32[512,256]{1,0:T(8,128)S(1)} custom-call(bf16[512,512]{1,0:T(8,128)(2,1)S(1)} %get-tuple-element.26.refs_0_, bf16[512,512]{1,0:T(8,128)(2,1)S(1)} %get-tuple-element.27.refs_1_, bf16[512,512]{1,0:T(8,128)(2,1)S(1)} %get-tuple-element.28.refs_2_, bf16[512,512]{1,0:T(8,128)(2,1)S(1)} %collective-permute-done.3.refs_3_, ...), custom_call_target="tpu_custom_call" | custom-call | flops 1207959552 | bytes 4194304 | tf_op jit(solution)/shard_map/pallas_call | solution.py:42
  69.6 0.0 collective-permute-done.10.refs_5_
  69.6 11.6 %collective-permute-done.13.refs_7_ = bf16[512,256]{1,0:T(8,128)(2,1)S(1)} collective-permute-done((bf16[512,256]{1,0:T(8,128)(2,1)S(1)}, bf16[512,256]{1,0:T(8,128)(2,1)S(1)}, u32[]{:S(2)}, u32[]{:S(2)}) %collective-permute-start.13) | collective-permute-done | bytes 262176 | tf_op jit(solution)/shard_map/ppermute | solution.py:26
  81.2 1.5 %shard_map.60 = f32[512,256]{1,0:T(8,128)} custom-call(bf16[512,512]{1,0:T(8,128)(2,1)S(1)} %get-tuple-element.22.refs_0_, bf16[512,512]{1,0:T(8,128)(2,1)S(1)} %get-tuple-element.23.refs_1_, bf16[512,512]{1,0:T(8,128)(2,1)S(1)} %get-tuple-element.24.refs_2_, bf16[512,256]{1,0:T(8,128)(2,1)S(1)} %collective-permute-done.8.refs_3_, ...), custom_call_target="tpu_custom_call" | custom-call | flops 402653184 | bytes 3932160 | tf_op jit(solution)/shard_map/pallas_call | solution.py:42
  (6 shorter events, 0.0 us)
Async XLA Ops:
  3.7 18.0 %collective-permute-start.5 = (bf16[2,512,256]{2,1,0:T(8,128)(2,1)S(1)}, bf16[2,512,256]{2,1,0:T(8,128)(2,1)S(1)}, u32[]{:S(2)}, u32[]{:S(2)}) collective-permute-start(bf16[2,512,256]{2,1,0:T(8,128)(2,1)S(1)} %get-tuple-element.30), channel_id=1, source_target_pairs={{0,1},{1,0},{2,3},{3,2},{4,5},{5,4},{6,7},{7,6},{8,9},{9,8},{10,11... | collective-permute-start | bytes 1572872 | tf_op jit(solution)/shard_map/ppermute | solution.py:30
  7.1 25.4 %collective-permute-start.6 = (bf16[2,512,256]{2,1,0:T(8,128)(2,1)S(1)}, bf16[2,512,256]{2,1,0:T(8,128)(2,1)S(1)}, u32[]{:S(2)}, u32[]{:S(2)}) collective-permute-start(bf16[2,512,256]{2,1,0:T(8,128)(2,1)S(1)} %get-tuple-element.31), channel_id=1, source_target_pairs={{0,31},{1,2},{2,1},{3,4},{4,3},{5,6},{6,5},{7,8},{8,7},{9,10},{10,... | collective-permute-start | bytes 1572872 | tf_op jit(solution)/shard_map/ppermute | solution.py:35
  7.1 13.9 %collective-permute-start = (bf16[512,256]{1,0:T(8,128)(2,1)S(1)}, bf16[512,256]{1,0:T(8,128)(2,1)S(1)}, u32[]{:S(2)}, u32[]{:S(2)}) collective-permute-start(bf16[512,256]{1,0:T(8,128)(2,1)S(1)} %get-tuple-element.25.refs_5_), channel_id=1, source_target_pairs={{0,224},{32,0},{64,32},{96,64},{128,96},{160,128},{192,160},{224,1... | collective-permute-start | bytes 786440 | tf_op jit(solution)/shard_map/ppermute | solution.py:26
  14.7 20.8 %collective-permute-start.3 = (bf16[512,512]{1,0:T(8,128)(2,1)S(1)}, bf16[512,512]{1,0:T(8,128)(2,1)S(1)}, u32[]{:S(2)}, u32[]{:S(2)}) collective-permute-start(bf16[512,512]{1,0:T(8,128)(2,1)S(1)} %get-tuple-element.27.refs_1_), channel_id=1, source_target_pairs={{0,1},{1,0},{2,3},{3,2},{4,5},{5,4},{6,7},{7,6},{8,9},{9,8},{10,11... | collective-permute-start | bytes 1572872 | tf_op jit(solution)/shard_map/ppermute | solution.py:30
  20.0 15.4 %collective-permute-start.4 = (bf16[512,512]{1,0:T(8,128)(2,1)S(1)}, bf16[512,512]{1,0:T(8,128)(2,1)S(1)}, u32[]{:S(2)}, u32[]{:S(2)}) collective-permute-start(bf16[512,512]{1,0:T(8,128)(2,1)S(1)} %get-tuple-element.28.refs_2_), channel_id=1, source_target_pairs={{0,31},{1,2},{2,1},{3,4},{4,3},{5,6},{6,5},{7,8},{8,7},{9,10},{10,... | collective-permute-start | bytes 1572872 | tf_op jit(solution)/shard_map/ppermute | solution.py:35
  21.0 16.0 %collective-permute-start.2 = (bf16[512,256]{1,0:T(8,128)(2,1)S(1)}, bf16[512,256]{1,0:T(8,128)(2,1)S(1)}, u32[]{:S(2)}, u32[]{:S(2)}) collective-permute-start(bf16[512,256]{1,0:T(8,128)(2,1)S(1)} %collective-permute-done.refs_3_), channel_id=1, source_target_pairs={{0,31},{1,2},{2,1},{3,4},{4,3},{5,6},{6,5},{7,8},{8,7},{9,10},{10,... | collective-permute-start | bytes 786440 | tf_op jit(solution)/shard_map/ppermute | solution.py:35
  21.8 15.1 %collective-permute-start.1 = (bf16[512,256]{1,0:T(8,128)(2,1)S(1)}, bf16[512,256]{1,0:T(8,128)(2,1)S(1)}, u32[]{:S(2)}, u32[]{:S(2)}) collective-permute-start(bf16[512,256]{1,0:T(8,128)(2,1)S(1)} %collective-permute-done.refs_3_), channel_id=1, source_target_pairs={{0,1},{1,0},{2,3},{3,2},{4,5},{5,4},{6,7},{7,6},{8,9},{9,8},{10,11... | collective-permute-start | bytes 786440 | tf_op jit(solution)/shard_map/ppermute | solution.py:30
  32.5 14.7 %collective-permute-start.7 = (bf16[512,256]{1,0:T(8,128)(2,1)S(1)}, bf16[512,256]{1,0:T(8,128)(2,1)S(1)}, u32[]{:S(2)}, u32[]{:S(2)}) collective-permute-start(bf16[512,256]{1,0:T(8,128)(2,1)S(1)} %fusion.1), channel_id=1, source_target_pairs={{0,32},{32,64},{64,96},{96,128},{128,160},{160,192},{192,224},{224... | collective-permute-start | bytes 786440 | tf_op jit(solution)/shard_map/ppermute | solution.py:26
  35.5 11.8 %copy-start = (f32[512,256]{1,0:T(8,128)S(1)}, f32[512,256]{1,0:T(8,128)}, u32[]{:S(2)}) copy-start(f32[512,256]{1,0:T(8,128)} %refs_8_.3) | copy-start | bytes 1572868
  49.6 16.9 %collective-permute-start.11 = (bf16[2,512,256]{2,1,0:T(8,128)(2,1)S(1)}, bf16[2,512,256]{2,1,0:T(8,128)(2,1)S(1)}, u32[]{:S(2)}, u32[]{:S(2)}) collective-permute-start(bf16[2,512,256]{2,1,0:T(8,128)(2,1)S(1)} %get-tuple-element.36), channel_id=1, source_target_pairs={{0,1},{1,0},{2,3},{3,2},{4,5},{5,4},{6,7},{7,6},{8,9},{9,8},{10,11... | collective-permute-start | bytes 1572872 | tf_op jit(solution)/shard_map/ppermute | solution.py:30
  50.1 16.4 %collective-permute-start.12 = (bf16[2,512,256]{2,1,0:T(8,128)(2,1)S(1)}, bf16[2,512,256]{2,1,0:T(8,128)(2,1)S(1)}, u32[]{:S(2)}, u32[]{:S(2)}) collective-permute-start(bf16[2,512,256]{2,1,0:T(8,128)(2,1)S(1)} %get-tuple-element.37), channel_id=1, source_target_pairs={{0,31},{1,2},{2,1},{3,4},{4,3},{5,6},{6,5},{7,8},{8,7},{9,10},{10,... | collective-permute-start | bytes 1572872 | tf_op jit(solution)/shard_map/ppermute | solution.py:35
  50.1 13.0 %collective-permute-start.8 = (bf16[512,256]{1,0:T(8,128)(2,1)S(1)}, bf16[512,256]{1,0:T(8,128)(2,1)S(1)}, u32[]{:S(2)}, u32[]{:S(2)}) collective-permute-start(bf16[512,256]{1,0:T(8,128)(2,1)S(1)} %get-tuple-element.34.refs_5_), channel_id=1, source_target_pairs={{0,224},{32,0},{64,32},{96,64},{128,96},{160,128},{192,160},{224,1... | collective-permute-start | bytes 786440 | tf_op jit(solution)/shard_map/ppermute | solution.py:26
  63.1 6.5 %collective-permute-start.10 = (bf16[512,256]{1,0:T(8,128)(2,1)S(1)}, bf16[512,256]{1,0:T(8,128)(2,1)S(1)}, u32[]{:S(2)}, u32[]{:S(2)}) collective-permute-start(bf16[512,256]{1,0:T(8,128)(2,1)S(1)} %collective-permute-done.8.refs_3_), channel_id=1, source_target_pairs={{0,31},{1,2},{2,1},{3,4},{4,3},{5,6},{6,5},{7,8},{8,7},{9,10},{10,... | collective-permute-start | bytes 786440 | tf_op jit(solution)/shard_map/ppermute | solution.py:35
  63.1 6.5 %collective-permute-start.9 = (bf16[512,256]{1,0:T(8,128)(2,1)S(1)}, bf16[512,256]{1,0:T(8,128)(2,1)S(1)}, u32[]{:S(2)}, u32[]{:S(2)}) collective-permute-start(bf16[512,256]{1,0:T(8,128)(2,1)S(1)} %collective-permute-done.8.refs_3_), channel_id=1, source_target_pairs={{0,1},{1,0},{2,3},{3,2},{4,5},{5,4},{6,7},{7,6},{8,9},{9,8},{10,11... | collective-permute-start | bytes 786440 | tf_op jit(solution)/shard_map/ppermute | solution.py:30
  66.6 14.6 %collective-permute-start.13 = (bf16[512,256]{1,0:T(8,128)(2,1)S(1)}, bf16[512,256]{1,0:T(8,128)(2,1)S(1)}, u32[]{:S(2)}, u32[]{:S(2)}) collective-permute-start(bf16[512,256]{1,0:T(8,128)(2,1)S(1)} %fusion), channel_id=1, source_target_pairs={{0,32},{32,64},{64,96},{96,128},{128,160},{160,192},{192,224},{224... | collective-permute-start | bytes 786440 | tf_op jit(solution)/shard_map/ppermute | solution.py:26

commit v3 on v2

--- a/solution.py
+++ b/solution.py
@@ -153,38 +153,51 @@
     build(0, sizes, blocks_hbm, row_hbm, col_hbm, *refs[3:], refs[:3])
 
 
+def sent_terms(sent, fields, scratch, other):
+    total = 0.0
+    for matrix, field in zip(sent, fields):
+        interleave(field[1].astype(F32), scratch, other)
+        total += dot_t(matrix[...], other[...])
+    return total
+
+
 def own_body(*refs):
-    mats, sent, (wire_ref, perm_ref, mate_ref, far_ref) = refs[:3], refs[3:5], refs[5:9]
-    out_ref, scratch, other = refs[9:]
+    mats, (wire_ref, perm_ref, mate_ref, far_ref), sent = refs[:3], refs[3:7], refs[7:-3]
+    out_ref, scratch, other = refs[-3:]
     total = dot_t(mats[0][...], perm_ref[...])
     straight = dot(mats[0][...], wire_ref[...])
-    for k, ref in ((0, mate_ref), (1, far_ref)):
-        wire = ref[1]
-        interleave(wire.astype(F32), scratch, other)
-        straight += dot(mats[k + 1][...], wire)
-        total += dot_t(sent[k][...], other[...])
+    straight += dot(mats[1][...], mate_ref[1])
+    straight += dot(mats[2][...], far_ref[1])
+    if sent:
+        total += sent_terms(sent, (mate_ref, far_ref), scratch, other)
     out_ref[...] = total + restored(straight, scratch)
 
 
-def new_field(cross, nexts, own_ref, received_ref, drive_ref, relax_ref, scratch):
+def new_field(cross, nexts, own, drive_ref, relax_ref, scratch):
     straight = dot(cross[0][...], nexts[0][...])
     straight += dot(cross[1][...], nexts[1][...])
     straight += dot(cross[2][...], nexts[2][...])
-    product = own_ref[...] + received_ref[...].astype(F32) + restored(straight, scratch)
+    product = own + restored(straight, scratch)
     scale = jnp.concatenate([relax_ref[...]] * (product.shape[1] // LANES), axis=1)
     return drive_ref[...] + scale * product
 
 
 def update_body(*refs):
-    cross, nexts, rest = refs[:3], refs[3:6], refs[6:10]
-    perm_ref, wire_ref, self_ref, mate_ref, far_ref, scratch = refs[10:]
-    field = new_field(cross, nexts, *rest, scratch)
+    cross, nexts, rest, (mate_in, far_in), sent = refs[:3], refs[3:6], refs[6:9], refs[9:11], refs[11:13]
+    perm_ref, wire_ref, self_ref, mate_ref, far_ref, scratch, other = refs[13:]
+    drive_ref, relax_ref = rest[1:]
+    late = sent_terms(sent, (mate_in, far_in), scratch, other)
+    field = new_field(cross, nexts, rest[0][...] + late, drive_ref, relax_ref, scratch)
     interleave(field, scratch, perm_ref)
     emit(cross, field.astype(BF16), perm_ref, wire_ref, self_ref, mate_ref, far_ref)
 
 
+def settle_body(own_ref, received_ref, out_ref):
+    out_ref[...] = own_ref[...] + received_ref[...].astype(F32)
+
+
 def final_body(*refs):
-    refs[10][...] = new_field(refs[:3], refs[3:6], *refs[6:10], refs[11])
+    refs[9][...] = new_field(refs[:3], refs[3:6], refs[6][...], *refs[7:9], refs[10])
 
 
 def local(drive, relax, blocks, row_block, col_block):
@@ -208,28 +221,30 @@
         [blocks, row2, col2, drive, relax2], [HBM] * 5,
         fetch + [pltpu.VMEM(drive.shape, F32), pltpu.VMEM((1, rows), F32), staging, pltpu.SemaphoreType.DMA((4 + PIECES,))],
     )
-    own = None
+
+    extra = [staging, pltpu.VMEM((rows, channels), BF16)]
     for sweep in range(ITERS):
         down = shifted(wire, "ka", -1)
         from_far = far(to_far)
         from_mate = mate(to_mate)
-        if own is None:
+        if sweep == 0:
             own = call(
                 functools.partial(second_body, sizes), matrices, 6 * work, [blocks, row2, col2], [HBM] * 3,
                 fetch + [pltpu.SemaphoreType.DMA((2 + PIECES,))],
             )
-            sent = [mate(own[1]), far(own[2])]
-        got = partial + from_mate[0].astype(F32) + from_far[0].astype(F32)
-        received = shifted(got.astype(BF16), "ka", 1)
+        got = (partial + from_mate[0].astype(F32) + from_far[0].astype(F32)).astype(BF16)
+        received = shifted(got, "ka", 1)
         nexts = [down, mate(down), far(down)]
-        own_product = call(
-            own_body, wide, 9 * work, [*own, *sent, wire, perm, from_mate, from_far],
-            scratch=[staging, pltpu.VMEM((rows, channels), BF16)],
-        )
-        args = [*cross, *nexts, own_product, received, drive, relax3]
+        if sweep == 0:
+            gated, _ = lax.optimization_barrier((own[1:], down))
+            sent = [mate(gated[0]), far(gated[1])]
+        args = [*own, wire, perm, from_mate, from_far, *(sent if sweep else [])]
+        own_product = call(own_body, wide, 9 * work, args, scratch=extra)
+        own_product = call(settle_body, wide, 90 * work, [own_product, received])
+        args = [*cross, *nexts, own_product, drive, relax3]
         if sweep + 1 == ITERS:
             return call(final_body, wide, 3 * work, args, scratch=[staging])
-        perm, wire, partial, to_mate, to_far = call(update_body, emitted, 6 * work, args, scratch=[staging])
+        perm, wire, partial, to_mate, to_far = call(update_body, emitted, 8 * work, [*args, from_mate, from_far, *sent], scratch=extra)
 
 
 def solution(mesh):

time: 82.8 us -> 68.2 us (0.82)
  the two profiles are of different devices: /device:TPU:1 before, /device:TPU:6 now
where the time goes in v3:
time: 68.2 us; the launch traced here: 68.1 us
  waiting for transfers between devices  33.8 us (50%)
  starting transfers between devices  20.9 us (31%)
  Pallas kernels  13.1 us (19%)
    ppermute x5, waiting for transfers between devices, far(): lax.ppermute(value, 'rows', [(i, (i + 1 if i & 1 else i - 1) % count) for...  22.7 us
    ppermute x5, starting transfers between devices, far(): lax.ppermute(value, 'rows', [(i, (i + 1 if i & 1 else i - 1) % count) for...  14.9 us
    pallas_call x8, Pallas kernels, call(): pl.pallas_call(kernel, out_shape=outs, in_specs=specs or [VMEM] * len(arg...  13.1 us
    ppermute x4, waiting for transfers between devices, shifted(): lax.ppermute(value, axis, [(source, (source + steps) % count) for source...  11.1 us
    ppermute x4, starting transfers between devices, shifted(): lax.ppermute(value, axis, [(source, (source + steps) % count) for source...  5.88 us
  transfers between devices with their start and end apart: 14, of which 7 were waited for; matrix products, arithmetic and copies ran while one was open for 0% of the time, Pallas kernels for 8%

profile of v3, /device:TPU:6, one launch (start us, length us, event | category | flops | bytes accessed | tf_op | source)
XLA Modules:
  0.0 68.1 jit_solution(16707476040130935213)
XLA Ops:
  0.0 3.7 %shard_map.55 = (bf16[512,512]{1,0:T(8,128)(2,1)S(1)}, bf16[512,512]{1,0:T(8,128)(2,1)S(1)}, bf16[512,512]{1,0:T(8,128)(2,1)S(1)}, bf16[512,256]{1,0:T(8,128)(2,...) custom-call(bf16[256,4096]{1,0:T(8,128)(2,1)} %blocks_hbm.3, ...), custom_call_target="tpu_custom_call" | custom-call | flops 1207959552 | bytes 2625536 | tf_op jit(solution)/shard_map/pallas_call | solution.py:42
  3.7 0.1 collective-permute-start.3
  3.8 6.2 %collective-permute-start.4 = (bf16[2,512,256]{2,1,0:T(8,128)(2,1)S(1)}, bf16[2,512,256]{2,1,0:T(8,128)(2,1)S(1)}, u32[]{:S(2)}, u32[]{:S(2)}) collective-permute-start(bf16[2,512,256]{2,1,0:T(8,128)(2,1)S(1)} %get-tuple-element.33), channel_id=1, source_target_pairs={{0,31},{1,2},{2,1},{3,4},{4,3},{5,6},{6,5},{7,8},{8,7},{9,10},{10,... | collective-permute-start | bytes 1572872 | tf_op jit(solution)/shard_map/ppermute | solution.py:35
  10.0 1.1 %collective-permute-start = (bf16[512,256]{1,0:T(8,128)(2,1)S(1)}, bf16[512,256]{1,0:T(8,128)(2,1)S(1)}, u32[]{:S(2)}, u32[]{:S(2)}) collective-permute-start(bf16[512,256]{1,0:T(8,128)(2,1)S(1)} %get-tuple-element.27.refs_3_), channel_id=1, source_target_pairs={{0,224},{32,0},{64,32},{96,64},{128,96},{160,128},{192,160},{224,1... | collective-permute-start | bytes 786440 | tf_op jit(solution)/shard_map/ppermute | solution.py:26
  11.2 0.0 collective-permute-done.3.refs_5_.refs_9_
  11.2 5.8 %collective-permute-done.4.refs_6_.refs_10_ = bf16[2,512,256]{2,1,0:T(8,128)(2,1)S(1)} collective-permute-done((bf16[2,512,256]{2,1,0:T(8,128)(2,1)S(1)}, bf16[2,512,256]{2,1,0:T(8,128)(2,1)S(1)}, u32[]{:S(2)}, u32[]{:S(2)}) %collective-permute-start.4) | collective-permute-done | bytes 524320 | tf_op jit(solution)/shard_map/ppermute | solution.py:35
  17.0 0.1 fusion.1
  17.1 2.2 %collective-permute-start.5 = (bf16[512,256]{1,0:T(8,128)(2,1)S(1)}, bf16[512,256]{1,0:T(8,128)(2,1)S(1)}, u32[]{:S(2)}, u32[]{:S(2)}) collective-permute-start(bf16[512,256]{1,0:T(8,128)(2,1)S(1)} %fusion.1), channel_id=1, source_target_pairs={{0,32},{32,64},{64,96},{96,128},{128,160},{160,192},{192,224},{224... | collective-permute-start | bytes 786440 | tf_op jit(solution)/shard_map/ppermute | solution.py:26
  19.3 2.5 %shard_map.56 = (bf16[512,512]{1,0:T(8,128)(2,1)S(1)}, bf16[512,512]{1,0:T(8,128)(2,1)S(1)}, bf16[512,512]{1,0:T(8,128)(2,1)S(1)}) custom-call(bf16[256,4096]{1,0:T(8,128)(2,1)} %blocks_hbm.3, s32[1,256]{1,0:T(1,128)} %bitcast.25, s32[1,256]{1,0:T(1,128)} %bitcast.27), custom_call_target="tpu_custom_call" | custom-call | flops 805306368 | bytes 2099200 | tf_op jit(solution)/shard_map/pallas_call | solution.py:42
  21.8 2.4 %collective-permute-done.refs_3_ = bf16[512,256]{1,0:T(8,128)(2,1)S(1)} collective-permute-done((bf16[512,256]{1,0:T(8,128)(2,1)S(1)}, bf16[512,256]{1,0:T(8,128)(2,1)S(1)}, u32[]{:S(2)}, u32[]{:S(2)}) %collective-permute-start) | collective-permute-done | bytes 262176 | tf_op jit(solution)/shard_map/ppermute | solution.py:26
  24.3 0.0 collective-permute-start.6
  24.3 2.6 %collective-permute-start.7 = (bf16[512,512]{1,0:T(8,128)(2,1)S(1)}, bf16[512,512]{1,0:T(8,128)(2,1)S(1)}, u32[]{:S(2)}, u32[]{:S(2)}) collective-permute-start(bf16[512,512]{1,0:T(8,128)(2,1)S(1)} %get-tuple-element.37.refs_2_), channel_id=1, source_target_pairs={{0,31},{1,2},{2,1},{3,4},{4,3},{5,6},{6,5},{7,8},{8,7},{9,10},{10,... | collective-permute-start | bytes 1572872 | tf_op jit(solution)/shard_map/ppermute | solution.py:35
  26.8 1.3 %collective-permute-start.2 = (bf16[512,256]{1,0:T(8,128)(2,1)S(1)}, bf16[512,256]{1,0:T(8,128)(2,1)S(1)}, u32[]{:S(2)}, u32[]{:S(2)}) collective-permute-start(bf16[512,256]{1,0:T(8,128)(2,1)S(1)} %collective-permute-done.refs_3_), channel_id=1, source_target_pairs={{0,31},{1,2},{2,1},{3,4},{4,3},{5,6},{6,5},{7,8},{8,7},{9,10},{10,... | collective-permute-start | bytes 786440 | tf_op jit(solution)/shard_map/ppermute | solution.py:35
  28.1 0.0 collective-permute-start.1
  28.1 0.8 %shard_map.57.own_ref = f32[512,256]{1,0:T(8,128)S(1)} custom-call(bf16[512,512]{1,0:T(8,128)(2,1)S(1)} %get-tuple-element.28.refs_0_, bf16[512,512]{1,0:T(8,128)(2,1)S(1)} %get-tuple-element.36.refs_1_, bf16[512,512]{1,0:T(8,128)(2,1)S(1)} %get-tuple-element.37.refs_2_, bf16[512,256]{1,0:T(8,128)(2,1)S(1)} %get-tuple-element.27.refs_3_, ...), custom_call_target="tpu_custom_call" | custom-call | flops 1207959552 | bytes 3145728 | tf_op jit(solution)/shard_map/pallas_call | solution.py:42
  28.9 0.0 copy-start
  29.0 8.8 %collective-permute-done.2.refs_5_ = bf16[512,256]{1,0:T(8,128)(2,1)S(1)} collective-permute-done((bf16[512,256]{1,0:T(8,128)(2,1)S(1)}, bf16[512,256]{1,0:T(8,128)(2,1)S(1)}, u32[]{:S(2)}, u32[]{:S(2)}) %collective-permute-start.2) | collective-permute-done | bytes 262176 | tf_op jit(solution)/shard_map/ppermute | solution.py:35
  37.8 0.0 collective-permute-done.7.refs_12_.refs_8_
  37.8 2.8 %shard_map.59 = (bf16[512,256]{1,0:T(8,128)(2,1)S(1)}, bf16[512,256]{1,0:T(8,128)(2,1)S(1)}, f32[512,256]{1,0:T(8,128)S(1)}, bf16[2,512,256]{2,1,0:T(8,128)(2,1)S(1)}, bf16[2,512,256]{2,1,0:T(8,128)(2,1)S(1)}) custom-call(bf16[512,512]{1,0:T(8,128)(2,1)S(1)} %get-tuple-element.24.refs_0_, bf16[512,512]{1,0:T(8,128)(2,1)S(1)} %get-tuple-element.25.refs_1_, ...), custom_call_target="tpu_custom_call" | custom-call | flops 1073741824 | bytes 5767168 | tf_op jit(solution)/shard_map/pallas_call | solution.py:42
  40.6 0.1 collective-permute-start.11
  40.7 3.3 %collective-permute-start.12 = (bf16[2,512,256]{2,1,0:T(8,128)(2,1)S(1)}, bf16[2,512,256]{2,1,0:T(8,128)(2,1)S(1)}, u32[]{:S(2)}, u32[]{:S(2)}) collective-permute-start(bf16[2,512,256]{2,1,0:T(8,128)(2,1)S(1)} %get-tuple-element.41), channel_id=1, source_target_pairs={{0,31},{1,2},{2,1},{3,4},{4,3},{5,6},{6,5},{7,8},{8,7},{9,10},{10,... | collective-permute-start | bytes 1572872 | tf_op jit(solution)/shard_map/ppermute | solution.py:35
  44.1 0.4 collective-permute-start.8
  44.4 0.0 collective-permute-done.11.refs_5_
  44.4 7.4 %collective-permute-done.12.refs_6_ = bf16[2,512,256]{2,1,0:T(8,128)(2,1)S(1)} collective-permute-done((bf16[2,512,256]{2,1,0:T(8,128)(2,1)S(1)}, bf16[2,512,256]{2,1,0:T(8,128)(2,1)S(1)}, u32[]{:S(2)}, u32[]{:S(2)}) %collective-permute-start.12) | collective-permute-done | bytes 524320 | tf_op jit(solution)/shard_map/ppermute | solution.py:35
  51.8 0.1 fusion
  51.9 2.2 %collective-permute-start.13 = (bf16[512,256]{1,0:T(8,128)(2,1)S(1)}, bf16[512,256]{1,0:T(8,128)(2,1)S(1)}, u32[]{:S(2)}, u32[]{:S(2)}) collective-permute-start(bf16[512,256]{1,0:T(8,128)(2,1)S(1)} %fusion), channel_id=1, source_target_pairs={{0,32},{32,64},{64,96},{96,128},{128,160},{160,192},{192,224},{224... | collective-permute-start | bytes 786440 | tf_op jit(solution)/shard_map/ppermute | solution.py:26
  54.1 4.7 %collective-permute-done.8.refs_3_ = bf16[512,256]{1,0:T(8,128)(2,1)S(1)} collective-permute-done((bf16[512,256]{1,0:T(8,128)(2,1)S(1)}, bf16[512,256]{1,0:T(8,128)(2,1)S(1)}, u32[]{:S(2)}, u32[]{:S(2)}) %collective-permute-start.8) | collective-permute-done | bytes 262176 | tf_op jit(solution)/shard_map/ppermute | solution.py:26
  58.8 1.4 %collective-permute-start.10 = (bf16[512,256]{1,0:T(8,128)(2,1)S(1)}, bf16[512,256]{1,0:T(8,128)(2,1)S(1)}, u32[]{:S(2)}, u32[]{:S(2)}) collective-permute-start(bf16[512,256]{1,0:T(8,128)(2,1)S(1)} %collective-permute-done.8.refs_3_), channel_id=1, source_target_pairs={{0,31},{1,2},{2,1},{3,4},{4,3},{5,6},{6,5},{7,8},{8,7},{9,10},{10,... | collective-permute-start | bytes 786440 | tf_op jit(solution)/shard_map/ppermute | solution.py:35
  60.2 1.8 %shard_map.60.own_ref = f32[512,256]{1,0:T(8,128)S(1)} custom-call(bf16[512,512]{1,0:T(8,128)(2,1)S(1)} %get-tuple-element.28.refs_0_, bf16[512,512]{1,0:T(8,128)(2,1)S(1)} %get-tuple-element.36.refs_1_, bf16[512,512]{1,0:T(8,128)(2,1)S(1)} %get-tuple-element.37.refs_2_, bf16[512,256]{1,0:T(8,128)(2,1)S(1)} %get-tuple-element.38.refs_3_, ...), custom_call_target="tpu_custom_call" | custom-call | flops 1207959552 | bytes 4194304 | tf_op jit(solution)/shard_map/pallas_call | solution.py:42
  62.0 4.0 %collective-permute-done.13.received_ref = bf16[512,256]{1,0:T(8,128)(2,1)S(1)} collective-permute-done((bf16[512,256]{1,0:T(8,128)(2,1)S(1)}, bf16[512,256]{1,0:T(8,128)(2,1)S(1)}, u32[]{:S(2)}, u32[]{:S(2)}) %collective-permute-start.13) | collective-permute-done | bytes 262176 | tf_op jit(solution)/shard_map/ppermute | solution.py:26
  66.1 0.6 collective-permute-done.10.refs_5_
  66.7 1.4 %shard_map.62 = f32[512,256]{1,0:T(8,128)} custom-call(bf16[512,512]{1,0:T(8,128)(2,1)S(1)} %get-tuple-element.24.refs_0_, bf16[512,512]{1,0:T(8,128)(2,1)S(1)} %get-tuple-element.25.refs_1_, bf16[512,512]{1,0:T(8,128)(2,1)S(1)} %get-tuple-element.26.refs_2_, bf16[512,256]{1,0:T(8,128)(2,1)S(1)} %collective-permute-done.8.refs_3_, ...), custom_call_target="tpu_custom_call" | custom-call | flops 402653184 | bytes 3670016 | tf_op jit(solution)/shard_map/pallas_call | solution.py:42
  (8 shorter events, 0.1 us)
Async XLA Ops:
  3.7 7.4 %collective-permute-start.3 = (bf16[2,512,256]{2,1,0:T(8,128)(2,1)S(1)}, bf16[2,512,256]{2,1,0:T(8,128)(2,1)S(1)}, u32[]{:S(2)}, u32[]{:S(2)}) collective-permute-start(bf16[2,512,256]{2,1,0:T(8,128)(2,1)S(1)} %get-tuple-element.32), channel_id=1, source_target_pairs={{0,1},{1,0},{2,3},{3,2},{4,5},{5,4},{6,7},{7,6},{8,9},{9,8},{10,11... | collective-permute-start | bytes 1572872 | tf_op jit(solution)/shard_map/ppermute | solution.py:30
  3.8 13.2 %collective-permute-start.4 = (bf16[2,512,256]{2,1,0:T(8,128)(2,1)S(1)}, bf16[2,512,256]{2,1,0:T(8,128)(2,1)S(1)}, u32[]{:S(2)}, u32[]{:S(2)}) collective-permute-start(bf16[2,512,256]{2,1,0:T(8,128)(2,1)S(1)} %get-tuple-element.33), channel_id=1, source_target_pairs={{0,31},{1,2},{2,1},{3,4},{4,3},{5,6},{6,5},{7,8},{8,7},{9,10},{10,... | collective-permute-start | bytes 1572872 | tf_op jit(solution)/shard_map/ppermute | solution.py:35
  10.0 14.2 %collective-permute-start = (bf16[512,256]{1,0:T(8,128)(2,1)S(1)}, bf16[512,256]{1,0:T(8,128)(2,1)S(1)}, u32[]{:S(2)}, u32[]{:S(2)}) collective-permute-start(bf16[512,256]{1,0:T(8,128)(2,1)S(1)} %get-tuple-element.27.refs_3_), channel_id=1, source_target_pairs={{0,224},{32,0},{64,32},{96,64},{128,96},{160,128},{192,160},{224,1... | collective-permute-start | bytes 786440 | tf_op jit(solution)/shard_map/ppermute | solution.py:26
  17.1 11.8 %collective-permute-start.5 = (bf16[512,256]{1,0:T(8,128)(2,1)S(1)}, bf16[512,256]{1,0:T(8,128)(2,1)S(1)}, u32[]{:S(2)}, u32[]{:S(2)}) collective-permute-start(bf16[512,256]{1,0:T(8,128)(2,1)S(1)} %fusion.1), channel_id=1, source_target_pairs={{0,32},{32,64},{64,96},{96,128},{128,160},{160,192},{192,224},{224... | collective-permute-start | bytes 786440 | tf_op jit(solution)/shard_map/ppermute | solution.py:26
  24.3 13.5 %collective-permute-start.6 = (bf16[512,512]{1,0:T(8,128)(2,1)S(1)}, bf16[512,512]{1,0:T(8,128)(2,1)S(1)}, u32[]{:S(2)}, u32[]{:S(2)}) collective-permute-start(bf16[512,512]{1,0:T(8,128)(2,1)S(1)} %get-tuple-element.36.refs_1_), channel_id=1, source_target_pairs={{0,1},{1,0},{2,3},{3,2},{4,5},{5,4},{6,7},{7,6},{8,9},{9,8},{10,11... | collective-permute-start | bytes 1572872 | tf_op jit(solution)/shard_map/ppermute | solution.py:30
  24.3 13.5 %collective-permute-start.7 = (bf16[512,512]{1,0:T(8,128)(2,1)S(1)}, bf16[512,512]{1,0:T(8,128)(2,1)S(1)}, u32[]{:S(2)}, u32[]{:S(2)}) collective-permute-start(bf16[512,512]{1,0:T(8,128)(2,1)S(1)} %get-tuple-element.37.refs_2_), channel_id=1, source_target_pairs={{0,31},{1,2},{2,1},{3,4},{4,3},{5,6},{6,5},{7,8},{8,7},{9,10},{10,... | collective-permute-start | bytes 1572872 | tf_op jit(solution)/shard_map/ppermute | solution.py:35
  26.8 10.9 %collective-permute-start.2 = (bf16[512,256]{1,0:T(8,128)(2,1)S(1)}, bf16[512,256]{1,0:T(8,128)(2,1)S(1)}, u32[]{:S(2)}, u32[]{:S(2)}) collective-permute-start(bf16[512,256]{1,0:T(8,128)(2,1)S(1)} %collective-permute-done.refs_3_), channel_id=1, source_target_pairs={{0,31},{1,2},{2,1},{3,4},{4,3},{5,6},{6,5},{7,8},{8,7},{9,10},{10,... | collective-permute-start | bytes 786440 | tf_op jit(solution)/shard_map/ppermute | solution.py:35
  28.1 9.7 %collective-permute-start.1 = (bf16[512,256]{1,0:T(8,128)(2,1)S(1)}, bf16[512,256]{1,0:T(8,128)(2,1)S(1)}, u32[]{:S(2)}, u32[]{:S(2)}) collective-permute-start(bf16[512,256]{1,0:T(8,128)(2,1)S(1)} %collective-permute-done.refs_3_), channel_id=1, source_target_pairs={{0,1},{1,0},{2,3},{3,2},{4,5},{5,4},{6,7},{7,6},{8,9},{9,8},{10,11... | collective-permute-start | bytes 786440 | tf_op jit(solution)/shard_map/ppermute | solution.py:30
  28.9 8.9 %copy-start = (f32[512,256]{1,0:T(8,128)S(1)}, f32[512,256]{1,0:T(8,128)}, u32[]{:S(2)}) copy-start(f32[512,256]{1,0:T(8,128)} %refs_7_.3) | copy-start | bytes 1572868
  40.6 3.8 %collective-permute-start.11 = (bf16[2,512,256]{2,1,0:T(8,128)(2,1)S(1)}, bf16[2,512,256]{2,1,0:T(8,128)(2,1)S(1)}, u32[]{:S(2)}, u32[]{:S(2)}) collective-permute-start(bf16[2,512,256]{2,1,0:T(8,128)(2,1)S(1)} %get-tuple-element.40), channel_id=1, source_target_pairs={{0,1},{1,0},{2,3},{3,2},{4,5},{5,4},{6,7},{7,6},{8,9},{9,8},{10,11... | collective-permute-start | bytes 1572872 | tf_op jit(solution)/shard_map/ppermute | solution.py:30
  40.7 11.1 %collective-permute-start.12 = (bf16[2,512,256]{2,1,0:T(8,128)(2,1)S(1)}, bf16[2,512,256]{2,1,0:T(8,128)(2,1)S(1)}, u32[]{:S(2)}, u32[]{:S(2)}) collective-permute-start(bf16[2,512,256]{2,1,0:T(8,128)(2,1)S(1)} %get-tuple-element.41), channel_id=1, source_target_pairs={{0,31},{1,2},{2,1},{3,4},{4,3},{5,6},{6,5},{7,8},{8,7},{9,10},{10,... | collective-permute-start | bytes 1572872 | tf_op jit(solution)/shard_map/ppermute | solution.py:35
  44.1 14.7 %collective-permute-start.8 = (bf16[512,256]{1,0:T(8,128)(2,1)S(1)}, bf16[512,256]{1,0:T(8,128)(2,1)S(1)}, u32[]{:S(2)}, u32[]{:S(2)}) collective-permute-start(bf16[512,256]{1,0:T(8,128)(2,1)S(1)} %get-tuple-element.38.refs_3_), channel_id=1, source_target_pairs={{0,224},{32,0},{64,32},{96,64},{128,96},{160,128},{192,160},{224,1... | collective-permute-start | bytes 786440 | tf_op jit(solution)/shard_map/ppermute | solution.py:26
  51.9 14.1 %collective-permute-start.13 = (bf16[512,256]{1,0:T(8,128)(2,1)S(1)}, bf16[512,256]{1,0:T(8,128)(2,1)S(1)}, u32[]{:S(2)}, u32[]{:S(2)}) collective-permute-start(bf16[512,256]{1,0:T(8,128)(2,1)S(1)} %fusion), channel_id=1, source_target_pairs={{0,32},{32,64},{64,96},{96,128},{128,160},{160,192},{192,224},{224... | collective-permute-start | bytes 786440 | tf_op jit(solution)/shard_map/ppermute | solution.py:26
  58.8 7.9 %collective-permute-start.10 = (bf16[512,256]{1,0:T(8,128)(2,1)S(1)}, bf16[512,256]{1,0:T(8,128)(2,1)S(1)}, u32[]{:S(2)}, u32[]{:S(2)}) collective-permute-start(bf16[512,256]{1,0:T(8,128)(2,1)S(1)} %collective-permute-done.8.refs_3_), channel_id=1, source_target_pairs={{0,31},{1,2},{2,1},{3,4},{4,3},{5,6},{6,5},{7,8},{8,7},{9,10},{10,... | collective-permute-start | bytes 786440 | tf_op jit(solution)/shard_map/ppermute | solution.py:35
  60.2 6.5 %collective-permute-start.9 = (bf16[512,256]{1,0:T(8,128)(2,1)S(1)}, bf16[512,256]{1,0:T(8,128)(2,1)S(1)}, u32[]{:S(2)}, u32[]{:S(2)}) collective-permute-start(bf16[512,256]{1,0:T(8,128)(2,1)S(1)} %collective-permute-done.8.refs_3_), channel_id=1, source_target_pairs={{0,1},{1,0},{2,3},{3,2},{4,5},{5,4},{6,7},{7,6},{8,9},{9,8},{10,11... | collective-permute-start | bytes 786440 | tf_op jit(solution)/shard_map/ppermute | solution.py:30

commit v4 on v3

--- a/solution.py
+++ b/solution.py
@@ -11,6 +11,7 @@
 LANES = 128
 ITERS = 2
 PIECES = 4
+HEAVY = 90
 BF16, F32 = jnp.bfloat16, jnp.float32
 VMEM = pl.BlockSpec(memory_space=pltpu.VMEM)
 HBM = pl.BlockSpec(memory_space=pltpu.HBM)
@@ -173,21 +174,27 @@
     out_ref[...] = total + restored(straight, scratch)
 
 
-def new_field(cross, nexts, own, drive_ref, relax_ref, scratch):
+def with_cross(cross, nexts, known_ref, scratch):
     straight = dot(cross[0][...], nexts[0][...])
     straight += dot(cross[1][...], nexts[1][...])
     straight += dot(cross[2][...], nexts[2][...])
-    product = own + restored(straight, scratch)
+    return known_ref[...] + restored(straight, scratch)
+
+
+def advanced(product, drive_ref, relax_ref):
     scale = jnp.concatenate([relax_ref[...]] * (product.shape[1] // LANES), axis=1)
     return drive_ref[...] + scale * product
 
 
+def cross_body(*refs):
+    refs[7][...] = with_cross(refs[:3], refs[3:6], refs[6], refs[8])
+
+
 def update_body(*refs):
-    cross, nexts, rest, (mate_in, far_in), sent = refs[:3], refs[3:6], refs[6:9], refs[9:11], refs[11:13]
-    perm_ref, wire_ref, self_ref, mate_ref, far_ref, scratch, other = refs[13:]
-    drive_ref, relax_ref = rest[1:]
+    cross, (known_ref, drive_ref, relax_ref, mate_in, far_in), sent = refs[:3], refs[3:8], refs[8:10]
+    perm_ref, wire_ref, self_ref, mate_ref, far_ref, scratch, other = refs[10:]
     late = sent_terms(sent, (mate_in, far_in), scratch, other)
-    field = new_field(cross, nexts, rest[0][...] + late, drive_ref, relax_ref, scratch)
+    field = advanced(known_ref[...] + late, drive_ref, relax_ref)
     interleave(field, scratch, perm_ref)
     emit(cross, field.astype(BF16), perm_ref, wire_ref, self_ref, mate_ref, far_ref)
 
@@ -197,7 +204,8 @@
 
 
 def final_body(*refs):
-    refs[9][...] = new_field(refs[:3], refs[3:6], refs[6][...], *refs[7:9], refs[10])
+    product = with_cross(refs[:3], refs[3:6], refs[6], refs[10])
+    refs[9][...] = advanced(product, *refs[7:9])
 
 
 def local(drive, relax, blocks, row_block, col_block):
@@ -232,19 +240,22 @@
                 functools.partial(second_body, sizes), matrices, 6 * work, [blocks, row2, col2], [HBM] * 3,
                 fetch + [pltpu.SemaphoreType.DMA((2 + PIECES,))],
             )
+        if sweep == 0:
+            from_far, _ = lax.optimization_barrier((from_far, own))
         got = (partial + from_mate[0].astype(F32) + from_far[0].astype(F32)).astype(BF16)
         received = shifted(got, "ka", 1)
+        if sweep == 0:
+            gated, down = lax.optimization_barrier((own[1:], down))
+            sent = [mate(gated[0]), far(gated[1])]
         nexts = [down, mate(down), far(down)]
-        if sweep == 0:
-            gated, _ = lax.optimization_barrier((own[1:], down))
-            sent = [mate(gated[0]), far(gated[1])]
         args = [*own, wire, perm, from_mate, from_far, *(sent if sweep else [])]
-        own_product = call(own_body, wide, 9 * work, args, scratch=extra)
-        own_product = call(settle_body, wide, 90 * work, [own_product, received])
-        args = [*cross, *nexts, own_product, drive, relax3]
+        known = call(own_body, wide, 9 * work, args, scratch=extra)
+        known = call(settle_body, wide, HEAVY * work, [known, received])
         if sweep + 1 == ITERS:
-            return call(final_body, wide, 3 * work, args, scratch=[staging])
-        perm, wire, partial, to_mate, to_far = call(update_body, emitted, 8 * work, [*args, from_mate, from_far, *sent], scratch=extra)
+            return call(final_body, wide, 3 * work, [*cross, *nexts, known, drive, relax3], scratch=[staging])
+        known = call(cross_body, wide, HEAVY * work, [*cross, *nexts, known], scratch=[staging])
+        args = [*cross, known, drive, relax3, from_mate, from_far, *sent]
+        perm, wire, partial, to_mate, to_far = call(update_body, emitted, 8 * work, args, scratch=extra)
 
 
 def solution(mesh):

time: 68.2 us -> 67.8 us (level)
  the two profiles are of different devices: /device:TPU:6 before, /device:TPU:24 now
where the time goes in v4:
time: 67.8 us; the launch traced here: 67.6 us
  starting transfers between devices  28.2 us (42%)
  waiting for transfers between devices  26 us (38%)
  Pallas kernels  13.2 us (19%)
    ppermute x5, waiting for transfers between devices, far(): lax.ppermute(value, 'rows', [(i, (i + 1 if i & 1 else i - 1) % count) for...  16.5 us
    ppermute x5, starting transfers between devices, far(): lax.ppermute(value, 'rows', [(i, (i + 1 if i & 1 else i - 1) % count) for...  13.9 us
    ppermute x4, starting transfers between devices, shifted(): lax.ppermute(value, axis, [(source, (source + steps) % count) for source...  13.7 us
    pallas_call x9, Pallas kernels, call(): pl.pallas_call(kernel, out_shape=outs, in_specs=specs or [VMEM] * len(arg...  13.2 us
    ppermute x4, waiting for transfers between devices, shifted(): lax.ppermute(value, axis, [(source, (source + steps) % count) for source...  9.45 us
  transfers between devices with their start and end apart: 14, of which 9 were waited for; matrix products, arithmetic and copies ran while one was open for 0% of the time, Pallas kernels for 9%

profile of v4, /device:TPU:24, one launch (start us, length us, event | category | flops | bytes accessed | tf_op | source)
XLA Modules:
  0.0 67.6 jit_solution(18098982159081197068)
XLA Ops:
  0.0 3.7 %shard_map.55 = (bf16[512,512]{1,0:T(8,128)(2,1)S(1)}, bf16[512,512]{1,0:T(8,128)(2,1)S(1)}, bf16[512,512]{1,0:T(8,128)(2,1)S(1)}, bf16[512,256]{1,0:T(8,128)(2,...) custom-call(bf16[256,4096]{1,0:T(8,128)(2,1)} %blocks_hbm.3, ...), custom_call_target="tpu_custom_call" | custom-call | flops 1207959552 | bytes 2625536 | tf_op jit(solution)/shard_map/pallas_call | solution.py:43
  3.8 6.3 %collective-permute-start.4 = (bf16[2,512,256]{2,1,0:T(8,128)(2,1)S(1)}, bf16[2,512,256]{2,1,0:T(8,128)(2,1)S(1)}, u32[]{:S(2)}, u32[]{:S(2)}) collective-permute-start(bf16[2,512,256]{2,1,0:T(8,128)(2,1)S(1)} %get-tuple-element.36), channel_id=1, source_target_pairs={{0,31},{1,2},{2,1},{3,4},{4,3},{5,6},{6,5},{7,8},{8,7},{9,10},{10,... | collective-permute-start | bytes 1572872 | tf_op jit(solution)/shard_map/ppermute | solution.py:36
  10.1 0.0 collective-permute-start.3
  10.1 2.9 %collective-permute-start = (bf16[512,256]{1,0:T(8,128)(2,1)S(1)}, bf16[512,256]{1,0:T(8,128)(2,1)S(1)}, u32[]{:S(2)}, u32[]{:S(2)}) collective-permute-start(bf16[512,256]{1,0:T(8,128)(2,1)S(1)} %get-tuple-element.31.refs_3_), channel_id=1, source_target_pairs={{0,224},{32,0},{64,32},{96,64},{128,96},{160,128},{192,160},{224,1... | collective-permute-start | bytes 786440 | tf_op jit(solution)/shard_map/ppermute | solution.py:27
  13.0 2.5 %shard_map.56 = (bf16[512,512]{1,0:T(8,128)(2,1)S(1)}, bf16[512,512]{1,0:T(8,128)(2,1)S(1)}, bf16[512,512]{1,0:T(8,128)(2,1)S(1)}) custom-call(bf16[256,4096]{1,0:T(8,128)(2,1)} %blocks_hbm.3, s32[1,256]{1,0:T(1,128)} %bitcast.23, s32[1,256]{1,0:T(1,128)} %bitcast.25), custom_call_target="tpu_custom_call" | custom-call | flops 805306368 | bytes 2099200 | tf_op jit(solution)/shard_map/pallas_call | solution.py:43
  15.5 1.5 %collective-permute-done.4.refs_6_.refs_7_ = bf16[2,512,256]{2,1,0:T(8,128)(2,1)S(1)} collective-permute-done((bf16[2,512,256]{2,1,0:T(8,128)(2,1)S(1)}, bf16[2,512,256]{2,1,0:T(8,128)(2,1)S(1)}, u32[]{:S(2)}, u32[]{:S(2)}) %collective-permute-start.4) | collective-permute-done | bytes 524320 | tf_op jit(solution)/shard_map/ppermute | solution.py:36
  17.0 0.0 collective-permute-done.3.refs_5_.refs_6_
  17.0 0.1 fusion.1
  17.1 2.8 %collective-permute-start.5 = (bf16[512,256]{1,0:T(8,128)(2,1)S(1)}, bf16[512,256]{1,0:T(8,128)(2,1)S(1)}, u32[]{:S(2)}, u32[]{:S(2)}) collective-permute-start(bf16[512,256]{1,0:T(8,128)(2,1)S(1)} %fusion.1), channel_id=1, source_target_pairs={{0,32},{32,64},{64,96},{96,128},{128,160},{160,192},{192,224},{224... | collective-permute-start | bytes 786440 | tf_op jit(solution)/shard_map/ppermute | solution.py:27
  19.9 4.2 %collective-permute-done.refs_3_ = bf16[512,256]{1,0:T(8,128)(2,1)S(1)} collective-permute-done((bf16[512,256]{1,0:T(8,128)(2,1)S(1)}, bf16[512,256]{1,0:T(8,128)(2,1)S(1)}, u32[]{:S(2)}, u32[]{:S(2)}) %collective-permute-start) | collective-permute-done | bytes 262176 | tf_op jit(solution)/shard_map/ppermute | solution.py:27
  24.1 2.1 %collective-permute-start.2 = (bf16[512,256]{1,0:T(8,128)(2,1)S(1)}, bf16[512,256]{1,0:T(8,128)(2,1)S(1)}, u32[]{:S(2)}, u32[]{:S(2)}) collective-permute-start(bf16[512,256]{1,0:T(8,128)(2,1)S(1)} %collective-permute-done.refs_3_), channel_id=1, source_target_pairs={{0,31},{1,2},{2,1},{3,4},{4,3},{5,6},{6,5},{7,8},{8,7},{9,10},{10,... | collective-permute-start | bytes 786440 | tf_op jit(solution)/shard_map/ppermute | solution.py:36
  26.2 0.5 collective-permute-start.6
  26.8 1.7 %collective-permute-start.7 = (bf16[512,512]{1,0:T(8,128)(2,1)S(1)}, bf16[512,512]{1,0:T(8,128)(2,1)S(1)}, u32[]{:S(2)}, u32[]{:S(2)}) collective-permute-start(bf16[512,512]{1,0:T(8,128)(2,1)S(1)} %get-tuple-element.41.refs_2_), channel_id=1, source_target_pairs={{0,31},{1,2},{2,1},{3,4},{4,3},{5,6},{6,5},{7,8},{8,7},{9,10},{10,... | collective-permute-start | bytes 1572872 | tf_op jit(solution)/shard_map/ppermute | solution.py:36
  28.5 0.8 %shard_map.57.own_ref = f32[512,256]{1,0:T(8,128)S(1)} custom-call(bf16[512,512]{1,0:T(8,128)(2,1)S(1)} %get-tuple-element.33.refs_0_, bf16[512,512]{1,0:T(8,128)(2,1)S(1)} %get-tuple-element.40.refs_1_, bf16[512,512]{1,0:T(8,128)(2,1)S(1)} %get-tuple-element.41.refs_2_, bf16[512,256]{1,0:T(8,128)(2,1)S(1)} %get-tuple-element.31.refs_3_, ...), custom_call_target="tpu_custom_call" | custom-call | flops 1207959552 | bytes 3145728 | tf_op jit(solution)/shard_map/pallas_call | solution.py:43
  29.2 0.6 collective-permute-done.5.received_ref
  29.9 2.1 %collective-permute-done.2.refs_5_ = bf16[512,256]{1,0:T(8,128)(2,1)S(1)} collective-permute-done((bf16[512,256]{1,0:T(8,128)(2,1)S(1)}, bf16[512,256]{1,0:T(8,128)(2,1)S(1)}, u32[]{:S(2)}, u32[]{:S(2)}) %collective-permute-start.2) | collective-permute-done | bytes 262176 | tf_op jit(solution)/shard_map/ppermute | solution.py:36
  32.0 0.0 collective-permute-done.1.refs_4_
  32.0 0.6 shard_map.59.refs_3_
  32.7 5.0 %collective-permute-done.7.refs_9_.refs_8_ = bf16[512,512]{1,0:T(8,128)(2,1)S(1)} collective-permute-done((bf16[512,512]{1,0:T(8,128)(2,1)S(1)}, bf16[512,512]{1,0:T(8,128)(2,1)S(1)}, u32[]{:S(2)}, u32[]{:S(2)}) %collective-permute-start.7) | collective-permute-done | bytes 524320 | tf_op jit(solution)/shard_map/ppermute | solution.py:36
  37.6 2.2 %shard_map.60 = (bf16[512,256]{1,0:T(8,128)(2,1)S(1)}, bf16[512,256]{1,0:T(8,128)(2,1)S(1)}, f32[512,256]{1,0:T(8,128)S(1)}, bf16[2,512,256]{2,1,0:T(8,128)(2,1)S(1)}, bf16[2,512,256]{2,1,0:T(8,128)(2,1)S(1)}) custom-call(bf16[512,512]{1,0:T(8,128)(2,1)S(1)} %get-tuple-element.26.refs_0_, bf16[512,512]{1,0:T(8,128)(2,1)S(1)} %get-tuple-element.27.refs_1_, ...), custom_call_target="tpu_custom_call" | custom-call | flops 1073741824 | bytes 4980736 | tf_op jit(solution)/shard_map/pallas_call | solution.py:43
  39.8 0.1 collective-permute-start.11
  39.9 2.5 %collective-permute-start.12 = (bf16[2,512,256]{2,1,0:T(8,128)(2,1)S(1)}, bf16[2,512,256]{2,1,0:T(8,128)(2,1)S(1)}, u32[]{:S(2)}, u32[]{:S(2)}) collective-permute-start(bf16[2,512,256]{2,1,0:T(8,128)(2,1)S(1)} %get-tuple-element.45), channel_id=1, source_target_pairs={{0,31},{1,2},{2,1},{3,4},{4,3},{5,6},{6,5},{7,8},{8,7},{9,10},{10,... | collective-permute-start | bytes 1572872 | tf_op jit(solution)/shard_map/ppermute | solution.py:36
  42.5 4.8 %collective-permute-start.8 = (bf16[512,256]{1,0:T(8,128)(2,1)S(1)}, bf16[512,256]{1,0:T(8,128)(2,1)S(1)}, u32[]{:S(2)}, u32[]{:S(2)}) collective-permute-start(bf16[512,256]{1,0:T(8,128)(2,1)S(1)} %get-tuple-element.42.refs_3_), channel_id=1, source_target_pairs={{0,224},{32,0},{64,32},{96,64},{128,96},{160,128},{192,160},{224,1... | collective-permute-start | bytes 786440 | tf_op jit(solution)/shard_map/ppermute | solution.py:27
  47.3 3.8 %collective-permute-done.12.refs_6_ = bf16[2,512,256]{2,1,0:T(8,128)(2,1)S(1)} collective-permute-done((bf16[2,512,256]{2,1,0:T(8,128)(2,1)S(1)}, bf16[2,512,256]{2,1,0:T(8,128)(2,1)S(1)}, u32[]{:S(2)}, u32[]{:S(2)}) %collective-permute-start.12) | collective-permute-done | bytes 524320 | tf_op jit(solution)/shard_map/ppermute | solution.py:36
  51.0 0.1 fusion
  51.1 3.2 %collective-permute-start.13 = (bf16[512,256]{1,0:T(8,128)(2,1)S(1)}, bf16[512,256]{1,0:T(8,128)(2,1)S(1)}, u32[]{:S(2)}, u32[]{:S(2)}) collective-permute-start(bf16[512,256]{1,0:T(8,128)(2,1)S(1)} %fusion), channel_id=1, source_target_pairs={{0,32},{32,64},{64,96},{96,128},{128,160},{160,192},{192,224},{224... | collective-permute-start | bytes 786440 | tf_op jit(solution)/shard_map/ppermute | solution.py:27
  54.3 4.0 %collective-permute-done.8.refs_3_ = bf16[512,256]{1,0:T(8,128)(2,1)S(1)} collective-permute-done((bf16[512,256]{1,0:T(8,128)(2,1)S(1)}, bf16[512,256]{1,0:T(8,128)(2,1)S(1)}, u32[]{:S(2)}, u32[]{:S(2)}) %collective-permute-start.8) | collective-permute-done | bytes 262176 | tf_op jit(solution)/shard_map/ppermute | solution.py:27
  58.3 1.2 %collective-permute-start.10 = (bf16[512,256]{1,0:T(8,128)(2,1)S(1)}, bf16[512,256]{1,0:T(8,128)(2,1)S(1)}, u32[]{:S(2)}, u32[]{:S(2)}) collective-permute-start(bf16[512,256]{1,0:T(8,128)(2,1)S(1)} %collective-permute-done.8.refs_3_), channel_id=1, source_target_pairs={{0,31},{1,2},{2,1},{3,4},{4,3},{5,6},{6,5},{7,8},{8,7},{9,10},{10,... | collective-permute-start | bytes 786440 | tf_op jit(solution)/shard_map/ppermute | solution.py:36
  59.5 1.8 %shard_map.61.own_ref = f32[512,256]{1,0:T(8,128)S(1)} custom-call(bf16[512,512]{1,0:T(8,128)(2,1)S(1)} %get-tuple-element.33.refs_0_, bf16[512,512]{1,0:T(8,128)(2,1)S(1)} %get-tuple-element.40.refs_1_, bf16[512,512]{1,0:T(8,128)(2,1)S(1)} %get-tuple-element.41.refs_2_, bf16[512,256]{1,0:T(8,128)(2,1)S(1)} %get-tuple-element.42.refs_3_, ...), custom_call_target="tpu_custom_call" | custom-call | flops 1207959552 | bytes 4194304 | tf_op jit(solution)/shard_map/pallas_call | solution.py:43
  61.3 0.6 collective-permute-done.13.received_ref
  62.0 4.2 %collective-permute-done.10.refs_5_ = bf16[512,256]{1,0:T(8,128)(2,1)S(1)} collective-permute-done((bf16[512,256]{1,0:T(8,128)(2,1)S(1)}, bf16[512,256]{1,0:T(8,128)(2,1)S(1)}, u32[]{:S(2)}, u32[]{:S(2)}) %collective-permute-start.10) | collective-permute-done | bytes 262176 | tf_op jit(solution)/shard_map/ppermute | solution.py:36
  66.2 1.4 %shard_map.63 = f32[512,256]{1,0:T(8,128)} custom-call(bf16[512,512]{1,0:T(8,128)(2,1)S(1)} %get-tuple-element.26.refs_0_, bf16[512,512]{1,0:T(8,128)(2,1)S(1)} %get-tuple-element.27.refs_1_, bf16[512,512]{1,0:T(8,128)(2,1)S(1)} %get-tuple-element.28.refs_2_, bf16[512,256]{1,0:T(8,128)(2,1)S(1)} %collective-permute-done.8.refs_3_, ...), custom_call_target="tpu_custom_call" | custom-call | flops 402653184 | bytes 3670016 | tf_op jit(solution)/shard_map/pallas_call | solution.py:43
  (9 shorter events, 0.1 us)
Async XLA Ops:
  3.8 13.3 %collective-permute-start.4 = (bf16[2,512,256]{2,1,0:T(8,128)(2,1)S(1)}, bf16[2,512,256]{2,1,0:T(8,128)(2,1)S(1)}, u32[]{:S(2)}, u32[]{:S(2)}) collective-permute-start(bf16[2,512,256]{2,1,0:T(8,128)(2,1)S(1)} %get-tuple-element.36), channel_id=1, source_target_pairs={{0,31},{1,2},{2,1},{3,4},{4,3},{5,6},{6,5},{7,8},{8,7},{9,10},{10,... | collective-permute-start | bytes 1572872 | tf_op jit(solution)/shard_map/ppermute | solution.py:36
  10.1 7.0 %collective-permute-start.3 = (bf16[2,512,256]{2,1,0:T(8,128)(2,1)S(1)}, bf16[2,512,256]{2,1,0:T(8,128)(2,1)S(1)}, u32[]{:S(2)}, u32[]{:S(2)}) collective-permute-start(bf16[2,512,256]{2,1,0:T(8,128)(2,1)S(1)} %get-tuple-element.35), channel_id=1, source_target_pairs={{0,1},{1,0},{2,3},{3,2},{4,5},{5,4},{6,7},{7,6},{8,9},{9,8},{10,11... | collective-permute-start | bytes 1572872 | tf_op jit(solution)/shard_map/ppermute | solution.py:31
  10.1 14.0 %collective-permute-start = (bf16[512,256]{1,0:T(8,128)(2,1)S(1)}, bf16[512,256]{1,0:T(8,128)(2,1)S(1)}, u32[]{:S(2)}, u32[]{:S(2)}) collective-permute-start(bf16[512,256]{1,0:T(8,128)(2,1)S(1)} %get-tuple-element.31.refs_3_), channel_id=1, source_target_pairs={{0,224},{32,0},{64,32},{96,64},{128,96},{160,128},{192,160},{224,1... | collective-permute-start | bytes 786440 | tf_op jit(solution)/shard_map/ppermute | solution.py:27
  17.1 12.8 %collective-permute-start.5 = (bf16[512,256]{1,0:T(8,128)(2,1)S(1)}, bf16[512,256]{1,0:T(8,128)(2,1)S(1)}, u32[]{:S(2)}, u32[]{:S(2)}) collective-permute-start(bf16[512,256]{1,0:T(8,128)(2,1)S(1)} %fusion.1), channel_id=1, source_target_pairs={{0,32},{32,64},{64,96},{96,128},{128,160},{160,192},{192,224},{224... | collective-permute-start | bytes 786440 | tf_op jit(solution)/shard_map/ppermute | solution.py:27
  24.1 7.9 %collective-permute-start.2 = (bf16[512,256]{1,0:T(8,128)(2,1)S(1)}, bf16[512,256]{1,0:T(8,128)(2,1)S(1)}, u32[]{:S(2)}, u32[]{:S(2)}) collective-permute-start(bf16[512,256]{1,0:T(8,128)(2,1)S(1)} %collective-permute-done.refs_3_), channel_id=1, source_target_pairs={{0,31},{1,2},{2,1},{3,4},{4,3},{5,6},{6,5},{7,8},{8,7},{9,10},{10,... | collective-permute-start | bytes 786440 | tf_op jit(solution)/shard_map/ppermute | solution.py:36
  26.2 5.8 %collective-permute-start.1 = (bf16[512,256]{1,0:T(8,128)(2,1)S(1)}, bf16[512,256]{1,0:T(8,128)(2,1)S(1)}, u32[]{:S(2)}, u32[]{:S(2)}) collective-permute-start(bf16[512,256]{1,0:T(8,128)(2,1)S(1)} %collective-permute-done.refs_3_), channel_id=1, source_target_pairs={{0,1},{1,0},{2,3},{3,2},{4,5},{5,4},{6,7},{7,6},{8,9},{9,8},{10,11... | collective-permute-start | bytes 786440 | tf_op jit(solution)/shard_map/ppermute | solution.py:31
  26.2 6.4 %collective-permute-start.6 = (bf16[512,512]{1,0:T(8,128)(2,1)S(1)}, bf16[512,512]{1,0:T(8,128)(2,1)S(1)}, u32[]{:S(2)}, u32[]{:S(2)}) collective-permute-start(bf16[512,512]{1,0:T(8,128)(2,1)S(1)} %get-tuple-element.40.refs_1_), channel_id=1, source_target_pairs={{0,1},{1,0},{2,3},{3,2},{4,5},{5,4},{6,7},{7,6},{8,9},{9,8},{10,11... | collective-permute-start | bytes 1572872 | tf_op jit(solution)/shard_map/ppermute | solution.py:31
  26.8 10.9 %collective-permute-start.7 = (bf16[512,512]{1,0:T(8,128)(2,1)S(1)}, bf16[512,512]{1,0:T(8,128)(2,1)S(1)}, u32[]{:S(2)}, u32[]{:S(2)}) collective-permute-start(bf16[512,512]{1,0:T(8,128)(2,1)S(1)} %get-tuple-element.41.refs_2_), channel_id=1, source_target_pairs={{0,31},{1,2},{2,1},{3,4},{4,3},{5,6},{6,5},{7,8},{8,7},{9,10},{10,... | collective-permute-start | bytes 1572872 | tf_op jit(solution)/shard_map/ppermute | solution.py:36
  32.0 5.6 %copy-start = (f32[512,256]{1,0:T(8,128)S(1)}, f32[512,256]{1,0:T(8,128)}, u32[]{:S(2)}) copy-start(f32[512,256]{1,0:T(8,128)} %refs_7_.1) | copy-start | bytes 1572868
  39.8 7.4 %collective-permute-start.11 = (bf16[2,512,256]{2,1,0:T(8,128)(2,1)S(1)}, bf16[2,512,256]{2,1,0:T(8,128)(2,1)S(1)}, u32[]{:S(2)}, u32[]{:S(2)}) collective-permute-start(bf16[2,512,256]{2,1,0:T(8,128)(2,1)S(1)} %get-tuple-element.44), channel_id=1, source_target_pairs={{0,1},{1,0},{2,3},{3,2},{4,5},{5,4},{6,7},{7,6},{8,9},{9,8},{10,11... | collective-permute-start | bytes 1572872 | tf_op jit(solution)/shard_map/ppermute | solution.py:31
  39.9 11.1 %collective-permute-start.12 = (bf16[2,512,256]{2,1,0:T(8,128)(2,1)S(1)}, bf16[2,512,256]{2,1,0:T(8,128)(2,1)S(1)}, u32[]{:S(2)}, u32[]{:S(2)}) collective-permute-start(bf16[2,512,256]{2,1,0:T(8,128)(2,1)S(1)} %get-tuple-element.45), channel_id=1, source_target_pairs={{0,31},{1,2},{2,1},{3,4},{4,3},{5,6},{6,5},{7,8},{8,7},{9,10},{10,... | collective-permute-start | bytes 1572872 | tf_op jit(solution)/shard_map/ppermute | solution.py:36
  42.5 15.8 %collective-permute-start.8 = (bf16[512,256]{1,0:T(8,128)(2,1)S(1)}, bf16[512,256]{1,0:T(8,128)(2,1)S(1)}, u32[]{:S(2)}, u32[]{:S(2)}) collective-permute-start(bf16[512,256]{1,0:T(8,128)(2,1)S(1)} %get-tuple-element.42.refs_3_), channel_id=1, source_target_pairs={{0,224},{32,0},{64,32},{96,64},{128,96},{160,128},{192,160},{224,1... | collective-permute-start | bytes 786440 | tf_op jit(solution)/shard_map/ppermute | solution.py:27
  51.1 10.9 %collective-permute-start.13 = (bf16[512,256]{1,0:T(8,128)(2,1)S(1)}, bf16[512,256]{1,0:T(8,128)(2,1)S(1)}, u32[]{:S(2)}, u32[]{:S(2)}) collective-permute-start(bf16[512,256]{1,0:T(8,128)(2,1)S(1)} %fusion), channel_id=1, source_target_pairs={{0,32},{32,64},{64,96},{96,128},{128,160},{160,192},{192,224},{224... | collective-permute-start | bytes 786440 | tf_op jit(solution)/shard_map/ppermute | solution.py:27
  58.3 7.9 %collective-permute-start.10 = (bf16[512,256]{1,0:T(8,128)(2,1)S(1)}, bf16[512,256]{1,0:T(8,128)(2,1)S(1)}, u32[]{:S(2)}, u32[]{:S(2)}) collective-permute-start(bf16[512,256]{1,0:T(8,128)(2,1)S(1)} %collective-permute-done.8.refs_3_), channel_id=1, source_target_pairs={{0,31},{1,2},{2,1},{3,4},{4,3},{5,6},{6,5},{7,8},{8,7},{9,10},{10,... | collective-permute-start | bytes 786440 | tf_op jit(solution)/shard_map/ppermute | solution.py:36
  59.5 6.7 %collective-permute-start.9 = (bf16[512,256]{1,0:T(8,128)(2,1)S(1)}, bf16[512,256]{1,0:T(8,128)(2,1)S(1)}, u32[]{:S(2)}, u32[]{:S(2)}) collective-permute-start(bf16[512,256]{1,0:T(8,128)(2,1)S(1)} %collective-permute-done.8.refs_3_), channel_id=1, source_target_pairs={{0,1},{1,0},{2,3},{3,2},{4,5},{5,4},{6,7},{7,6},{8,9},{9,8},{10,11... | collective-permute-start | bytes 786440 | tf_op jit(solution)/shard_map/ppermute | solution.py:31

commit v5 on v3

--- a/solution.py
+++ b/solution.py
@@ -11,6 +11,7 @@
 LANES = 128
 ITERS = 2
 PIECES = 4
+HEAVY = 90
 BF16, F32 = jnp.bfloat16, jnp.float32
 VMEM = pl.BlockSpec(memory_space=pltpu.VMEM)
 HBM = pl.BlockSpec(memory_space=pltpu.HBM)
@@ -37,7 +38,7 @@
 
 def call(kernel, outs, flops, args, specs=None, scratch=()):
     if specs:
-        args = [pltpu.with_memory_space_constraint(a, pltpu.HBM) for a in args]
+        args = [pltpu.with_memory_space_constraint(a, pltpu.HBM) if s is HBM else a for a, s in zip(args, specs)]
     nbytes = sum(a.size * a.dtype.itemsize for a in args)
     return pl.pallas_call(
         kernel,
@@ -149,45 +150,46 @@
     emit(cross, field.astype(BF16), perm_ref, wire_ref, self_ref, mate_ref, far_ref)
 
 
-def second_body(sizes, blocks_hbm, row_hbm, col_hbm, *refs):
-    build(0, sizes, blocks_hbm, row_hbm, col_hbm, *refs[3:], refs[:3])
-
-
-def sent_terms(sent, fields, scratch, other):
-    total = 0.0
-    for matrix, field in zip(sent, fields):
-        interleave(field[1].astype(F32), scratch, other)
-        total += dot_t(matrix[...], other[...])
-    return total
+def second_body(sizes, blocks_hbm, row_hbm, col_hbm, perm_ref, *refs):
+    own, outs, (blocks, ids, sems) = refs[:3], refs[3:6], refs[6:]
+    build(0, sizes, blocks_hbm, row_hbm, col_hbm, blocks, ids, sems, own)
+    partials(own, perm_ref, outs)
+
+
+def partials(mats, perm_ref, outs):
+    perm = perm_ref[...]
+    for matrix, ref in zip(mats, outs):
+        ref[...] = dot_t(matrix[...], perm).astype(ref.dtype)
+
+
+def third_body(*refs):
+    partials(refs[:3], refs[3], refs[4:])
 
 
 def own_body(*refs):
-    mats, (wire_ref, perm_ref, mate_ref, far_ref), sent = refs[:3], refs[3:7], refs[7:-3]
-    out_ref, scratch, other = refs[-3:]
-    total = dot_t(mats[0][...], perm_ref[...])
+    mats, (wire_ref, mate_ref, far_ref, self_ref), (out_ref, scratch) = refs[:3], refs[3:7], refs[7:]
     straight = dot(mats[0][...], wire_ref[...])
     straight += dot(mats[1][...], mate_ref[1])
     straight += dot(mats[2][...], far_ref[1])
-    if sent:
-        total += sent_terms(sent, (mate_ref, far_ref), scratch, other)
-    out_ref[...] = total + restored(straight, scratch)
-
-
-def new_field(cross, nexts, own, drive_ref, relax_ref, scratch):
-    straight = dot(cross[0][...], nexts[0][...])
-    straight += dot(cross[1][...], nexts[1][...])
-    straight += dot(cross[2][...], nexts[2][...])
-    product = own + restored(straight, scratch)
+    out_ref[...] = self_ref[...] + restored(straight, scratch)
+
+
+def with_cross(cross, down_ref, mate_ref, far_ref, known_ref, scratch):
+    straight = dot(cross[0][...], down_ref[...])
+    straight += dot(cross[1][...], mate_ref[0])
+    straight += dot(cross[2][...], far_ref[0])
+    return known_ref[...] + mate_ref[1].astype(F32) + far_ref[1].astype(F32) + restored(straight, scratch)
+
+
+def advanced(product, drive_ref, relax_ref):
     scale = jnp.concatenate([relax_ref[...]] * (product.shape[1] // LANES), axis=1)
     return drive_ref[...] + scale * product
 
 
 def update_body(*refs):
-    cross, nexts, rest, (mate_in, far_in), sent = refs[:3], refs[3:6], refs[6:9], refs[9:11], refs[11:13]
-    perm_ref, wire_ref, self_ref, mate_ref, far_ref, scratch, other = refs[13:]
-    drive_ref, relax_ref = rest[1:]
-    late = sent_terms(sent, (mate_in, far_in), scratch, other)
-    field = new_field(cross, nexts, rest[0][...] + late, drive_ref, relax_ref, scratch)
+    cross, nexts, (drive_ref, relax_ref) = refs[:3], refs[3:7], refs[7:9]
+    perm_ref, wire_ref, self_ref, mate_ref, far_ref, scratch = refs[9:]
+    field = advanced(with_cross(cross, *nexts, scratch), drive_ref, relax_ref)
     interleave(field, scratch, perm_ref)
     emit(cross, field.astype(BF16), perm_ref, wire_ref, self_ref, mate_ref, far_ref)
 
@@ -197,7 +199,8 @@
 
 
 def final_body(*refs):
-    refs[9][...] = new_field(refs[:3], refs[3:6], refs[6][...], *refs[7:9], refs[10])
+    product = with_cross(refs[:3], *refs[3:7], refs[10])
+    refs[9][...] = advanced(product, *refs[7:9])
 
 
 def local(drive, relax, blocks, row_block, col_block):
@@ -222,29 +225,28 @@
         fetch + [pltpu.VMEM(drive.shape, F32), pltpu.VMEM((1, rows), F32), staging, pltpu.SemaphoreType.DMA((4 + PIECES,))],
     )
 
-    extra = [staging, pltpu.VMEM((rows, channels), BF16)]
     for sweep in range(ITERS):
         down = shifted(wire, "ka", -1)
         from_far = far(to_far)
         from_mate = mate(to_mate)
         if sweep == 0:
-            own = call(
-                functools.partial(second_body, sizes), matrices, 6 * work, [blocks, row2, col2], [HBM] * 3,
-                fetch + [pltpu.SemaphoreType.DMA((2 + PIECES,))],
+            *own, own_self, own_mate, own_far = call(
+                functools.partial(second_body, sizes), (*matrices, wide, small, small), 9 * work,
+                [blocks, row2, col2, perm], [HBM] * 3 + [VMEM], fetch + [pltpu.SemaphoreType.DMA((2 + PIECES,))],
             )
+        else:
+            own_self, own_mate, own_far = call(third_body, (wide, small, small), 3 * work, [*own, perm])
+        from_far, _ = lax.optimization_barrier((from_far, own_self))
         got = (partial + from_mate[0].astype(F32) + from_far[0].astype(F32)).astype(BF16)
         received = shifted(got, "ka", 1)
-        nexts = [down, mate(down), far(down)]
-        if sweep == 0:
-            gated, _ = lax.optimization_barrier((own[1:], down))
-            sent = [mate(gated[0]), far(gated[1])]
-        args = [*own, wire, perm, from_mate, from_far, *(sent if sweep else [])]
-        own_product = call(own_body, wide, 9 * work, args, scratch=extra)
-        own_product = call(settle_body, wide, 90 * work, [own_product, received])
-        args = [*cross, *nexts, own_product, drive, relax3]
+        second_mate = mate(jnp.stack([down, own_mate]))
+        second_far = far(jnp.stack([down, own_far]))
+        known = call(own_body, wide, 3 * work, [*own, wire, from_mate, from_far, own_self], scratch=[staging])
+        known = call(settle_body, wide, HEAVY * work, [known, received])
+        args = [*cross, down, second_mate, second_far, known, drive, relax3]
         if sweep + 1 == ITERS:
             return call(final_body, wide, 3 * work, args, scratch=[staging])
-        perm, wire, partial, to_mate, to_far = call(update_body, emitted, 8 * work, [*args, from_mate, from_far, *sent], scratch=extra)
+        perm, wire, partial, to_mate, to_far = call(update_body, emitted, 6 * work, args, scratch=[staging])
 
 
 def solution(mesh):

time: 68.2 us -> 68.9 us (1.010)
  the two profiles are of different devices: /device:TPU:6 before, /device:TPU:1 now
where the time goes in v5:
time: 68.9 us; the launch traced here: 68.6 us
  waiting for transfers between devices  28.8 us (42%)
  starting transfers between devices  26.6 us (39%)
  Pallas kernels  12.6 us (18%)
    ppermute x4, waiting for transfers between devices, shifted(): lax.ppermute(value, axis, [(source, (source + steps) % count) for source...  27.9 us
    ppermute x4, starting transfers between devices, mate(): lax.ppermute(value, 'rows', [(i, i ^ 1) for i in range(lax.axis_size('row...  12.6 us
    pallas_call x9, Pallas kernels, call(): pl.pallas_call(kernel, out_shape=outs, in_specs=specs or [VMEM] * len(arg...  12.6 us
    ppermute x4, starting transfers between devices, shifted(): lax.ppermute(value, axis, [(source, (source + steps) % count) for source...  10.6 us
    ppermute x4, starting transfers between devices, far(): lax.ppermute(value, 'rows', [(i, (i + 1 if i & 1 else i - 1) % count) for...  3.39 us
  transfers between devices with their start and end apart: 12, of which 5 were waited for; matrix products, arithmetic and copies ran while one was open for 1% of the time, Pallas kernels for 7%

profile of v5, /device:TPU:1, one launch (start us, length us, event | category | flops | bytes accessed | tf_op | source)
XLA Modules:
  0.0 68.6 jit_solution(3646229315970099911)
XLA Ops:
  0.0 3.7 %shard_map.55 = (bf16[512,512]{1,0:T(8,128)(2,1)S(1)}, bf16[512,512]{1,0:T(8,128)(2,1)S(1)}, bf16[512,512]{1,0:T(8,128)(2,1)S(1)}, bf16[512,256]{1,0:T(8,128)(2,...) custom-call(bf16[256,4096]{1,0:T(8,128)(2,1)} %blocks_hbm.3, ...), custom_call_target="tpu_custom_call" | custom-call | flops 1207959552 | bytes 2625536 | tf_op jit(solution)/shard_map/pallas_call | solution.py:43
  3.7 3.1 %collective-permute-start.4 = (bf16[2,512,256]{2,1,0:T(8,128)(2,1)S(1)}, bf16[2,512,256]{2,1,0:T(8,128)(2,1)S(1)}, u32[]{:S(2)}, u32[]{:S(2)}) collective-permute-start(bf16[2,512,256]{2,1,0:T(8,128)(2,1)S(1)} %get-tuple-element.41), channel_id=1, source_target_pairs={{0,31},{1,2},{2,1},{3,4},{4,3},{5,6},{6,5},{7,8},{8,7},{9,10},{10,... | collective-permute-start | bytes 1572872 | tf_op jit(solution)/shard_map/ppermute | solution.py:36
  6.9 4.7 %collective-permute-start.3 = (bf16[2,512,256]{2,1,0:T(8,128)(2,1)S(1)}, bf16[2,512,256]{2,1,0:T(8,128)(2,1)S(1)}, u32[]{:S(2)}, u32[]{:S(2)}) collective-permute-start(bf16[2,512,256]{2,1,0:T(8,128)(2,1)S(1)} %get-tuple-element.40), channel_id=1, source_target_pairs={{0,1},{1,0},{2,3},{3,2},{4,5},{5,4},{6,7},{7,6},{8,9},{9,8},{10,11... | collective-permute-start | bytes 1572872 | tf_op jit(solution)/shard_map/ppermute | solution.py:31
  11.6 4.9 %collective-permute-start = (bf16[512,256]{1,0:T(8,128)(2,1)S(1)}, bf16[512,256]{1,0:T(8,128)(2,1)S(1)}, u32[]{:S(2)}, u32[]{:S(2)}) collective-permute-start(bf16[512,256]{1,0:T(8,128)(2,1)S(1)} %get-tuple-element.33.refs_3_), channel_id=1, source_target_pairs={{0,224},{32,0},{64,32},{96,64},{128,96},{160,128},{192,160},{224,1... | collective-permute-start | bytes 786440 | tf_op jit(solution)/shard_map/ppermute | solution.py:27
  16.5 3.1 %shard_map.56 = (bf16[512,512]{1,0:T(8,128)(2,1)S(1)}, bf16[512,512]{1,0:T(8,128)(2,1)S(1)}, bf16[512,512]{1,0:T(8,128)(2,1)S(1)}, f32[512,256]{1,0:T(8,128)S(1)...) custom-call(bf16[256,4096]{1,0:T(8,128)(2,1)} %blocks_hbm.3, s32[1,256]{1,0:T(1,128)} %bitcast.33, ...), custom_call_target="tpu_custom_call" | custom-call | flops 1207959552 | bytes 2361344 | tf_op jit(solution)/shard_map/pallas_call | solution.py:43
  19.6 0.0 collective-permute-done.4.refs_5_
  19.6 0.0 collective-permute-done.3.refs_4_
  19.6 0.1 fusion.1
  19.7 0.1 collective-permute-start.5
  19.8 5.3 %collective-permute-done.refs_3_ = bf16[512,256]{1,0:T(8,128)(2,1)S(1)} collective-permute-done((bf16[512,256]{1,0:T(8,128)(2,1)S(1)}, bf16[512,256]{1,0:T(8,128)(2,1)S(1)}, u32[]{:S(2)}, u32[]{:S(2)}) %collective-permute-start) | collective-permute-done | bytes 262176 | tf_op jit(solution)/shard_map/ppermute | solution.py:27
  25.1 0.1 pad_maximum_fusion
  25.2 0.1 collective-permute-start.2
  25.3 2.6 %collective-permute-start.1 = (bf16[2,512,256]{2,1,0:T(8,128)(2,1)S(1)}, bf16[2,512,256]{2,1,0:T(8,128)(2,1)S(1)}, u32[]{:S(2)}, u32[]{:S(2)}) collective-permute-start(bf16[2,512,256]{2,1,0:T(8,128)(2,1)S(1)} %get-tuple-element.58), channel_id=1, source_target_pairs={{0,1},{1,0},{2,3},{3,2},{4,5},{5,4},{6,7},{7,6},{8,9},{9,8},{10,11... | collective-permute-start | bytes 1572872 | tf_op jit(solution)/shard_map/ppermute | solution.py:31
  27.9 0.6 shard_map.57.own_ref
  28.5 0.0 copy-start
  28.5 4.7 %collective-permute-done.5.received_ref = bf16[512,256]{1,0:T(8,128)(2,1)S(1)} collective-permute-done((bf16[512,256]{1,0:T(8,128)(2,1)S(1)}, bf16[512,256]{1,0:T(8,128)(2,1)S(1)}, u32[]{:S(2)}, u32[]{:S(2)}) %collective-permute-start.5) | collective-permute-done | bytes 262176 | tf_op jit(solution)/shard_map/ppermute | solution.py:27
  33.2 1.0 %collective-permute-done.2.refs_5_ = bf16[2,512,256]{2,1,0:T(8,128)(2,1)S(1)} collective-permute-done((bf16[2,512,256]{2,1,0:T(8,128)(2,1)S(1)}, bf16[2,512,256]{2,1,0:T(8,128)(2,1)S(1)}, u32[]{:S(2)}, u32[]{:S(2)}) %collective-permute-start.2) | collective-permute-done | bytes 524320 | tf_op jit(solution)/shard_map/ppermute | solution.py:36
  34.2 2.4 %shard_map.59 = (bf16[512,256]{1,0:T(8,128)(2,1)S(1)}, bf16[512,256]{1,0:T(8,128)(2,1)S(1)}, f32[512,256]{1,0:T(8,128)S(1)}, bf16[2,512,256]{2,1,0:T(8,128)(2,1)S(1)}, bf16[2,512,256]{2,1,0:T(8,128)(2,1)S(1)}) custom-call(bf16[512,512]{1,0:T(8,128)(2,1)S(1)} %get-tuple-element.30.refs_0_, bf16[512,512]{1,0:T(8,128)(2,1)S(1)} %get-tuple-element.31.refs_1_, ...), custom_call_target="tpu_custom_call" | custom-call | flops 805306368 | bytes 4194304 | tf_op jit(solution)/shard_map/pallas_call | solution.py:43
  36.6 0.1 collective-permute-start.10
  36.7 4.5 %collective-permute-start.9 = (bf16[2,512,256]{2,1,0:T(8,128)(2,1)S(1)}, bf16[2,512,256]{2,1,0:T(8,128)(2,1)S(1)}, u32[]{:S(2)}, u32[]{:S(2)}) collective-permute-start(bf16[2,512,256]{2,1,0:T(8,128)(2,1)S(1)} %get-tuple-element.50), channel_id=1, source_target_pairs={{0,1},{1,0},{2,3},{3,2},{4,5},{5,4},{6,7},{7,6},{8,9},{9,8},{10,11... | collective-permute-start | bytes 1572872 | tf_op jit(solution)/shard_map/ppermute | solution.py:31
  41.2 5.5 %collective-permute-start.6 = (bf16[512,256]{1,0:T(8,128)(2,1)S(1)}, bf16[512,256]{1,0:T(8,128)(2,1)S(1)}, u32[]{:S(2)}, u32[]{:S(2)}) collective-permute-start(bf16[512,256]{1,0:T(8,128)(2,1)S(1)} %get-tuple-element.46.refs_3_), channel_id=1, source_target_pairs={{0,224},{32,0},{64,32},{96,64},{128,96},{160,128},{192,160},{224,1... | collective-permute-start | bytes 786440 | tf_op jit(solution)/shard_map/ppermute | solution.py:27
  46.7 0.6 shard_map.60
  47.4 0.1 fusion
  47.5 0.1 collective-permute-start.11
  47.6 8.9 %collective-permute-done.6.refs_3_ = bf16[512,256]{1,0:T(8,128)(2,1)S(1)} collective-permute-done((bf16[512,256]{1,0:T(8,128)(2,1)S(1)}, bf16[512,256]{1,0:T(8,128)(2,1)S(1)}, u32[]{:S(2)}, u32[]{:S(2)}) %collective-permute-start.6) | collective-permute-done | bytes 262176 | tf_op jit(solution)/shard_map/ppermute | solution.py:27
  56.5 0.1 pad_maximum_fusion.2
  56.5 0.1 collective-permute-start.8
  56.6 0.8 %collective-permute-start.7 = (bf16[2,512,256]{2,1,0:T(8,128)(2,1)S(1)}, bf16[2,512,256]{2,1,0:T(8,128)(2,1)S(1)}, u32[]{:S(2)}, u32[]{:S(2)}) collective-permute-start(bf16[2,512,256]{2,1,0:T(8,128)(2,1)S(1)} %get-tuple-element.56), channel_id=1, source_target_pairs={{0,1},{1,0},{2,3},{3,2},{4,5},{5,4},{6,7},{7,6},{8,9},{9,8},{10,11... | collective-permute-start | bytes 1572872 | tf_op jit(solution)/shard_map/ppermute | solution.py:31
  57.5 0.6 shard_map.61.own_ref
  58.1 9.0 %collective-permute-done.11.received_ref = bf16[512,256]{1,0:T(8,128)(2,1)S(1)} collective-permute-done((bf16[512,256]{1,0:T(8,128)(2,1)S(1)}, bf16[512,256]{1,0:T(8,128)(2,1)S(1)}, u32[]{:S(2)}, u32[]{:S(2)}) %collective-permute-start.11) | collective-permute-done | bytes 262176 | tf_op jit(solution)/shard_map/ppermute | solution.py:27
  67.1 0.0 collective-permute-done.7.refs_4_
  67.1 1.5 %shard_map.63 = f32[512,256]{1,0:T(8,128)} custom-call(bf16[512,512]{1,0:T(8,128)(2,1)S(1)} %get-tuple-element.30.refs_0_, bf16[512,512]{1,0:T(8,128)(2,1)S(1)} %get-tuple-element.31.refs_1_, bf16[512,512]{1,0:T(8,128)(2,1)S(1)} %get-tuple-element.32.refs_2_, bf16[512,256]{1,0:T(8,128)(2,1)S(1)} %collective-permute-done.6.refs_3_, ...), custom_call_target="tpu_custom_call" | custom-call | flops 402653184 | bytes 4194304 | tf_op jit(solution)/shard_map/pallas_call | solution.py:43
  (7 shorter events, 0.1 us)
Async XLA Ops:
  3.7 15.8 %collective-permute-start.4 = (bf16[2,512,256]{2,1,0:T(8,128)(2,1)S(1)}, bf16[2,512,256]{2,1,0:T(8,128)(2,1)S(1)}, u32[]{:S(2)}, u32[]{:S(2)}) collective-permute-start(bf16[2,512,256]{2,1,0:T(8,128)(2,1)S(1)} %get-tuple-element.41), channel_id=1, source_target_pairs={{0,31},{1,2},{2,1},{3,4},{4,3},{5,6},{6,5},{7,8},{8,7},{9,10},{10,... | collective-permute-start | bytes 1572872 | tf_op jit(solution)/shard_map/ppermute | solution.py:36
  6.9 12.7 %collective-permute-start.3 = (bf16[2,512,256]{2,1,0:T(8,128)(2,1)S(1)}, bf16[2,512,256]{2,1,0:T(8,128)(2,1)S(1)}, u32[]{:S(2)}, u32[]{:S(2)}) collective-permute-start(bf16[2,512,256]{2,1,0:T(8,128)(2,1)S(1)} %get-tuple-element.40), channel_id=1, source_target_pairs={{0,1},{1,0},{2,3},{3,2},{4,5},{5,4},{6,7},{7,6},{8,9},{9,8},{10,11... | collective-permute-start | bytes 1572872 | tf_op jit(solution)/shard_map/ppermute | solution.py:31
  11.6 13.6 %collective-permute-start = (bf16[512,256]{1,0:T(8,128)(2,1)S(1)}, bf16[512,256]{1,0:T(8,128)(2,1)S(1)}, u32[]{:S(2)}, u32[]{:S(2)}) collective-permute-start(bf16[512,256]{1,0:T(8,128)(2,1)S(1)} %get-tuple-element.33.refs_3_), channel_id=1, source_target_pairs={{0,224},{32,0},{64,32},{96,64},{128,96},{160,128},{192,160},{224,1... | collective-permute-start | bytes 786440 | tf_op jit(solution)/shard_map/ppermute | solution.py:27
  19.7 13.5 %collective-permute-start.5 = (bf16[512,256]{1,0:T(8,128)(2,1)S(1)}, bf16[512,256]{1,0:T(8,128)(2,1)S(1)}, u32[]{:S(2)}, u32[]{:S(2)}) collective-permute-start(bf16[512,256]{1,0:T(8,128)(2,1)S(1)} %fusion.1), channel_id=1, source_target_pairs={{0,32},{32,64},{64,96},{96,128},{128,160},{160,192},{192,224},{224... | collective-permute-start | bytes 786440 | tf_op jit(solution)/shard_map/ppermute | solution.py:27
  25.2 9.0 %collective-permute-start.2 = (bf16[2,512,256]{2,1,0:T(8,128)(2,1)S(1)}, bf16[2,512,256]{2,1,0:T(8,128)(2,1)S(1)}, u32[]{:S(2)}, u32[]{:S(2)}) collective-permute-start(bf16[2,512,256]{2,1,0:T(8,128)(2,1)S(1)} %get-tuple-element.57), channel_id=1, source_target_pairs={{0,31},{1,2},{2,1},{3,4},{4,3},{5,6},{6,5},{7,8},{8,7},{9,10},{10,... | collective-permute-start | bytes 1572872 | tf_op jit(solution)/shard_map/ppermute | solution.py:36
  25.3 8.9 %collective-permute-start.1 = (bf16[2,512,256]{2,1,0:T(8,128)(2,1)S(1)}, bf16[2,512,256]{2,1,0:T(8,128)(2,1)S(1)}, u32[]{:S(2)}, u32[]{:S(2)}) collective-permute-start(bf16[2,512,256]{2,1,0:T(8,128)(2,1)S(1)} %get-tuple-element.58), channel_id=1, source_target_pairs={{0,1},{1,0},{2,3},{3,2},{4,5},{5,4},{6,7},{7,6},{8,9},{9,8},{10,11... | collective-permute-start | bytes 1572872 | tf_op jit(solution)/shard_map/ppermute | solution.py:31
  28.5 5.7 %copy-start = (f32[512,256]{1,0:T(8,128)S(1)}, f32[512,256]{1,0:T(8,128)}, u32[]{:S(2)}) copy-start(f32[512,256]{1,0:T(8,128)} %refs_7_.3) | copy-start | bytes 1572868
  36.6 10.8 %collective-permute-start.10 = (bf16[2,512,256]{2,1,0:T(8,128)(2,1)S(1)}, bf16[2,512,256]{2,1,0:T(8,128)(2,1)S(1)}, u32[]{:S(2)}, u32[]{:S(2)}) collective-permute-start(bf16[2,512,256]{2,1,0:T(8,128)(2,1)S(1)} %get-tuple-element.51), channel_id=1, source_target_pairs={{0,31},{1,2},{2,1},{3,4},{4,3},{5,6},{6,5},{7,8},{8,7},{9,10},{10,... | collective-permute-start | bytes 1572872 | tf_op jit(solution)/shard_map/ppermute | solution.py:36
  36.7 10.7 %collective-permute-start.9 = (bf16[2,512,256]{2,1,0:T(8,128)(2,1)S(1)}, bf16[2,512,256]{2,1,0:T(8,128)(2,1)S(1)}, u32[]{:S(2)}, u32[]{:S(2)}) collective-permute-start(bf16[2,512,256]{2,1,0:T(8,128)(2,1)S(1)} %get-tuple-element.50), channel_id=1, source_target_pairs={{0,1},{1,0},{2,3},{3,2},{4,5},{5,4},{6,7},{7,6},{8,9},{9,8},{10,11... | collective-permute-start | bytes 1572872 | tf_op jit(solution)/shard_map/ppermute | solution.py:31
  41.2 15.3 %collective-permute-start.6 = (bf16[512,256]{1,0:T(8,128)(2,1)S(1)}, bf16[512,256]{1,0:T(8,128)(2,1)S(1)}, u32[]{:S(2)}, u32[]{:S(2)}) collective-permute-start(bf16[512,256]{1,0:T(8,128)(2,1)S(1)} %get-tuple-element.46.refs_3_), channel_id=1, source_target_pairs={{0,224},{32,0},{64,32},{96,64},{128,96},{160,128},{192,160},{224,1... | collective-permute-start | bytes 786440 | tf_op jit(solution)/shard_map/ppermute | solution.py:27
  47.5 19.6 %collective-permute-start.11 = (bf16[512,256]{1,0:T(8,128)(2,1)S(1)}, bf16[512,256]{1,0:T(8,128)(2,1)S(1)}, u32[]{:S(2)}, u32[]{:S(2)}) collective-permute-start(bf16[512,256]{1,0:T(8,128)(2,1)S(1)} %fusion), channel_id=1, source_target_pairs={{0,32},{32,64},{64,96},{96,128},{128,160},{160,192},{192,224},{224... | collective-permute-start | bytes 786440 | tf_op jit(solution)/shard_map/ppermute | solution.py:27
  56.5 10.5 %collective-permute-start.8 = (bf16[2,512,256]{2,1,0:T(8,128)(2,1)S(1)}, bf16[2,512,256]{2,1,0:T(8,128)(2,1)S(1)}, u32[]{:S(2)}, u32[]{:S(2)}) collective-permute-start(bf16[2,512,256]{2,1,0:T(8,128)(2,1)S(1)} %get-tuple-element.55), channel_id=1, source_target_pairs={{0,31},{1,2},{2,1},{3,4},{4,3},{5,6},{6,5},{7,8},{8,7},{9,10},{10,... | collective-permute-start | bytes 1572872 | tf_op jit(solution)/shard_map/ppermute | solution.py:36
  56.6 10.4 %collective-permute-start.7 = (bf16[2,512,256]{2,1,0:T(8,128)(2,1)S(1)}, bf16[2,512,256]{2,1,0:T(8,128)(2,1)S(1)}, u32[]{:S(2)}, u32[]{:S(2)}) collective-permute-start(bf16[2,512,256]{2,1,0:T(8,128)(2,1)S(1)} %get-tuple-element.56), channel_id=1, source_target_pairs={{0,1},{1,0},{2,3},{3,2},{4,5},{5,4},{6,7},{7,6},{8,9},{9,8},{10,11... | collective-permute-start | bytes 1572872 | tf_op jit(solution)/shard_map/ppermute | solution.py:31

commit v6 on v5

--- a/solution.py
+++ b/solution.py
@@ -127,9 +127,9 @@
     perm = perm_ref[...]
     wire_ref[...] = wire
     self_ref[...] = dot_t(cross[0][...], perm)
-    for k, ref in ((2, far_ref), (1, mate_ref)):
-        ref[0] = dot_t(cross[k][...], perm).astype(BF16)
-        ref[1] = wire
+    far_ref[...] = dot_t(cross[2][...], perm).astype(BF16)
+    mate_ref[0] = dot_t(cross[1][...], perm).astype(BF16)
+    mate_ref[1] = wire
 
 
 def first_body(sizes, blocks_hbm, row_hbm, col_hbm, drive_hbm, relax_hbm, *refs):
@@ -150,35 +150,33 @@
     emit(cross, field.astype(BF16), perm_ref, wire_ref, self_ref, mate_ref, far_ref)
 
 
-def second_body(sizes, blocks_hbm, row_hbm, col_hbm, perm_ref, *refs):
+def second_body(sizes, blocks_hbm, row_hbm, col_hbm, perm_ref, wire_ref, *refs):
     own, outs, (blocks, ids, sems) = refs[:3], refs[3:6], refs[6:]
     build(0, sizes, blocks_hbm, row_hbm, col_hbm, blocks, ids, sems, own)
-    partials(own, perm_ref, outs)
-
-
-def partials(mats, perm_ref, outs):
+    own_partials(*own, perm_ref, wire_ref, *outs)
+
+
+def own_partials(self_in, mate_in, far_in, perm_ref, wire_ref, self_ref, mate_ref, far_ref):
     perm = perm_ref[...]
-    for matrix, ref in zip(mats, outs):
-        ref[...] = dot_t(matrix[...], perm).astype(ref.dtype)
-
-
-def third_body(*refs):
-    partials(refs[:3], refs[3], refs[4:])
+    far_ref[0] = wire_ref[...]
+    far_ref[1] = dot_t(far_in[...], perm).astype(BF16)
+    mate_ref[...] = dot_t(mate_in[...], perm).astype(BF16)
+    self_ref[...] = dot_t(self_in[...], perm)
 
 
 def own_body(*refs):
     mats, (wire_ref, mate_ref, far_ref, self_ref), (out_ref, scratch) = refs[:3], refs[3:7], refs[7:]
     straight = dot(mats[0][...], wire_ref[...])
     straight += dot(mats[1][...], mate_ref[1])
-    straight += dot(mats[2][...], far_ref[1])
+    straight += dot(mats[2][...], far_ref[0])
     out_ref[...] = self_ref[...] + restored(straight, scratch)
 
 
-def with_cross(cross, down_ref, mate_ref, far_ref, known_ref, scratch):
+def with_cross(cross, down_ref, mate_ref, far_ref, other_ref, known_ref, scratch):
     straight = dot(cross[0][...], down_ref[...])
     straight += dot(cross[1][...], mate_ref[0])
-    straight += dot(cross[2][...], far_ref[0])
-    return known_ref[...] + mate_ref[1].astype(F32) + far_ref[1].astype(F32) + restored(straight, scratch)
+    straight += dot(cross[2][...], far_ref[...])
+    return known_ref[...] + mate_ref[1].astype(F32) + other_ref[1].astype(F32) + restored(straight, scratch)
 
 
 def advanced(product, drive_ref, relax_ref):
@@ -187,8 +185,8 @@
 
 
 def update_body(*refs):
-    cross, nexts, (drive_ref, relax_ref) = refs[:3], refs[3:7], refs[7:9]
-    perm_ref, wire_ref, self_ref, mate_ref, far_ref, scratch = refs[9:]
+    cross, nexts, (drive_ref, relax_ref) = refs[:3], refs[3:8], refs[8:10]
+    perm_ref, wire_ref, self_ref, mate_ref, far_ref, scratch = refs[10:]
     field = advanced(with_cross(cross, *nexts, scratch), drive_ref, relax_ref)
     interleave(field, scratch, perm_ref)
     emit(cross, field.astype(BF16), perm_ref, wire_ref, self_ref, mate_ref, far_ref)
@@ -199,8 +197,8 @@
 
 
 def final_body(*refs):
-    product = with_cross(refs[:3], *refs[3:7], refs[10])
-    refs[9][...] = advanced(product, *refs[7:9])
+    product = with_cross(refs[:3], *refs[3:8], refs[11])
+    refs[10][...] = advanced(product, *refs[8:10])
 
 
 def local(drive, relax, blocks, row_block, col_block):
@@ -211,7 +209,7 @@
     double = jax.ShapeDtypeStruct((2, rows, channels), BF16)
     wide = jax.ShapeDtypeStruct((rows, channels), F32)
     matrices = (jax.ShapeDtypeStruct((rows, rows), BF16),) * 3
-    emitted = (small, small, wide, double, double)
+    emitted = (small, small, wide, double, small)
     staging = pltpu.VMEM((channels // LANES, rows, LANES), F32)
     fetch = [pltpu.VMEM(blocks.shape, BF16), pltpu.VMEM((2, slots), jnp.int32)]
     row2 = row_block.reshape(1, -1)
@@ -231,19 +229,20 @@
         from_mate = mate(to_mate)
         if sweep == 0:
             *own, own_self, own_mate, own_far = call(
-                functools.partial(second_body, sizes), (*matrices, wide, small, small), 9 * work,
-                [blocks, row2, col2, perm], [HBM] * 3 + [VMEM], fetch + [pltpu.SemaphoreType.DMA((2 + PIECES,))],
+                functools.partial(second_body, sizes), (*matrices, wide, small, double), 9 * work,
+                [blocks, row2, col2, perm, wire], [HBM] * 3 + [VMEM] * 2, fetch + [pltpu.SemaphoreType.DMA((2 + PIECES,))],
             )
         else:
-            own_self, own_mate, own_far = call(third_body, (wide, small, small), 3 * work, [*own, perm])
+            own_self, own_mate, own_far = call(own_partials, (wide, small, double), 3 * work, [*own, perm, wire])
+        other_far = far(own_far)
         from_far, _ = lax.optimization_barrier((from_far, own_self))
-        got = (partial + from_mate[0].astype(F32) + from_far[0].astype(F32)).astype(BF16)
+        got = (partial + from_mate[0].astype(F32) + from_far.astype(F32)).astype(BF16)
         received = shifted(got, "ka", 1)
-        second_mate = mate(jnp.stack([down, own_mate]))
-        second_far = far(jnp.stack([down, own_far]))
-        known = call(own_body, wide, 3 * work, [*own, wire, from_mate, from_far, own_self], scratch=[staging])
+        next_mate = mate(jnp.stack([down, own_mate]))
+        next_far = far(down)
+        known = call(own_body, wide, 3 * work, [*own, wire, from_mate, other_far, own_self], scratch=[staging])
         known = call(settle_body, wide, HEAVY * work, [known, received])
-        args = [*cross, down, second_mate, second_far, known, drive, relax3]
+        args = [*cross, down, next_mate, next_far, other_far, known, drive, relax3]
         if sweep + 1 == ITERS:
             return call(final_body, wide, 3 * work, args, scratch=[staging])
         perm, wire, partial, to_mate, to_far = call(update_body, emitted, 6 * work, args, scratch=[staging])

time: 68.9 us -> 72.4 us (1.051)
  waiting for transfers between devices: 28.8 us -> 34 us
  starting transfers between devices: 26.6 us -> 25.2 us
    ppermute x4 -> x6, waiting for transfers between devices: 0.96 us -> 4.66 us  [far(): lax.ppermute(value, 'rows', [(i, (i + 1 if i & 1 else i - 1) % count) for...]
    ppermute x4, starting transfers between devices: 10.6 us -> 8.33 us  [shifted(): lax.ppermute(value, axis, [(source, (source + steps) % count) for source...]
    ppermute x4, waiting for transfers between devices: 27.9 us -> 29.4 us  [shifted(): lax.ppermute(value, axis, [(source, (source + steps) % count) for source...]
    ppermute x4 -> x6, starting transfers between devices: 3.39 us -> 3.85 us  [far(): lax.ppermute(value, 'rows', [(i, (i + 1 if i & 1 else i - 1) % count) for...]
  transfers between devices with their start and end apart: 12 -> 14, of which waited for: 5 -> 5; matrix products, arithmetic and copies ran while one was open for 1% -> 0% of each run, Pallas kernels for 7% -> 7%
where the time goes in v6:
time: 72.4 us; the launch traced here: 72.3 us
  waiting for transfers between devices  34 us (47%)
  starting transfers between devices  25.2 us (35%)
  Pallas kernels  12.7 us (18%)
    ppermute x4, waiting for transfers between devices, shifted(): lax.ppermute(value, axis, [(source, (source + steps) % count) for source...  29.4 us
    ppermute x4, starting transfers between devices, mate(): lax.ppermute(value, 'rows', [(i, i ^ 1) for i in range(lax.axis_size('row...  13 us
    pallas_call x9, Pallas kernels, call(): pl.pallas_call(kernel, out_shape=outs, in_specs=specs or [VMEM] * len(arg...  12.7 us
    ppermute x4, starting transfers between devices, shifted(): lax.ppermute(value, axis, [(source, (source + steps) % count) for source...  8.33 us
    ppermute x6, waiting for transfers between devices, far(): lax.ppermute(value, 'rows', [(i, (i + 1 if i & 1 else i - 1) % count) for...  4.66 us
    ppermute x6, starting transfers between devices, far(): lax.ppermute(value, 'rows', [(i, (i + 1 if i & 1 else i - 1) % count) for...  3.85 us
  transfers between devices with their start and end apart: 14, of which 5 were waited for; matrix products, arithmetic and copies ran while one was open for 0% of the time, Pallas kernels for 7%

profile of v6, /device:TPU:1, one launch (start us, length us, event | category | flops | bytes accessed | tf_op | source)
XLA Modules:
  0.0 72.3 jit_solution(16119790235413084575)
XLA Ops:
  0.0 3.7 %shard_map.55 = (bf16[512,512]{1,0:T(8,128)(2,1)S(1)}, bf16[512,512]{1,0:T(8,128)(2,1)S(1)}, bf16[512,512]{1,0:T(8,128)(2,1)S(1)}, bf16[512,256]{1,0:T(8,128)(2,...) custom-call(bf16[256,4096]{1,0:T(8,128)(2,1)} %blocks_hbm.3, ...), custom_call_target="tpu_custom_call" | custom-call | flops 1207959552 | bytes 2625536 | tf_op jit(solution)/shard_map/pallas_call | solution.py:43
  3.7 3.3 %collective-permute-start.4 = (bf16[2,512,256]{2,1,0:T(8,128)(2,1)S(1)}, bf16[2,512,256]{2,1,0:T(8,128)(2,1)S(1)}, u32[]{:S(2)}, u32[]{:S(2)}) collective-permute-start(bf16[2,512,256]{2,1,0:T(8,128)(2,1)S(1)} %get-tuple-element.40), channel_id=1, source_target_pairs={{0,1},{1,0},{2,3},{3,2},{4,5},{5,4},{6,7},{7,6},{8,9},{9,8},{10,11... | collective-permute-start | bytes 1572872 | tf_op jit(solution)/shard_map/ppermute | solution.py:31
  7.0 0.0 collective-permute-start.5
  7.1 3.2 %shard_map.56 = (bf16[512,512]{1,0:T(8,128)(2,1)S(1)}, bf16[512,512]{1,0:T(8,128)(2,1)S(1)}, bf16[512,512]{1,0:T(8,128)(2,1)S(1)}, f32[512,256]{1,0:T(8,128)S(1)...) custom-call(bf16[256,4096]{1,0:T(8,128)(2,1)} %blocks_hbm.3, s32[1,256]{1,0:T(1,128)} %bitcast.23, ...), custom_call_target="tpu_custom_call" | custom-call | flops 1207959552 | bytes 2623488 | tf_op jit(solution)/shard_map/pallas_call | solution.py:43
  10.2 1.8 %collective-permute-start.3 = (bf16[2,512,256]{2,1,0:T(8,128)(2,1)S(1)}, bf16[2,512,256]{2,1,0:T(8,128)(2,1)S(1)}, u32[]{:S(2)}, u32[]{:S(2)}) collective-permute-start(bf16[2,512,256]{2,1,0:T(8,128)(2,1)S(1)} %get-tuple-element.36), channel_id=1, source_target_pairs={{0,31},{1,2},{2,1},{3,4},{4,3},{5,6},{6,5},{7,8},{8,7},{9,10},{10,... | collective-permute-start | bytes 1572872 | tf_op jit(solution)/shard_map/ppermute | solution.py:36
  12.1 3.5 %collective-permute-start = (bf16[512,256]{1,0:T(8,128)(2,1)S(1)}, bf16[512,256]{1,0:T(8,128)(2,1)S(1)}, u32[]{:S(2)}, u32[]{:S(2)}) collective-permute-start(bf16[512,256]{1,0:T(8,128)(2,1)S(1)} %get-tuple-element.33.wire_ref.refs_3_), channel_id=1, source_target_pairs={{0,224},{32,0},{64,32},{96,64},{128,96},{160,128},{192,160},{224,1... | collective-permute-start | bytes 786440 | tf_op jit(solution)/shard_map/ppermute | solution.py:27
  15.5 0.1 fusion.3
  15.6 0.1 collective-permute-start.6
  15.7 9.2 %collective-permute-done.refs_3_ = bf16[512,256]{1,0:T(8,128)(2,1)S(1)} collective-permute-done((bf16[512,256]{1,0:T(8,128)(2,1)S(1)}, bf16[512,256]{1,0:T(8,128)(2,1)S(1)}, u32[]{:S(2)}, u32[]{:S(2)}) %collective-permute-start) | collective-permute-done | bytes 262176 | tf_op jit(solution)/shard_map/ppermute | solution.py:27
  24.9 0.1 pad_maximum_fusion
  24.9 7.0 %collective-permute-start.1 = (bf16[2,512,256]{2,1,0:T(8,128)(2,1)S(1)}, bf16[2,512,256]{2,1,0:T(8,128)(2,1)S(1)}, u32[]{:S(2)}, u32[]{:S(2)}) collective-permute-start(bf16[2,512,256]{2,1,0:T(8,128)(2,1)S(1)} %pad_maximum_fusion), channel_id=1, source_target_pairs={{0,1},{1,0},{2,3},{3,2},{4,5},{5,4},{6,7},{7,6},{8,9},{9,8},{10,11... | collective-permute-start | bytes 1572872 | tf_op jit(solution)/shard_map/ppermute | solution.py:31
  32.0 0.6 shard_map.57.own_ref
  32.6 0.0 copy-start
  32.6 0.8 %collective-permute-done.6.received_ref = bf16[512,256]{1,0:T(8,128)(2,1)S(1)} collective-permute-done((bf16[512,256]{1,0:T(8,128)(2,1)S(1)}, bf16[512,256]{1,0:T(8,128)(2,1)S(1)}, u32[]{:S(2)}, u32[]{:S(2)}) %collective-permute-start.6) | collective-permute-done | bytes 262176 | tf_op jit(solution)/shard_map/ppermute | solution.py:27
  33.4 4.6 %collective-permute-done.2.refs_5_ = bf16[512,256]{1,0:T(8,128)(2,1)S(1)} collective-permute-done((bf16[512,256]{1,0:T(8,128)(2,1)S(1)}, bf16[512,256]{1,0:T(8,128)(2,1)S(1)}, u32[]{:S(2)}, u32[]{:S(2)}) %collective-permute-start.2) | collective-permute-done | bytes 262176 | tf_op jit(solution)/shard_map/ppermute | solution.py:36
  38.1 0.0 collective-permute-done.1.refs_4_
  38.1 2.4 %shard_map.59 = (bf16[512,256]{1,0:T(8,128)(2,1)S(1)}, bf16[512,256]{1,0:T(8,128)(2,1)S(1)}, f32[512,256]{1,0:T(8,128)S(1)}, bf16[2,512,256]{2,1,0:T(8,128)(2,1)S(1)}, bf16[512,256]{1,0:T(8,128)(2,1)S(1)}) custom-call(bf16[512,512]{1,0:T(8,128)(2,1)S(1)} %get-tuple-element.30.refs_0_, bf16[512,512]{1,0:T(8,128)(2,1)S(1)} %get-tuple-element.31.refs_1_, ...), custom_call_target="tpu_custom_call" | custom-call | flops 805306368 | bytes 4456448 | tf_op jit(solution)/shard_map/pallas_call | solution.py:43
  40.4 2.0 %collective-permute-start.11 = (bf16[2,512,256]{2,1,0:T(8,128)(2,1)S(1)}, bf16[2,512,256]{2,1,0:T(8,128)(2,1)S(1)}, u32[]{:S(2)}, u32[]{:S(2)}) collective-permute-start(bf16[2,512,256]{2,1,0:T(8,128)(2,1)S(1)} %get-tuple-element.50), channel_id=1, source_target_pairs={{0,1},{1,0},{2,3},{3,2},{4,5},{5,4},{6,7},{7,6},{8,9},{9,8},{10,11... | collective-permute-start | bytes 1572872 | tf_op jit(solution)/shard_map/ppermute | solution.py:31
  42.5 0.0 collective-permute-start.12
  42.5 0.6 shard_map.60
  43.1 2.0 %collective-permute-start.10 = (bf16[2,512,256]{2,1,0:T(8,128)(2,1)S(1)}, bf16[2,512,256]{2,1,0:T(8,128)(2,1)S(1)}, u32[]{:S(2)}, u32[]{:S(2)}) collective-permute-start(bf16[2,512,256]{2,1,0:T(8,128)(2,1)S(1)} %get-tuple-element.49), channel_id=1, source_target_pairs={{0,31},{1,2},{2,1},{3,4},{4,3},{5,6},{6,5},{7,8},{8,7},{9,10},{10,... | collective-permute-start | bytes 1572872 | tf_op jit(solution)/shard_map/ppermute | solution.py:36
  45.1 4.0 %collective-permute-start.7 = (bf16[512,256]{1,0:T(8,128)(2,1)S(1)}, bf16[512,256]{1,0:T(8,128)(2,1)S(1)}, u32[]{:S(2)}, u32[]{:S(2)}) collective-permute-start(bf16[512,256]{1,0:T(8,128)(2,1)S(1)} %get-tuple-element.46.wire_ref.refs_3_), channel_id=1, source_target_pairs={{0,224},{32,0},{64,32},{96,64},{128,96},{160,128},{192,160},{224,1... | collective-permute-start | bytes 786440 | tf_op jit(solution)/shard_map/ppermute | solution.py:27
  49.1 0.1 fusion.1
  49.2 0.8 %collective-permute-start.13 = (bf16[512,256]{1,0:T(8,128)(2,1)S(1)}, bf16[512,256]{1,0:T(8,128)(2,1)S(1)}, u32[]{:S(2)}, u32[]{:S(2)}) collective-permute-start(bf16[512,256]{1,0:T(8,128)(2,1)S(1)} %fusion.1), channel_id=1, source_target_pairs={{0,32},{32,64},{64,96},{96,128},{128,160},{160,192},{192,224},{224... | collective-permute-start | bytes 786440 | tf_op jit(solution)/shard_map/ppermute | solution.py:27
  50.0 12.8 %collective-permute-done.7.refs_3_ = bf16[512,256]{1,0:T(8,128)(2,1)S(1)} collective-permute-done((bf16[512,256]{1,0:T(8,128)(2,1)S(1)}, bf16[512,256]{1,0:T(8,128)(2,1)S(1)}, u32[]{:S(2)}, u32[]{:S(2)}) %collective-permute-start.7) | collective-permute-done | bytes 262176 | tf_op jit(solution)/shard_map/ppermute | solution.py:27
  62.8 0.1 pad_maximum_fusion.1
  62.8 0.7 collective-permute-start.8
  63.5 0.0 collective-permute-done.10.refs_5_.refs_6_
  63.5 0.6 shard_map.61.own_ref
  64.1 6.6 %collective-permute-done.13.received_ref = bf16[512,256]{1,0:T(8,128)(2,1)S(1)} collective-permute-done((bf16[512,256]{1,0:T(8,128)(2,1)S(1)}, bf16[512,256]{1,0:T(8,128)(2,1)S(1)}, u32[]{:S(2)}, u32[]{:S(2)}) %collective-permute-start.13) | collective-permute-done | bytes 262176 | tf_op jit(solution)/shard_map/ppermute | solution.py:27
  70.8 0.0 collective-permute-done.9.refs_5_
  70.8 1.5 %shard_map.63 = f32[512,256]{1,0:T(8,128)} custom-call(bf16[512,512]{1,0:T(8,128)(2,1)S(1)} %get-tuple-element.30.refs_0_, bf16[512,512]{1,0:T(8,128)(2,1)S(1)} %get-tuple-element.31.refs_1_, bf16[512,512]{1,0:T(8,128)(2,1)S(1)} %get-tuple-element.32.refs_2_, bf16[512,256]{1,0:T(8,128)(2,1)S(1)} %collective-permute-done.7.refs_3_, ...), custom_call_target="tpu_custom_call" | custom-call | flops 402653184 | bytes 4456448 | tf_op jit(solution)/shard_map/pallas_call | solution.py:43
  (11 shorter events, 0.1 us)
Async XLA Ops:
  3.7 11.8 %collective-permute-start.4 = (bf16[2,512,256]{2,1,0:T(8,128)(2,1)S(1)}, bf16[2,512,256]{2,1,0:T(8,128)(2,1)S(1)}, u32[]{:S(2)}, u32[]{:S(2)}) collective-permute-start(bf16[2,512,256]{2,1,0:T(8,128)(2,1)S(1)} %get-tuple-element.40), channel_id=1, source_target_pairs={{0,1},{1,0},{2,3},{3,2},{4,5},{5,4},{6,7},{7,6},{8,9},{9,8},{10,11... | collective-permute-start | bytes 1572872 | tf_op jit(solution)/shard_map/ppermute | solution.py:31
  7.0 8.5 %collective-permute-start.5 = (bf16[512,256]{1,0:T(8,128)(2,1)S(1)}, bf16[512,256]{1,0:T(8,128)(2,1)S(1)}, u32[]{:S(2)}, u32[]{:S(2)}) collective-permute-start(bf16[512,256]{1,0:T(8,128)(2,1)S(1)} %get-tuple-element.43), channel_id=1, source_target_pairs={{0,31},{1,2},{2,1},{3,4},{4,3},{5,6},{6,5},{7,8},{8,7},{9,10},{10,... | collective-permute-start | bytes 786440 | tf_op jit(solution)/shard_map/ppermute | solution.py:36
  10.2 21.8 %collective-permute-start.3 = (bf16[2,512,256]{2,1,0:T(8,128)(2,1)S(1)}, bf16[2,512,256]{2,1,0:T(8,128)(2,1)S(1)}, u32[]{:S(2)}, u32[]{:S(2)}) collective-permute-start(bf16[2,512,256]{2,1,0:T(8,128)(2,1)S(1)} %get-tuple-element.36), channel_id=1, source_target_pairs={{0,31},{1,2},{2,1},{3,4},{4,3},{5,6},{6,5},{7,8},{8,7},{9,10},{10,... | collective-permute-start | bytes 1572872 | tf_op jit(solution)/shard_map/ppermute | solution.py:36
  12.1 12.8 %collective-permute-start = (bf16[512,256]{1,0:T(8,128)(2,1)S(1)}, bf16[512,256]{1,0:T(8,128)(2,1)S(1)}, u32[]{:S(2)}, u32[]{:S(2)}) collective-permute-start(bf16[512,256]{1,0:T(8,128)(2,1)S(1)} %get-tuple-element.33.wire_ref.refs_3_), channel_id=1, source_target_pairs={{0,224},{32,0},{64,32},{96,64},{128,96},{160,128},{192,160},{224,1... | collective-permute-start | bytes 786440 | tf_op jit(solution)/shard_map/ppermute | solution.py:27
  15.6 17.8 %collective-permute-start.6 = (bf16[512,256]{1,0:T(8,128)(2,1)S(1)}, bf16[512,256]{1,0:T(8,128)(2,1)S(1)}, u32[]{:S(2)}, u32[]{:S(2)}) collective-permute-start(bf16[512,256]{1,0:T(8,128)(2,1)S(1)} %fusion.3), channel_id=1, source_target_pairs={{0,32},{32,64},{64,96},{96,128},{128,160},{160,192},{192,224},{224... | collective-permute-start | bytes 786440 | tf_op jit(solution)/shard_map/ppermute | solution.py:27
  24.9 13.1 %collective-permute-start.1 = (bf16[2,512,256]{2,1,0:T(8,128)(2,1)S(1)}, bf16[2,512,256]{2,1,0:T(8,128)(2,1)S(1)}, u32[]{:S(2)}, u32[]{:S(2)}) collective-permute-start(bf16[2,512,256]{2,1,0:T(8,128)(2,1)S(1)} %pad_maximum_fusion), channel_id=1, source_target_pairs={{0,1},{1,0},{2,3},{3,2},{4,5},{5,4},{6,7},{7,6},{8,9},{9,8},{10,11... | collective-permute-start | bytes 1572872 | tf_op jit(solution)/shard_map/ppermute | solution.py:31
  32.0 6.1 %collective-permute-start.2 = (bf16[512,256]{1,0:T(8,128)(2,1)S(1)}, bf16[512,256]{1,0:T(8,128)(2,1)S(1)}, u32[]{:S(2)}, u32[]{:S(2)}) collective-permute-start(bf16[512,256]{1,0:T(8,128)(2,1)S(1)} %collective-permute-done.refs_3_), channel_id=1, source_target_pairs={{0,31},{1,2},{2,1},{3,4},{4,3},{5,6},{6,5},{7,8},{8,7},{9,10},{10,... | collective-permute-start | bytes 786440 | tf_op jit(solution)/shard_map/ppermute | solution.py:36
  32.6 5.5 %copy-start = (f32[512,256]{1,0:T(8,128)S(1)}, f32[512,256]{1,0:T(8,128)}, u32[]{:S(2)}) copy-start(f32[512,256]{1,0:T(8,128)} %refs_8_.3) | copy-start | bytes 1572868
  40.4 8.6 %collective-permute-start.11 = (bf16[2,512,256]{2,1,0:T(8,128)(2,1)S(1)}, bf16[2,512,256]{2,1,0:T(8,128)(2,1)S(1)}, u32[]{:S(2)}, u32[]{:S(2)}) collective-permute-start(bf16[2,512,256]{2,1,0:T(8,128)(2,1)S(1)} %get-tuple-element.50), channel_id=1, source_target_pairs={{0,1},{1,0},{2,3},{3,2},{4,5},{5,4},{6,7},{7,6},{8,9},{9,8},{10,11... | collective-permute-start | bytes 1572872 | tf_op jit(solution)/shard_map/ppermute | solution.py:31
  42.5 6.6 %collective-permute-start.12 = (bf16[512,256]{1,0:T(8,128)(2,1)S(1)}, bf16[512,256]{1,0:T(8,128)(2,1)S(1)}, u32[]{:S(2)}, u32[]{:S(2)}) collective-permute-start(bf16[512,256]{1,0:T(8,128)(2,1)S(1)} %get-tuple-element.53), channel_id=1, source_target_pairs={{0,31},{1,2},{2,1},{3,4},{4,3},{5,6},{6,5},{7,8},{8,7},{9,10},{10,... | collective-permute-start | bytes 786440 | tf_op jit(solution)/shard_map/ppermute | solution.py:36
  43.1 20.5 %collective-permute-start.10 = (bf16[2,512,256]{2,1,0:T(8,128)(2,1)S(1)}, bf16[2,512,256]{2,1,0:T(8,128)(2,1)S(1)}, u32[]{:S(2)}, u32[]{:S(2)}) collective-permute-start(bf16[2,512,256]{2,1,0:T(8,128)(2,1)S(1)} %get-tuple-element.49), channel_id=1, source_target_pairs={{0,31},{1,2},{2,1},{3,4},{4,3},{5,6},{6,5},{7,8},{8,7},{9,10},{10,... | collective-permute-start | bytes 1572872 | tf_op jit(solution)/shard_map/ppermute | solution.py:36
  45.1 17.7 %collective-permute-start.7 = (bf16[512,256]{1,0:T(8,128)(2,1)S(1)}, bf16[512,256]{1,0:T(8,128)(2,1)S(1)}, u32[]{:S(2)}, u32[]{:S(2)}) collective-permute-start(bf16[512,256]{1,0:T(8,128)(2,1)S(1)} %get-tuple-element.46.wire_ref.refs_3_), channel_id=1, source_target_pairs={{0,224},{32,0},{64,32},{96,64},{128,96},{160,128},{192,160},{224,1... | collective-permute-start | bytes 786440 | tf_op jit(solution)/shard_map/ppermute | solution.py:27
  49.2 21.5 %collective-permute-start.13 = (bf16[512,256]{1,0:T(8,128)(2,1)S(1)}, bf16[512,256]{1,0:T(8,128)(2,1)S(1)}, u32[]{:S(2)}, u32[]{:S(2)}) collective-permute-start(bf16[512,256]{1,0:T(8,128)(2,1)S(1)} %fusion.1), channel_id=1, source_target_pairs={{0,32},{32,64},{64,96},{96,128},{128,160},{160,192},{192,224},{224... | collective-permute-start | bytes 786440 | tf_op jit(solution)/shard_map/ppermute | solution.py:27
  62.8 7.9 %collective-permute-start.8 = (bf16[2,512,256]{2,1,0:T(8,128)(2,1)S(1)}, bf16[2,512,256]{2,1,0:T(8,128)(2,1)S(1)}, u32[]{:S(2)}, u32[]{:S(2)}) collective-permute-start(bf16[2,512,256]{2,1,0:T(8,128)(2,1)S(1)} %pad_maximum_fusion.1), channel_id=1, source_target_pairs={{0,1},{1,0},{2,3},{3,2},{4,5},{5,4},{6,7},{7,6},{8,9},{9,8},{10,11... | collective-permute-start | bytes 1572872 | tf_op jit(solution)/shard_map/ppermute | solution.py:31
  63.5 7.2 %collective-permute-start.9 = (bf16[512,256]{1,0:T(8,128)(2,1)S(1)}, bf16[512,256]{1,0:T(8,128)(2,1)S(1)}, u32[]{:S(2)}, u32[]{:S(2)}) collective-permute-start(bf16[512,256]{1,0:T(8,128)(2,1)S(1)} %collective-permute-done.7.refs_3_), channel_id=1, source_target_pairs={{0,31},{1,2},{2,1},{3,4},{4,3},{5,6},{6,5},{7,8},{8,7},{9,10},{10,... | collective-permute-start | bytes 786440 | tf_op jit(solution)/shard_map/ppermute | solution.py:36

commit v7 on v5

--- a/solution.py
+++ b/solution.py
@@ -198,6 +198,12 @@
     out_ref[...] = own_ref[...] + received_ref[...].astype(F32)
 
 
+def pack_body(down_ref, own_mate, own_far, mate_ref, far_ref):
+    for ref, own in ((mate_ref, own_mate), (far_ref, own_far)):
+        ref[0] = down_ref[...]
+        ref[1] = own[...]
+
+
 def final_body(*refs):
     product = with_cross(refs[:3], *refs[3:7], refs[10])
     refs[9][...] = advanced(product, *refs[7:9])
@@ -236,11 +242,12 @@
             )
         else:
             own_self, own_mate, own_far = call(third_body, (wide, small, small), 3 * work, [*own, perm])
-        from_far, _ = lax.optimization_barrier((from_far, own_self))
+        next_mate, next_far = call(pack_body, (double, double), HEAVY * work, [down, own_mate, own_far])
+        from_far, _ = lax.optimization_barrier((from_far, next_far))
         got = (partial + from_mate[0].astype(F32) + from_far[0].astype(F32)).astype(BF16)
         received = shifted(got, "ka", 1)
-        second_mate = mate(jnp.stack([down, own_mate]))
-        second_far = far(jnp.stack([down, own_far]))
+        second_mate = mate(next_mate)
+        second_far = far(next_far)
         known = call(own_body, wide, 3 * work, [*own, wire, from_mate, from_far, own_self], scratch=[staging])
         known = call(settle_body, wide, HEAVY * work, [known, received])
         args = [*cross, down, second_mate, second_far, known, drive, relax3]

time: 68.9 us -> 74 us (1.074)
  the two profiles are of different devices: /device:TPU:1 before, /device:TPU:224 now
where the time goes in v7:
time: 74 us; the launch traced here: 73.9 us
  waiting for transfers between devices  48.2 us (65%)
  Pallas kernels  12.8 us (17%)
  starting transfers between devices  12.5 us (17%)
    ppermute x4, waiting for transfers between devices, shifted(): lax.ppermute(value, axis, [(source, (source + steps) % count) for source...  48.2 us
    pallas_call x11, Pallas kernels, call(): pl.pallas_call(kernel, out_shape=outs, in_specs=specs or [VMEM] * len(arg...  12.8 us
    ppermute x4, starting transfers between devices, shifted(): lax.ppermute(value, axis, [(source, (source + steps) % count) for source...  10.7 us
  transfers between devices with their start and end apart: 12, of which 4 were waited for; matrix products, arithmetic and copies ran while one was open for 0% of the time, Pallas kernels for 7%

profile of v7, /device:TPU:224, one launch (start us, length us, event | category | flops | bytes accessed | tf_op | source)
XLA Modules:
  0.0 73.9 jit_solution(16383313205237653396)
XLA Ops:
  0.0 3.7 %shard_map.55 = (bf16[512,512]{1,0:T(8,128)(2,1)S(1)}, bf16[512,512]{1,0:T(8,128)(2,1)S(1)}, bf16[512,512]{1,0:T(8,128)(2,1)S(1)}, bf16[512,256]{1,0:T(8,128)(2,...) custom-call(bf16[256,4096]{1,0:T(8,128)(2,1)} %blocks_hbm.3, ...), custom_call_target="tpu_custom_call" | custom-call | flops 1207959552 | bytes 2625536 | tf_op jit(solution)/shard_map/pallas_call | solution.py:43
  3.7 5.5 %collective-permute-start = (bf16[512,256]{1,0:T(8,128)(2,1)S(1)}, bf16[512,256]{1,0:T(8,128)(2,1)S(1)}, u32[]{:S(2)}, u32[]{:S(2)}) collective-permute-start(bf16[512,256]{1,0:T(8,128)(2,1)S(1)} %get-tuple-element.37.refs_3_), channel_id=1, source_target_pairs={{0,224},{32,0},{64,32},{96,64},{128,96},{160,128},{192,160},{224,1... | collective-permute-start | bytes 786440 | tf_op jit(solution)/shard_map/ppermute | solution.py:27
  9.3 0.0 collective-permute-start.3
  9.3 1.1 %collective-permute-start.4 = (bf16[2,512,256]{2,1,0:T(8,128)(2,1)S(1)}, bf16[2,512,256]{2,1,0:T(8,128)(2,1)S(1)}, u32[]{:S(2)}, u32[]{:S(2)}) collective-permute-start(bf16[2,512,256]{2,1,0:T(8,128)(2,1)S(1)} %get-tuple-element.47), channel_id=1, source_target_pairs={{0,31},{1,2},{2,1},{3,4},{4,3},{5,6},{6,5},{7,8},{8,7},{9,10},{10,... | collective-permute-start | bytes 1572872 | tf_op jit(solution)/shard_map/ppermute | solution.py:36
  10.4 3.1 %shard_map.56 = (bf16[512,512]{1,0:T(8,128)(2,1)S(1)}, bf16[512,512]{1,0:T(8,128)(2,1)S(1)}, bf16[512,512]{1,0:T(8,128)(2,1)S(1)}, f32[512,256]{1,0:T(8,128)S(1)...) custom-call(bf16[256,4096]{1,0:T(8,128)(2,1)} %blocks_hbm.3, s32[1,256]{1,0:T(1,128)} %bitcast.21, ...), custom_call_target="tpu_custom_call" | custom-call | flops 1207959552 | bytes 2361344 | tf_op jit(solution)/shard_map/pallas_call | solution.py:43
  13.6 6.9 %collective-permute-done.down_ref.refs_3_ = bf16[512,256]{1,0:T(8,128)(2,1)S(1)} collective-permute-done((bf16[512,256]{1,0:T(8,128)(2,1)S(1)}, bf16[512,256]{1,0:T(8,128)(2,1)S(1)}, u32[]{:S(2)}, u32[]{:S(2)}) %collective-permute-start) | collective-permute-done | bytes 262176 | tf_op jit(solution)/shard_map/ppermute | solution.py:27
  20.5 0.1 shard_map.57
  20.5 0.0 collective-permute-done.4.refs_5_
  20.5 0.0 collective-permute-done.3.refs_4_
  20.6 0.1 fusion.1
  20.6 2.5 %collective-permute-start.5 = (bf16[512,256]{1,0:T(8,128)(2,1)S(1)}, bf16[512,256]{1,0:T(8,128)(2,1)S(1)}, u32[]{:S(2)}, u32[]{:S(2)}) collective-permute-start(bf16[512,256]{1,0:T(8,128)(2,1)S(1)} %fusion.1), channel_id=1, source_target_pairs={{0,32},{32,64},{64,96},{96,128},{128,160},{160,192},{192,224},{224... | collective-permute-start | bytes 786440 | tf_op jit(solution)/shard_map/ppermute | solution.py:27
  23.2 0.0 collective-permute-start.2
  23.2 0.6 shard_map.58.own_ref
  23.8 0.0 copy-start
  23.8 14.4 %collective-permute-done.5.received_ref = bf16[512,256]{1,0:T(8,128)(2,1)S(1)} collective-permute-done((bf16[512,256]{1,0:T(8,128)(2,1)S(1)}, bf16[512,256]{1,0:T(8,128)(2,1)S(1)}, u32[]{:S(2)}, u32[]{:S(2)}) %collective-permute-start.5) | collective-permute-done | bytes 262176 | tf_op jit(solution)/shard_map/ppermute | solution.py:27
  38.3 0.0 collective-permute-done.1.refs_4_
  38.3 2.4 %shard_map.60 = (bf16[512,256]{1,0:T(8,128)(2,1)S(1)}, bf16[512,256]{1,0:T(8,128)(2,1)S(1)}, f32[512,256]{1,0:T(8,128)S(1)}, bf16[2,512,256]{2,1,0:T(8,128)(2,1)S(1)}, bf16[2,512,256]{2,1,0:T(8,128)(2,1)S(1)}) custom-call(bf16[512,512]{1,0:T(8,128)(2,1)S(1)} %get-tuple-element.34.refs_0_, bf16[512,512]{1,0:T(8,128)(2,1)S(1)} %get-tuple-element.35.refs_1_, ...), custom_call_target="tpu_custom_call" | custom-call | flops 805306368 | bytes 4194304 | tf_op jit(solution)/shard_map/pallas_call | solution.py:43
  40.7 2.6 %collective-permute-start.6 = (bf16[512,256]{1,0:T(8,128)(2,1)S(1)}, bf16[512,256]{1,0:T(8,128)(2,1)S(1)}, u32[]{:S(2)}, u32[]{:S(2)}) collective-permute-start(bf16[512,256]{1,0:T(8,128)(2,1)S(1)} %get-tuple-element.52.refs_3_), channel_id=1, source_target_pairs={{0,224},{32,0},{64,32},{96,64},{128,96},{160,128},{192,160},{224,1... | collective-permute-start | bytes 786440 | tf_op jit(solution)/shard_map/ppermute | solution.py:27
  43.3 0.0 collective-permute-start.10
  43.3 0.6 shard_map.61
  43.9 10.7 %collective-permute-done.6.down_ref.refs_3_ = bf16[512,256]{1,0:T(8,128)(2,1)S(1)} collective-permute-done((bf16[512,256]{1,0:T(8,128)(2,1)S(1)}, bf16[512,256]{1,0:T(8,128)(2,1)S(1)}, u32[]{:S(2)}, u32[]{:S(2)}) %collective-permute-start.6) | collective-permute-done | bytes 262176 | tf_op jit(solution)/shard_map/ppermute | solution.py:27
  54.7 0.1 shard_map.62
  54.7 0.0 collective-permute-done.10.refs_5_
  54.7 0.0 collective-permute-done.9.refs_4_
  54.8 0.1 fusion
  54.8 0.1 collective-permute-start.11
  54.9 0.1 collective-permute-start.8
  55.0 0.5 collective-permute-start.7
  55.5 0.6 shard_map.63.own_ref
  56.1 16.1 %collective-permute-done.11.received_ref = bf16[512,256]{1,0:T(8,128)(2,1)S(1)} collective-permute-done((bf16[512,256]{1,0:T(8,128)(2,1)S(1)}, bf16[512,256]{1,0:T(8,128)(2,1)S(1)}, u32[]{:S(2)}, u32[]{:S(2)}) %collective-permute-start.11) | collective-permute-done | bytes 262176 | tf_op jit(solution)/shard_map/ppermute | solution.py:27
  72.3 0.0 collective-permute-done.7.refs_4_
  72.3 1.5 %shard_map.65 = f32[512,256]{1,0:T(8,128)} custom-call(bf16[512,512]{1,0:T(8,128)(2,1)S(1)} %get-tuple-element.34.refs_0_, bf16[512,512]{1,0:T(8,128)(2,1)S(1)} %get-tuple-element.35.refs_1_, bf16[512,512]{1,0:T(8,128)(2,1)S(1)} %get-tuple-element.36.refs_2_, bf16[512,256]{1,0:T(8,128)(2,1)S(1)} %collective-permute-done.6.down_ref.refs_3_, ...), custom_call_target="tpu_custom_call" | custom-call | flops 402653184 | bytes 4194304 | tf_op jit(solution)/shard_map/pallas_call | solution.py:43
  (7 shorter events, 0.1 us)
Async XLA Ops:
  3.7 16.7 %collective-permute-start = (bf16[512,256]{1,0:T(8,128)(2,1)S(1)}, bf16[512,256]{1,0:T(8,128)(2,1)S(1)}, u32[]{:S(2)}, u32[]{:S(2)}) collective-permute-start(bf16[512,256]{1,0:T(8,128)(2,1)S(1)} %get-tuple-element.37.refs_3_), channel_id=1, source_target_pairs={{0,224},{32,0},{64,32},{96,64},{128,96},{160,128},{192,160},{224,1... | collective-permute-start | bytes 786440 | tf_op jit(solution)/shard_map/ppermute | solution.py:27
  9.3 11.3 %collective-permute-start.3 = (bf16[2,512,256]{2,1,0:T(8,128)(2,1)S(1)}, bf16[2,512,256]{2,1,0:T(8,128)(2,1)S(1)}, u32[]{:S(2)}, u32[]{:S(2)}) collective-permute-start(bf16[2,512,256]{2,1,0:T(8,128)(2,1)S(1)} %get-tuple-element.46), channel_id=1, source_target_pairs={{0,1},{1,0},{2,3},{3,2},{4,5},{5,4},{6,7},{7,6},{8,9},{9,8},{10,11... | collective-permute-start | bytes 1572872 | tf_op jit(solution)/shard_map/ppermute | solution.py:31
  9.3 11.3 %collective-permute-start.4 = (bf16[2,512,256]{2,1,0:T(8,128)(2,1)S(1)}, bf16[2,512,256]{2,1,0:T(8,128)(2,1)S(1)}, u32[]{:S(2)}, u32[]{:S(2)}) collective-permute-start(bf16[2,512,256]{2,1,0:T(8,128)(2,1)S(1)} %get-tuple-element.47), channel_id=1, source_target_pairs={{0,31},{1,2},{2,1},{3,4},{4,3},{5,6},{6,5},{7,8},{8,7},{9,10},{10,... | collective-permute-start | bytes 1572872 | tf_op jit(solution)/shard_map/ppermute | solution.py:36
  20.6 17.6 %collective-permute-start.5 = (bf16[512,256]{1,0:T(8,128)(2,1)S(1)}, bf16[512,256]{1,0:T(8,128)(2,1)S(1)}, u32[]{:S(2)}, u32[]{:S(2)}) collective-permute-start(bf16[512,256]{1,0:T(8,128)(2,1)S(1)} %fusion.1), channel_id=1, source_target_pairs={{0,32},{32,64},{64,96},{96,128},{128,160},{160,192},{192,224},{224... | collective-permute-start | bytes 786440 | tf_op jit(solution)/shard_map/ppermute | solution.py:27
  23.2 15.1 %collective-permute-start.2 = (bf16[2,512,256]{2,1,0:T(8,128)(2,1)S(1)}, bf16[2,512,256]{2,1,0:T(8,128)(2,1)S(1)}, u32[]{:S(2)}, u32[]{:S(2)}) collective-permute-start(bf16[2,512,256]{2,1,0:T(8,128)(2,1)S(1)} %get-tuple-element.42), channel_id=1, source_target_pairs={{0,31},{1,2},{2,1},{3,4},{4,3},{5,6},{6,5},{7,8},{8,7},{9,10},{10,... | collective-permute-start | bytes 1572872 | tf_op jit(solution)/shard_map/ppermute | solution.py:36
  23.2 15.1 %collective-permute-start.1 = (bf16[2,512,256]{2,1,0:T(8,128)(2,1)S(1)}, bf16[2,512,256]{2,1,0:T(8,128)(2,1)S(1)}, u32[]{:S(2)}, u32[]{:S(2)}) collective-permute-start(bf16[2,512,256]{2,1,0:T(8,128)(2,1)S(1)} %get-tuple-element.41), channel_id=1, source_target_pairs={{0,1},{1,0},{2,3},{3,2},{4,5},{5,4},{6,7},{7,6},{8,9},{9,8},{10,11... | collective-permute-start | bytes 1572872 | tf_op jit(solution)/shard_map/ppermute | solution.py:31
  23.8 14.5 %copy-start = (f32[512,256]{1,0:T(8,128)S(1)}, f32[512,256]{1,0:T(8,128)}, u32[]{:S(2)}) copy-start(f32[512,256]{1,0:T(8,128)} %refs_7_.3) | copy-start | bytes 1572868
  40.7 14.0 %collective-permute-start.6 = (bf16[512,256]{1,0:T(8,128)(2,1)S(1)}, bf16[512,256]{1,0:T(8,128)(2,1)S(1)}, u32[]{:S(2)}, u32[]{:S(2)}) collective-permute-start(bf16[512,256]{1,0:T(8,128)(2,1)S(1)} %get-tuple-element.52.refs_3_), channel_id=1, source_target_pairs={{0,224},{32,0},{64,32},{96,64},{128,96},{160,128},{192,160},{224,1... | collective-permute-start | bytes 786440 | tf_op jit(solution)/shard_map/ppermute | solution.py:27
  43.3 11.4 %collective-permute-start.9 = (bf16[2,512,256]{2,1,0:T(8,128)(2,1)S(1)}, bf16[2,512,256]{2,1,0:T(8,128)(2,1)S(1)}, u32[]{:S(2)}, u32[]{:S(2)}) collective-permute-start(bf16[2,512,256]{2,1,0:T(8,128)(2,1)S(1)} %get-tuple-element.58), channel_id=1, source_target_pairs={{0,1},{1,0},{2,3},{3,2},{4,5},{5,4},{6,7},{7,6},{8,9},{9,8},{10,11... | collective-permute-start | bytes 1572872 | tf_op jit(solution)/shard_map/ppermute | solution.py:31
  43.3 11.4 %collective-permute-start.10 = (bf16[2,512,256]{2,1,0:T(8,128)(2,1)S(1)}, bf16[2,512,256]{2,1,0:T(8,128)(2,1)S(1)}, u32[]{:S(2)}, u32[]{:S(2)}) collective-permute-start(bf16[2,512,256]{2,1,0:T(8,128)(2,1)S(1)} %get-tuple-element.59), channel_id=1, source_target_pairs={{0,31},{1,2},{2,1},{3,4},{4,3},{5,6},{6,5},{7,8},{8,7},{9,10},{10,... | collective-permute-start | bytes 1572872 | tf_op jit(solution)/shard_map/ppermute | solution.py:36
  54.8 17.4 %collective-permute-start.11 = (bf16[512,256]{1,0:T(8,128)(2,1)S(1)}, bf16[512,256]{1,0:T(8,128)(2,1)S(1)}, u32[]{:S(2)}, u32[]{:S(2)}) collective-permute-start(bf16[512,256]{1,0:T(8,128)(2,1)S(1)} %fusion), channel_id=1, source_target_pairs={{0,32},{32,64},{64,96},{96,128},{128,160},{160,192},{192,224},{224... | collective-permute-start | bytes 786440 | tf_op jit(solution)/shard_map/ppermute | solution.py:27
  54.9 17.4 %collective-permute-start.8 = (bf16[2,512,256]{2,1,0:T(8,128)(2,1)S(1)}, bf16[2,512,256]{2,1,0:T(8,128)(2,1)S(1)}, u32[]{:S(2)}, u32[]{:S(2)}) collective-permute-start(bf16[2,512,256]{2,1,0:T(8,128)(2,1)S(1)} %get-tuple-element.57), channel_id=1, source_target_pairs={{0,31},{1,2},{2,1},{3,4},{4,3},{5,6},{6,5},{7,8},{8,7},{9,10},{10,... | collective-permute-start | bytes 1572872 | tf_op jit(solution)/shard_map/ppermute | solution.py:36
  55.0 17.3 %collective-permute-start.7 = (bf16[2,512,256]{2,1,0:T(8,128)(2,1)S(1)}, bf16[2,512,256]{2,1,0:T(8,128)(2,1)S(1)}, u32[]{:S(2)}, u32[]{:S(2)}) collective-permute-start(bf16[2,512,256]{2,1,0:T(8,128)(2,1)S(1)} %get-tuple-element.56), channel_id=1, source_target_pairs={{0,1},{1,0},{2,3},{3,2},{4,5},{5,4},{6,7},{7,6},{8,9},{9,8},{10,11... | collective-permute-start | bytes 1572872 | tf_op jit(solution)/shard_map/ppermute | solution.py:31

commit v8 on v6

--- a/solution.py
+++ b/solution.py
@@ -165,17 +165,17 @@
 
 
 def own_body(*refs):
-    mats, (wire_ref, mate_ref, far_ref, self_ref), (out_ref, scratch) = refs[:3], refs[3:7], refs[7:]
+    mats, (wire_ref, mate_ref, self_ref), (out_ref, scratch) = refs[:2], refs[2:5], refs[5:]
     straight = dot(mats[0][...], wire_ref[...])
     straight += dot(mats[1][...], mate_ref[1])
-    straight += dot(mats[2][...], far_ref[0])
     out_ref[...] = self_ref[...] + restored(straight, scratch)
 
 
-def with_cross(cross, down_ref, mate_ref, far_ref, other_ref, known_ref, scratch):
-    straight = dot(cross[0][...], down_ref[...])
-    straight += dot(cross[1][...], mate_ref[0])
-    straight += dot(cross[2][...], far_ref[...])
+def with_cross(mats, down_ref, mate_ref, far_ref, other_ref, known_ref, scratch):
+    straight = dot(mats[0][...], down_ref[...])
+    straight += dot(mats[1][...], mate_ref[0])
+    straight += dot(mats[2][...], far_ref[...])
+    straight += dot(mats[3][...], other_ref[0])
     return known_ref[...] + mate_ref[1].astype(F32) + other_ref[1].astype(F32) + restored(straight, scratch)
 
 
@@ -185,11 +185,11 @@
 
 
 def update_body(*refs):
-    cross, nexts, (drive_ref, relax_ref) = refs[:3], refs[3:8], refs[8:10]
-    perm_ref, wire_ref, self_ref, mate_ref, far_ref, scratch = refs[10:]
-    field = advanced(with_cross(cross, *nexts, scratch), drive_ref, relax_ref)
+    mats, nexts, (drive_ref, relax_ref) = refs[:4], refs[4:9], refs[9:11]
+    perm_ref, wire_ref, self_ref, mate_ref, far_ref, scratch = refs[11:]
+    field = advanced(with_cross(mats, *nexts, scratch), drive_ref, relax_ref)
     interleave(field, scratch, perm_ref)
-    emit(cross, field.astype(BF16), perm_ref, wire_ref, self_ref, mate_ref, far_ref)
+    emit(mats, field.astype(BF16), perm_ref, wire_ref, self_ref, mate_ref, far_ref)
 
 
 def settle_body(own_ref, received_ref, out_ref):
@@ -197,8 +197,8 @@
 
 
 def final_body(*refs):
-    product = with_cross(refs[:3], *refs[3:8], refs[11])
-    refs[10][...] = advanced(product, *refs[8:10])
+    product = with_cross(refs[:4], *refs[4:9], refs[12])
+    refs[11][...] = advanced(product, *refs[9:11])
 
 
 def local(drive, relax, blocks, row_block, col_block):
@@ -235,14 +235,15 @@
         else:
             own_self, own_mate, own_far = call(own_partials, (wide, small, double), 3 * work, [*own, perm, wire])
         other_far = far(own_far)
-        from_far, _ = lax.optimization_barrier((from_far, own_self))
+        if sweep == 0:
+            from_far, _ = lax.optimization_barrier((from_far, own_self))
         got = (partial + from_mate[0].astype(F32) + from_far.astype(F32)).astype(BF16)
         received = shifted(got, "ka", 1)
         next_mate = mate(jnp.stack([down, own_mate]))
         next_far = far(down)
-        known = call(own_body, wide, 3 * work, [*own, wire, from_mate, other_far, own_self], scratch=[staging])
+        known = call(own_body, wide, 2 * work, [*own[:2], wire, from_mate, own_self], scratch=[staging])
         known = call(settle_body, wide, HEAVY * work, [known, received])
-        args = [*cross, down, next_mate, next_far, other_far, known, drive, relax3]
+        args = [*cross, own[2], down, next_mate, next_far, other_far, known, drive, relax3]
         if sweep + 1 == ITERS:
             return call(final_body, wide, 3 * work, args, scratch=[staging])
         perm, wire, partial, to_mate, to_far = call(update_body, emitted, 6 * work, args, scratch=[staging])

time: 72.4 us -> 68.7 us (0.949)
  the two profiles are of different devices: /device:TPU:1 before, /device:TPU:8 now
where the time goes in v8:
time: 68.7 us; the launch traced here: 68.5 us
  starting transfers between devices  32.3 us (47%)
  waiting for transfers between devices  23 us (33%)
  Pallas kernels  12.7 us (18%)
    ppermute x4, waiting for transfers between devices, shifted(): lax.ppermute(value, axis, [(source, (source + steps) % count) for source...  22.5 us
    ppermute x6, starting transfers between devices, far(): lax.ppermute(value, 'rows', [(i, (i + 1 if i & 1 else i - 1) % count) for...  21.2 us
    pallas_call x9, Pallas kernels, call(): pl.pallas_call(kernel, out_shape=outs, in_specs=specs or [VMEM] * len(arg...  12.7 us
    ppermute x4, starting transfers between devices, shifted(): lax.ppermute(value, axis, [(source, (source + steps) % count) for source...  10.8 us
  transfers between devices with their start and end apart: 14, of which 4 were waited for; matrix products, arithmetic and copies ran while one was open for 0% of the time, Pallas kernels for 7%

profile of v8, /device:TPU:8, one launch (start us, length us, event | category | flops | bytes accessed | tf_op | source)
XLA Modules:
  0.0 68.5 jit_solution(11008762293303084440)
XLA Ops:
  0.0 3.7 %shard_map.55 = (bf16[512,512]{1,0:T(8,128)(2,1)S(1)}, bf16[512,512]{1,0:T(8,128)(2,1)S(1)}, bf16[512,512]{1,0:T(8,128)(2,1)S(1)}, bf16[512,256]{1,0:T(8,128)(2,...) custom-call(bf16[256,4096]{1,0:T(8,128)(2,1)} %blocks_hbm.3, ...), custom_call_target="tpu_custom_call" | custom-call | flops 1207959552 | bytes 2625536 | tf_op jit(solution)/shard_map/pallas_call | solution.py:43
  3.7 0.1 collective-permute-start.4
  3.8 6.9 %collective-permute-start.5 = (bf16[512,256]{1,0:T(8,128)(2,1)S(1)}, bf16[512,256]{1,0:T(8,128)(2,1)S(1)}, u32[]{:S(2)}, u32[]{:S(2)}) collective-permute-start(bf16[512,256]{1,0:T(8,128)(2,1)S(1)} %get-tuple-element.42), channel_id=1, source_target_pairs={{0,31},{1,2},{2,1},{3,4},{4,3},{5,6},{6,5},{7,8},{8,7},{9,10},{10,... | collective-permute-start | bytes 786440 | tf_op jit(solution)/shard_map/ppermute | solution.py:36
  10.7 2.6 %collective-permute-start = (bf16[512,256]{1,0:T(8,128)(2,1)S(1)}, bf16[512,256]{1,0:T(8,128)(2,1)S(1)}, u32[]{:S(2)}, u32[]{:S(2)}) collective-permute-start(bf16[512,256]{1,0:T(8,128)(2,1)S(1)} %get-tuple-element.33.wire_ref.refs_2_), channel_id=1, source_target_pairs={{0,224},{32,0},{64,32},{96,64},{128,96},{160,128},{192,160},{224,1... | collective-permute-start | bytes 786440 | tf_op jit(solution)/shard_map/ppermute | solution.py:27
  13.3 3.2 %shard_map.56 = (bf16[512,512]{1,0:T(8,128)(2,1)S(1)}, bf16[512,512]{1,0:T(8,128)(2,1)S(1)}, bf16[512,512]{1,0:T(8,128)(2,1)S(1)}, f32[512,256]{1,0:T(8,128)S(1)...) custom-call(bf16[256,4096]{1,0:T(8,128)(2,1)} %blocks_hbm.3, s32[1,256]{1,0:T(1,128)} %bitcast.23, ...), custom_call_target="tpu_custom_call" | custom-call | flops 1207959552 | bytes 2623488 | tf_op jit(solution)/shard_map/pallas_call | solution.py:43
  16.5 0.0 collective-permute-done.5
  16.5 0.1 fusion.3
  16.6 1.1 %collective-permute-start.6 = (bf16[512,256]{1,0:T(8,128)(2,1)S(1)}, bf16[512,256]{1,0:T(8,128)(2,1)S(1)}, u32[]{:S(2)}, u32[]{:S(2)}) collective-permute-start(bf16[512,256]{1,0:T(8,128)(2,1)S(1)} %fusion.3), channel_id=1, source_target_pairs={{0,32},{32,64},{64,96},{96,128},{128,160},{160,192},{192,224},{224... | collective-permute-start | bytes 786440 | tf_op jit(solution)/shard_map/ppermute | solution.py:27
  17.8 3.0 %collective-permute-start.3 = (bf16[2,512,256]{2,1,0:T(8,128)(2,1)S(1)}, bf16[2,512,256]{2,1,0:T(8,128)(2,1)S(1)}, u32[]{:S(2)}, u32[]{:S(2)}) collective-permute-start(bf16[2,512,256]{2,1,0:T(8,128)(2,1)S(1)} %get-tuple-element.36), channel_id=1, source_target_pairs={{0,31},{1,2},{2,1},{3,4},{4,3},{5,6},{6,5},{7,8},{8,7},{9,10},{10,... | collective-permute-start | bytes 1572872 | tf_op jit(solution)/shard_map/ppermute | solution.py:36
  20.7 0.4 collective-permute-done.refs_4_
  21.1 0.1 pad_maximum_fusion
  21.2 0.1 collective-permute-start.1
  21.3 2.6 %collective-permute-start.2 = (bf16[512,256]{1,0:T(8,128)(2,1)S(1)}, bf16[512,256]{1,0:T(8,128)(2,1)S(1)}, u32[]{:S(2)}, u32[]{:S(2)}) collective-permute-start(bf16[512,256]{1,0:T(8,128)(2,1)S(1)} %collective-permute-done.refs_4_), channel_id=1, source_target_pairs={{0,31},{1,2},{2,1},{3,4},{4,3},{5,6},{6,5},{7,8},{8,7},{9,10},{10,... | collective-permute-start | bytes 786440 | tf_op jit(solution)/shard_map/ppermute | solution.py:36
  23.9 0.5 shard_map.57.own_ref
  24.4 0.0 copy-start
  24.4 9.5 %collective-permute-done.6.received_ref = bf16[512,256]{1,0:T(8,128)(2,1)S(1)} collective-permute-done((bf16[512,256]{1,0:T(8,128)(2,1)S(1)}, bf16[512,256]{1,0:T(8,128)(2,1)S(1)}, u32[]{:S(2)}, u32[]{:S(2)}) %collective-permute-start.6) | collective-permute-done | bytes 262176 | tf_op jit(solution)/shard_map/ppermute | solution.py:27
  33.9 0.0 collective-permute-done.2.refs_6_
  34.0 2.5 %shard_map.59 = (bf16[512,256]{1,0:T(8,128)(2,1)S(1)}, bf16[512,256]{1,0:T(8,128)(2,1)S(1)}, f32[512,256]{1,0:T(8,128)S(1)}, bf16[2,512,256]{2,1,0:T(8,128)(2,1)S(1)}, bf16[512,256]{1,0:T(8,128)(2,1)S(1)}) custom-call(bf16[512,512]{1,0:T(8,128)(2,1)S(1)} %get-tuple-element.29.refs_0_, bf16[512,512]{1,0:T(8,128)(2,1)S(1)} %get-tuple-element.30.refs_1_, ...), custom_call_target="tpu_custom_call" | custom-call | flops 805306368 | bytes 4980736 | tf_op jit(solution)/shard_map/pallas_call | solution.py:43
  36.5 0.1 collective-permute-start.11
  36.6 3.2 %collective-permute-start.12 = (bf16[512,256]{1,0:T(8,128)(2,1)S(1)}, bf16[512,256]{1,0:T(8,128)(2,1)S(1)}, u32[]{:S(2)}, u32[]{:S(2)}) collective-permute-start(bf16[512,256]{1,0:T(8,128)(2,1)S(1)} %get-tuple-element.52), channel_id=1, source_target_pairs={{0,31},{1,2},{2,1},{3,4},{4,3},{5,6},{6,5},{7,8},{8,7},{9,10},{10,... | collective-permute-start | bytes 786440 | tf_op jit(solution)/shard_map/ppermute | solution.py:36
  39.8 4.4 %collective-permute-start.7 = (bf16[512,256]{1,0:T(8,128)(2,1)S(1)}, bf16[512,256]{1,0:T(8,128)(2,1)S(1)}, u32[]{:S(2)}, u32[]{:S(2)}) collective-permute-start(bf16[512,256]{1,0:T(8,128)(2,1)S(1)} %get-tuple-element.45.wire_ref.refs_2_), channel_id=1, source_target_pairs={{0,224},{32,0},{64,32},{96,64},{128,96},{160,128},{192,160},{224,1... | collective-permute-start | bytes 786440 | tf_op jit(solution)/shard_map/ppermute | solution.py:27
  44.2 0.5 collective-permute-done.12
  44.7 0.1 fusion.1
  44.8 2.6 %collective-permute-start.13 = (bf16[512,256]{1,0:T(8,128)(2,1)S(1)}, bf16[512,256]{1,0:T(8,128)(2,1)S(1)}, u32[]{:S(2)}, u32[]{:S(2)}) collective-permute-start(bf16[512,256]{1,0:T(8,128)(2,1)S(1)} %fusion.1), channel_id=1, source_target_pairs={{0,32},{32,64},{64,96},{96,128},{128,160},{160,192},{192,224},{224... | collective-permute-start | bytes 786440 | tf_op jit(solution)/shard_map/ppermute | solution.py:27
  47.4 0.6 shard_map.60
  48.0 3.3 %collective-permute-start.10 = (bf16[2,512,256]{2,1,0:T(8,128)(2,1)S(1)}, bf16[2,512,256]{2,1,0:T(8,128)(2,1)S(1)}, u32[]{:S(2)}, u32[]{:S(2)}) collective-permute-start(bf16[2,512,256]{2,1,0:T(8,128)(2,1)S(1)} %get-tuple-element.48), channel_id=1, source_target_pairs={{0,31},{1,2},{2,1},{3,4},{4,3},{5,6},{6,5},{7,8},{8,7},{9,10},{10,... | collective-permute-start | bytes 1572872 | tf_op jit(solution)/shard_map/ppermute | solution.py:36
  51.4 0.1 pad_maximum_fusion.1
  51.4 0.1 collective-permute-start.8
  51.5 2.2 %collective-permute-start.9 = (bf16[512,256]{1,0:T(8,128)(2,1)S(1)}, bf16[512,256]{1,0:T(8,128)(2,1)S(1)}, u32[]{:S(2)}, u32[]{:S(2)}) collective-permute-start(bf16[512,256]{1,0:T(8,128)(2,1)S(1)} %collective-permute-done.7.refs_4_), channel_id=1, source_target_pairs={{0,31},{1,2},{2,1},{3,4},{4,3},{5,6},{6,5},{7,8},{8,7},{9,10},{10,... | collective-permute-start | bytes 786440 | tf_op jit(solution)/shard_map/ppermute | solution.py:36
  53.8 0.5 shard_map.61.own_ref
  54.2 12.6 %collective-permute-done.13.received_ref = bf16[512,256]{1,0:T(8,128)(2,1)S(1)} collective-permute-done((bf16[512,256]{1,0:T(8,128)(2,1)S(1)}, bf16[512,256]{1,0:T(8,128)(2,1)S(1)}, u32[]{:S(2)}, u32[]{:S(2)}) %collective-permute-start.13) | collective-permute-done | bytes 262176 | tf_op jit(solution)/shard_map/ppermute | solution.py:27
  66.9 1.6 %shard_map.63 = f32[512,256]{1,0:T(8,128)} custom-call(bf16[512,512]{1,0:T(8,128)(2,1)S(1)} %get-tuple-element.29.refs_0_, bf16[512,512]{1,0:T(8,128)(2,1)S(1)} %get-tuple-element.30.refs_1_, bf16[512,512]{1,0:T(8,128)(2,1)S(1)} %get-tuple-element.31.refs_2_, bf16[512,512]{1,0:T(8,128)(2,1)S(1)} %get-tuple-element.34.refs_3_.far_in, ...), custom_call_target="tpu_custom_call" | custom-call | flops 402653184 | bytes 4980736 | tf_op jit(solution)/shard_map/pallas_call | solution.py:43
  (11 shorter events, 0.1 us)
Async XLA Ops:
  3.7 12.8 %collective-permute-start.4 = (bf16[2,512,256]{2,1,0:T(8,128)(2,1)S(1)}, bf16[2,512,256]{2,1,0:T(8,128)(2,1)S(1)}, u32[]{:S(2)}, u32[]{:S(2)}) collective-permute-start(bf16[2,512,256]{2,1,0:T(8,128)(2,1)S(1)} %get-tuple-element.39), channel_id=1, source_target_pairs={{0,1},{1,0},{2,3},{3,2},{4,5},{5,4},{6,7},{7,6},{8,9},{9,8},{10,11... | collective-permute-start | bytes 1572872 | tf_op jit(solution)/shard_map/ppermute | solution.py:31
  3.8 12.7 %collective-permute-start.5 = (bf16[512,256]{1,0:T(8,128)(2,1)S(1)}, bf16[512,256]{1,0:T(8,128)(2,1)S(1)}, u32[]{:S(2)}, u32[]{:S(2)}) collective-permute-start(bf16[512,256]{1,0:T(8,128)(2,1)S(1)} %get-tuple-element.42), channel_id=1, source_target_pairs={{0,31},{1,2},{2,1},{3,4},{4,3},{5,6},{6,5},{7,8},{8,7},{9,10},{10,... | collective-permute-start | bytes 786440 | tf_op jit(solution)/shard_map/ppermute | solution.py:36
  10.7 10.4 %collective-permute-start = (bf16[512,256]{1,0:T(8,128)(2,1)S(1)}, bf16[512,256]{1,0:T(8,128)(2,1)S(1)}, u32[]{:S(2)}, u32[]{:S(2)}) collective-permute-start(bf16[512,256]{1,0:T(8,128)(2,1)S(1)} %get-tuple-element.33.wire_ref.refs_2_), channel_id=1, source_target_pairs={{0,224},{32,0},{64,32},{96,64},{128,96},{160,128},{192,160},{224,1... | collective-permute-start | bytes 786440 | tf_op jit(solution)/shard_map/ppermute | solution.py:27
  16.6 17.3 %collective-permute-start.6 = (bf16[512,256]{1,0:T(8,128)(2,1)S(1)}, bf16[512,256]{1,0:T(8,128)(2,1)S(1)}, u32[]{:S(2)}, u32[]{:S(2)}) collective-permute-start(bf16[512,256]{1,0:T(8,128)(2,1)S(1)} %fusion.3), channel_id=1, source_target_pairs={{0,32},{32,64},{64,96},{96,128},{128,160},{160,192},{192,224},{224... | collective-permute-start | bytes 786440 | tf_op jit(solution)/shard_map/ppermute | solution.py:27
  17.8 16.2 %collective-permute-start.3 = (bf16[2,512,256]{2,1,0:T(8,128)(2,1)S(1)}, bf16[2,512,256]{2,1,0:T(8,128)(2,1)S(1)}, u32[]{:S(2)}, u32[]{:S(2)}) collective-permute-start(bf16[2,512,256]{2,1,0:T(8,128)(2,1)S(1)} %get-tuple-element.36), channel_id=1, source_target_pairs={{0,31},{1,2},{2,1},{3,4},{4,3},{5,6},{6,5},{7,8},{8,7},{9,10},{10,... | collective-permute-start | bytes 1572872 | tf_op jit(solution)/shard_map/ppermute | solution.py:36
  21.2 12.8 %collective-permute-start.1 = (bf16[2,512,256]{2,1,0:T(8,128)(2,1)S(1)}, bf16[2,512,256]{2,1,0:T(8,128)(2,1)S(1)}, u32[]{:S(2)}, u32[]{:S(2)}) collective-permute-start(bf16[2,512,256]{2,1,0:T(8,128)(2,1)S(1)} %pad_maximum_fusion), channel_id=1, source_target_pairs={{0,1},{1,0},{2,3},{3,2},{4,5},{5,4},{6,7},{7,6},{8,9},{9,8},{10,11... | collective-permute-start | bytes 1572872 | tf_op jit(solution)/shard_map/ppermute | solution.py:31
  21.3 12.7 %collective-permute-start.2 = (bf16[512,256]{1,0:T(8,128)(2,1)S(1)}, bf16[512,256]{1,0:T(8,128)(2,1)S(1)}, u32[]{:S(2)}, u32[]{:S(2)}) collective-permute-start(bf16[512,256]{1,0:T(8,128)(2,1)S(1)} %collective-permute-done.refs_4_), channel_id=1, source_target_pairs={{0,31},{1,2},{2,1},{3,4},{4,3},{5,6},{6,5},{7,8},{8,7},{9,10},{10,... | collective-permute-start | bytes 786440 | tf_op jit(solution)/shard_map/ppermute | solution.py:36
  24.4 9.6 %copy-start = (f32[512,256]{1,0:T(8,128)S(1)}, f32[512,256]{1,0:T(8,128)}, u32[]{:S(2)}) copy-start(f32[512,256]{1,0:T(8,128)} %refs_9_.3) | copy-start | bytes 1572868
  36.5 8.2 %collective-permute-start.11 = (bf16[2,512,256]{2,1,0:T(8,128)(2,1)S(1)}, bf16[2,512,256]{2,1,0:T(8,128)(2,1)S(1)}, u32[]{:S(2)}, u32[]{:S(2)}) collective-permute-start(bf16[2,512,256]{2,1,0:T(8,128)(2,1)S(1)} %get-tuple-element.49), channel_id=1, source_target_pairs={{0,1},{1,0},{2,3},{3,2},{4,5},{5,4},{6,7},{7,6},{8,9},{9,8},{10,11... | collective-permute-start | bytes 1572872 | tf_op jit(solution)/shard_map/ppermute | solution.py:31
  36.6 8.1 %collective-permute-start.12 = (bf16[512,256]{1,0:T(8,128)(2,1)S(1)}, bf16[512,256]{1,0:T(8,128)(2,1)S(1)}, u32[]{:S(2)}, u32[]{:S(2)}) collective-permute-start(bf16[512,256]{1,0:T(8,128)(2,1)S(1)} %get-tuple-element.52), channel_id=1, source_target_pairs={{0,31},{1,2},{2,1},{3,4},{4,3},{5,6},{6,5},{7,8},{8,7},{9,10},{10,... | collective-permute-start | bytes 786440 | tf_op jit(solution)/shard_map/ppermute | solution.py:36
  39.8 11.5 %collective-permute-start.7 = (bf16[512,256]{1,0:T(8,128)(2,1)S(1)}, bf16[512,256]{1,0:T(8,128)(2,1)S(1)}, u32[]{:S(2)}, u32[]{:S(2)}) collective-permute-start(bf16[512,256]{1,0:T(8,128)(2,1)S(1)} %get-tuple-element.45.wire_ref.refs_2_), channel_id=1, source_target_pairs={{0,224},{32,0},{64,32},{96,64},{128,96},{160,128},{192,160},{224,1... | collective-permute-start | bytes 786440 | tf_op jit(solution)/shard_map/ppermute | solution.py:27
  44.8 22.0 %collective-permute-start.13 = (bf16[512,256]{1,0:T(8,128)(2,1)S(1)}, bf16[512,256]{1,0:T(8,128)(2,1)S(1)}, u32[]{:S(2)}, u32[]{:S(2)}) collective-permute-start(bf16[512,256]{1,0:T(8,128)(2,1)S(1)} %fusion.1), channel_id=1, source_target_pairs={{0,32},{32,64},{64,96},{96,128},{128,160},{160,192},{192,224},{224... | collective-permute-start | bytes 786440 | tf_op jit(solution)/shard_map/ppermute | solution.py:27
  48.0 18.8 %collective-permute-start.10 = (bf16[2,512,256]{2,1,0:T(8,128)(2,1)S(1)}, bf16[2,512,256]{2,1,0:T(8,128)(2,1)S(1)}, u32[]{:S(2)}, u32[]{:S(2)}) collective-permute-start(bf16[2,512,256]{2,1,0:T(8,128)(2,1)S(1)} %get-tuple-element.48), channel_id=1, source_target_pairs={{0,31},{1,2},{2,1},{3,4},{4,3},{5,6},{6,5},{7,8},{8,7},{9,10},{10,... | collective-permute-start | bytes 1572872 | tf_op jit(solution)/shard_map/ppermute | solution.py:36
  51.4 15.5 %collective-permute-start.8 = (bf16[2,512,256]{2,1,0:T(8,128)(2,1)S(1)}, bf16[2,512,256]{2,1,0:T(8,128)(2,1)S(1)}, u32[]{:S(2)}, u32[]{:S(2)}) collective-permute-start(bf16[2,512,256]{2,1,0:T(8,128)(2,1)S(1)} %pad_maximum_fusion.1), channel_id=1, source_target_pairs={{0,1},{1,0},{2,3},{3,2},{4,5},{5,4},{6,7},{7,6},{8,9},{9,8},{10,11... | collective-permute-start | bytes 1572872 | tf_op jit(solution)/shard_map/ppermute | solution.py:31
  51.5 15.4 %collective-permute-start.9 = (bf16[512,256]{1,0:T(8,128)(2,1)S(1)}, bf16[512,256]{1,0:T(8,128)(2,1)S(1)}, u32[]{:S(2)}, u32[]{:S(2)}) collective-permute-start(bf16[512,256]{1,0:T(8,128)(2,1)S(1)} %collective-permute-done.7.refs_4_), channel_id=1, source_target_pairs={{0,31},{1,2},{2,1},{3,4},{4,3},{5,6},{6,5},{7,8},{8,7},{9,10},{10,... | collective-permute-start | bytes 786440 | tf_op jit(solution)/shard_map/ppermute | solution.py:36

commit v9 on v8

--- a/solution.py
+++ b/solution.py
@@ -34,6 +34,21 @@
 def far(value):
     count = lax.axis_size("rows")
     return lax.ppermute(value, "rows", [(i, (i + 1 if i & 1 else i - 1) % count) for i in range(count)])
+
+
+def wrapped(place, count):
+    return ((place + 1) % (count // 2) == 0) | (place % (count // 2) == 0)
+
+
+def far_slanted(value, step):
+    devices, count = lax.axis_size("ka"), lax.axis_size("rows")
+    pairs = []
+    for ka in range(devices):
+        for i in range(count):
+            other = (i + 1 if i & 1 else i - 1) % count
+            target = (ka + step) % devices if wrapped(i, count) else ka
+            pairs.append((ka * count + i, target * count + other))
+    return lax.ppermute(value, ("ka", "rows"), pairs)
 
 
 def call(kernel, outs, flops, args, specs=None, scratch=()):
@@ -133,8 +148,8 @@
 
 
 def first_body(sizes, blocks_hbm, row_hbm, col_hbm, drive_hbm, relax_hbm, *refs):
-    cross, (perm_ref, wire_ref, self_ref, mate_ref, far_ref, spread_ref) = refs[:3], refs[3:9]
-    blocks, ids, drive, relax, scratch, sems = refs[9:]
+    cross, (perm_ref, wire_ref, self_ref, mate_ref, far_ref, spread_ref, flag_ref) = refs[:3], refs[3:10]
+    blocks, ids, drive, relax, scratch, sems = refs[10:]
     later = [
         pltpu.make_async_copy(drive_hbm, drive, sems.at[2 + PIECES]),
         pltpu.make_async_copy(relax_hbm, relax, sems.at[3 + PIECES]),
@@ -144,6 +159,10 @@
     build(1, sizes, blocks_hbm, row_hbm, col_hbm, blocks, ids, sems, cross)
     for copy in later:
         copy.wait()
+    place = (jnp.max(ids[0:1, :], axis=1, keepdims=True) >> log2(sizes[0])) & (sizes[1] - 1)
+    half = sizes[1] // 2 - 1
+    slanted = (((place + 1) & half) == 0) | ((place & half) == 0)
+    flag_ref[...] = jnp.broadcast_to(jnp.where(slanted, 1.0, 0.0), flag_ref.shape)
     spread_ref[...] = jnp.broadcast_to(relax[...], (LANES, relax.shape[1])).T
     field = drive[...]
     interleave(field, scratch, perm_ref)
@@ -165,10 +184,11 @@
 
 
 def own_body(*refs):
-    mats, (wire_ref, mate_ref, self_ref), (out_ref, scratch) = refs[:2], refs[2:5], refs[5:]
+    mats, (wire_ref, mate_ref, self_ref, partial_ref, flag_ref), (out_ref, scratch) = refs[:2], refs[2:7], refs[7:]
     straight = dot(mats[0][...], wire_ref[...])
     straight += dot(mats[1][...], mate_ref[1])
-    out_ref[...] = self_ref[...] + restored(straight, scratch)
+    here = jnp.where(flag_ref[...] > 0, partial_ref[...].astype(F32), 0.0)
+    out_ref[...] = self_ref[...] + here + restored(straight, scratch)
 
 
 def with_cross(mats, down_ref, mate_ref, far_ref, other_ref, known_ref, scratch):
@@ -217,15 +237,16 @@
     relax2 = relax.reshape(1, -1)
     work = 2 * rows * rows * channels
     spread = jax.ShapeDtypeStruct((rows, LANES), F32)
-    *cross, perm, wire, partial, to_mate, to_far, relax3 = call(
-        functools.partial(first_body, sizes), (*matrices, *emitted, spread), 9 * work,
+    *cross, perm, wire, partial, to_mate, to_far, relax3, flag = call(
+        functools.partial(first_body, sizes), (*matrices, *emitted, spread, jax.ShapeDtypeStruct((1, channels), F32)), 9 * work,
         [blocks, row2, col2, drive, relax2], [HBM] * 5,
         fetch + [pltpu.VMEM(drive.shape, F32), pltpu.VMEM((1, rows), F32), staging, pltpu.SemaphoreType.DMA((4 + PIECES,))],
     )
 
+    slanted = flag > 0
     for sweep in range(ITERS):
         down = shifted(wire, "ka", -1)
-        from_far = far(to_far)
+        from_far = far_slanted(to_far, 1)
         from_mate = mate(to_mate)
         if sweep == 0:
             *own, own_self, own_mate, own_far = call(
@@ -237,11 +258,14 @@
         other_far = far(own_far)
         if sweep == 0:
             from_far, _ = lax.optimization_barrier((from_far, own_self))
-        got = (partial + from_mate[0].astype(F32) + from_far.astype(F32)).astype(BF16)
+        got = partial + from_mate[0].astype(F32) + jnp.where(slanted, 0.0, from_far.astype(F32))
+        got = got.astype(BF16)
         received = shifted(got, "ka", 1)
         next_mate = mate(jnp.stack([down, own_mate]))
-        next_far = far(down)
-        known = call(own_body, wide, 2 * work, [*own[:2], wire, from_mate, own_self], scratch=[staging])
+        next_far = far_slanted(jnp.where(slanted, wire, down), -1)
+        known = call(
+            own_body, wide, 2 * work, [*own[:2], wire, from_mate, own_self, from_far, flag], scratch=[staging]
+        )
         known = call(settle_body, wide, HEAVY * work, [known, received])
         args = [*cross, own[2], down, next_mate, next_far, other_far, known, drive, relax3]
         if sweep + 1 == ITERS:

time: 68.7 us -> 72.6 us (1.057)
  the two profiles are of different devices: /device:TPU:8 before, /device:TPU:30 now
where the time goes in v9:
time: 72.6 us; the launch traced here: 72.4 us
  waiting for transfers between devices  36.8 us (51%)
  starting transfers between devices  22.2 us (31%)
  Pallas kernels  12.8 us (18%)
    ppermute x4, waiting for transfers between devices, shifted(): lax.ppermute(value, axis, [(source, (source + steps) % count) for source...  20.3 us
    ppermute x4, waiting for transfers between devices, far_slanted(): return lax.ppermute(value, ('ka', 'rows'), pairs)  16.5 us
    pallas_call x9, Pallas kernels, call(): pl.pallas_call(kernel, out_shape=outs, in_specs=specs or [VMEM] * len(arg...  12.8 us
    ppermute x4, starting transfers between devices, far_slanted(): return lax.ppermute(value, ('ka', 'rows'), pairs)  12.5 us
    ppermute x4, starting transfers between devices, shifted(): lax.ppermute(value, axis, [(source, (source + steps) % count) for source...  9.18 us
  transfers between devices with their start and end apart: 14, of which 8 were waited for; matrix products, arithmetic and copies ran while one was open for 1% of the time, Pallas kernels for 7%

profile of v9, /device:TPU:30, one launch (start us, length us, event | category | flops | bytes accessed | tf_op | source)
XLA Modules:
  0.0 72.4 jit_solution(7618015013135191974)
XLA Ops:
  0.0 3.8 %shard_map.55 = (bf16[512,512]{1,0:T(8,128)(2,1)S(1)}, bf16[512,512]{1,0:T(8,128)(2,1)S(1)}, bf16[512,512]{1,0:T(8,128)(2,1)S(1)}, bf16[512,256]{1,0:T(8,128)(2,...) custom-call(bf16[256,4096]{1,0:T(8,128)(2,1)} %blocks_hbm.3, ...), custom_call_target="tpu_custom_call" | custom-call | flops 1207959552 | bytes 2625536 | tf_op jit(solution)/shard_map/pallas_call | solution.py:58
  3.8 0.1 collective-permute-start.4
  3.9 5.5 %collective-permute-start.5 = (bf16[512,256]{1,0:T(8,128)(2,1)S(1)}, bf16[512,256]{1,0:T(8,128)(2,1)S(1)}, u32[]{:S(2)}, u32[]{:S(2)}) collective-permute-start(bf16[512,256]{1,0:T(8,128)(2,1)S(1)} %get-tuple-element.43), channel_id=1, source_target_pairs={{0,63},{1,2},{2,1},{3,4},{4,3},{5,6},{6,5},{7,8},{8,7},{9,10},{10,... | collective-permute-start | bytes 786440 | tf_op jit(solution)/shard_map/ppermute | solution.py:51
  9.4 2.8 %collective-permute-start = (bf16[512,256]{1,0:T(8,128)(2,1)S(1)}, bf16[512,256]{1,0:T(8,128)(2,1)S(1)}, u32[]{:S(2)}, u32[]{:S(2)}) collective-permute-start(bf16[512,256]{1,0:T(8,128)(2,1)S(1)} %get-tuple-element.34.wire_ref.refs_2_), channel_id=1, source_target_pairs={{0,224},{32,0},{64,32},{96,64},{128,96},{160,128},{192,160},{224,1... | collective-permute-start | bytes 786440 | tf_op jit(solution)/shard_map/ppermute | solution.py:27
  12.2 3.2 %shard_map.56 = (bf16[512,512]{1,0:T(8,128)(2,1)S(1)}, bf16[512,512]{1,0:T(8,128)(2,1)S(1)}, bf16[512,512]{1,0:T(8,128)(2,1)S(1)}, f32[512,256]{1,0:T(8,128)S(1)...) custom-call(bf16[256,4096]{1,0:T(8,128)(2,1)} %blocks_hbm.3, s32[1,256]{1,0:T(1,128)} %bitcast.23, ...), custom_call_target="tpu_custom_call" | custom-call | flops 1207959552 | bytes 2623488 | tf_op jit(solution)/shard_map/pallas_call | solution.py:58
  15.4 0.1 collective-permute-start.3
  15.5 0.4 collective-permute-done.5.refs_5_
  15.9 0.1 fusion.3
  16.0 3.5 %collective-permute-start.6 = (bf16[512,256]{1,0:T(8,128)(2,1)S(1)}, bf16[512,256]{1,0:T(8,128)(2,1)S(1)}, u32[]{:S(2)}, u32[]{:S(2)}) collective-permute-start(bf16[512,256]{1,0:T(8,128)(2,1)S(1)} %fusion.3), channel_id=1, source_target_pairs={{0,32},{32,64},{64,96},{96,128},{128,160},{160,192},{192,224},{224... | collective-permute-start | bytes 786440 | tf_op jit(solution)/shard_map/ppermute | solution.py:27
  19.6 2.3 %collective-permute-done.refs_4_ = bf16[512,256]{1,0:T(8,128)(2,1)S(1)} collective-permute-done((bf16[512,256]{1,0:T(8,128)(2,1)S(1)}, bf16[512,256]{1,0:T(8,128)(2,1)S(1)}, u32[]{:S(2)}, u32[]{:S(2)}) %collective-permute-start) | collective-permute-done | bytes 262176 | tf_op jit(solution)/shard_map/ppermute | solution.py:27
  22.0 0.9 %collective-permute-start.2 = (bf16[512,256]{1,0:T(8,128)(2,1)S(1)}, bf16[512,256]{1,0:T(8,128)(2,1)S(1)}, u32[]{:S(2)}, u32[]{:S(2)}) collective-permute-start(bf16[512,256]{1,0:T(8,128)(2,1)S(1)} %broadcast_select_fusion.1), channel_id=1, source_target_pairs={{0,255},{1,2},{2,1},{3,4},{4,3},{5,6},{6,5},{7,8},{8,7},{9,10},{10... | collective-permute-start | bytes 786440 | tf_op jit(solution)/shard_map/ppermute | solution.py:51
  22.9 0.1 collective-permute-start.1
  23.0 0.5 shard_map.57.own_ref
  23.5 7.5 %collective-permute-done.6.received_ref = bf16[512,256]{1,0:T(8,128)(2,1)S(1)} collective-permute-done((bf16[512,256]{1,0:T(8,128)(2,1)S(1)}, bf16[512,256]{1,0:T(8,128)(2,1)S(1)}, u32[]{:S(2)}, u32[]{:S(2)}) %collective-permute-start.6) | collective-permute-done | bytes 262176 | tf_op jit(solution)/shard_map/ppermute | solution.py:27
  31.1 2.2 %collective-permute-done.2.refs_6_ = bf16[512,256]{1,0:T(8,128)(2,1)S(1)} collective-permute-done((bf16[512,256]{1,0:T(8,128)(2,1)S(1)}, bf16[512,256]{1,0:T(8,128)(2,1)S(1)}, u32[]{:S(2)}, u32[]{:S(2)}) %collective-permute-start.2) | collective-permute-done | bytes 262176 | tf_op jit(solution)/shard_map/ppermute | solution.py:51
  33.3 2.5 %shard_map.59 = (bf16[512,256]{1,0:T(8,128)(2,1)S(1)}, bf16[512,256]{1,0:T(8,128)(2,1)S(1)}, f32[512,256]{1,0:T(8,128)S(1)}, bf16[2,512,256]{2,1,0:T(8,128)(2,1)S(1)}, bf16[512,256]{1,0:T(8,128)(2,1)S(1)}) custom-call(bf16[512,512]{1,0:T(8,128)(2,1)S(1)} %get-tuple-element.30.refs_0_, bf16[512,512]{1,0:T(8,128)(2,1)S(1)} %get-tuple-element.31.refs_1_, ...), custom_call_target="tpu_custom_call" | custom-call | flops 805306368 | bytes 4980736 | tf_op jit(solution)/shard_map/pallas_call | solution.py:58
  35.8 0.1 collective-permute-start.11
  35.9 6.0 %collective-permute-start.12 = (bf16[512,256]{1,0:T(8,128)(2,1)S(1)}, bf16[512,256]{1,0:T(8,128)(2,1)S(1)}, u32[]{:S(2)}, u32[]{:S(2)}) collective-permute-start(bf16[512,256]{1,0:T(8,128)(2,1)S(1)} %get-tuple-element.53), channel_id=1, source_target_pairs={{0,63},{1,2},{2,1},{3,4},{4,3},{5,6},{6,5},{7,8},{8,7},{9,10},{10,... | collective-permute-start | bytes 786440 | tf_op jit(solution)/shard_map/ppermute | solution.py:51
  41.9 0.2 collective-permute-start.7
  42.1 0.6 shard_map.60
  42.8 0.1 collective-permute-start.10
  42.9 3.7 %collective-permute-done.12.refs_5_ = bf16[512,256]{1,0:T(8,128)(2,1)S(1)} collective-permute-done((bf16[512,256]{1,0:T(8,128)(2,1)S(1)}, bf16[512,256]{1,0:T(8,128)(2,1)S(1)}, u32[]{:S(2)}, u32[]{:S(2)}) %collective-permute-start.12) | collective-permute-done | bytes 262176 | tf_op jit(solution)/shard_map/ppermute | solution.py:51
  46.5 0.1 fusion.1
  46.6 2.6 %collective-permute-start.13 = (bf16[512,256]{1,0:T(8,128)(2,1)S(1)}, bf16[512,256]{1,0:T(8,128)(2,1)S(1)}, u32[]{:S(2)}, u32[]{:S(2)}) collective-permute-start(bf16[512,256]{1,0:T(8,128)(2,1)S(1)} %fusion.1), channel_id=1, source_target_pairs={{0,32},{32,64},{64,96},{96,128},{128,160},{160,192},{192,224},{224... | collective-permute-start | bytes 786440 | tf_op jit(solution)/shard_map/ppermute | solution.py:27
  49.2 10.2 %collective-permute-done.7.refs_4_ = bf16[512,256]{1,0:T(8,128)(2,1)S(1)} collective-permute-done((bf16[512,256]{1,0:T(8,128)(2,1)S(1)}, bf16[512,256]{1,0:T(8,128)(2,1)S(1)}, u32[]{:S(2)}, u32[]{:S(2)}) %collective-permute-start.7) | collective-permute-done | bytes 262176 | tf_op jit(solution)/shard_map/ppermute | solution.py:27
  59.5 0.1 collective-permute-start.9
  59.6 0.1 pad_maximum_fusion.1
  59.6 0.1 collective-permute-start.8
  59.7 0.5 shard_map.61.own_ref
  60.2 0.3 collective-permute-done.13.received_ref
  60.5 10.2 %collective-permute-done.9.refs_6_ = bf16[512,256]{1,0:T(8,128)(2,1)S(1)} collective-permute-done((bf16[512,256]{1,0:T(8,128)(2,1)S(1)}, bf16[512,256]{1,0:T(8,128)(2,1)S(1)}, u32[]{:S(2)}, u32[]{:S(2)}) %collective-permute-start.9) | collective-permute-done | bytes 262176 | tf_op jit(solution)/shard_map/ppermute | solution.py:51
  70.8 1.6 %shard_map.63 = f32[512,256]{1,0:T(8,128)} custom-call(bf16[512,512]{1,0:T(8,128)(2,1)S(1)} %get-tuple-element.30.refs_0_, bf16[512,512]{1,0:T(8,128)(2,1)S(1)} %get-tuple-element.31.refs_1_, bf16[512,512]{1,0:T(8,128)(2,1)S(1)} %get-tuple-element.32.refs_2_, bf16[512,512]{1,0:T(8,128)(2,1)S(1)} %get-tuple-element.35.refs_3_.far_in, ...), custom_call_target="tpu_custom_call" | custom-call | flops 402653184 | bytes 4980736 | tf_op jit(solution)/shard_map/pallas_call | solution.py:58
  (14 shorter events, 0.2 us)
Async XLA Ops:
  3.8 12.1 %collective-permute-start.4 = (bf16[2,512,256]{2,1,0:T(8,128)(2,1)S(1)}, bf16[2,512,256]{2,1,0:T(8,128)(2,1)S(1)}, u32[]{:S(2)}, u32[]{:S(2)}) collective-permute-start(bf16[2,512,256]{2,1,0:T(8,128)(2,1)S(1)} %get-tuple-element.41), channel_id=1, source_target_pairs={{0,1},{1,0},{2,3},{3,2},{4,5},{5,4},{6,7},{7,6},{8,9},{9,8},{10,11... | collective-permute-start | bytes 1572872 | tf_op jit(solution)/shard_map/ppermute | solution.py:31
  3.9 12.0 %collective-permute-start.5 = (bf16[512,256]{1,0:T(8,128)(2,1)S(1)}, bf16[512,256]{1,0:T(8,128)(2,1)S(1)}, u32[]{:S(2)}, u32[]{:S(2)}) collective-permute-start(bf16[512,256]{1,0:T(8,128)(2,1)S(1)} %get-tuple-element.43), channel_id=1, source_target_pairs={{0,63},{1,2},{2,1},{3,4},{4,3},{5,6},{6,5},{7,8},{8,7},{9,10},{10,... | collective-permute-start | bytes 786440 | tf_op jit(solution)/shard_map/ppermute | solution.py:51
  9.4 12.5 %collective-permute-start = (bf16[512,256]{1,0:T(8,128)(2,1)S(1)}, bf16[512,256]{1,0:T(8,128)(2,1)S(1)}, u32[]{:S(2)}, u32[]{:S(2)}) collective-permute-start(bf16[512,256]{1,0:T(8,128)(2,1)S(1)} %get-tuple-element.34.wire_ref.refs_2_), channel_id=1, source_target_pairs={{0,224},{32,0},{64,32},{96,64},{128,96},{160,128},{192,160},{224,1... | collective-permute-start | bytes 786440 | tf_op jit(solution)/shard_map/ppermute | solution.py:27
  15.4 17.9 %collective-permute-start.3 = (bf16[2,512,256]{2,1,0:T(8,128)(2,1)S(1)}, bf16[2,512,256]{2,1,0:T(8,128)(2,1)S(1)}, u32[]{:S(2)}, u32[]{:S(2)}) collective-permute-start(bf16[2,512,256]{2,1,0:T(8,128)(2,1)S(1)} %get-tuple-element.38), channel_id=1, source_target_pairs={{0,31},{1,2},{2,1},{3,4},{4,3},{5,6},{6,5},{7,8},{8,7},{9,10},{10,... | collective-permute-start | bytes 1572872 | tf_op jit(solution)/shard_map/ppermute | solution.py:36
  16.0 15.0 %collective-permute-start.6 = (bf16[512,256]{1,0:T(8,128)(2,1)S(1)}, bf16[512,256]{1,0:T(8,128)(2,1)S(1)}, u32[]{:S(2)}, u32[]{:S(2)}) collective-permute-start(bf16[512,256]{1,0:T(8,128)(2,1)S(1)} %fusion.3), channel_id=1, source_target_pairs={{0,32},{32,64},{64,96},{96,128},{128,160},{160,192},{192,224},{224... | collective-permute-start | bytes 786440 | tf_op jit(solution)/shard_map/ppermute | solution.py:27
  22.0 11.3 %collective-permute-start.2 = (bf16[512,256]{1,0:T(8,128)(2,1)S(1)}, bf16[512,256]{1,0:T(8,128)(2,1)S(1)}, u32[]{:S(2)}, u32[]{:S(2)}) collective-permute-start(bf16[512,256]{1,0:T(8,128)(2,1)S(1)} %broadcast_select_fusion.1), channel_id=1, source_target_pairs={{0,255},{1,2},{2,1},{3,4},{4,3},{5,6},{6,5},{7,8},{8,7},{9,10},{10... | collective-permute-start | bytes 786440 | tf_op jit(solution)/shard_map/ppermute | solution.py:51
  22.9 10.4 %collective-permute-start.1 = (bf16[2,512,256]{2,1,0:T(8,128)(2,1)S(1)}, bf16[2,512,256]{2,1,0:T(8,128)(2,1)S(1)}, u32[]{:S(2)}, u32[]{:S(2)}) collective-permute-start(bf16[2,512,256]{2,1,0:T(8,128)(2,1)S(1)} %pad_maximum_fusion), channel_id=1, source_target_pairs={{0,1},{1,0},{2,3},{3,2},{4,5},{5,4},{6,7},{7,6},{8,9},{9,8},{10,11... | collective-permute-start | bytes 1572872 | tf_op jit(solution)/shard_map/ppermute | solution.py:31
  23.5 9.8 %copy-start = (f32[512,256]{1,0:T(8,128)S(1)}, f32[512,256]{1,0:T(8,128)}, u32[]{:S(2)}) copy-start(f32[512,256]{1,0:T(8,128)} %refs_9_.3) | copy-start | bytes 1572868
  35.8 10.7 %collective-permute-start.11 = (bf16[2,512,256]{2,1,0:T(8,128)(2,1)S(1)}, bf16[2,512,256]{2,1,0:T(8,128)(2,1)S(1)}, u32[]{:S(2)}, u32[]{:S(2)}) collective-permute-start(bf16[2,512,256]{2,1,0:T(8,128)(2,1)S(1)} %get-tuple-element.51), channel_id=1, source_target_pairs={{0,1},{1,0},{2,3},{3,2},{4,5},{5,4},{6,7},{7,6},{8,9},{9,8},{10,11... | collective-permute-start | bytes 1572872 | tf_op jit(solution)/shard_map/ppermute | solution.py:31
  35.9 10.6 %collective-permute-start.12 = (bf16[512,256]{1,0:T(8,128)(2,1)S(1)}, bf16[512,256]{1,0:T(8,128)(2,1)S(1)}, u32[]{:S(2)}, u32[]{:S(2)}) collective-permute-start(bf16[512,256]{1,0:T(8,128)(2,1)S(1)} %get-tuple-element.53), channel_id=1, source_target_pairs={{0,63},{1,2},{2,1},{3,4},{4,3},{5,6},{6,5},{7,8},{8,7},{9,10},{10,... | collective-permute-start | bytes 786440 | tf_op jit(solution)/shard_map/ppermute | solution.py:51
  41.9 17.5 %collective-permute-start.7 = (bf16[512,256]{1,0:T(8,128)(2,1)S(1)}, bf16[512,256]{1,0:T(8,128)(2,1)S(1)}, u32[]{:S(2)}, u32[]{:S(2)}) collective-permute-start(bf16[512,256]{1,0:T(8,128)(2,1)S(1)} %get-tuple-element.47.wire_ref.refs_2_), channel_id=1, source_target_pairs={{0,224},{32,0},{64,32},{96,64},{128,96},{160,128},{192,160},{224,1... | collective-permute-start | bytes 786440 | tf_op jit(solution)/shard_map/ppermute | solution.py:27
  42.8 28.0 %collective-permute-start.10 = (bf16[2,512,256]{2,1,0:T(8,128)(2,1)S(1)}, bf16[2,512,256]{2,1,0:T(8,128)(2,1)S(1)}, u32[]{:S(2)}, u32[]{:S(2)}) collective-permute-start(bf16[2,512,256]{2,1,0:T(8,128)(2,1)S(1)} %get-tuple-element.50), channel_id=1, source_target_pairs={{0,31},{1,2},{2,1},{3,4},{4,3},{5,6},{6,5},{7,8},{8,7},{9,10},{10,... | collective-permute-start | bytes 1572872 | tf_op jit(solution)/shard_map/ppermute | solution.py:36
  46.6 13.9 %collective-permute-start.13 = (bf16[512,256]{1,0:T(8,128)(2,1)S(1)}, bf16[512,256]{1,0:T(8,128)(2,1)S(1)}, u32[]{:S(2)}, u32[]{:S(2)}) collective-permute-start(bf16[512,256]{1,0:T(8,128)(2,1)S(1)} %fusion.1), channel_id=1, source_target_pairs={{0,32},{32,64},{64,96},{96,128},{128,160},{160,192},{192,224},{224... | collective-permute-start | bytes 786440 | tf_op jit(solution)/shard_map/ppermute | solution.py:27
  59.5 11.3 %collective-permute-start.9 = (bf16[512,256]{1,0:T(8,128)(2,1)S(1)}, bf16[512,256]{1,0:T(8,128)(2,1)S(1)}, u32[]{:S(2)}, u32[]{:S(2)}) collective-permute-start(bf16[512,256]{1,0:T(8,128)(2,1)S(1)} %broadcast_select_fusion), channel_id=1, source_target_pairs={{0,255},{1,2},{2,1},{3,4},{4,3},{5,6},{6,5},{7,8},{8,7},{9,10},{10... | collective-permute-start | bytes 786440 | tf_op jit(solution)/shard_map/ppermute | solution.py:51
  59.6 11.2 %collective-permute-start.8 = (bf16[2,512,256]{2,1,0:T(8,128)(2,1)S(1)}, bf16[2,512,256]{2,1,0:T(8,128)(2,1)S(1)}, u32[]{:S(2)}, u32[]{:S(2)}) collective-permute-start(bf16[2,512,256]{2,1,0:T(8,128)(2,1)S(1)} %pad_maximum_fusion.1), channel_id=1, source_target_pairs={{0,1},{1,0},{2,3},{3,2},{4,5},{5,4},{6,7},{7,6},{8,9},{9,8},{10,11... | collective-permute-start | bytes 1572872 | tf_op jit(solution)/shard_map/ppermute | solution.py:31

commit v10 on v9

--- a/solution.py
+++ b/solution.py
@@ -255,12 +255,13 @@
             )
         else:
             own_self, own_mate, own_far = call(own_partials, (wide, small, double), 3 * work, [*own, perm, wire])
-        other_far = far(own_far)
         if sweep == 0:
             from_far, _ = lax.optimization_barrier((from_far, own_self))
         got = partial + from_mate[0].astype(F32) + jnp.where(slanted, 0.0, from_far.astype(F32))
         got = got.astype(BF16)
         received = shifted(got, "ka", 1)
+        own_far, _ = lax.optimization_barrier((own_far, got))
+        other_far = far(own_far)
         next_mate = mate(jnp.stack([down, own_mate]))
         next_far = far_slanted(jnp.where(slanted, wire, down), -1)
         known = call(

time: 72.6 us -> 74.5 us (1.026)
  the two profiles are of different devices: /device:TPU:30 before, /device:TPU:1 now
where the time goes in v10:
time: 74.5 us; the launch traced here: 73.3 us
  starting transfers between devices  32 us (43%)
  waiting for transfers between devices  27.9 us (37%)
  Pallas kernels  12.8 us (17%)
    ppermute x4, starting transfers between devices, mate(): lax.ppermute(value, 'rows', [(i, i ^ 1) for i in range(lax.axis_size('row...  23.2 us
    ppermute x2, waiting for transfers between devices, far(): lax.ppermute(value, 'rows', [(i, (i + 1 if i & 1 else i - 1) % count) for...  14.7 us
    pallas_call x9, Pallas kernels, call(): pl.pallas_call(kernel, out_shape=outs, in_specs=specs or [VMEM] * len(arg...  12.8 us
    ppermute x4, waiting for transfers between devices, shifted(): lax.ppermute(value, axis, [(source, (source + steps) % count) for source...  6.66 us
    ppermute x4, starting transfers between devices, shifted(): lax.ppermute(value, axis, [(source, (source + steps) % count) for source...  6.17 us
    ppermute x4, waiting for transfers between devices, far_slanted(): return lax.ppermute(value, ('ka', 'rows'), pairs)  4.56 us
    ppermute x4, starting transfers between devices, far_slanted(): return lax.ppermute(value, ('ka', 'rows'), pairs)  2.68 us
    ppermute x4, waiting for transfers between devices, mate(): lax.ppermute(value, 'rows', [(i, i ^ 1) for i in range(lax.axis_size('row...  1.93 us
  transfers between devices with their start and end apart: 14, of which 7 were waited for; matrix products, arithmetic and copies ran while one was open for 1% of the time, Pallas kernels for 7%

profile of v10, /device:TPU:1, one launch (start us, length us, event | category | flops | bytes accessed | tf_op | source)
XLA Modules:
  0.0 73.3 jit_solution(2688720695026626348)
XLA Ops:
  0.0 3.8 %shard_map.55 = (bf16[512,512]{1,0:T(8,128)(2,1)S(1)}, bf16[512,512]{1,0:T(8,128)(2,1)S(1)}, bf16[512,512]{1,0:T(8,128)(2,1)S(1)}, bf16[512,256]{1,0:T(8,128)(2,...) custom-call(bf16[256,4096]{1,0:T(8,128)(2,1)} %blocks_hbm.3, ...), custom_call_target="tpu_custom_call" | custom-call | flops 1207959552 | bytes 2625536 | tf_op jit(solution)/shard_map/pallas_call | solution.py:58
  3.8 3.3 %collective-permute-start.3 = (bf16[2,512,256]{2,1,0:T(8,128)(2,1)S(1)}, bf16[2,512,256]{2,1,0:T(8,128)(2,1)S(1)}, u32[]{:S(2)}, u32[]{:S(2)}) collective-permute-start(bf16[2,512,256]{2,1,0:T(8,128)(2,1)S(1)} %get-tuple-element.42), channel_id=1, source_target_pairs={{0,1},{1,0},{2,3},{3,2},{4,5},{5,4},{6,7},{7,6},{8,9},{9,8},{10,11... | collective-permute-start | bytes 1572872 | tf_op jit(solution)/shard_map/ppermute | solution.py:31
  7.1 5.1 %collective-permute-start = (bf16[512,256]{1,0:T(8,128)(2,1)S(1)}, bf16[512,256]{1,0:T(8,128)(2,1)S(1)}, u32[]{:S(2)}, u32[]{:S(2)}) collective-permute-start(bf16[512,256]{1,0:T(8,128)(2,1)S(1)} %get-tuple-element.36.wire_ref.refs_2_), channel_id=1, source_target_pairs={{0,224},{32,0},{64,32},{96,64},{128,96},{160,128},{192,160},{224,1... | collective-permute-start | bytes 786440 | tf_op jit(solution)/shard_map/ppermute | solution.py:27
  12.2 3.2 %shard_map.56 = (bf16[512,512]{1,0:T(8,128)(2,1)S(1)}, bf16[512,512]{1,0:T(8,128)(2,1)S(1)}, bf16[512,512]{1,0:T(8,128)(2,1)S(1)}, f32[512,256]{1,0:T(8,128)S(1)...) custom-call(bf16[256,4096]{1,0:T(8,128)(2,1)} %blocks_hbm.3, s32[1,256]{1,0:T(1,128)} %bitcast.23, ...), custom_call_target="tpu_custom_call" | custom-call | flops 1207959552 | bytes 2623488 | tf_op jit(solution)/shard_map/pallas_call | solution.py:58
  15.4 0.1 fusion.3
  15.5 0.1 collective-permute-start.6
  15.6 1.2 %collective-permute-done.refs_4_ = bf16[512,256]{1,0:T(8,128)(2,1)S(1)} collective-permute-done((bf16[512,256]{1,0:T(8,128)(2,1)S(1)}, bf16[512,256]{1,0:T(8,128)(2,1)S(1)}, u32[]{:S(2)}, u32[]{:S(2)}) %collective-permute-start) | collective-permute-done | bytes 262176 | tf_op jit(solution)/shard_map/ppermute | solution.py:27
  16.8 2.1 %collective-permute-start.2 = (bf16[512,256]{1,0:T(8,128)(2,1)S(1)}, bf16[512,256]{1,0:T(8,128)(2,1)S(1)}, u32[]{:S(2)}, u32[]{:S(2)}) collective-permute-start(bf16[512,256]{1,0:T(8,128)(2,1)S(1)} %broadcast_select_fusion.1), channel_id=1, source_target_pairs={{0,255},{1,2},{2,1},{3,4},{4,3},{5,6},{6,5},{7,8},{8,7},{9,10},{10... | collective-permute-start | bytes 786440 | tf_op jit(solution)/shard_map/ppermute | solution.py:51
  18.9 0.1 pad_maximum_fusion
  18.9 10.6 %collective-permute-start.1 = (bf16[2,512,256]{2,1,0:T(8,128)(2,1)S(1)}, bf16[2,512,256]{2,1,0:T(8,128)(2,1)S(1)}, u32[]{:S(2)}, u32[]{:S(2)}) collective-permute-start(bf16[2,512,256]{2,1,0:T(8,128)(2,1)S(1)} %pad_maximum_fusion), channel_id=1, source_target_pairs={{0,1},{1,0},{2,3},{3,2},{4,5},{5,4},{6,7},{7,6},{8,9},{9,8},{10,11... | collective-permute-start | bytes 1572872 | tf_op jit(solution)/shard_map/ppermute | solution.py:31
  29.5 0.5 shard_map.57.own_ref
  30.0 0.0 copy-start
  30.0 0.0 collective-permute-done.6.received_ref
  30.0 0.1 shard_map.58.refs_8_
  30.1 0.0 collective-permute-done.2.refs_6_
  30.1 0.9 %collective-permute-done.1.refs_5_ = bf16[2,512,256]{2,1,0:T(8,128)(2,1)S(1)} collective-permute-done((bf16[2,512,256]{2,1,0:T(8,128)(2,1)S(1)}, bf16[2,512,256]{2,1,0:T(8,128)(2,1)S(1)}, u32[]{:S(2)}, u32[]{:S(2)}) %collective-permute-start.1) | collective-permute-done | bytes 524320 | tf_op jit(solution)/shard_map/ppermute | solution.py:31
  31.1 7.4 %collective-permute-done.5.refs_7_ = bf16[2,512,256]{2,1,0:T(8,128)(2,1)S(1)} collective-permute-done((bf16[2,512,256]{2,1,0:T(8,128)(2,1)S(1)}, bf16[2,512,256]{2,1,0:T(8,128)(2,1)S(1)}, u32[]{:S(2)}, u32[]{:S(2)}) %collective-permute-start.5) | collective-permute-done | bytes 524320 | tf_op jit(solution)/shard_map/ppermute | solution.py:36
  38.4 2.5 %shard_map.59 = (bf16[512,256]{1,0:T(8,128)(2,1)S(1)}, bf16[512,256]{1,0:T(8,128)(2,1)S(1)}, f32[512,256]{1,0:T(8,128)S(1)}, bf16[2,512,256]{2,1,0:T(8,128)(2,1)S(1)}, bf16[512,256]{1,0:T(8,128)(2,1)S(1)}) custom-call(bf16[512,512]{1,0:T(8,128)(2,1)S(1)} %get-tuple-element.32.refs_0_, bf16[512,512]{1,0:T(8,128)(2,1)S(1)} %get-tuple-element.33.refs_1_, ...), custom_call_target="tpu_custom_call" | custom-call | flops 805306368 | bytes 4980736 | tf_op jit(solution)/shard_map/pallas_call | solution.py:58
  41.0 2.2 %collective-permute-start.10 = (bf16[2,512,256]{2,1,0:T(8,128)(2,1)S(1)}, bf16[2,512,256]{2,1,0:T(8,128)(2,1)S(1)}, u32[]{:S(2)}, u32[]{:S(2)}) collective-permute-start(bf16[2,512,256]{2,1,0:T(8,128)(2,1)S(1)} %get-tuple-element.55), channel_id=1, source_target_pairs={{0,1},{1,0},{2,3},{3,2},{4,5},{5,4},{6,7},{7,6},{8,9},{9,8},{10,11... | collective-permute-start | bytes 1572872 | tf_op jit(solution)/shard_map/ppermute | solution.py:31
  43.2 0.9 %collective-permute-start.7 = (bf16[512,256]{1,0:T(8,128)(2,1)S(1)}, bf16[512,256]{1,0:T(8,128)(2,1)S(1)}, u32[]{:S(2)}, u32[]{:S(2)}) collective-permute-start(bf16[512,256]{1,0:T(8,128)(2,1)S(1)} %get-tuple-element.50.wire_ref.refs_2_), channel_id=1, source_target_pairs={{0,224},{32,0},{64,32},{96,64},{128,96},{160,128},{192,160},{224,1... | collective-permute-start | bytes 786440 | tf_op jit(solution)/shard_map/ppermute | solution.py:27
  44.1 0.6 shard_map.60
  44.7 4.6 %collective-permute-done.11.refs_5_ = bf16[512,256]{1,0:T(8,128)(2,1)S(1)} collective-permute-done((bf16[512,256]{1,0:T(8,128)(2,1)S(1)}, bf16[512,256]{1,0:T(8,128)(2,1)S(1)}, u32[]{:S(2)}, u32[]{:S(2)}) %collective-permute-start.11) | collective-permute-done | bytes 262176 | tf_op jit(solution)/shard_map/ppermute | solution.py:51
  49.3 0.1 fusion.1
  49.4 0.1 collective-permute-start.13
  49.4 5.5 %collective-permute-done.7.refs_4_ = bf16[512,256]{1,0:T(8,128)(2,1)S(1)} collective-permute-done((bf16[512,256]{1,0:T(8,128)(2,1)S(1)}, bf16[512,256]{1,0:T(8,128)(2,1)S(1)}, u32[]{:S(2)}, u32[]{:S(2)}) %collective-permute-start.7) | collective-permute-done | bytes 262176 | tf_op jit(solution)/shard_map/ppermute | solution.py:27
  55.0 0.6 collective-permute-start.9
  55.6 0.1 pad_maximum_fusion.1
  55.6 7.1 %collective-permute-start.8 = (bf16[2,512,256]{2,1,0:T(8,128)(2,1)S(1)}, bf16[2,512,256]{2,1,0:T(8,128)(2,1)S(1)}, u32[]{:S(2)}, u32[]{:S(2)}) collective-permute-start(bf16[2,512,256]{2,1,0:T(8,128)(2,1)S(1)} %pad_maximum_fusion.1), channel_id=1, source_target_pairs={{0,1},{1,0},{2,3},{3,2},{4,5},{5,4},{6,7},{7,6},{8,9},{9,8},{10,11... | collective-permute-start | bytes 1572872 | tf_op jit(solution)/shard_map/ppermute | solution.py:31
  62.7 0.5 shard_map.61.own_ref
  63.3 1.0 %collective-permute-done.8.refs_5_ = bf16[2,512,256]{2,1,0:T(8,128)(2,1)S(1)} collective-permute-done((bf16[2,512,256]{2,1,0:T(8,128)(2,1)S(1)}, bf16[2,512,256]{2,1,0:T(8,128)(2,1)S(1)}, u32[]{:S(2)}, u32[]{:S(2)}) %collective-permute-start.8) | collective-permute-done | bytes 524320 | tf_op jit(solution)/shard_map/ppermute | solution.py:31
  64.3 7.4 %collective-permute-done.12.refs_7_ = bf16[2,512,256]{2,1,0:T(8,128)(2,1)S(1)} collective-permute-done((bf16[2,512,256]{2,1,0:T(8,128)(2,1)S(1)}, bf16[2,512,256]{2,1,0:T(8,128)(2,1)S(1)}, u32[]{:S(2)}, u32[]{:S(2)}) %collective-permute-start.12) | collective-permute-done | bytes 524320 | tf_op jit(solution)/shard_map/ppermute | solution.py:36
  71.6 1.6 %shard_map.63 = f32[512,256]{1,0:T(8,128)} custom-call(bf16[512,512]{1,0:T(8,128)(2,1)S(1)} %get-tuple-element.32.refs_0_, bf16[512,512]{1,0:T(8,128)(2,1)S(1)} %get-tuple-element.33.refs_1_, bf16[512,512]{1,0:T(8,128)(2,1)S(1)} %get-tuple-element.34.refs_2_, bf16[512,512]{1,0:T(8,128)(2,1)S(1)} %get-tuple-element.37.refs_3_.far_in, ...), custom_call_target="tpu_custom_call" | custom-call | flops 402653184 | bytes 4980736 | tf_op jit(solution)/shard_map/pallas_call | solution.py:58
  (14 shorter events, 0.2 us)
Async XLA Ops:
  3.8 11.6 %collective-permute-start.3 = (bf16[2,512,256]{2,1,0:T(8,128)(2,1)S(1)}, bf16[2,512,256]{2,1,0:T(8,128)(2,1)S(1)}, u32[]{:S(2)}, u32[]{:S(2)}) collective-permute-start(bf16[2,512,256]{2,1,0:T(8,128)(2,1)S(1)} %get-tuple-element.42), channel_id=1, source_target_pairs={{0,1},{1,0},{2,3},{3,2},{4,5},{5,4},{6,7},{7,6},{8,9},{9,8},{10,11... | collective-permute-start | bytes 1572872 | tf_op jit(solution)/shard_map/ppermute | solution.py:31
  7.1 8.3 %collective-permute-start.4 = (bf16[512,256]{1,0:T(8,128)(2,1)S(1)}, bf16[512,256]{1,0:T(8,128)(2,1)S(1)}, u32[]{:S(2)}, u32[]{:S(2)}) collective-permute-start(bf16[512,256]{1,0:T(8,128)(2,1)S(1)} %get-tuple-element.43), channel_id=1, source_target_pairs={{0,63},{1,2},{2,1},{3,4},{4,3},{5,6},{6,5},{7,8},{8,7},{9,10},{10,... | collective-permute-start | bytes 786440 | tf_op jit(solution)/shard_map/ppermute | solution.py:51
  7.1 9.7 %collective-permute-start = (bf16[512,256]{1,0:T(8,128)(2,1)S(1)}, bf16[512,256]{1,0:T(8,128)(2,1)S(1)}, u32[]{:S(2)}, u32[]{:S(2)}) collective-permute-start(bf16[512,256]{1,0:T(8,128)(2,1)S(1)} %get-tuple-element.36.wire_ref.refs_2_), channel_id=1, source_target_pairs={{0,224},{32,0},{64,32},{96,64},{128,96},{160,128},{192,160},{224,1... | collective-permute-start | bytes 786440 | tf_op jit(solution)/shard_map/ppermute | solution.py:27
  15.5 14.5 %collective-permute-start.6 = (bf16[512,256]{1,0:T(8,128)(2,1)S(1)}, bf16[512,256]{1,0:T(8,128)(2,1)S(1)}, u32[]{:S(2)}, u32[]{:S(2)}) collective-permute-start(bf16[512,256]{1,0:T(8,128)(2,1)S(1)} %fusion.3), channel_id=1, source_target_pairs={{0,32},{32,64},{64,96},{96,128},{128,160},{160,192},{192,224},{224... | collective-permute-start | bytes 786440 | tf_op jit(solution)/shard_map/ppermute | solution.py:27
  16.8 13.3 %collective-permute-start.2 = (bf16[512,256]{1,0:T(8,128)(2,1)S(1)}, bf16[512,256]{1,0:T(8,128)(2,1)S(1)}, u32[]{:S(2)}, u32[]{:S(2)}) collective-permute-start(bf16[512,256]{1,0:T(8,128)(2,1)S(1)} %broadcast_select_fusion.1), channel_id=1, source_target_pairs={{0,255},{1,2},{2,1},{3,4},{4,3},{5,6},{6,5},{7,8},{8,7},{9,10},{10... | collective-permute-start | bytes 786440 | tf_op jit(solution)/shard_map/ppermute | solution.py:51
  18.9 12.1 %collective-permute-start.1 = (bf16[2,512,256]{2,1,0:T(8,128)(2,1)S(1)}, bf16[2,512,256]{2,1,0:T(8,128)(2,1)S(1)}, u32[]{:S(2)}, u32[]{:S(2)}) collective-permute-start(bf16[2,512,256]{2,1,0:T(8,128)(2,1)S(1)} %pad_maximum_fusion), channel_id=1, source_target_pairs={{0,1},{1,0},{2,3},{3,2},{4,5},{5,4},{6,7},{7,6},{8,9},{9,8},{10,11... | collective-permute-start | bytes 1572872 | tf_op jit(solution)/shard_map/ppermute | solution.py:31
  29.5 8.9 %collective-permute-start.5 = (bf16[2,512,256]{2,1,0:T(8,128)(2,1)S(1)}, bf16[2,512,256]{2,1,0:T(8,128)(2,1)S(1)}, u32[]{:S(2)}, u32[]{:S(2)}) collective-permute-start(bf16[2,512,256]{2,1,0:T(8,128)(2,1)S(1)} %get-tuple-element.46), channel_id=1, source_target_pairs={{0,31},{1,2},{2,1},{3,4},{4,3},{5,6},{6,5},{7,8},{8,7},{9,10},{10,... | collective-permute-start | bytes 1572872 | tf_op jit(solution)/shard_map/ppermute | solution.py:36
  30.0 8.4 %copy-start = (f32[512,256]{1,0:T(8,128)S(1)}, f32[512,256]{1,0:T(8,128)}, u32[]{:S(2)}) copy-start(f32[512,256]{1,0:T(8,128)} %refs_9_.3) | copy-start | bytes 1572868
  41.0 8.3 %collective-permute-start.10 = (bf16[2,512,256]{2,1,0:T(8,128)(2,1)S(1)}, bf16[2,512,256]{2,1,0:T(8,128)(2,1)S(1)}, u32[]{:S(2)}, u32[]{:S(2)}) collective-permute-start(bf16[2,512,256]{2,1,0:T(8,128)(2,1)S(1)} %get-tuple-element.55), channel_id=1, source_target_pairs={{0,1},{1,0},{2,3},{3,2},{4,5},{5,4},{6,7},{7,6},{8,9},{9,8},{10,11... | collective-permute-start | bytes 1572872 | tf_op jit(solution)/shard_map/ppermute | solution.py:31
  43.2 6.1 %collective-permute-start.11 = (bf16[512,256]{1,0:T(8,128)(2,1)S(1)}, bf16[512,256]{1,0:T(8,128)(2,1)S(1)}, u32[]{:S(2)}, u32[]{:S(2)}) collective-permute-start(bf16[512,256]{1,0:T(8,128)(2,1)S(1)} %get-tuple-element.56), channel_id=1, source_target_pairs={{0,63},{1,2},{2,1},{3,4},{4,3},{5,6},{6,5},{7,8},{8,7},{9,10},{10,... | collective-permute-start | bytes 786440 | tf_op jit(solution)/shard_map/ppermute | solution.py:51
  43.2 11.8 %collective-permute-start.7 = (bf16[512,256]{1,0:T(8,128)(2,1)S(1)}, bf16[512,256]{1,0:T(8,128)(2,1)S(1)}, u32[]{:S(2)}, u32[]{:S(2)}) collective-permute-start(bf16[512,256]{1,0:T(8,128)(2,1)S(1)} %get-tuple-element.50.wire_ref.refs_2_), channel_id=1, source_target_pairs={{0,224},{32,0},{64,32},{96,64},{128,96},{160,128},{192,160},{224,1... | collective-permute-start | bytes 786440 | tf_op jit(solution)/shard_map/ppermute | solution.py:27
  49.4 13.8 %collective-permute-start.13 = (bf16[512,256]{1,0:T(8,128)(2,1)S(1)}, bf16[512,256]{1,0:T(8,128)(2,1)S(1)}, u32[]{:S(2)}, u32[]{:S(2)}) collective-permute-start(bf16[512,256]{1,0:T(8,128)(2,1)S(1)} %fusion.1), channel_id=1, source_target_pairs={{0,32},{32,64},{64,96},{96,128},{128,160},{160,192},{192,224},{224... | collective-permute-start | bytes 786440 | tf_op jit(solution)/shard_map/ppermute | solution.py:27
  55.0 8.3 %collective-permute-start.9 = (bf16[512,256]{1,0:T(8,128)(2,1)S(1)}, bf16[512,256]{1,0:T(8,128)(2,1)S(1)}, u32[]{:S(2)}, u32[]{:S(2)}) collective-permute-start(bf16[512,256]{1,0:T(8,128)(2,1)S(1)} %broadcast_select_fusion), channel_id=1, source_target_pairs={{0,255},{1,2},{2,1},{3,4},{4,3},{5,6},{6,5},{7,8},{8,7},{9,10},{10... | collective-permute-start | bytes 786440 | tf_op jit(solution)/shard_map/ppermute | solution.py:51
  55.6 8.6 %collective-permute-start.8 = (bf16[2,512,256]{2,1,0:T(8,128)(2,1)S(1)}, bf16[2,512,256]{2,1,0:T(8,128)(2,1)S(1)}, u32[]{:S(2)}, u32[]{:S(2)}) collective-permute-start(bf16[2,512,256]{2,1,0:T(8,128)(2,1)S(1)} %pad_maximum_fusion.1), channel_id=1, source_target_pairs={{0,1},{1,0},{2,3},{3,2},{4,5},{5,4},{6,7},{7,6},{8,9},{9,8},{10,11... | collective-permute-start | bytes 1572872 | tf_op jit(solution)/shard_map/ppermute | solution.py:31
  62.7 8.9 %collective-permute-start.12 = (bf16[2,512,256]{2,1,0:T(8,128)(2,1)S(1)}, bf16[2,512,256]{2,1,0:T(8,128)(2,1)S(1)}, u32[]{:S(2)}, u32[]{:S(2)}) collective-permute-start(bf16[2,512,256]{2,1,0:T(8,128)(2,1)S(1)} %get-tuple-element.57), channel_id=1, source_target_pairs={{0,31},{1,2},{2,1},{3,4},{4,3},{5,6},{6,5},{7,8},{8,7},{9,10},{10,... | collective-permute-start | bytes 1572872 | tf_op jit(solution)/shard_map/ppermute | solution.py:36

commit v11 on v10

--- a/solution.py
+++ b/solution.py
@@ -191,12 +191,11 @@
     out_ref[...] = self_ref[...] + here + restored(straight, scratch)
 
 
-def with_cross(mats, down_ref, mate_ref, far_ref, other_ref, known_ref, scratch):
+def with_cross(mats, down_ref, mate_ref, far_ref, known_ref, scratch):
     straight = dot(mats[0][...], down_ref[...])
     straight += dot(mats[1][...], mate_ref[0])
     straight += dot(mats[2][...], far_ref[...])
-    straight += dot(mats[3][...], other_ref[0])
-    return known_ref[...] + mate_ref[1].astype(F32) + other_ref[1].astype(F32) + restored(straight, scratch)
+    return known_ref[...] + mate_ref[1].astype(F32) + restored(straight, scratch)
 
 
 def advanced(product, drive_ref, relax_ref):
@@ -205,20 +204,21 @@
 
 
 def update_body(*refs):
-    mats, nexts, (drive_ref, relax_ref) = refs[:4], refs[4:9], refs[9:11]
-    perm_ref, wire_ref, self_ref, mate_ref, far_ref, scratch = refs[11:]
+    mats, nexts, (drive_ref, relax_ref) = refs[:3], refs[3:7], refs[7:9]
+    perm_ref, wire_ref, self_ref, mate_ref, far_ref, scratch = refs[9:]
     field = advanced(with_cross(mats, *nexts, scratch), drive_ref, relax_ref)
     interleave(field, scratch, perm_ref)
     emit(mats, field.astype(BF16), perm_ref, wire_ref, self_ref, mate_ref, far_ref)
 
 
-def settle_body(own_ref, received_ref, out_ref):
-    out_ref[...] = own_ref[...] + received_ref[...].astype(F32)
+def settle_body(far_in, other_ref, known_ref, received_ref, out_ref, scratch):
+    known = known_ref[...] + other_ref[1].astype(F32) + received_ref[...].astype(F32)
+    out_ref[...] = known + restored(dot(far_in[...], other_ref[0]), scratch)
 
 
 def final_body(*refs):
-    product = with_cross(refs[:4], *refs[4:9], refs[12])
-    refs[11][...] = advanced(product, *refs[9:11])
+    product = with_cross(refs[:3], *refs[3:7], refs[10])
+    refs[9][...] = advanced(product, *refs[7:9])
 
 
 def local(drive, relax, blocks, row_block, col_block):
@@ -267,8 +267,8 @@
         known = call(
             own_body, wide, 2 * work, [*own[:2], wire, from_mate, own_self, from_far, flag], scratch=[staging]
         )
-        known = call(settle_body, wide, HEAVY * work, [known, received])
-        args = [*cross, own[2], down, next_mate, next_far, other_far, known, drive, relax3]
+        known = call(settle_body, wide, HEAVY * work, [own[2], other_far, known, received], scratch=[staging])
+        args = [*cross, down, next_mate, next_far, known, drive, relax3]
         if sweep + 1 == ITERS:
             return call(final_body, wide, 3 * work, args, scratch=[staging])
         perm, wire, partial, to_mate, to_far = call(update_body, emitted, 6 * work, args, scratch=[staging])

time: 74.5 us -> 74.9 us (level)
  the two profiles are of different devices: /device:TPU:1 before, /device:TPU:4 now
where the time goes in v11:
time: 74.9 us; the launch traced here: 74.8 us
  starting transfers between devices  31.9 us (43%)
  waiting for transfers between devices  28.6 us (38%)
  Pallas kernels  13 us (17%)
    ppermute x4, waiting for transfers between devices, shifted(): lax.ppermute(value, axis, [(source, (source + steps) % count) for source...  24.9 us
    ppermute x4, starting transfers between devices, far_slanted(): return lax.ppermute(value, ('ka', 'rows'), pairs)  13 us
    pallas_call x9, Pallas kernels, call(): pl.pallas_call(kernel, out_shape=outs, in_specs=specs or [VMEM] * len(arg...  13 us
    ppermute x2, starting transfers between devices, far(): lax.ppermute(value, 'rows', [(i, (i + 1 if i & 1 else i - 1) % count) for...  10.9 us
    ppermute x4, starting transfers between devices, shifted(): lax.ppermute(value, axis, [(source, (source + steps) % count) for source...  7.6 us
    ppermute x4, waiting for transfers between devices, far_slanted(): return lax.ppermute(value, ('ka', 'rows'), pairs)  3.71 us
  transfers between devices with their start and end apart: 14, of which 3 were waited for; matrix products, arithmetic and copies ran while one was open for 1% of the time, Pallas kernels for 7%

profile of v11, /device:TPU:4, one launch (start us, length us, event | category | flops | bytes accessed | tf_op | source)
XLA Modules:
  0.0 74.8 jit_solution(4257694725820530456)
XLA Ops:
  0.0 3.8 %shard_map.55 = (bf16[512,512]{1,0:T(8,128)(2,1)S(1)}, bf16[512,512]{1,0:T(8,128)(2,1)S(1)}, bf16[512,512]{1,0:T(8,128)(2,1)S(1)}, bf16[512,256]{1,0:T(8,128)(2,...) custom-call(bf16[256,4096]{1,0:T(8,128)(2,1)} %blocks_hbm.3, ...), custom_call_target="tpu_custom_call" | custom-call | flops 1207959552 | bytes 2625536 | tf_op jit(solution)/shard_map/pallas_call | solution.py:58
  3.8 0.1 collective-permute-start.3
  3.9 6.9 %collective-permute-start.4 = (bf16[512,256]{1,0:T(8,128)(2,1)S(1)}, bf16[512,256]{1,0:T(8,128)(2,1)S(1)}, u32[]{:S(2)}, u32[]{:S(2)}) collective-permute-start(bf16[512,256]{1,0:T(8,128)(2,1)S(1)} %get-tuple-element.43), channel_id=1, source_target_pairs={{0,63},{1,2},{2,1},{3,4},{4,3},{5,6},{6,5},{7,8},{8,7},{9,10},{10,... | collective-permute-start | bytes 786440 | tf_op jit(solution)/shard_map/ppermute | solution.py:51
  10.8 1.7 %collective-permute-start = (bf16[512,256]{1,0:T(8,128)(2,1)S(1)}, bf16[512,256]{1,0:T(8,128)(2,1)S(1)}, u32[]{:S(2)}, u32[]{:S(2)}) collective-permute-start(bf16[512,256]{1,0:T(8,128)(2,1)S(1)} %get-tuple-element.35.wire_ref.refs_2_), channel_id=1, source_target_pairs={{0,224},{32,0},{64,32},{96,64},{128,96},{160,128},{192,160},{224,1... | collective-permute-start | bytes 786440 | tf_op jit(solution)/shard_map/ppermute | solution.py:27
  12.6 3.2 %shard_map.56 = (bf16[512,512]{1,0:T(8,128)(2,1)S(1)}, bf16[512,512]{1,0:T(8,128)(2,1)S(1)}, bf16[512,512]{1,0:T(8,128)(2,1)S(1)}, f32[512,256]{1,0:T(8,128)S(1)...) custom-call(bf16[256,4096]{1,0:T(8,128)(2,1)} %blocks_hbm.3, s32[1,256]{1,0:T(1,128)} %bitcast.23, ...), custom_call_target="tpu_custom_call" | custom-call | flops 1207959552 | bytes 2623488 | tf_op jit(solution)/shard_map/pallas_call | solution.py:58
  15.8 0.1 fusion.3
  15.9 6.0 %collective-permute-start.5 = (bf16[2,512,256]{2,1,0:T(8,128)(2,1)S(1)}, bf16[2,512,256]{2,1,0:T(8,128)(2,1)S(1)}, u32[]{:S(2)}, u32[]{:S(2)}) collective-permute-start(bf16[2,512,256]{2,1,0:T(8,128)(2,1)S(1)} %get-tuple-element.46), channel_id=1, source_target_pairs={{0,31},{1,2},{2,1},{3,4},{4,3},{5,6},{6,5},{7,8},{8,7},{9,10},{10,... | collective-permute-start | bytes 1572872 | tf_op jit(solution)/shard_map/ppermute | solution.py:36
  21.9 0.1 pad_maximum_fusion
  21.9 0.1 collective-permute-start.1
  22.0 1.6 %collective-permute-start.6 = (bf16[512,256]{1,0:T(8,128)(2,1)S(1)}, bf16[512,256]{1,0:T(8,128)(2,1)S(1)}, u32[]{:S(2)}, u32[]{:S(2)}) collective-permute-start(bf16[512,256]{1,0:T(8,128)(2,1)S(1)} %fusion.3), channel_id=1, source_target_pairs={{0,32},{32,64},{64,96},{96,128},{128,160},{160,192},{192,224},{224... | collective-permute-start | bytes 786440 | tf_op jit(solution)/shard_map/ppermute | solution.py:27
  23.7 2.2 %collective-permute-start.2 = (bf16[512,256]{1,0:T(8,128)(2,1)S(1)}, bf16[512,256]{1,0:T(8,128)(2,1)S(1)}, u32[]{:S(2)}, u32[]{:S(2)}) collective-permute-start(bf16[512,256]{1,0:T(8,128)(2,1)S(1)} %broadcast_select_fusion.1), channel_id=1, source_target_pairs={{0,255},{1,2},{2,1},{3,4},{4,3},{5,6},{6,5},{7,8},{8,7},{9,10},{10... | collective-permute-start | bytes 786440 | tf_op jit(solution)/shard_map/ppermute | solution.py:51
  25.9 0.5 shard_map.57.known_ref
  26.4 12.3 %collective-permute-done.6.received_ref = bf16[512,256]{1,0:T(8,128)(2,1)S(1)} collective-permute-done((bf16[512,256]{1,0:T(8,128)(2,1)S(1)}, bf16[512,256]{1,0:T(8,128)(2,1)S(1)}, u32[]{:S(2)}, u32[]{:S(2)}) %collective-permute-start.6) | collective-permute-done | bytes 262176 | tf_op jit(solution)/shard_map/ppermute | solution.py:27
  38.6 0.0 collective-permute-done.5.other_ref
  38.6 0.4 shard_map.58.refs_6_
  39.0 0.7 copy-done
  39.7 2.3 %shard_map.59 = (bf16[512,256]{1,0:T(8,128)(2,1)S(1)}, bf16[512,256]{1,0:T(8,128)(2,1)S(1)}, f32[512,256]{1,0:T(8,128)S(1)}, bf16[2,512,256]{2,1,0:T(8,128)(2,1)S(1)}, bf16[512,256]{1,0:T(8,128)(2,1)S(1)}) custom-call(bf16[512,512]{1,0:T(8,128)(2,1)S(1)} %get-tuple-element.32.refs_0_, bf16[512,512]{1,0:T(8,128)(2,1)S(1)} %get-tuple-element.33.refs_1_, ...), custom_call_target="tpu_custom_call" | custom-call | flops 805306368 | bytes 3932160 | tf_op jit(solution)/shard_map/pallas_call | solution.py:58
  42.0 0.1 collective-permute-start.10
  42.1 2.2 %collective-permute-start.11 = (bf16[512,256]{1,0:T(8,128)(2,1)S(1)}, bf16[512,256]{1,0:T(8,128)(2,1)S(1)}, u32[]{:S(2)}, u32[]{:S(2)}) collective-permute-start(bf16[512,256]{1,0:T(8,128)(2,1)S(1)} %get-tuple-element.56), channel_id=1, source_target_pairs={{0,63},{1,2},{2,1},{3,4},{4,3},{5,6},{6,5},{7,8},{8,7},{9,10},{10,... | collective-permute-start | bytes 786440 | tf_op jit(solution)/shard_map/ppermute | solution.py:51
  44.3 4.3 %collective-permute-start.7 = (bf16[512,256]{1,0:T(8,128)(2,1)S(1)}, bf16[512,256]{1,0:T(8,128)(2,1)S(1)}, u32[]{:S(2)}, u32[]{:S(2)}) collective-permute-start(bf16[512,256]{1,0:T(8,128)(2,1)S(1)} %get-tuple-element.50.wire_ref.refs_2_), channel_id=1, source_target_pairs={{0,224},{32,0},{64,32},{96,64},{128,96},{160,128},{192,160},{224,1... | collective-permute-start | bytes 786440 | tf_op jit(solution)/shard_map/ppermute | solution.py:27
  48.6 0.6 shard_map.60
  49.2 3.7 %collective-permute-done.11.refs_5_ = bf16[512,256]{1,0:T(8,128)(2,1)S(1)} collective-permute-done((bf16[512,256]{1,0:T(8,128)(2,1)S(1)}, bf16[512,256]{1,0:T(8,128)(2,1)S(1)}, u32[]{:S(2)}, u32[]{:S(2)}) %collective-permute-start.11) | collective-permute-done | bytes 262176 | tf_op jit(solution)/shard_map/ppermute | solution.py:51
  52.9 0.1 fusion.1
  53.0 4.9 %collective-permute-start.12 = (bf16[2,512,256]{2,1,0:T(8,128)(2,1)S(1)}, bf16[2,512,256]{2,1,0:T(8,128)(2,1)S(1)}, u32[]{:S(2)}, u32[]{:S(2)}) collective-permute-start(bf16[2,512,256]{2,1,0:T(8,128)(2,1)S(1)} %get-tuple-element.57), channel_id=1, source_target_pairs={{0,31},{1,2},{2,1},{3,4},{4,3},{5,6},{6,5},{7,8},{8,7},{9,10},{10,... | collective-permute-start | bytes 1572872 | tf_op jit(solution)/shard_map/ppermute | solution.py:36
  57.9 0.0 collective-permute-start.13
  58.0 1.7 %collective-permute-start.9 = (bf16[512,256]{1,0:T(8,128)(2,1)S(1)}, bf16[512,256]{1,0:T(8,128)(2,1)S(1)}, u32[]{:S(2)}, u32[]{:S(2)}) collective-permute-start(bf16[512,256]{1,0:T(8,128)(2,1)S(1)} %broadcast_select_fusion), channel_id=1, source_target_pairs={{0,255},{1,2},{2,1},{3,4},{4,3},{5,6},{6,5},{7,8},{8,7},{9,10},{10... | collective-permute-start | bytes 786440 | tf_op jit(solution)/shard_map/ppermute | solution.py:51
  59.7 0.1 pad_maximum_fusion.1
  59.7 0.1 collective-permute-start.8
  59.8 0.5 shard_map.61.known_ref
  60.3 12.6 %collective-permute-done.13.received_ref = bf16[512,256]{1,0:T(8,128)(2,1)S(1)} collective-permute-done((bf16[512,256]{1,0:T(8,128)(2,1)S(1)}, bf16[512,256]{1,0:T(8,128)(2,1)S(1)}, u32[]{:S(2)}, u32[]{:S(2)}) %collective-permute-start.13) | collective-permute-done | bytes 262176 | tf_op jit(solution)/shard_map/ppermute | solution.py:27
  72.9 0.3 shard_map.62.refs_6_
  73.3 1.5 %shard_map.63 = f32[512,256]{1,0:T(8,128)} custom-call(bf16[512,512]{1,0:T(8,128)(2,1)S(1)} %get-tuple-element.32.refs_0_, bf16[512,512]{1,0:T(8,128)(2,1)S(1)} %get-tuple-element.33.refs_1_, bf16[512,512]{1,0:T(8,128)(2,1)S(1)} %get-tuple-element.34.refs_2_, bf16[512,256]{1,0:T(8,128)(2,1)S(1)} %collective-permute-done.7.refs_3_, ...), custom_call_target="tpu_custom_call" | custom-call | flops 402653184 | bytes 3932160 | tf_op jit(solution)/shard_map/pallas_call | solution.py:58
  (14 shorter events, 0.1 us)
Async XLA Ops:
  3.8 12.0 %collective-permute-start.3 = (bf16[2,512,256]{2,1,0:T(8,128)(2,1)S(1)}, bf16[2,512,256]{2,1,0:T(8,128)(2,1)S(1)}, u32[]{:S(2)}, u32[]{:S(2)}) collective-permute-start(bf16[2,512,256]{2,1,0:T(8,128)(2,1)S(1)} %get-tuple-element.42), channel_id=1, source_target_pairs={{0,1},{1,0},{2,3},{3,2},{4,5},{5,4},{6,7},{7,6},{8,9},{9,8},{10,11... | collective-permute-start | bytes 1572872 | tf_op jit(solution)/shard_map/ppermute | solution.py:31
  3.9 11.9 %collective-permute-start.4 = (bf16[512,256]{1,0:T(8,128)(2,1)S(1)}, bf16[512,256]{1,0:T(8,128)(2,1)S(1)}, u32[]{:S(2)}, u32[]{:S(2)}) collective-permute-start(bf16[512,256]{1,0:T(8,128)(2,1)S(1)} %get-tuple-element.43), channel_id=1, source_target_pairs={{0,63},{1,2},{2,1},{3,4},{4,3},{5,6},{6,5},{7,8},{8,7},{9,10},{10,... | collective-permute-start | bytes 786440 | tf_op jit(solution)/shard_map/ppermute | solution.py:51
  10.8 11.0 %collective-permute-start = (bf16[512,256]{1,0:T(8,128)(2,1)S(1)}, bf16[512,256]{1,0:T(8,128)(2,1)S(1)}, u32[]{:S(2)}, u32[]{:S(2)}) collective-permute-start(bf16[512,256]{1,0:T(8,128)(2,1)S(1)} %get-tuple-element.35.wire_ref.refs_2_), channel_id=1, source_target_pairs={{0,224},{32,0},{64,32},{96,64},{128,96},{160,128},{192,160},{224,1... | collective-permute-start | bytes 786440 | tf_op jit(solution)/shard_map/ppermute | solution.py:27
  15.9 22.8 %collective-permute-start.5 = (bf16[2,512,256]{2,1,0:T(8,128)(2,1)S(1)}, bf16[2,512,256]{2,1,0:T(8,128)(2,1)S(1)}, u32[]{:S(2)}, u32[]{:S(2)}) collective-permute-start(bf16[2,512,256]{2,1,0:T(8,128)(2,1)S(1)} %get-tuple-element.46), channel_id=1, source_target_pairs={{0,31},{1,2},{2,1},{3,4},{4,3},{5,6},{6,5},{7,8},{8,7},{9,10},{10,... | collective-permute-start | bytes 1572872 | tf_op jit(solution)/shard_map/ppermute | solution.py:36
  21.9 17.1 %collective-permute-start.1 = (bf16[2,512,256]{2,1,0:T(8,128)(2,1)S(1)}, bf16[2,512,256]{2,1,0:T(8,128)(2,1)S(1)}, u32[]{:S(2)}, u32[]{:S(2)}) collective-permute-start(bf16[2,512,256]{2,1,0:T(8,128)(2,1)S(1)} %pad_maximum_fusion), channel_id=1, source_target_pairs={{0,1},{1,0},{2,3},{3,2},{4,5},{5,4},{6,7},{7,6},{8,9},{9,8},{10,11... | collective-permute-start | bytes 1572872 | tf_op jit(solution)/shard_map/ppermute | solution.py:31
  22.0 16.6 %collective-permute-start.6 = (bf16[512,256]{1,0:T(8,128)(2,1)S(1)}, bf16[512,256]{1,0:T(8,128)(2,1)S(1)}, u32[]{:S(2)}, u32[]{:S(2)}) collective-permute-start(bf16[512,256]{1,0:T(8,128)(2,1)S(1)} %fusion.3), channel_id=1, source_target_pairs={{0,32},{32,64},{64,96},{96,128},{128,160},{160,192},{192,224},{224... | collective-permute-start | bytes 786440 | tf_op jit(solution)/shard_map/ppermute | solution.py:27
  23.7 15.3 %collective-permute-start.2 = (bf16[512,256]{1,0:T(8,128)(2,1)S(1)}, bf16[512,256]{1,0:T(8,128)(2,1)S(1)}, u32[]{:S(2)}, u32[]{:S(2)}) collective-permute-start(bf16[512,256]{1,0:T(8,128)(2,1)S(1)} %broadcast_select_fusion.1), channel_id=1, source_target_pairs={{0,255},{1,2},{2,1},{3,4},{4,3},{5,6},{6,5},{7,8},{8,7},{9,10},{10... | collective-permute-start | bytes 786440 | tf_op jit(solution)/shard_map/ppermute | solution.py:51
  38.6 1.0 %copy-start = (f32[512,256]{1,0:T(8,128)S(1)}, f32[512,256]{1,0:T(8,128)}, u32[]{:S(2)}) copy-start(f32[512,256]{1,0:T(8,128)} %refs_7_.3) | copy-start | bytes 1572868
  42.0 10.9 %collective-permute-start.10 = (bf16[2,512,256]{2,1,0:T(8,128)(2,1)S(1)}, bf16[2,512,256]{2,1,0:T(8,128)(2,1)S(1)}, u32[]{:S(2)}, u32[]{:S(2)}) collective-permute-start(bf16[2,512,256]{2,1,0:T(8,128)(2,1)S(1)} %get-tuple-element.55), channel_id=1, source_target_pairs={{0,1},{1,0},{2,3},{3,2},{4,5},{5,4},{6,7},{7,6},{8,9},{9,8},{10,11... | collective-permute-start | bytes 1572872 | tf_op jit(solution)/shard_map/ppermute | solution.py:31
  42.1 10.8 %collective-permute-start.11 = (bf16[512,256]{1,0:T(8,128)(2,1)S(1)}, bf16[512,256]{1,0:T(8,128)(2,1)S(1)}, u32[]{:S(2)}, u32[]{:S(2)}) collective-permute-start(bf16[512,256]{1,0:T(8,128)(2,1)S(1)} %get-tuple-element.56), channel_id=1, source_target_pairs={{0,63},{1,2},{2,1},{3,4},{4,3},{5,6},{6,5},{7,8},{8,7},{9,10},{10,... | collective-permute-start | bytes 786440 | tf_op jit(solution)/shard_map/ppermute | solution.py:51
  44.3 13.6 %collective-permute-start.7 = (bf16[512,256]{1,0:T(8,128)(2,1)S(1)}, bf16[512,256]{1,0:T(8,128)(2,1)S(1)}, u32[]{:S(2)}, u32[]{:S(2)}) collective-permute-start(bf16[512,256]{1,0:T(8,128)(2,1)S(1)} %get-tuple-element.50.wire_ref.refs_2_), channel_id=1, source_target_pairs={{0,224},{32,0},{64,32},{96,64},{128,96},{160,128},{192,160},{224,1... | collective-permute-start | bytes 786440 | tf_op jit(solution)/shard_map/ppermute | solution.py:27
  53.0 19.9 %collective-permute-start.12 = (bf16[2,512,256]{2,1,0:T(8,128)(2,1)S(1)}, bf16[2,512,256]{2,1,0:T(8,128)(2,1)S(1)}, u32[]{:S(2)}, u32[]{:S(2)}) collective-permute-start(bf16[2,512,256]{2,1,0:T(8,128)(2,1)S(1)} %get-tuple-element.57), channel_id=1, source_target_pairs={{0,31},{1,2},{2,1},{3,4},{4,3},{5,6},{6,5},{7,8},{8,7},{9,10},{10,... | collective-permute-start | bytes 1572872 | tf_op jit(solution)/shard_map/ppermute | solution.py:36
  57.9 15.0 %collective-permute-start.13 = (bf16[512,256]{1,0:T(8,128)(2,1)S(1)}, bf16[512,256]{1,0:T(8,128)(2,1)S(1)}, u32[]{:S(2)}, u32[]{:S(2)}) collective-permute-start(bf16[512,256]{1,0:T(8,128)(2,1)S(1)} %fusion.1), channel_id=1, source_target_pairs={{0,32},{32,64},{64,96},{96,128},{128,160},{160,192},{192,224},{224... | collective-permute-start | bytes 786440 | tf_op jit(solution)/shard_map/ppermute | solution.py:27
  58.0 15.3 %collective-permute-start.9 = (bf16[512,256]{1,0:T(8,128)(2,1)S(1)}, bf16[512,256]{1,0:T(8,128)(2,1)S(1)}, u32[]{:S(2)}, u32[]{:S(2)}) collective-permute-start(bf16[512,256]{1,0:T(8,128)(2,1)S(1)} %broadcast_select_fusion), channel_id=1, source_target_pairs={{0,255},{1,2},{2,1},{3,4},{4,3},{5,6},{6,5},{7,8},{8,7},{9,10},{10... | collective-permute-start | bytes 786440 | tf_op jit(solution)/shard_map/ppermute | solution.py:51
  59.7 13.6 %collective-permute-start.8 = (bf16[2,512,256]{2,1,0:T(8,128)(2,1)S(1)}, bf16[2,512,256]{2,1,0:T(8,128)(2,1)S(1)}, u32[]{:S(2)}, u32[]{:S(2)}) collective-permute-start(bf16[2,512,256]{2,1,0:T(8,128)(2,1)S(1)} %pad_maximum_fusion.1), channel_id=1, source_target_pairs={{0,1},{1,0},{2,3},{3,2},{4,5},{5,4},{6,7},{7,6},{8,9},{9,8},{10,11... | collective-permute-start | bytes 1572872 | tf_op jit(solution)/shard_map/ppermute | solution.py:31

commit v12 on v5

--- a/solution.py
+++ b/solution.py
@@ -123,18 +123,24 @@
                 stores[q // per][2 * t * count : (2 * t + 2) * count, lanes] = tile
 
 
-def emit(cross, wire, perm_ref, wire_ref, self_ref, mate_ref, far_ref):
-    perm = perm_ref[...]
-    wire_ref[...] = wire
+def emit(cross, wire, perm, self_ref, mate_ref, far_ref):
     self_ref[...] = dot_t(cross[0][...], perm)
     for k, ref in ((2, far_ref), (1, mate_ref)):
         ref[0] = dot_t(cross[k][...], perm).astype(BF16)
         ref[1] = wire
 
 
+def emit_body(*refs):
+    emit(refs[:3], refs[4][...], refs[3][...], *refs[5:])
+
+
+def lanes_of(half):
+    return slice(half * LANES, (half + 1) * LANES)
+
+
 def first_body(sizes, blocks_hbm, row_hbm, col_hbm, drive_hbm, relax_hbm, *refs):
-    cross, (perm_ref, wire_ref, self_ref, mate_ref, far_ref, spread_ref) = refs[:3], refs[3:9]
-    blocks, ids, drive, relax, scratch, sems = refs[9:]
+    cross, perms, wires, spread_ref = refs[:3], refs[3:5], refs[5:7], refs[7]
+    blocks, ids, drive, relax, scratch, sems = refs[8:]
     later = [
         pltpu.make_async_copy(drive_hbm, drive, sems.at[2 + PIECES]),
         pltpu.make_async_copy(relax_hbm, relax, sems.at[3 + PIECES]),
@@ -145,15 +151,14 @@
     for copy in later:
         copy.wait()
     spread_ref[...] = jnp.broadcast_to(relax[...], (LANES, relax.shape[1])).T
-    field = drive[...]
-    interleave(field, scratch, perm_ref)
-    emit(cross, field.astype(BF16), perm_ref, wire_ref, self_ref, mate_ref, far_ref)
-
-
-def second_body(sizes, blocks_hbm, row_hbm, col_hbm, perm_ref, *refs):
-    own, outs, (blocks, ids, sems) = refs[:3], refs[3:6], refs[6:]
-    build(0, sizes, blocks_hbm, row_hbm, col_hbm, blocks, ids, sems, own)
-    partials(own, perm_ref, outs)
+    for half in range(2):
+        field = drive[:, lanes_of(half)]
+        interleave(field, scratch, perms[half])
+        wires[half][...] = field.astype(BF16)
+
+
+def second_body(sizes, blocks_hbm, row_hbm, col_hbm, *refs):
+    build(0, sizes, blocks_hbm, row_hbm, col_hbm, *refs[3:], refs[:3])
 
 
 def partials(mats, perm_ref, outs):
@@ -181,72 +186,79 @@
     return known_ref[...] + mate_ref[1].astype(F32) + far_ref[1].astype(F32) + restored(straight, scratch)
 
 
-def advanced(product, drive_ref, relax_ref):
-    scale = jnp.concatenate([relax_ref[...]] * (product.shape[1] // LANES), axis=1)
-    return drive_ref[...] + scale * product
-
-
-def update_body(*refs):
+def advanced(half, product, drive_ref, relax_ref):
+    return drive_ref[:, lanes_of(half)] + relax_ref[...] * product
+
+
+def update_body(half, *refs):
     cross, nexts, (drive_ref, relax_ref) = refs[:3], refs[3:7], refs[7:9]
     perm_ref, wire_ref, self_ref, mate_ref, far_ref, scratch = refs[9:]
-    field = advanced(with_cross(cross, *nexts, scratch), drive_ref, relax_ref)
+    field = advanced(half, with_cross(cross, *nexts, scratch), drive_ref, relax_ref)
     interleave(field, scratch, perm_ref)
-    emit(cross, field.astype(BF16), perm_ref, wire_ref, self_ref, mate_ref, far_ref)
+    wire_ref[...] = field.astype(BF16)
+    emit(cross, wire_ref[...], perm_ref[...], self_ref, mate_ref, far_ref)
 
 
 def settle_body(own_ref, received_ref, out_ref):
     out_ref[...] = own_ref[...] + received_ref[...].astype(F32)
 
 
-def final_body(*refs):
-    product = with_cross(refs[:3], *refs[3:7], refs[10])
-    refs[9][...] = advanced(product, *refs[7:9])
+def final_body(half, *refs):
+    product = with_cross(refs[:3], *refs[3:7], refs[-1])
+    refs[-2][:, lanes_of(half) if half else slice(None)] = advanced(half, product, *refs[7:9])
+    if half:
+        refs[-2][:, lanes_of(0)] = refs[9][...]
 
 
 def local(drive, relax, blocks, row_block, col_block):
     rows, channels = drive.shape
     slots = blocks.shape[0]
     sizes = (rows // SIDE, lax.axis_size("rows"), lax.axis_size("ka"))
-    small = jax.ShapeDtypeStruct((rows, channels), BF16)
-    double = jax.ShapeDtypeStruct((2, rows, channels), BF16)
-    wide = jax.ShapeDtypeStruct((rows, channels), F32)
+    full = jax.ShapeDtypeStruct((rows, channels), F32)
+    small = jax.ShapeDtypeStruct((rows, LANES), BF16)
+    double = jax.ShapeDtypeStruct((2, rows, LANES), BF16)
+    wide = jax.ShapeDtypeStruct((rows, LANES), F32)
+    emitted = (wide, double, double)
     matrices = (jax.ShapeDtypeStruct((rows, rows), BF16),) * 3
-    emitted = (small, small, wide, double, double)
-    staging = pltpu.VMEM((channels // LANES, rows, LANES), F32)
+    staging = pltpu.VMEM((1, rows, LANES), F32)
     fetch = [pltpu.VMEM(blocks.shape, BF16), pltpu.VMEM((2, slots), jnp.int32)]
     row2 = row_block.reshape(1, -1)
     col2 = col_block.reshape(1, -1)
     relax2 = relax.reshape(1, -1)
-    work = 2 * rows * rows * channels
-    spread = jax.ShapeDtypeStruct((rows, LANES), F32)
-    *cross, perm, wire, partial, to_mate, to_far, relax3 = call(
-        functools.partial(first_body, sizes), (*matrices, *emitted, spread), 9 * work,
+    work = rows * rows * channels
+    *cross, perm0, perm1, wire0, wire1, relax3 = call(
+        functools.partial(first_body, sizes), (*matrices, small, small, small, small, wide), 12 * work,
         [blocks, row2, col2, drive, relax2], [HBM] * 5,
         fetch + [pltpu.VMEM(drive.shape, F32), pltpu.VMEM((1, rows), F32), staging, pltpu.SemaphoreType.DMA((4 + PIECES,))],
     )
-
+    streams = [(perm, wire, *call(emit_body, emitted, 3 * work, [*cross, perm, wire])) for perm, wire in ((perm0, wire0), (perm1, wire1))]
+    own = call(
+        functools.partial(second_body, sizes), matrices, 9 * work, [blocks, row2, col2], [HBM] * 3,
+        fetch + [pltpu.SemaphoreType.DMA((2 + PIECES,))],
+    )
+    done = []
     for sweep in range(ITERS):
-        down = shifted(wire, "ka", -1)
-        from_far = far(to_far)
-        from_mate = mate(to_mate)
-        if sweep == 0:
-            *own, own_self, own_mate, own_far = call(
-                functools.partial(second_body, sizes), (*matrices, wide, small, small), 9 * work,
-                [blocks, row2, col2, perm], [HBM] * 3 + [VMEM], fetch + [pltpu.SemaphoreType.DMA((2 + PIECES,))],
-            )
-        else:
+        for half in range(2):
+            perm, wire, partial, to_mate, to_far = streams[half]
+            down = shifted(wire, "ka", -1)
+            from_far = far(to_far)
+            from_mate = mate(to_mate)
             own_self, own_mate, own_far = call(third_body, (wide, small, small), 3 * work, [*own, perm])
-        from_far, _ = lax.optimization_barrier((from_far, own_self))
-        got = (partial + from_mate[0].astype(F32) + from_far[0].astype(F32)).astype(BF16)
-        received = shifted(got, "ka", 1)
-        second_mate = mate(jnp.stack([down, own_mate]))
-        second_far = far(jnp.stack([down, own_far]))
-        known = call(own_body, wide, 3 * work, [*own, wire, from_mate, from_far, own_self], scratch=[staging])
-        known = call(settle_body, wide, HEAVY * work, [known, received])
-        args = [*cross, down, second_mate, second_far, known, drive, relax3]
-        if sweep + 1 == ITERS:
-            return call(final_body, wide, 3 * work, args, scratch=[staging])
-        perm, wire, partial, to_mate, to_far = call(update_body, emitted, 6 * work, args, scratch=[staging])
+            from_far, _ = lax.optimization_barrier((from_far, own_self))
+            got = (partial + from_mate[0].astype(F32) + from_far[0].astype(F32)).astype(BF16)
+            received = shifted(got, "ka", 1)
+            second_mate = mate(jnp.stack([down, own_mate]))
+            second_far = far(jnp.stack([down, own_far]))
+            known = call(own_body, wide, 3 * work, [*own, wire, from_mate, from_far, own_self], scratch=[staging])
+            known = call(settle_body, wide, HEAVY * work, [known, received])
+            args = [*cross, down, second_mate, second_far, known, drive, relax3]
+            if sweep + 1 == ITERS:
+                out = full if half else wide
+                done.append(call(functools.partial(final_body, half), out, 3 * work, [*args, *done], scratch=[staging]))
+            else:
+                body = functools.partial(update_body, half)
+                streams[half] = call(body, (small, small, *emitted), 6 * work, args, scratch=[staging])
+    return done[1]
 
 
 def solution(mesh):

time: 68.9 us -> 92.7 us (1.35)
  starting transfers between devices: 26.6 us -> 36.6 us
  waiting for transfers between devices: 28.8 us -> 37 us
  Pallas kernels: 12.6 us -> 18.2 us
    ppermute x4 -> x8, waiting for transfers between devices: 27.9 us -> 37 us  [shifted(): lax.ppermute(value, axis, [(source, (source + steps) % count) for source...]
    ppermute x4 -> x8, starting transfers between devices: 10.6 us -> 16.8 us  [shifted(): lax.ppermute(value, axis, [(source, (source + steps) % count) for source...]
    pallas_call x9 -> x20, Pallas kernels: 12.6 us -> 18.2 us  [call(): pl.pallas_call(kernel, out_shape=outs, in_specs=specs or [VMEM] * len(arg...]
    ppermute x4 -> x8, starting transfers between devices: 12.6 us -> 16.7 us  [mate(): lax.ppermute(value, 'rows', [(i, i ^ 1) for i in range(lax.axis_size('row...]
    ppermute x4 -> x8, waiting for transfers between devices: 0.96 us -> 0.02 us  [far(): lax.ppermute(value, 'rows', [(i, (i + 1 if i & 1 else i - 1) % count) for...]
    ppermute x4 -> x8, starting transfers between devices: 3.39 us -> 3.16 us  [far(): lax.ppermute(value, 'rows', [(i, (i + 1 if i & 1 else i - 1) % count) for...]
  transfers between devices with their start and end apart: 12 -> 24, of which waited for: 5 -> 6; matrix products, arithmetic and copies ran while one was open for 1% -> 0% of each run, Pallas kernels for 7% -> 15%
where the time goes in v12:
time: 92.7 us; the launch traced here: 92.5 us
  waiting for transfers between devices  37 us (40%)
  starting transfers between devices  36.6 us (39%)
  Pallas kernels  18.2 us (20%)
    ppermute x8, waiting for transfers between devices, shifted(): lax.ppermute(value, axis, [(source, (source + steps) % count) for source...  37 us
    pallas_call x20, Pallas kernels, call(): pl.pallas_call(kernel, out_shape=outs, in_specs=specs or [VMEM] * len(arg...  18.2 us
    ppermute x8, starting transfers between devices, shifted(): lax.ppermute(value, axis, [(source, (source + steps) % count) for source...  16.8 us
    ppermute x8, starting transfers between devices, mate(): lax.ppermute(value, 'rows', [(i, i ^ 1) for i in range(lax.axis_size('row...  16.7 us
    ppermute x8, starting transfers between devices, far(): lax.ppermute(value, 'rows', [(i, (i + 1 if i & 1 else i - 1) % count) for...  3.16 us
  transfers between devices with their start and end apart: 24, of which 6 were waited for; matrix products, arithmetic and copies ran while one was open for 0% of the time, Pallas kernels for 15%

profile of v12, /device:TPU:1, one launch (start us, length us, event | category | flops | bytes accessed | tf_op | source)
XLA Modules:
  0.0 92.5 jit_solution(8606478775849576617)
XLA Ops:
  0.0 3.2 %shard_map.55 = (bf16[512,512]{1,0:T(8,128)(2,1)S(1)}, bf16[512,512]{1,0:T(8,128)(2,1)S(1)}, bf16[512,512]{1,0:T(8,128)(2,1)S(1)}, bf16[512,128]{1,0:T(8,128)(2,...) custom-call(bf16[256,4096]{1,0:T(8,128)(2,1)} %blocks_hbm.3, ...), custom_call_target="tpu_custom_call" | custom-call | flops 805306368 | bytes 2625536 | tf_op jit(solution)/shard_map/pallas_call | solution.py:43
  3.2 6.1 %collective-permute-start.12 = (bf16[512,128]{1,0:T(8,128)(2,1)S(1)}, bf16[512,128]{1,0:T(8,128)(2,1)S(1)}, u32[]{:S(2)}, u32[]{:S(2)}) collective-permute-start(bf16[512,128]{1,0:T(8,128)(2,1)S(1)} %get-tuple-element.73.refs_4_.refs_3_), channel_id=1, source_target_pairs={{0,224},{32,0},{64,32},{96,64},{128,96},{160,128},{192,160},{224,1... | collective-permute-start | bytes 393224 | tf_op jit(solution)/shard_map/ppermute | solution.py:27
  9.3 0.6 shard_map.66
  9.9 2.6 %collective-permute-start.16 = (bf16[2,512,128]{2,1,0:T(8,128)(2,1)S(1)}, bf16[2,512,128]{2,1,0:T(8,128)(2,1)S(1)}, u32[]{:S(2)}, u32[]{:S(2)}) collective-permute-start(bf16[2,512,128]{2,1,0:T(8,128)(2,1)S(1)} %get-tuple-element.78), channel_id=1, source_target_pairs={{0,31},{1,2},{2,1},{3,4},{4,3},{5,6},{6,5},{7,8},{8,7},{9,10},{10,... | collective-permute-start | bytes 786440 | tf_op jit(solution)/shard_map/ppermute | solution.py:36
  12.5 3.5 %collective-permute-start.15 = (bf16[2,512,128]{2,1,0:T(8,128)(2,1)S(1)}, bf16[2,512,128]{2,1,0:T(8,128)(2,1)S(1)}, u32[]{:S(2)}, u32[]{:S(2)}) collective-permute-start(bf16[2,512,128]{2,1,0:T(8,128)(2,1)S(1)} %get-tuple-element.77), channel_id=1, source_target_pairs={{0,1},{1,0},{2,3},{3,2},{4,5},{5,4},{6,7},{7,6},{8,9},{9,8},{10,11... | collective-permute-start | bytes 786440 | tf_op jit(solution)/shard_map/ppermute | solution.py:31
  16.0 1.7 %collective-permute-start = (bf16[512,128]{1,0:T(8,128)(2,1)S(1)}, bf16[512,128]{1,0:T(8,128)(2,1)S(1)}, u32[]{:S(2)}, u32[]{:S(2)}) collective-permute-start(bf16[512,128]{1,0:T(8,128)(2,1)S(1)} %get-tuple-element.51.refs_4_.refs_3_), channel_id=1, source_target_pairs={{0,224},{32,0},{64,32},{96,64},{128,96},{160,128},{192,160},{224,1... | collective-permute-start | bytes 393224 | tf_op jit(solution)/shard_map/ppermute | solution.py:27
  17.7 0.6 shard_map.58
  18.5 2.5 %shard_map.56 = (bf16[512,512]{1,0:T(8,128)(2,1)S(1)}, bf16[512,512]{1,0:T(8,128)(2,1)S(1)}, bf16[512,512]{1,0:T(8,128)(2,1)S(1)}) custom-call(bf16[256,4096]{1,0:T(8,128)(2,1)} %blocks_hbm.3, s32[1,256]{1,0:T(1,128)} %bitcast.61, s32[1,256]{1,0:T(1,128)} %bitcast.63), custom_call_target="tpu_custom_call" | custom-call | flops 603979776 | bytes 2099200 | tf_op jit(solution)/shard_map/pallas_call | solution.py:43
  21.0 0.6 shard_map.65
  21.6 0.6 shard_map.57
  22.9 1.3 %collective-permute-done.refs_3_ = bf16[512,128]{1,0:T(8,128)(2,1)S(1)} collective-permute-done((bf16[512,128]{1,0:T(8,128)(2,1)S(1)}, bf16[512,128]{1,0:T(8,128)(2,1)S(1)}, u32[]{:S(2)}, u32[]{:S(2)}) %collective-permute-start) | collective-permute-done | bytes 131104 | tf_op jit(solution)/shard_map/ppermute | solution.py:27
  24.9 2.9 %collective-permute-start.1 = (bf16[2,512,128]{2,1,0:T(8,128)(2,1)S(1)}, bf16[2,512,128]{2,1,0:T(8,128)(2,1)S(1)}, u32[]{:S(2)}, u32[]{:S(2)}) collective-permute-start(bf16[2,512,128]{2,1,0:T(8,128)(2,1)S(1)} %get-tuple-element.98), channel_id=1, source_target_pairs={{0,1},{1,0},{2,3},{3,2},{4,5},{5,4},{6,7},{7,6},{8,9},{9,8},{10,11... | collective-permute-start | bytes 786440 | tf_op jit(solution)/shard_map/ppermute | solution.py:31
  27.7 0.6 shard_map.67.own_ref
  28.4 3.0 %collective-permute-start.17 = (bf16[512,128]{1,0:T(8,128)(2,1)S(1)}, bf16[512,128]{1,0:T(8,128)(2,1)S(1)}, u32[]{:S(2)}, u32[]{:S(2)}) collective-permute-start(bf16[512,128]{1,0:T(8,128)(2,1)S(1)} %fusion.1), channel_id=1, source_target_pairs={{0,32},{32,64},{64,96},{96,128},{128,160},{160,192},{192,224},{224... | collective-permute-start | bytes 393224 | tf_op jit(solution)/shard_map/ppermute | solution.py:27
  31.4 0.6 shard_map.59.own_ref
  32.1 10.0 %collective-permute-done.17.received_ref = bf16[512,128]{1,0:T(8,128)(2,1)S(1)} collective-permute-done((bf16[512,128]{1,0:T(8,128)(2,1)S(1)}, bf16[512,128]{1,0:T(8,128)(2,1)S(1)}, u32[]{:S(2)}, u32[]{:S(2)}) %collective-permute-start.17) | collective-permute-done | bytes 131104 | tf_op jit(solution)/shard_map/ppermute | solution.py:27
  42.2 2.1 %shard_map.69 = (bf16[512,128]{1,0:T(8,128)(2,1)S(1)}, bf16[512,128]{1,0:T(8,128)(2,1)S(1)}, f32[512,128]{1,0:T(8,128)S(1)}, bf16[2,512,128]{2,1,0:T(8,128)(2,1)S(1)}, bf16[2,512,128]{2,1,0:T(8,128)(2,1)S(1)}) custom-call(bf16[512,512]{1,0:T(8,128)(2,1)S(1)} %get-tuple-element.48.refs_0_, bf16[512,512]{1,0:T(8,128)(2,1)S(1)} %get-tuple-element.49.refs_1_, ...), custom_call_target="tpu_custom_call" | custom-call | flops 402653184 | bytes 3276800 | tf_op jit(solution)/shard_map/pallas_call | solution.py:43
  44.4 3.8 %collective-permute-start.21 = (bf16[2,512,128]{2,1,0:T(8,128)(2,1)S(1)}, bf16[2,512,128]{2,1,0:T(8,128)(2,1)S(1)}, u32[]{:S(2)}, u32[]{:S(2)}) collective-permute-start(bf16[2,512,128]{2,1,0:T(8,128)(2,1)S(1)} %get-tuple-element.86), channel_id=1, source_target_pairs={{0,1},{1,0},{2,3},{3,2},{4,5},{5,4},{6,7},{7,6},{8,9},{9,8},{10,11... | collective-permute-start | bytes 786440 | tf_op jit(solution)/shard_map/ppermute | solution.py:31
  48.2 2.0 %collective-permute-done.5.received_ref = bf16[512,128]{1,0:T(8,128)(2,1)S(1)} collective-permute-done((bf16[512,128]{1,0:T(8,128)(2,1)S(1)}, bf16[512,128]{1,0:T(8,128)(2,1)S(1)}, u32[]{:S(2)}, u32[]{:S(2)}) %collective-permute-start.5) | collective-permute-done | bytes 131104 | tf_op jit(solution)/shard_map/ppermute | solution.py:27
  50.2 3.7 %collective-permute-start.18 = (bf16[512,128]{1,0:T(8,128)(2,1)S(1)}, bf16[512,128]{1,0:T(8,128)(2,1)S(1)}, u32[]{:S(2)}, u32[]{:S(2)}) collective-permute-start(bf16[512,128]{1,0:T(8,128)(2,1)S(1)} %get-tuple-element.82.refs_3_), channel_id=1, source_target_pairs={{0,224},{32,0},{64,32},{96,64},{128,96},{160,128},{192,160},{224,1... | collective-permute-start | bytes 393224 | tf_op jit(solution)/shard_map/ppermute | solution.py:27
  54.0 2.1 %shard_map.61 = (bf16[512,128]{1,0:T(8,128)(2,1)S(1)}, bf16[512,128]{1,0:T(8,128)(2,1)S(1)}, f32[512,128]{1,0:T(8,128)S(1)}, bf16[2,512,128]{2,1,0:T(8,128)(2,1)S(1)}, bf16[2,512,128]{2,1,0:T(8,128)(2,1)S(1)}) custom-call(bf16[512,512]{1,0:T(8,128)(2,1)S(1)} %get-tuple-element.48.refs_0_, bf16[512,512]{1,0:T(8,128)(2,1)S(1)} %get-tuple-element.49.refs_1_, ...), custom_call_target="tpu_custom_call" | custom-call | flops 402653184 | bytes 3276800 | tf_op jit(solution)/shard_map/pallas_call | solution.py:43
  56.3 0.6 shard_map.70
  56.9 0.6 shard_map.62
  57.5 2.2 %collective-permute-start.9 = (bf16[2,512,128]{2,1,0:T(8,128)(2,1)S(1)}, bf16[2,512,128]{2,1,0:T(8,128)(2,1)S(1)}, u32[]{:S(2)}, u32[]{:S(2)}) collective-permute-start(bf16[2,512,128]{2,1,0:T(8,128)(2,1)S(1)} %get-tuple-element.68), channel_id=1, source_target_pairs={{0,1},{1,0},{2,3},{3,2},{4,5},{5,4},{6,7},{7,6},{8,9},{9,8},{10,11... | collective-permute-start | bytes 786440 | tf_op jit(solution)/shard_map/ppermute | solution.py:31
  59.8 5.3 %collective-permute-done.6.refs_3_ = bf16[512,128]{1,0:T(8,128)(2,1)S(1)} collective-permute-done((bf16[512,128]{1,0:T(8,128)(2,1)S(1)}, bf16[512,128]{1,0:T(8,128)(2,1)S(1)}, u32[]{:S(2)}, u32[]{:S(2)}) %collective-permute-start.6) | collective-permute-done | bytes 131104 | tf_op jit(solution)/shard_map/ppermute | solution.py:27
  65.0 1.5 %collective-permute-start.19 = (bf16[2,512,128]{2,1,0:T(8,128)(2,1)S(1)}, bf16[2,512,128]{2,1,0:T(8,128)(2,1)S(1)}, u32[]{:S(2)}, u32[]{:S(2)}) collective-permute-start(bf16[2,512,128]{2,1,0:T(8,128)(2,1)S(1)} %get-tuple-element.92), channel_id=1, source_target_pairs={{0,1},{1,0},{2,3},{3,2},{4,5},{5,4},{6,7},{7,6},{8,9},{9,8},{10,11... | collective-permute-start | bytes 786440 | tf_op jit(solution)/shard_map/ppermute | solution.py:31
  66.7 1.8 %collective-permute-start.7 = (bf16[2,512,128]{2,1,0:T(8,128)(2,1)S(1)}, bf16[2,512,128]{2,1,0:T(8,128)(2,1)S(1)}, u32[]{:S(2)}, u32[]{:S(2)}) collective-permute-start(bf16[2,512,128]{2,1,0:T(8,128)(2,1)S(1)} %get-tuple-element.96), channel_id=1, source_target_pairs={{0,1},{1,0},{2,3},{3,2},{4,5},{5,4},{6,7},{7,6},{8,9},{9,8},{10,11... | collective-permute-start | bytes 786440 | tf_op jit(solution)/shard_map/ppermute | solution.py:31
  69.2 2.1 %collective-permute-start.23 = (bf16[512,128]{1,0:T(8,128)(2,1)S(1)}, bf16[512,128]{1,0:T(8,128)(2,1)S(1)}, u32[]{:S(2)}, u32[]{:S(2)}) collective-permute-start(bf16[512,128]{1,0:T(8,128)(2,1)S(1)} %fusion), channel_id=1, source_target_pairs={{0,32},{32,64},{64,96},{96,128},{128,160},{160,192},{192,224},{224... | collective-permute-start | bytes 393224 | tf_op jit(solution)/shard_map/ppermute | solution.py:27
  72.0 10.3 %collective-permute-done.23.received_ref = bf16[512,128]{1,0:T(8,128)(2,1)S(1)} collective-permute-done((bf16[512,128]{1,0:T(8,128)(2,1)S(1)}, bf16[512,128]{1,0:T(8,128)(2,1)S(1)}, u32[]{:S(2)}, u32[]{:S(2)}) %collective-permute-start.23) | collective-permute-done | bytes 131104 | tf_op jit(solution)/shard_map/ppermute | solution.py:27
  82.3 8.2 %collective-permute-done.11.received_ref = bf16[512,128]{1,0:T(8,128)(2,1)S(1)} collective-permute-done((bf16[512,128]{1,0:T(8,128)(2,1)S(1)}, bf16[512,128]{1,0:T(8,128)(2,1)S(1)}, u32[]{:S(2)}, u32[]{:S(2)}) %collective-permute-start.11) | collective-permute-done | bytes 131104 | tf_op jit(solution)/shard_map/ppermute | solution.py:27
  90.5 0.6 shard_map.73.refs_9_
  91.1 1.4 %shard_map.74 = f32[512,256]{1,0:T(8,128)} custom-call(bf16[512,512]{1,0:T(8,128)(2,1)S(1)} %get-tuple-element.48.refs_0_, bf16[512,512]{1,0:T(8,128)(2,1)S(1)} %get-tuple-element.49.refs_1_, bf16[512,512]{1,0:T(8,128)(2,1)S(1)} %get-tuple-element.50.refs_2_, bf16[512,128]{1,0:T(8,128)(2,1)S(1)} %collective-permute-done.6.refs_3_, ...), custom_call_target="tpu_custom_call" | custom-call | flops 201326592 | bytes 3538944 | tf_op jit(solution)/shard_map/pallas_call | solution.py:43
  (46 shorter events, 3.5 us)
Async XLA Ops:
  3.2 19.1 %collective-permute-start.12 = (bf16[512,128]{1,0:T(8,128)(2,1)S(1)}, bf16[512,128]{1,0:T(8,128)(2,1)S(1)}, u32[]{:S(2)}, u32[]{:S(2)}) collective-permute-start(bf16[512,128]{1,0:T(8,128)(2,1)S(1)} %get-tuple-element.73.refs_4_.refs_3_), channel_id=1, source_target_pairs={{0,224},{32,0},{64,32},{96,64},{128,96},{160,128},{192,160},{224,1... | collective-permute-start | bytes 393224 | tf_op jit(solution)/shard_map/ppermute | solution.py:27
  9.9 14.8 %collective-permute-start.16 = (bf16[2,512,128]{2,1,0:T(8,128)(2,1)S(1)}, bf16[2,512,128]{2,1,0:T(8,128)(2,1)S(1)}, u32[]{:S(2)}, u32[]{:S(2)}) collective-permute-start(bf16[2,512,128]{2,1,0:T(8,128)(2,1)S(1)} %get-tuple-element.78), channel_id=1, source_target_pairs={{0,31},{1,2},{2,1},{3,4},{4,3},{5,6},{6,5},{7,8},{8,7},{9,10},{10,... | collective-permute-start | bytes 786440 | tf_op jit(solution)/shard_map/ppermute | solution.py:36
  12.5 15.2 %collective-permute-start.15 = (bf16[2,512,128]{2,1,0:T(8,128)(2,1)S(1)}, bf16[2,512,128]{2,1,0:T(8,128)(2,1)S(1)}, u32[]{:S(2)}, u32[]{:S(2)}) collective-permute-start(bf16[2,512,128]{2,1,0:T(8,128)(2,1)S(1)} %get-tuple-element.77), channel_id=1, source_target_pairs={{0,1},{1,0},{2,3},{3,2},{4,5},{5,4},{6,7},{7,6},{8,9},{9,8},{10,11... | collective-permute-start | bytes 786440 | tf_op jit(solution)/shard_map/ppermute | solution.py:31
  16.0 8.1 %collective-permute-start = (bf16[512,128]{1,0:T(8,128)(2,1)S(1)}, bf16[512,128]{1,0:T(8,128)(2,1)S(1)}, u32[]{:S(2)}, u32[]{:S(2)}) collective-permute-start(bf16[512,128]{1,0:T(8,128)(2,1)S(1)} %get-tuple-element.51.refs_4_.refs_3_), channel_id=1, source_target_pairs={{0,224},{32,0},{64,32},{96,64},{128,96},{160,128},{192,160},{224,1... | collective-permute-start | bytes 393224 | tf_op jit(solution)/shard_map/ppermute | solution.py:27
  18.4 6.5 %collective-permute-start.4 = (bf16[2,512,128]{2,1,0:T(8,128)(2,1)S(1)}, bf16[2,512,128]{2,1,0:T(8,128)(2,1)S(1)}, u32[]{:S(2)}, u32[]{:S(2)}) collective-permute-start(bf16[2,512,128]{2,1,0:T(8,128)(2,1)S(1)} %get-tuple-element.59), channel_id=1, source_target_pairs={{0,31},{1,2},{2,1},{3,4},{4,3},{5,6},{6,5},{7,8},{8,7},{9,10},{10,... | collective-permute-start | bytes 786440 | tf_op jit(solution)/shard_map/ppermute | solution.py:36
  22.3 6.1 %collective-permute-start.3 = (bf16[2,512,128]{2,1,0:T(8,128)(2,1)S(1)}, bf16[2,512,128]{2,1,0:T(8,128)(2,1)S(1)}, u32[]{:S(2)}, u32[]{:S(2)}) collective-permute-start(bf16[2,512,128]{2,1,0:T(8,128)(2,1)S(1)} %get-tuple-element.58), channel_id=1, source_target_pairs={{0,1},{1,0},{2,3},{3,2},{4,5},{5,4},{6,7},{7,6},{8,9},{9,8},{10,11... | collective-permute-start | bytes 786440 | tf_op jit(solution)/shard_map/ppermute | solution.py:31
  24.2 18.0 %collective-permute-start.13 = (bf16[2,512,128]{2,1,0:T(8,128)(2,1)S(1)}, bf16[2,512,128]{2,1,0:T(8,128)(2,1)S(1)}, u32[]{:S(2)}, u32[]{:S(2)}) collective-permute-start(bf16[2,512,128]{2,1,0:T(8,128)(2,1)S(1)} %get-tuple-element.94), channel_id=1, source_target_pairs={{0,1},{1,0},{2,3},{3,2},{4,5},{5,4},{6,7},{7,6},{8,9},{9,8},{10,11... | collective-permute-start | bytes 786440 | tf_op jit(solution)/shard_map/ppermute | solution.py:31
  24.7 17.5 %collective-permute-start.14 = (bf16[2,512,128]{2,1,0:T(8,128)(2,1)S(1)}, bf16[2,512,128]{2,1,0:T(8,128)(2,1)S(1)}, u32[]{:S(2)}, u32[]{:S(2)}) collective-permute-start(bf16[2,512,128]{2,1,0:T(8,128)(2,1)S(1)} %get-tuple-element.93), channel_id=1, source_target_pairs={{0,31},{1,2},{2,1},{3,4},{4,3},{5,6},{6,5},{7,8},{8,7},{9,10},{10,... | collective-permute-start | bytes 786440 | tf_op jit(solution)/shard_map/ppermute | solution.py:36
  24.9 29.1 %collective-permute-start.1 = (bf16[2,512,128]{2,1,0:T(8,128)(2,1)S(1)}, bf16[2,512,128]{2,1,0:T(8,128)(2,1)S(1)}, u32[]{:S(2)}, u32[]{:S(2)}) collective-permute-start(bf16[2,512,128]{2,1,0:T(8,128)(2,1)S(1)} %get-tuple-element.98), channel_id=1, source_target_pairs={{0,1},{1,0},{2,3},{3,2},{4,5},{5,4},{6,7},{7,6},{8,9},{9,8},{10,11... | collective-permute-start | bytes 786440 | tf_op jit(solution)/shard_map/ppermute | solution.py:31
  27.7 26.2 %collective-permute-start.2 = (bf16[2,512,128]{2,1,0:T(8,128)(2,1)S(1)}, bf16[2,512,128]{2,1,0:T(8,128)(2,1)S(1)}, u32[]{:S(2)}, u32[]{:S(2)}) collective-permute-start(bf16[2,512,128]{2,1,0:T(8,128)(2,1)S(1)} %get-tuple-element.97), channel_id=1, source_target_pairs={{0,31},{1,2},{2,1},{3,4},{4,3},{5,6},{6,5},{7,8},{8,7},{9,10},{10,... | collective-permute-start | bytes 786440 | tf_op jit(solution)/shard_map/ppermute | solution.py:36
  28.4 13.7 %collective-permute-start.17 = (bf16[512,128]{1,0:T(8,128)(2,1)S(1)}, bf16[512,128]{1,0:T(8,128)(2,1)S(1)}, u32[]{:S(2)}, u32[]{:S(2)}) collective-permute-start(bf16[512,128]{1,0:T(8,128)(2,1)S(1)} %fusion.1), channel_id=1, source_target_pairs={{0,32},{32,64},{64,96},{96,128},{128,160},{160,192},{192,224},{224... | collective-permute-start | bytes 393224 | tf_op jit(solution)/shard_map/ppermute | solution.py:27
  32.1 10.1 %copy-start = (f32[512,256]{1,0:T(8,128)S(1)}, f32[512,256]{1,0:T(8,128)}, u32[]{:S(2)}) copy-start(f32[512,256]{1,0:T(8,128)} %refs_7_.7) | copy-start | bytes 1572868
  42.1 8.1 %collective-permute-start.5 = (bf16[512,128]{1,0:T(8,128)(2,1)S(1)}, bf16[512,128]{1,0:T(8,128)(2,1)S(1)}, u32[]{:S(2)}, u32[]{:S(2)}) collective-permute-start(bf16[512,128]{1,0:T(8,128)(2,1)S(1)} %fusion.3), channel_id=1, source_target_pairs={{0,32},{32,64},{64,96},{96,128},{128,160},{160,192},{192,224},{224... | collective-permute-start | bytes 393224 | tf_op jit(solution)/shard_map/ppermute | solution.py:27
  44.3 22.2 %collective-permute-start.22 = (bf16[2,512,128]{2,1,0:T(8,128)(2,1)S(1)}, bf16[2,512,128]{2,1,0:T(8,128)(2,1)S(1)}, u32[]{:S(2)}, u32[]{:S(2)}) collective-permute-start(bf16[2,512,128]{2,1,0:T(8,128)(2,1)S(1)} %get-tuple-element.87), channel_id=1, source_target_pairs={{0,31},{1,2},{2,1},{3,4},{4,3},{5,6},{6,5},{7,8},{8,7},{9,10},{10,... | collective-permute-start | bytes 786440 | tf_op jit(solution)/shard_map/ppermute | solution.py:36
  44.4 24.0 %collective-permute-start.21 = (bf16[2,512,128]{2,1,0:T(8,128)(2,1)S(1)}, bf16[2,512,128]{2,1,0:T(8,128)(2,1)S(1)}, u32[]{:S(2)}, u32[]{:S(2)}) collective-permute-start(bf16[2,512,128]{2,1,0:T(8,128)(2,1)S(1)} %get-tuple-element.86), channel_id=1, source_target_pairs={{0,1},{1,0},{2,3},{3,2},{4,5},{5,4},{6,7},{7,6},{8,9},{9,8},{10,11... | collective-permute-start | bytes 786440 | tf_op jit(solution)/shard_map/ppermute | solution.py:31
  50.2 7.3 %collective-permute-start.18 = (bf16[512,128]{1,0:T(8,128)(2,1)S(1)}, bf16[512,128]{1,0:T(8,128)(2,1)S(1)}, u32[]{:S(2)}, u32[]{:S(2)}) collective-permute-start(bf16[512,128]{1,0:T(8,128)(2,1)S(1)} %get-tuple-element.82.refs_3_), channel_id=1, source_target_pairs={{0,224},{32,0},{64,32},{96,64},{128,96},{160,128},{192,160},{224,1... | collective-permute-start | bytes 393224 | tf_op jit(solution)/shard_map/ppermute | solution.py:27
  56.1 10.6 %collective-permute-start.10 = (bf16[2,512,128]{2,1,0:T(8,128)(2,1)S(1)}, bf16[2,512,128]{2,1,0:T(8,128)(2,1)S(1)}, u32[]{:S(2)}, u32[]{:S(2)}) collective-permute-start(bf16[2,512,128]{2,1,0:T(8,128)(2,1)S(1)} %get-tuple-element.69), channel_id=1, source_target_pairs={{0,31},{1,2},{2,1},{3,4},{4,3},{5,6},{6,5},{7,8},{8,7},{9,10},{10,... | collective-permute-start | bytes 786440 | tf_op jit(solution)/shard_map/ppermute | solution.py:36
  56.2 8.8 %collective-permute-start.6 = (bf16[512,128]{1,0:T(8,128)(2,1)S(1)}, bf16[512,128]{1,0:T(8,128)(2,1)S(1)}, u32[]{:S(2)}, u32[]{:S(2)}) collective-permute-start(bf16[512,128]{1,0:T(8,128)(2,1)S(1)} %get-tuple-element.64.refs_3_), channel_id=1, source_target_pairs={{0,224},{32,0},{64,32},{96,64},{128,96},{160,128},{192,160},{224,1... | collective-permute-start | bytes 393224 | tf_op jit(solution)/shard_map/ppermute | solution.py:27
  57.5 11.6 %collective-permute-start.9 = (bf16[2,512,128]{2,1,0:T(8,128)(2,1)S(1)}, bf16[2,512,128]{2,1,0:T(8,128)(2,1)S(1)}, u32[]{:S(2)}, u32[]{:S(2)}) collective-permute-start(bf16[2,512,128]{2,1,0:T(8,128)(2,1)S(1)} %get-tuple-element.68), channel_id=1, source_target_pairs={{0,1},{1,0},{2,3},{3,2},{4,5},{5,4},{6,7},{7,6},{8,9},{9,8},{10,11... | collective-permute-start | bytes 786440 | tf_op jit(solution)/shard_map/ppermute | solution.py:31
  65.0 25.5 %collective-permute-start.19 = (bf16[2,512,128]{2,1,0:T(8,128)(2,1)S(1)}, bf16[2,512,128]{2,1,0:T(8,128)(2,1)S(1)}, u32[]{:S(2)}, u32[]{:S(2)}) collective-permute-start(bf16[2,512,128]{2,1,0:T(8,128)(2,1)S(1)} %get-tuple-element.92), channel_id=1, source_target_pairs={{0,1},{1,0},{2,3},{3,2},{4,5},{5,4},{6,7},{7,6},{8,9},{9,8},{10,11... | collective-permute-start | bytes 786440 | tf_op jit(solution)/shard_map/ppermute | solution.py:31
  66.5 23.9 %collective-permute-start.20 = (bf16[2,512,128]{2,1,0:T(8,128)(2,1)S(1)}, bf16[2,512,128]{2,1,0:T(8,128)(2,1)S(1)}, u32[]{:S(2)}, u32[]{:S(2)}) collective-permute-start(bf16[2,512,128]{2,1,0:T(8,128)(2,1)S(1)} %get-tuple-element.91), channel_id=1, source_target_pairs={{0,31},{1,2},{2,1},{3,4},{4,3},{5,6},{6,5},{7,8},{8,7},{9,10},{10,... | collective-permute-start | bytes 786440 | tf_op jit(solution)/shard_map/ppermute | solution.py:36
  66.7 24.5 %collective-permute-start.7 = (bf16[2,512,128]{2,1,0:T(8,128)(2,1)S(1)}, bf16[2,512,128]{2,1,0:T(8,128)(2,1)S(1)}, u32[]{:S(2)}, u32[]{:S(2)}) collective-permute-start(bf16[2,512,128]{2,1,0:T(8,128)(2,1)S(1)} %get-tuple-element.96), channel_id=1, source_target_pairs={{0,1},{1,0},{2,3},{3,2},{4,5},{5,4},{6,7},{7,6},{8,9},{9,8},{10,11... | collective-permute-start | bytes 786440 | tf_op jit(solution)/shard_map/ppermute | solution.py:31
  68.4 22.7 %collective-permute-start.8 = (bf16[2,512,128]{2,1,0:T(8,128)(2,1)S(1)}, bf16[2,512,128]{2,1,0:T(8,128)(2,1)S(1)}, u32[]{:S(2)}, u32[]{:S(2)}) collective-permute-start(bf16[2,512,128]{2,1,0:T(8,128)(2,1)S(1)} %get-tuple-element.95), channel_id=1, source_target_pairs={{0,31},{1,2},{2,1},{3,4},{4,3},{5,6},{6,5},{7,8},{8,7},{9,10},{10,... | collective-permute-start | bytes 786440 | tf_op jit(solution)/shard_map/ppermute | solution.py:36
  69.2 13.1 %collective-permute-start.23 = (bf16[512,128]{1,0:T(8,128)(2,1)S(1)}, bf16[512,128]{1,0:T(8,128)(2,1)S(1)}, u32[]{:S(2)}, u32[]{:S(2)}) collective-permute-start(bf16[512,128]{1,0:T(8,128)(2,1)S(1)} %fusion), channel_id=1, source_target_pairs={{0,32},{32,64},{64,96},{96,128},{128,160},{160,192},{192,224},{224... | collective-permute-start | bytes 393224 | tf_op jit(solution)/shard_map/ppermute | solution.py:27
  82.3 8.2 %collective-permute-start.11 = (bf16[512,128]{1,0:T(8,128)(2,1)S(1)}, bf16[512,128]{1,0:T(8,128)(2,1)S(1)}, u32[]{:S(2)}, u32[]{:S(2)}) collective-permute-start(bf16[512,128]{1,0:T(8,128)(2,1)S(1)} %fusion.2), channel_id=1, source_target_pairs={{0,32},{32,64},{64,96},{96,128},{128,160},{160,192},{192,224},{224... | collective-permute-start | bytes 393224 | tf_op jit(solution)/shard_map/ppermute | solution.py:27

commit v13 on v4

--- a/solution.py
+++ b/solution.py
@@ -127,9 +127,9 @@
     perm = perm_ref[...]
     wire_ref[...] = wire
     self_ref[...] = dot_t(cross[0][...], perm)
-    for k, ref in ((2, far_ref), (1, mate_ref)):
-        ref[0] = dot_t(cross[k][...], perm).astype(BF16)
-        ref[1] = wire
+    far_ref[...] = dot_t(cross[2][...], perm).astype(BF16)
+    mate_ref[0] = dot_t(cross[1][...], perm).astype(BF16)
+    mate_ref[1] = wire
 
 
 def first_body(sizes, blocks_hbm, row_hbm, col_hbm, drive_hbm, relax_hbm, *refs):
@@ -157,20 +157,20 @@
 def sent_terms(sent, fields, scratch, other):
     total = 0.0
     for matrix, field in zip(sent, fields):
-        interleave(field[1].astype(F32), scratch, other)
+        interleave(field.astype(F32), scratch, other)
         total += dot_t(matrix[...], other[...])
     return total
 
 
 def own_body(*refs):
-    mats, (wire_ref, perm_ref, mate_ref, far_ref), sent = refs[:3], refs[3:7], refs[7:-3]
+    mats, (wire_ref, perm_ref, mate_ref, field_ref), sent = refs[:3], refs[3:7], refs[7:-3]
     out_ref, scratch, other = refs[-3:]
-    total = dot_t(mats[0][...], perm_ref[...])
     straight = dot(mats[0][...], wire_ref[...])
     straight += dot(mats[1][...], mate_ref[1])
-    straight += dot(mats[2][...], far_ref[1])
+    straight += dot(mats[2][...], field_ref[...])
+    total = dot_t(mats[0][...], perm_ref[...])
     if sent:
-        total += sent_terms(sent, (mate_ref, far_ref), scratch, other)
+        total += sent_terms(sent, (mate_ref[1], field_ref[...]), scratch, other)
     out_ref[...] = total + restored(straight, scratch)
 
 
@@ -191,9 +191,9 @@
 
 
 def update_body(*refs):
-    cross, (known_ref, drive_ref, relax_ref, mate_in, far_in), sent = refs[:3], refs[3:8], refs[8:10]
+    cross, (known_ref, drive_ref, relax_ref, mate_in, field_in), sent = refs[:3], refs[3:8], refs[8:10]
     perm_ref, wire_ref, self_ref, mate_ref, far_ref, scratch, other = refs[10:]
-    late = sent_terms(sent, (mate_in, far_in), scratch, other)
+    late = sent_terms(sent, (mate_in[1], field_in[...]), scratch, other)
     field = advanced(known_ref[...] + late, drive_ref, relax_ref)
     interleave(field, scratch, perm_ref)
     emit(cross, field.astype(BF16), perm_ref, wire_ref, self_ref, mate_ref, far_ref)
@@ -216,7 +216,7 @@
     double = jax.ShapeDtypeStruct((2, rows, channels), BF16)
     wide = jax.ShapeDtypeStruct((rows, channels), F32)
     matrices = (jax.ShapeDtypeStruct((rows, rows), BF16),) * 3
-    emitted = (small, small, wide, double, double)
+    emitted = (small, small, wide, double, small)
     staging = pltpu.VMEM((channels // LANES, rows, LANES), F32)
     fetch = [pltpu.VMEM(blocks.shape, BF16), pltpu.VMEM((2, slots), jnp.int32)]
     row2 = row_block.reshape(1, -1)
@@ -242,19 +242,21 @@
             )
         if sweep == 0:
             from_far, _ = lax.optimization_barrier((from_far, own))
-        got = (partial + from_mate[0].astype(F32) + from_far[0].astype(F32)).astype(BF16)
+        got = (partial + from_mate[0].astype(F32) + from_far.astype(F32)).astype(BF16)
         received = shifted(got, "ka", 1)
         if sweep == 0:
             gated, down = lax.optimization_barrier((own[1:], down))
             sent = [mate(gated[0]), far(gated[1])]
         nexts = [down, mate(down), far(down)]
-        args = [*own, wire, perm, from_mate, from_far, *(sent if sweep else [])]
+        gated, _ = lax.optimization_barrier((wire, got))
+        from_other = far(gated)
+        args = [*own, wire, perm, from_mate, from_other, *(sent if sweep else [])]
         known = call(own_body, wide, 9 * work, args, scratch=extra)
         known = call(settle_body, wide, HEAVY * work, [known, received])
         if sweep + 1 == ITERS:
             return call(final_body, wide, 3 * work, [*cross, *nexts, known, drive, relax3], scratch=[staging])
         known = call(cross_body, wide, HEAVY * work, [*cross, *nexts, known], scratch=[staging])
-        args = [*cross, known, drive, relax3, from_mate, from_far, *sent]
+        args = [*cross, known, drive, relax3, from_mate, from_other, *sent]
         perm, wire, partial, to_mate, to_far = call(update_body, emitted, 8 * work, args, scratch=extra)
 
 

time: 67.8 us -> 69.2 us (1.021)
  the two profiles are of different devices: /device:TPU:24 before, /device:TPU:1 now
where the time goes in v13:
time: 69.2 us; the launch traced here: 68.1 us
  starting transfers between devices  38.8 us (56%)
  waiting for transfers between devices  15.9 us (23%)
  Pallas kernels  13.1 us (19%)
    ppermute x5, starting transfers between devices, mate(): lax.ppermute(value, 'rows', [(i, i ^ 1) for i in range(lax.axis_size('row...  24.9 us
    ppermute x7, waiting for transfers between devices, far(): lax.ppermute(value, 'rows', [(i, (i + 1 if i & 1 else i - 1) % count) for...  14 us
    pallas_call x9, Pallas kernels, call(): pl.pallas_call(kernel, out_shape=outs, in_specs=specs or [VMEM] * len(arg...  13.1 us
    ppermute x4, starting transfers between devices, shifted(): lax.ppermute(value, axis, [(source, (source + steps) % count) for source...  13 us
    ppermute x4, waiting for transfers between devices, shifted(): lax.ppermute(value, axis, [(source, (source + steps) % count) for source...  1.82 us
  transfers between devices with their start and end apart: 16, of which 6 were waited for; matrix products, arithmetic and copies ran while one was open for 0% of the time, Pallas kernels for 8%

profile of v13, /device:TPU:1, one launch (start us, length us, event | category | flops | bytes accessed | tf_op | source)
XLA Modules:
  0.0 68.1 jit_solution(4790257726958922275)
XLA Ops:
  0.0 3.7 %shard_map.55 = (bf16[512,512]{1,0:T(8,128)(2,1)S(1)}, bf16[512,512]{1,0:T(8,128)(2,1)S(1)}, bf16[512,512]{1,0:T(8,128)(2,1)S(1)}, bf16[512,256]{1,0:T(8,128)(2,...) custom-call(bf16[256,4096]{1,0:T(8,128)(2,1)} %blocks_hbm.3, ...), custom_call_target="tpu_custom_call" | custom-call | flops 1207959552 | bytes 2625536 | tf_op jit(solution)/shard_map/pallas_call | solution.py:43
  3.7 3.3 %collective-permute-start.3 = (bf16[2,512,256]{2,1,0:T(8,128)(2,1)S(1)}, bf16[2,512,256]{2,1,0:T(8,128)(2,1)S(1)}, u32[]{:S(2)}, u32[]{:S(2)}) collective-permute-start(bf16[2,512,256]{2,1,0:T(8,128)(2,1)S(1)} %get-tuple-element.37), channel_id=1, source_target_pairs={{0,1},{1,0},{2,3},{3,2},{4,5},{5,4},{6,7},{7,6},{8,9},{9,8},{10,11... | collective-permute-start | bytes 1572872 | tf_op jit(solution)/shard_map/ppermute | solution.py:31
  7.1 0.0 collective-permute-start.4
  7.1 5.1 %collective-permute-start = (bf16[512,256]{1,0:T(8,128)(2,1)S(1)}, bf16[512,256]{1,0:T(8,128)(2,1)S(1)}, u32[]{:S(2)}, u32[]{:S(2)}) collective-permute-start(bf16[512,256]{1,0:T(8,128)(2,1)S(1)} %get-tuple-element.41.refs_3_), channel_id=1, source_target_pairs={{0,224},{32,0},{64,32},{96,64},{128,96},{160,128},{192,160},{224,1... | collective-permute-start | bytes 786440 | tf_op jit(solution)/shard_map/ppermute | solution.py:27
  12.1 2.5 %shard_map.56 = (bf16[512,512]{1,0:T(8,128)(2,1)S(1)}, bf16[512,512]{1,0:T(8,128)(2,1)S(1)}, bf16[512,512]{1,0:T(8,128)(2,1)S(1)}) custom-call(bf16[256,4096]{1,0:T(8,128)(2,1)} %blocks_hbm.3, s32[1,256]{1,0:T(1,128)} %bitcast.15, s32[1,256]{1,0:T(1,128)} %bitcast.17), custom_call_target="tpu_custom_call" | custom-call | flops 805306368 | bytes 2099200 | tf_op jit(solution)/shard_map/pallas_call | solution.py:43
  14.7 0.0 collective-permute-done.4
  14.7 0.1 fusion.3
  14.8 0.5 collective-permute-start.5
  15.3 0.4 collective-permute-start.6
  15.7 1.1 %collective-permute-done.refs_3_ = bf16[512,256]{1,0:T(8,128)(2,1)S(1)} collective-permute-done((bf16[512,256]{1,0:T(8,128)(2,1)S(1)}, bf16[512,256]{1,0:T(8,128)(2,1)S(1)}, u32[]{:S(2)}, u32[]{:S(2)}) %collective-permute-start) | collective-permute-done | bytes 262176 | tf_op jit(solution)/shard_map/ppermute | solution.py:27
  16.7 6.4 %collective-permute-start.1 = (bf16[512,256]{1,0:T(8,128)(2,1)S(1)}, bf16[512,256]{1,0:T(8,128)(2,1)S(1)}, u32[]{:S(2)}, u32[]{:S(2)}) collective-permute-start(bf16[512,256]{1,0:T(8,128)(2,1)S(1)} %collective-permute-done.refs_3_), channel_id=1, source_target_pairs={{0,1},{1,0},{2,3},{3,2},{4,5},{5,4},{6,7},{7,6},{8,9},{9,8},{10,11... | collective-permute-start | bytes 786440 | tf_op jit(solution)/shard_map/ppermute | solution.py:31
  23.1 2.1 %collective-permute-start.7 = (bf16[512,512]{1,0:T(8,128)(2,1)S(1)}, bf16[512,512]{1,0:T(8,128)(2,1)S(1)}, u32[]{:S(2)}, u32[]{:S(2)}) collective-permute-start(bf16[512,512]{1,0:T(8,128)(2,1)S(1)} %get-tuple-element.43.refs_1_), channel_id=1, source_target_pairs={{0,1},{1,0},{2,3},{3,2},{4,5},{5,4},{6,7},{7,6},{8,9},{9,8},{10,11... | collective-permute-start | bytes 1572872 | tf_op jit(solution)/shard_map/ppermute | solution.py:31
  25.3 0.0 collective-permute-done.5.refs_6_.refs_7_
  25.3 0.8 %shard_map.57.own_ref = f32[512,256]{1,0:T(8,128)S(1)} custom-call(bf16[512,512]{1,0:T(8,128)(2,1)S(1)} %get-tuple-element.35.refs_0_, bf16[512,512]{1,0:T(8,128)(2,1)S(1)} %get-tuple-element.43.refs_1_, bf16[512,512]{1,0:T(8,128)(2,1)S(1)} %get-tuple-element.44.refs_2_, bf16[512,256]{1,0:T(8,128)(2,1)S(1)} %get-tuple-element.41.refs_3_, ...), custom_call_target="tpu_custom_call" | custom-call | flops 1207959552 | bytes 2883584 | tf_op jit(solution)/shard_map/pallas_call | solution.py:43
  26.1 0.0 collective-permute-done.1.refs_4_
  26.1 3.1 %collective-permute-done.2.refs_5_ = bf16[512,256]{1,0:T(8,128)(2,1)S(1)} collective-permute-done((bf16[512,256]{1,0:T(8,128)(2,1)S(1)}, bf16[512,256]{1,0:T(8,128)(2,1)S(1)}, u32[]{:S(2)}, u32[]{:S(2)}) %collective-permute-start.2) | collective-permute-done | bytes 262176 | tf_op jit(solution)/shard_map/ppermute | solution.py:36
  29.2 0.6 shard_map.59.refs_3_
  29.9 5.0 %collective-permute-done.8.refs_9_.refs_8_ = bf16[512,512]{1,0:T(8,128)(2,1)S(1)} collective-permute-done((bf16[512,512]{1,0:T(8,128)(2,1)S(1)}, bf16[512,512]{1,0:T(8,128)(2,1)S(1)}, u32[]{:S(2)}, u32[]{:S(2)}) %collective-permute-start.8) | collective-permute-done | bytes 524320 | tf_op jit(solution)/shard_map/ppermute | solution.py:36
  34.8 2.2 %shard_map.60 = (bf16[512,256]{1,0:T(8,128)(2,1)S(1)}, bf16[512,256]{1,0:T(8,128)(2,1)S(1)}, f32[512,256]{1,0:T(8,128)S(1)}, bf16[2,512,256]{2,1,0:T(8,128)(2,1)S(1)}, bf16[512,256]{1,0:T(8,128)(2,1)S(1)}) custom-call(bf16[512,512]{1,0:T(8,128)(2,1)S(1)} %get-tuple-element.28.refs_0_, bf16[512,512]{1,0:T(8,128)(2,1)S(1)} %get-tuple-element.29.refs_1_, ...), custom_call_target="tpu_custom_call" | custom-call | flops 1073741824 | bytes 4718592 | tf_op jit(solution)/shard_map/pallas_call | solution.py:43
  37.0 4.4 %collective-permute-start.12 = (bf16[2,512,256]{2,1,0:T(8,128)(2,1)S(1)}, bf16[2,512,256]{2,1,0:T(8,128)(2,1)S(1)}, u32[]{:S(2)}, u32[]{:S(2)}) collective-permute-start(bf16[2,512,256]{2,1,0:T(8,128)(2,1)S(1)} %get-tuple-element.47), channel_id=1, source_target_pairs={{0,1},{1,0},{2,3},{3,2},{4,5},{5,4},{6,7},{7,6},{8,9},{9,8},{10,11... | collective-permute-start | bytes 1572872 | tf_op jit(solution)/shard_map/ppermute | solution.py:31
  41.4 0.0 collective-permute-start.13
  41.4 4.4 %collective-permute-start.9 = (bf16[512,256]{1,0:T(8,128)(2,1)S(1)}, bf16[512,256]{1,0:T(8,128)(2,1)S(1)}, u32[]{:S(2)}, u32[]{:S(2)}) collective-permute-start(bf16[512,256]{1,0:T(8,128)(2,1)S(1)} %get-tuple-element.50.refs_3_), channel_id=1, source_target_pairs={{0,224},{32,0},{64,32},{96,64},{128,96},{160,128},{192,160},{224,1... | collective-permute-start | bytes 786440 | tf_op jit(solution)/shard_map/ppermute | solution.py:27
  45.8 1.7 %collective-permute-done.13 = bf16[512,256]{1,0:T(8,128)(2,1)S(1)} collective-permute-done((bf16[512,256]{1,0:T(8,128)(2,1)S(1)}, bf16[512,256]{1,0:T(8,128)(2,1)S(1)}, u32[]{:S(2)}, u32[]{:S(2)}) %collective-permute-start.13) | collective-permute-done | bytes 262176 | tf_op jit(solution)/shard_map/ppermute | solution.py:36
  47.5 0.0 collective-permute-done.12.refs_5_
  47.5 0.1 fusion.1
  47.6 0.4 collective-permute-start.14
  48.0 3.2 %collective-permute-start.15 = (bf16[512,256]{1,0:T(8,128)(2,1)S(1)}, bf16[512,256]{1,0:T(8,128)(2,1)S(1)}, u32[]{:S(2)}, u32[]{:S(2)}) collective-permute-start(bf16[512,256]{1,0:T(8,128)(2,1)S(1)} %fusion.1), channel_id=1, source_target_pairs={{0,32},{32,64},{64,96},{96,128},{128,160},{160,192},{192,224},{224... | collective-permute-start | bytes 786440 | tf_op jit(solution)/shard_map/ppermute | solution.py:27
  51.2 0.7 %collective-permute-done.9.refs_3_ = bf16[512,256]{1,0:T(8,128)(2,1)S(1)} collective-permute-done((bf16[512,256]{1,0:T(8,128)(2,1)S(1)}, bf16[512,256]{1,0:T(8,128)(2,1)S(1)}, u32[]{:S(2)}, u32[]{:S(2)}) %collective-permute-start.9) | collective-permute-done | bytes 262176 | tf_op jit(solution)/shard_map/ppermute | solution.py:27
  51.9 8.7 %collective-permute-start.10 = (bf16[512,256]{1,0:T(8,128)(2,1)S(1)}, bf16[512,256]{1,0:T(8,128)(2,1)S(1)}, u32[]{:S(2)}, u32[]{:S(2)}) collective-permute-start(bf16[512,256]{1,0:T(8,128)(2,1)S(1)} %collective-permute-done.9.refs_3_), channel_id=1, source_target_pairs={{0,1},{1,0},{2,3},{3,2},{4,5},{5,4},{6,7},{7,6},{8,9},{9,8},{10,11... | collective-permute-start | bytes 786440 | tf_op jit(solution)/shard_map/ppermute | solution.py:31
  60.6 1.8 %shard_map.61.own_ref = f32[512,256]{1,0:T(8,128)S(1)} custom-call(bf16[512,512]{1,0:T(8,128)(2,1)S(1)} %get-tuple-element.35.refs_0_, bf16[512,512]{1,0:T(8,128)(2,1)S(1)} %get-tuple-element.43.refs_1_, bf16[512,512]{1,0:T(8,128)(2,1)S(1)} %get-tuple-element.44.refs_2_, bf16[512,256]{1,0:T(8,128)(2,1)S(1)} %get-tuple-element.50.refs_3_, ...), custom_call_target="tpu_custom_call" | custom-call | flops 1207959552 | bytes 3932160 | tf_op jit(solution)/shard_map/pallas_call | solution.py:43
  62.5 4.2 %collective-permute-done.11.refs_5_ = bf16[512,256]{1,0:T(8,128)(2,1)S(1)} collective-permute-done((bf16[512,256]{1,0:T(8,128)(2,1)S(1)}, bf16[512,256]{1,0:T(8,128)(2,1)S(1)}, u32[]{:S(2)}, u32[]{:S(2)}) %collective-permute-start.11) | collective-permute-done | bytes 262176 | tf_op jit(solution)/shard_map/ppermute | solution.py:36
  66.7 1.4 %shard_map.63 = f32[512,256]{1,0:T(8,128)} custom-call(bf16[512,512]{1,0:T(8,128)(2,1)S(1)} %get-tuple-element.28.refs_0_, bf16[512,512]{1,0:T(8,128)(2,1)S(1)} %get-tuple-element.29.refs_1_, bf16[512,512]{1,0:T(8,128)(2,1)S(1)} %get-tuple-element.30.refs_2_, bf16[512,256]{1,0:T(8,128)(2,1)S(1)} %collective-permute-done.9.refs_3_, ...), custom_call_target="tpu_custom_call" | custom-call | flops 402653184 | bytes 3670016 | tf_op jit(solution)/shard_map/pallas_call | solution.py:43
  (13 shorter events, 0.1 us)
Async XLA Ops:
  3.7 11.0 %collective-permute-start.3 = (bf16[2,512,256]{2,1,0:T(8,128)(2,1)S(1)}, bf16[2,512,256]{2,1,0:T(8,128)(2,1)S(1)}, u32[]{:S(2)}, u32[]{:S(2)}) collective-permute-start(bf16[2,512,256]{2,1,0:T(8,128)(2,1)S(1)} %get-tuple-element.37), channel_id=1, source_target_pairs={{0,1},{1,0},{2,3},{3,2},{4,5},{5,4},{6,7},{7,6},{8,9},{9,8},{10,11... | collective-permute-start | bytes 1572872 | tf_op jit(solution)/shard_map/ppermute | solution.py:31
  7.1 7.6 %collective-permute-start.4 = (bf16[512,256]{1,0:T(8,128)(2,1)S(1)}, bf16[512,256]{1,0:T(8,128)(2,1)S(1)}, u32[]{:S(2)}, u32[]{:S(2)}) collective-permute-start(bf16[512,256]{1,0:T(8,128)(2,1)S(1)} %get-tuple-element.39), channel_id=1, source_target_pairs={{0,31},{1,2},{2,1},{3,4},{4,3},{5,6},{6,5},{7,8},{8,7},{9,10},{10,... | collective-permute-start | bytes 786440 | tf_op jit(solution)/shard_map/ppermute | solution.py:36
  7.1 9.7 %collective-permute-start = (bf16[512,256]{1,0:T(8,128)(2,1)S(1)}, bf16[512,256]{1,0:T(8,128)(2,1)S(1)}, u32[]{:S(2)}, u32[]{:S(2)}) collective-permute-start(bf16[512,256]{1,0:T(8,128)(2,1)S(1)} %get-tuple-element.41.refs_3_), channel_id=1, source_target_pairs={{0,224},{32,0},{64,32},{96,64},{128,96},{160,128},{192,160},{224,1... | collective-permute-start | bytes 786440 | tf_op jit(solution)/shard_map/ppermute | solution.py:27
  14.8 10.5 %collective-permute-start.5 = (bf16[512,256]{1,0:T(8,128)(2,1)S(1)}, bf16[512,256]{1,0:T(8,128)(2,1)S(1)}, u32[]{:S(2)}, u32[]{:S(2)}) collective-permute-start(bf16[512,256]{1,0:T(8,128)(2,1)S(1)} %get-tuple-element.41.refs_3_), channel_id=1, source_target_pairs={{0,31},{1,2},{2,1},{3,4},{4,3},{5,6},{6,5},{7,8},{8,7},{9,10},{10,... | collective-permute-start | bytes 786440 | tf_op jit(solution)/shard_map/ppermute | solution.py:36
  15.3 10.8 %collective-permute-start.6 = (bf16[512,256]{1,0:T(8,128)(2,1)S(1)}, bf16[512,256]{1,0:T(8,128)(2,1)S(1)}, u32[]{:S(2)}, u32[]{:S(2)}) collective-permute-start(bf16[512,256]{1,0:T(8,128)(2,1)S(1)} %fusion.3), channel_id=1, source_target_pairs={{0,32},{32,64},{64,96},{96,128},{128,160},{160,192},{192,224},{224... | collective-permute-start | bytes 786440 | tf_op jit(solution)/shard_map/ppermute | solution.py:27
  16.7 9.3 %collective-permute-start.1 = (bf16[512,256]{1,0:T(8,128)(2,1)S(1)}, bf16[512,256]{1,0:T(8,128)(2,1)S(1)}, u32[]{:S(2)}, u32[]{:S(2)}) collective-permute-start(bf16[512,256]{1,0:T(8,128)(2,1)S(1)} %collective-permute-done.refs_3_), channel_id=1, source_target_pairs={{0,1},{1,0},{2,3},{3,2},{4,5},{5,4},{6,7},{7,6},{8,9},{9,8},{10,11... | collective-permute-start | bytes 786440 | tf_op jit(solution)/shard_map/ppermute | solution.py:31
  23.1 6.1 %collective-permute-start.2 = (bf16[512,256]{1,0:T(8,128)(2,1)S(1)}, bf16[512,256]{1,0:T(8,128)(2,1)S(1)}, u32[]{:S(2)}, u32[]{:S(2)}) collective-permute-start(bf16[512,256]{1,0:T(8,128)(2,1)S(1)} %collective-permute-done.refs_3_), channel_id=1, source_target_pairs={{0,31},{1,2},{2,1},{3,4},{4,3},{5,6},{6,5},{7,8},{8,7},{9,10},{10,... | collective-permute-start | bytes 786440 | tf_op jit(solution)/shard_map/ppermute | solution.py:36
  23.1 6.7 %collective-permute-start.7 = (bf16[512,512]{1,0:T(8,128)(2,1)S(1)}, bf16[512,512]{1,0:T(8,128)(2,1)S(1)}, u32[]{:S(2)}, u32[]{:S(2)}) collective-permute-start(bf16[512,512]{1,0:T(8,128)(2,1)S(1)} %get-tuple-element.43.refs_1_), channel_id=1, source_target_pairs={{0,1},{1,0},{2,3},{3,2},{4,5},{5,4},{6,7},{7,6},{8,9},{9,8},{10,11... | collective-permute-start | bytes 1572872 | tf_op jit(solution)/shard_map/ppermute | solution.py:31
  25.3 9.6 %collective-permute-start.8 = (bf16[512,512]{1,0:T(8,128)(2,1)S(1)}, bf16[512,512]{1,0:T(8,128)(2,1)S(1)}, u32[]{:S(2)}, u32[]{:S(2)}) collective-permute-start(bf16[512,512]{1,0:T(8,128)(2,1)S(1)} %get-tuple-element.44.refs_2_), channel_id=1, source_target_pairs={{0,31},{1,2},{2,1},{3,4},{4,3},{5,6},{6,5},{7,8},{8,7},{9,10},{10,... | collective-permute-start | bytes 1572872 | tf_op jit(solution)/shard_map/ppermute | solution.py:36
  29.2 5.6 %copy-start = (f32[512,256]{1,0:T(8,128)S(1)}, f32[512,256]{1,0:T(8,128)}, u32[]{:S(2)}) copy-start(f32[512,256]{1,0:T(8,128)} %refs_7_.1) | copy-start | bytes 1572868
  37.0 10.5 %collective-permute-start.12 = (bf16[2,512,256]{2,1,0:T(8,128)(2,1)S(1)}, bf16[2,512,256]{2,1,0:T(8,128)(2,1)S(1)}, u32[]{:S(2)}, u32[]{:S(2)}) collective-permute-start(bf16[2,512,256]{2,1,0:T(8,128)(2,1)S(1)} %get-tuple-element.47), channel_id=1, source_target_pairs={{0,1},{1,0},{2,3},{3,2},{4,5},{5,4},{6,7},{7,6},{8,9},{9,8},{10,11... | collective-permute-start | bytes 1572872 | tf_op jit(solution)/shard_map/ppermute | solution.py:31
  41.4 6.1 %collective-permute-start.13 = (bf16[512,256]{1,0:T(8,128)(2,1)S(1)}, bf16[512,256]{1,0:T(8,128)(2,1)S(1)}, u32[]{:S(2)}, u32[]{:S(2)}) collective-permute-start(bf16[512,256]{1,0:T(8,128)(2,1)S(1)} %get-tuple-element.49), channel_id=1, source_target_pairs={{0,31},{1,2},{2,1},{3,4},{4,3},{5,6},{6,5},{7,8},{8,7},{9,10},{10,... | collective-permute-start | bytes 786440 | tf_op jit(solution)/shard_map/ppermute | solution.py:36
  41.4 10.5 %collective-permute-start.9 = (bf16[512,256]{1,0:T(8,128)(2,1)S(1)}, bf16[512,256]{1,0:T(8,128)(2,1)S(1)}, u32[]{:S(2)}, u32[]{:S(2)}) collective-permute-start(bf16[512,256]{1,0:T(8,128)(2,1)S(1)} %get-tuple-element.50.refs_3_), channel_id=1, source_target_pairs={{0,224},{32,0},{64,32},{96,64},{128,96},{160,128},{192,160},{224,1... | collective-permute-start | bytes 786440 | tf_op jit(solution)/shard_map/ppermute | solution.py:27
  47.6 13.0 %collective-permute-start.14 = (bf16[512,256]{1,0:T(8,128)(2,1)S(1)}, bf16[512,256]{1,0:T(8,128)(2,1)S(1)}, u32[]{:S(2)}, u32[]{:S(2)}) collective-permute-start(bf16[512,256]{1,0:T(8,128)(2,1)S(1)} %get-tuple-element.50.refs_3_), channel_id=1, source_target_pairs={{0,31},{1,2},{2,1},{3,4},{4,3},{5,6},{6,5},{7,8},{8,7},{9,10},{10,... | collective-permute-start | bytes 786440 | tf_op jit(solution)/shard_map/ppermute | solution.py:36
  48.0 14.5 %collective-permute-start.15 = (bf16[512,256]{1,0:T(8,128)(2,1)S(1)}, bf16[512,256]{1,0:T(8,128)(2,1)S(1)}, u32[]{:S(2)}, u32[]{:S(2)}) collective-permute-start(bf16[512,256]{1,0:T(8,128)(2,1)S(1)} %fusion.1), channel_id=1, source_target_pairs={{0,32},{32,64},{64,96},{96,128},{128,160},{160,192},{192,224},{224... | collective-permute-start | bytes 786440 | tf_op jit(solution)/shard_map/ppermute | solution.py:27
  51.9 10.6 %collective-permute-start.10 = (bf16[512,256]{1,0:T(8,128)(2,1)S(1)}, bf16[512,256]{1,0:T(8,128)(2,1)S(1)}, u32[]{:S(2)}, u32[]{:S(2)}) collective-permute-start(bf16[512,256]{1,0:T(8,128)(2,1)S(1)} %collective-permute-done.9.refs_3_), channel_id=1, source_target_pairs={{0,1},{1,0},{2,3},{3,2},{4,5},{5,4},{6,7},{7,6},{8,9},{9,8},{10,11... | collective-permute-start | bytes 786440 | tf_op jit(solution)/shard_map/ppermute | solution.py:31
  60.6 6.1 %collective-permute-start.11 = (bf16[512,256]{1,0:T(8,128)(2,1)S(1)}, bf16[512,256]{1,0:T(8,128)(2,1)S(1)}, u32[]{:S(2)}, u32[]{:S(2)}) collective-permute-start(bf16[512,256]{1,0:T(8,128)(2,1)S(1)} %collective-permute-done.9.refs_3_), channel_id=1, source_target_pairs={{0,31},{1,2},{2,1},{3,4},{4,3},{5,6},{6,5},{7,8},{8,7},{9,10},{10,... | collective-permute-start | bytes 786440 | tf_op jit(solution)/shard_map/ppermute | solution.py:36

commit v14 on v13

--- a/solution.py
+++ b/solution.py
@@ -248,8 +248,7 @@
             gated, down = lax.optimization_barrier((own[1:], down))
             sent = [mate(gated[0]), far(gated[1])]
         nexts = [down, mate(down), far(down)]
-        gated, _ = lax.optimization_barrier((wire, got))
-        from_other = far(gated)
+        from_other = far(wire)
         args = [*own, wire, perm, from_mate, from_other, *(sent if sweep else [])]
         known = call(own_body, wide, 9 * work, args, scratch=extra)
         known = call(settle_body, wide, HEAVY * work, [known, received])

time: 69.2 us -> 70.3 us (1.016)
  waiting for transfers between devices: 15.9 us -> 27.8 us
  starting transfers between devices: 38.8 us -> 28 us
    ppermute x4, waiting for transfers between devices: 1.82 us -> 19.8 us  [shifted(): lax.ppermute(value, axis, [(source, (source + steps) % count) for source...]
    ppermute x5, starting transfers between devices: 24.9 us -> 14.6 us  [mate(): lax.ppermute(value, 'rows', [(i, i ^ 1) for i in range(lax.axis_size('row...]
    ppermute x7, waiting for transfers between devices: 14 us -> 7.95 us  [far(): lax.ppermute(value, 'rows', [(i, (i + 1 if i & 1 else i - 1) % count) for...]
    ppermute x4, starting transfers between devices: 13 us -> 9.91 us  [shifted(): lax.ppermute(value, axis, [(source, (source + steps) % count) for source...]
    ppermute x7, starting transfers between devices: 0.91 us -> 3.5 us  [far(): lax.ppermute(value, 'rows', [(i, (i + 1 if i & 1 else i - 1) % count) for...]
where the time goes in v14:
time: 70.3 us; the launch traced here: 69.2 us
  starting transfers between devices  28 us (40%)
  waiting for transfers between devices  27.8 us (40%)
  Pallas kernels  13.1 us (19%)
    ppermute x4, waiting for transfers between devices, shifted(): lax.ppermute(value, axis, [(source, (source + steps) % count) for source...  19.8 us
    ppermute x5, starting transfers between devices, mate(): lax.ppermute(value, 'rows', [(i, i ^ 1) for i in range(lax.axis_size('row...  14.6 us
    pallas_call x9, Pallas kernels, call(): pl.pallas_call(kernel, out_shape=outs, in_specs=specs or [VMEM] * len(arg...  13.1 us
    ppermute x4, starting transfers between devices, shifted(): lax.ppermute(value, axis, [(source, (source + steps) % count) for source...  9.91 us
    ppermute x7, waiting for transfers between devices, far(): lax.ppermute(value, 'rows', [(i, (i + 1 if i & 1 else i - 1) % count) for...  7.95 us
    ppermute x7, starting transfers between devices, far(): lax.ppermute(value, 'rows', [(i, (i + 1 if i & 1 else i - 1) % count) for...  3.5 us
  transfers between devices with their start and end apart: 16, of which 6 were waited for; matrix products, arithmetic and copies ran while one was open for 0% of the time, Pallas kernels for 8%

profile of v14, /device:TPU:1, one launch (start us, length us, event | category | flops | bytes accessed | tf_op | source)
XLA Modules:
  0.0 69.2 jit_solution(15645256180924500292)
XLA Ops:
  0.0 3.7 %shard_map.55 = (bf16[512,512]{1,0:T(8,128)(2,1)S(1)}, bf16[512,512]{1,0:T(8,128)(2,1)S(1)}, bf16[512,512]{1,0:T(8,128)(2,1)S(1)}, bf16[512,256]{1,0:T(8,128)(2,...) custom-call(bf16[256,4096]{1,0:T(8,128)(2,1)} %blocks_hbm.3, ...), custom_call_target="tpu_custom_call" | custom-call | flops 1207959552 | bytes 2625536 | tf_op jit(solution)/shard_map/pallas_call | solution.py:43
  3.7 3.3 %collective-permute-start.3 = (bf16[2,512,256]{2,1,0:T(8,128)(2,1)S(1)}, bf16[2,512,256]{2,1,0:T(8,128)(2,1)S(1)}, u32[]{:S(2)}, u32[]{:S(2)}) collective-permute-start(bf16[2,512,256]{2,1,0:T(8,128)(2,1)S(1)} %get-tuple-element.35), channel_id=1, source_target_pairs={{0,1},{1,0},{2,3},{3,2},{4,5},{5,4},{6,7},{7,6},{8,9},{9,8},{10,11... | collective-permute-start | bytes 1572872 | tf_op jit(solution)/shard_map/ppermute | solution.py:31
  7.1 0.0 collective-permute-start.5
  7.1 1.7 %collective-permute-start.4 = (bf16[512,256]{1,0:T(8,128)(2,1)S(1)}, bf16[512,256]{1,0:T(8,128)(2,1)S(1)}, u32[]{:S(2)}, u32[]{:S(2)}) collective-permute-start(bf16[512,256]{1,0:T(8,128)(2,1)S(1)} %get-tuple-element.31.refs_3_), channel_id=1, source_target_pairs={{0,31},{1,2},{2,1},{3,4},{4,3},{5,6},{6,5},{7,8},{8,7},{9,10},{10,... | collective-permute-start | bytes 786440 | tf_op jit(solution)/shard_map/ppermute | solution.py:36
  8.8 3.5 %collective-permute-start = (bf16[512,256]{1,0:T(8,128)(2,1)S(1)}, bf16[512,256]{1,0:T(8,128)(2,1)S(1)}, u32[]{:S(2)}, u32[]{:S(2)}) collective-permute-start(bf16[512,256]{1,0:T(8,128)(2,1)S(1)} %get-tuple-element.31.refs_3_), channel_id=1, source_target_pairs={{0,224},{32,0},{64,32},{96,64},{128,96},{160,128},{192,160},{224,1... | collective-permute-start | bytes 786440 | tf_op jit(solution)/shard_map/ppermute | solution.py:27
  12.3 2.5 %shard_map.56 = (bf16[512,512]{1,0:T(8,128)(2,1)S(1)}, bf16[512,512]{1,0:T(8,128)(2,1)S(1)}, bf16[512,512]{1,0:T(8,128)(2,1)S(1)}) custom-call(bf16[256,4096]{1,0:T(8,128)(2,1)} %blocks_hbm.3, s32[1,256]{1,0:T(1,128)} %bitcast.15, s32[1,256]{1,0:T(1,128)} %bitcast.17), custom_call_target="tpu_custom_call" | custom-call | flops 805306368 | bytes 2099200 | tf_op jit(solution)/shard_map/pallas_call | solution.py:43
  14.8 0.0 collective-permute-done.5
  14.8 0.0 collective-permute-done.3.refs_5_.refs_6_
  14.8 0.1 fusion.3
  14.9 0.1 collective-permute-start.6
  15.0 7.5 %collective-permute-done.refs_3_ = bf16[512,256]{1,0:T(8,128)(2,1)S(1)} collective-permute-done((bf16[512,256]{1,0:T(8,128)(2,1)S(1)}, bf16[512,256]{1,0:T(8,128)(2,1)S(1)}, u32[]{:S(2)}, u32[]{:S(2)}) %collective-permute-start) | collective-permute-done | bytes 262176 | tf_op jit(solution)/shard_map/ppermute | solution.py:27
  22.5 3.9 %collective-permute-start.1 = (bf16[512,256]{1,0:T(8,128)(2,1)S(1)}, bf16[512,256]{1,0:T(8,128)(2,1)S(1)}, u32[]{:S(2)}, u32[]{:S(2)}) collective-permute-start(bf16[512,256]{1,0:T(8,128)(2,1)S(1)} %collective-permute-done.refs_3_), channel_id=1, source_target_pairs={{0,1},{1,0},{2,3},{3,2},{4,5},{5,4},{6,7},{7,6},{8,9},{9,8},{10,11... | collective-permute-start | bytes 786440 | tf_op jit(solution)/shard_map/ppermute | solution.py:31
  26.4 0.0 collective-permute-start.2
  26.4 3.7 %collective-permute-start.7 = (bf16[512,512]{1,0:T(8,128)(2,1)S(1)}, bf16[512,512]{1,0:T(8,128)(2,1)S(1)}, u32[]{:S(2)}, u32[]{:S(2)}) collective-permute-start(bf16[512,512]{1,0:T(8,128)(2,1)S(1)} %get-tuple-element.40.refs_1_), channel_id=1, source_target_pairs={{0,1},{1,0},{2,3},{3,2},{4,5},{5,4},{6,7},{7,6},{8,9},{9,8},{10,11... | collective-permute-start | bytes 1572872 | tf_op jit(solution)/shard_map/ppermute | solution.py:31
  30.1 0.0 collective-permute-start.8
  30.1 0.8 %shard_map.57.own_ref = f32[512,256]{1,0:T(8,128)S(1)} custom-call(bf16[512,512]{1,0:T(8,128)(2,1)S(1)} %get-tuple-element.33.refs_0_, bf16[512,512]{1,0:T(8,128)(2,1)S(1)} %get-tuple-element.40.refs_1_, bf16[512,512]{1,0:T(8,128)(2,1)S(1)} %get-tuple-element.41.refs_2_, bf16[512,256]{1,0:T(8,128)(2,1)S(1)} %get-tuple-element.31.refs_3_, ...), custom_call_target="tpu_custom_call" | custom-call | flops 1207959552 | bytes 2883584 | tf_op jit(solution)/shard_map/pallas_call | solution.py:43
  30.8 0.0 collective-permute-done.6.received_ref
  30.9 1.6 %collective-permute-done.2.refs_5_ = bf16[512,256]{1,0:T(8,128)(2,1)S(1)} collective-permute-done((bf16[512,256]{1,0:T(8,128)(2,1)S(1)}, bf16[512,256]{1,0:T(8,128)(2,1)S(1)}, u32[]{:S(2)}, u32[]{:S(2)}) %collective-permute-start.2) | collective-permute-done | bytes 262176 | tf_op jit(solution)/shard_map/ppermute | solution.py:36
  32.5 0.6 shard_map.59.refs_3_
  33.1 5.9 %collective-permute-done.8.refs_9_.refs_8_ = bf16[512,512]{1,0:T(8,128)(2,1)S(1)} collective-permute-done((bf16[512,512]{1,0:T(8,128)(2,1)S(1)}, bf16[512,512]{1,0:T(8,128)(2,1)S(1)}, u32[]{:S(2)}, u32[]{:S(2)}) %collective-permute-start.8) | collective-permute-done | bytes 524320 | tf_op jit(solution)/shard_map/ppermute | solution.py:36
  39.0 2.2 %shard_map.60 = (bf16[512,256]{1,0:T(8,128)(2,1)S(1)}, bf16[512,256]{1,0:T(8,128)(2,1)S(1)}, f32[512,256]{1,0:T(8,128)S(1)}, bf16[2,512,256]{2,1,0:T(8,128)(2,1)S(1)}, bf16[512,256]{1,0:T(8,128)(2,1)S(1)}) custom-call(bf16[512,512]{1,0:T(8,128)(2,1)S(1)} %get-tuple-element.26.refs_0_, bf16[512,512]{1,0:T(8,128)(2,1)S(1)} %get-tuple-element.27.refs_1_, ...), custom_call_target="tpu_custom_call" | custom-call | flops 1073741824 | bytes 4718592 | tf_op jit(solution)/shard_map/pallas_call | solution.py:43
  41.2 2.1 %collective-permute-start.12 = (bf16[2,512,256]{2,1,0:T(8,128)(2,1)S(1)}, bf16[2,512,256]{2,1,0:T(8,128)(2,1)S(1)}, u32[]{:S(2)}, u32[]{:S(2)}) collective-permute-start(bf16[2,512,256]{2,1,0:T(8,128)(2,1)S(1)} %get-tuple-element.44), channel_id=1, source_target_pairs={{0,1},{1,0},{2,3},{3,2},{4,5},{5,4},{6,7},{7,6},{8,9},{9,8},{10,11... | collective-permute-start | bytes 1572872 | tf_op jit(solution)/shard_map/ppermute | solution.py:31
  43.2 1.7 %collective-permute-start.13 = (bf16[512,256]{1,0:T(8,128)(2,1)S(1)}, bf16[512,256]{1,0:T(8,128)(2,1)S(1)}, u32[]{:S(2)}, u32[]{:S(2)}) collective-permute-start(bf16[512,256]{1,0:T(8,128)(2,1)S(1)} %get-tuple-element.42.refs_3_), channel_id=1, source_target_pairs={{0,31},{1,2},{2,1},{3,4},{4,3},{5,6},{6,5},{7,8},{8,7},{9,10},{10,... | collective-permute-start | bytes 786440 | tf_op jit(solution)/shard_map/ppermute | solution.py:36
  45.0 3.5 %collective-permute-start.9 = (bf16[512,256]{1,0:T(8,128)(2,1)S(1)}, bf16[512,256]{1,0:T(8,128)(2,1)S(1)}, u32[]{:S(2)}, u32[]{:S(2)}) collective-permute-start(bf16[512,256]{1,0:T(8,128)(2,1)S(1)} %get-tuple-element.42.refs_3_), channel_id=1, source_target_pairs={{0,224},{32,0},{64,32},{96,64},{128,96},{160,128},{192,160},{224,1... | collective-permute-start | bytes 786440 | tf_op jit(solution)/shard_map/ppermute | solution.py:27
  48.5 0.5 collective-permute-done.14
  49.0 0.1 fusion.1
  49.1 2.8 %collective-permute-start.15 = (bf16[512,256]{1,0:T(8,128)(2,1)S(1)}, bf16[512,256]{1,0:T(8,128)(2,1)S(1)}, u32[]{:S(2)}, u32[]{:S(2)}) collective-permute-start(bf16[512,256]{1,0:T(8,128)(2,1)S(1)} %fusion.1), channel_id=1, source_target_pairs={{0,32},{32,64},{64,96},{96,128},{128,160},{160,192},{192,224},{224... | collective-permute-start | bytes 786440 | tf_op jit(solution)/shard_map/ppermute | solution.py:27
  52.0 7.9 %collective-permute-done.9.refs_3_ = bf16[512,256]{1,0:T(8,128)(2,1)S(1)} collective-permute-done((bf16[512,256]{1,0:T(8,128)(2,1)S(1)}, bf16[512,256]{1,0:T(8,128)(2,1)S(1)}, u32[]{:S(2)}, u32[]{:S(2)}) %collective-permute-start.9) | collective-permute-done | bytes 262176 | tf_op jit(solution)/shard_map/ppermute | solution.py:27
  59.8 1.6 %collective-permute-start.10 = (bf16[512,256]{1,0:T(8,128)(2,1)S(1)}, bf16[512,256]{1,0:T(8,128)(2,1)S(1)}, u32[]{:S(2)}, u32[]{:S(2)}) collective-permute-start(bf16[512,256]{1,0:T(8,128)(2,1)S(1)} %collective-permute-done.9.refs_3_), channel_id=1, source_target_pairs={{0,1},{1,0},{2,3},{3,2},{4,5},{5,4},{6,7},{7,6},{8,9},{9,8},{10,11... | collective-permute-start | bytes 786440 | tf_op jit(solution)/shard_map/ppermute | solution.py:31
  61.4 1.8 %shard_map.61.own_ref = f32[512,256]{1,0:T(8,128)S(1)} custom-call(bf16[512,512]{1,0:T(8,128)(2,1)S(1)} %get-tuple-element.33.refs_0_, bf16[512,512]{1,0:T(8,128)(2,1)S(1)} %get-tuple-element.40.refs_1_, bf16[512,512]{1,0:T(8,128)(2,1)S(1)} %get-tuple-element.41.refs_2_, bf16[512,256]{1,0:T(8,128)(2,1)S(1)} %get-tuple-element.42.refs_3_, ...), custom_call_target="tpu_custom_call" | custom-call | flops 1207959552 | bytes 3932160 | tf_op jit(solution)/shard_map/pallas_call | solution.py:43
  63.3 4.4 %collective-permute-done.15.received_ref = bf16[512,256]{1,0:T(8,128)(2,1)S(1)} collective-permute-done((bf16[512,256]{1,0:T(8,128)(2,1)S(1)}, bf16[512,256]{1,0:T(8,128)(2,1)S(1)}, u32[]{:S(2)}, u32[]{:S(2)}) %collective-permute-start.15) | collective-permute-done | bytes 262176 | tf_op jit(solution)/shard_map/ppermute | solution.py:27
  67.7 1.4 %shard_map.63 = f32[512,256]{1,0:T(8,128)} custom-call(bf16[512,512]{1,0:T(8,128)(2,1)S(1)} %get-tuple-element.26.refs_0_, bf16[512,512]{1,0:T(8,128)(2,1)S(1)} %get-tuple-element.27.refs_1_, bf16[512,512]{1,0:T(8,128)(2,1)S(1)} %get-tuple-element.28.refs_2_, bf16[512,256]{1,0:T(8,128)(2,1)S(1)} %collective-permute-done.9.refs_3_, ...), custom_call_target="tpu_custom_call" | custom-call | flops 402653184 | bytes 3670016 | tf_op jit(solution)/shard_map/pallas_call | solution.py:43
  (13 shorter events, 0.1 us)
Async XLA Ops:
  3.7 11.1 %collective-permute-start.3 = (bf16[2,512,256]{2,1,0:T(8,128)(2,1)S(1)}, bf16[2,512,256]{2,1,0:T(8,128)(2,1)S(1)}, u32[]{:S(2)}, u32[]{:S(2)}) collective-permute-start(bf16[2,512,256]{2,1,0:T(8,128)(2,1)S(1)} %get-tuple-element.35), channel_id=1, source_target_pairs={{0,1},{1,0},{2,3},{3,2},{4,5},{5,4},{6,7},{7,6},{8,9},{9,8},{10,11... | collective-permute-start | bytes 1572872 | tf_op jit(solution)/shard_map/ppermute | solution.py:31
  7.1 7.7 %collective-permute-start.5 = (bf16[512,256]{1,0:T(8,128)(2,1)S(1)}, bf16[512,256]{1,0:T(8,128)(2,1)S(1)}, u32[]{:S(2)}, u32[]{:S(2)}) collective-permute-start(bf16[512,256]{1,0:T(8,128)(2,1)S(1)} %get-tuple-element.37), channel_id=1, source_target_pairs={{0,31},{1,2},{2,1},{3,4},{4,3},{5,6},{6,5},{7,8},{8,7},{9,10},{10,... | collective-permute-start | bytes 786440 | tf_op jit(solution)/shard_map/ppermute | solution.py:36
  7.1 23.0 %collective-permute-start.4 = (bf16[512,256]{1,0:T(8,128)(2,1)S(1)}, bf16[512,256]{1,0:T(8,128)(2,1)S(1)}, u32[]{:S(2)}, u32[]{:S(2)}) collective-permute-start(bf16[512,256]{1,0:T(8,128)(2,1)S(1)} %get-tuple-element.31.refs_3_), channel_id=1, source_target_pairs={{0,31},{1,2},{2,1},{3,4},{4,3},{5,6},{6,5},{7,8},{8,7},{9,10},{10,... | collective-permute-start | bytes 786440 | tf_op jit(solution)/shard_map/ppermute | solution.py:36
  8.8 13.7 %collective-permute-start = (bf16[512,256]{1,0:T(8,128)(2,1)S(1)}, bf16[512,256]{1,0:T(8,128)(2,1)S(1)}, u32[]{:S(2)}, u32[]{:S(2)}) collective-permute-start(bf16[512,256]{1,0:T(8,128)(2,1)S(1)} %get-tuple-element.31.refs_3_), channel_id=1, source_target_pairs={{0,224},{32,0},{64,32},{96,64},{128,96},{160,128},{192,160},{224,1... | collective-permute-start | bytes 786440 | tf_op jit(solution)/shard_map/ppermute | solution.py:27
  14.9 15.9 %collective-permute-start.6 = (bf16[512,256]{1,0:T(8,128)(2,1)S(1)}, bf16[512,256]{1,0:T(8,128)(2,1)S(1)}, u32[]{:S(2)}, u32[]{:S(2)}) collective-permute-start(bf16[512,256]{1,0:T(8,128)(2,1)S(1)} %fusion.3), channel_id=1, source_target_pairs={{0,32},{32,64},{64,96},{96,128},{128,160},{160,192},{192,224},{224... | collective-permute-start | bytes 786440 | tf_op jit(solution)/shard_map/ppermute | solution.py:27
  22.5 8.4 %collective-permute-start.1 = (bf16[512,256]{1,0:T(8,128)(2,1)S(1)}, bf16[512,256]{1,0:T(8,128)(2,1)S(1)}, u32[]{:S(2)}, u32[]{:S(2)}) collective-permute-start(bf16[512,256]{1,0:T(8,128)(2,1)S(1)} %collective-permute-done.refs_3_), channel_id=1, source_target_pairs={{0,1},{1,0},{2,3},{3,2},{4,5},{5,4},{6,7},{7,6},{8,9},{9,8},{10,11... | collective-permute-start | bytes 786440 | tf_op jit(solution)/shard_map/ppermute | solution.py:31
  26.4 6.1 %collective-permute-start.2 = (bf16[512,256]{1,0:T(8,128)(2,1)S(1)}, bf16[512,256]{1,0:T(8,128)(2,1)S(1)}, u32[]{:S(2)}, u32[]{:S(2)}) collective-permute-start(bf16[512,256]{1,0:T(8,128)(2,1)S(1)} %collective-permute-done.refs_3_), channel_id=1, source_target_pairs={{0,31},{1,2},{2,1},{3,4},{4,3},{5,6},{6,5},{7,8},{8,7},{9,10},{10,... | collective-permute-start | bytes 786440 | tf_op jit(solution)/shard_map/ppermute | solution.py:36
  26.4 6.7 %collective-permute-start.7 = (bf16[512,512]{1,0:T(8,128)(2,1)S(1)}, bf16[512,512]{1,0:T(8,128)(2,1)S(1)}, u32[]{:S(2)}, u32[]{:S(2)}) collective-permute-start(bf16[512,512]{1,0:T(8,128)(2,1)S(1)} %get-tuple-element.40.refs_1_), channel_id=1, source_target_pairs={{0,1},{1,0},{2,3},{3,2},{4,5},{5,4},{6,7},{7,6},{8,9},{9,8},{10,11... | collective-permute-start | bytes 1572872 | tf_op jit(solution)/shard_map/ppermute | solution.py:31
  30.1 8.9 %collective-permute-start.8 = (bf16[512,512]{1,0:T(8,128)(2,1)S(1)}, bf16[512,512]{1,0:T(8,128)(2,1)S(1)}, u32[]{:S(2)}, u32[]{:S(2)}) collective-permute-start(bf16[512,512]{1,0:T(8,128)(2,1)S(1)} %get-tuple-element.41.refs_2_), channel_id=1, source_target_pairs={{0,31},{1,2},{2,1},{3,4},{4,3},{5,6},{6,5},{7,8},{8,7},{9,10},{10,... | collective-permute-start | bytes 1572872 | tf_op jit(solution)/shard_map/ppermute | solution.py:36
  32.5 6.5 %copy-start = (f32[512,256]{1,0:T(8,128)S(1)}, f32[512,256]{1,0:T(8,128)}, u32[]{:S(2)}) copy-start(f32[512,256]{1,0:T(8,128)} %refs_7_.1) | copy-start | bytes 1572868
  41.2 7.9 %collective-permute-start.12 = (bf16[2,512,256]{2,1,0:T(8,128)(2,1)S(1)}, bf16[2,512,256]{2,1,0:T(8,128)(2,1)S(1)}, u32[]{:S(2)}, u32[]{:S(2)}) collective-permute-start(bf16[2,512,256]{2,1,0:T(8,128)(2,1)S(1)} %get-tuple-element.44), channel_id=1, source_target_pairs={{0,1},{1,0},{2,3},{3,2},{4,5},{5,4},{6,7},{7,6},{8,9},{9,8},{10,11... | collective-permute-start | bytes 1572872 | tf_op jit(solution)/shard_map/ppermute | solution.py:31
  43.2 5.8 %collective-permute-start.14 = (bf16[512,256]{1,0:T(8,128)(2,1)S(1)}, bf16[512,256]{1,0:T(8,128)(2,1)S(1)}, u32[]{:S(2)}, u32[]{:S(2)}) collective-permute-start(bf16[512,256]{1,0:T(8,128)(2,1)S(1)} %get-tuple-element.46), channel_id=1, source_target_pairs={{0,31},{1,2},{2,1},{3,4},{4,3},{5,6},{6,5},{7,8},{8,7},{9,10},{10,... | collective-permute-start | bytes 786440 | tf_op jit(solution)/shard_map/ppermute | solution.py:36
  43.2 18.2 %collective-permute-start.13 = (bf16[512,256]{1,0:T(8,128)(2,1)S(1)}, bf16[512,256]{1,0:T(8,128)(2,1)S(1)}, u32[]{:S(2)}, u32[]{:S(2)}) collective-permute-start(bf16[512,256]{1,0:T(8,128)(2,1)S(1)} %get-tuple-element.42.refs_3_), channel_id=1, source_target_pairs={{0,31},{1,2},{2,1},{3,4},{4,3},{5,6},{6,5},{7,8},{8,7},{9,10},{10,... | collective-permute-start | bytes 786440 | tf_op jit(solution)/shard_map/ppermute | solution.py:36
  45.0 14.9 %collective-permute-start.9 = (bf16[512,256]{1,0:T(8,128)(2,1)S(1)}, bf16[512,256]{1,0:T(8,128)(2,1)S(1)}, u32[]{:S(2)}, u32[]{:S(2)}) collective-permute-start(bf16[512,256]{1,0:T(8,128)(2,1)S(1)} %get-tuple-element.42.refs_3_), channel_id=1, source_target_pairs={{0,224},{32,0},{64,32},{96,64},{128,96},{160,128},{192,160},{224,1... | collective-permute-start | bytes 786440 | tf_op jit(solution)/shard_map/ppermute | solution.py:27
  49.1 18.5 %collective-permute-start.15 = (bf16[512,256]{1,0:T(8,128)(2,1)S(1)}, bf16[512,256]{1,0:T(8,128)(2,1)S(1)}, u32[]{:S(2)}, u32[]{:S(2)}) collective-permute-start(bf16[512,256]{1,0:T(8,128)(2,1)S(1)} %fusion.1), channel_id=1, source_target_pairs={{0,32},{32,64},{64,96},{96,128},{128,160},{160,192},{192,224},{224... | collective-permute-start | bytes 786440 | tf_op jit(solution)/shard_map/ppermute | solution.py:27
  59.8 7.9 %collective-permute-start.10 = (bf16[512,256]{1,0:T(8,128)(2,1)S(1)}, bf16[512,256]{1,0:T(8,128)(2,1)S(1)}, u32[]{:S(2)}, u32[]{:S(2)}) collective-permute-start(bf16[512,256]{1,0:T(8,128)(2,1)S(1)} %collective-permute-done.9.refs_3_), channel_id=1, source_target_pairs={{0,1},{1,0},{2,3},{3,2},{4,5},{5,4},{6,7},{7,6},{8,9},{9,8},{10,11... | collective-permute-start | bytes 786440 | tf_op jit(solution)/shard_map/ppermute | solution.py:31
  61.4 6.3 %collective-permute-start.11 = (bf16[512,256]{1,0:T(8,128)(2,1)S(1)}, bf16[512,256]{1,0:T(8,128)(2,1)S(1)}, u32[]{:S(2)}, u32[]{:S(2)}) collective-permute-start(bf16[512,256]{1,0:T(8,128)(2,1)S(1)} %collective-permute-done.9.refs_3_), channel_id=1, source_target_pairs={{0,31},{1,2},{2,1},{3,4},{4,3},{5,6},{6,5},{7,8},{8,7},{9,10},{10,... | collective-permute-start | bytes 786440 | tf_op jit(solution)/shard_map/ppermute | solution.py:36

commit v15 on v14

--- a/solution.py
+++ b/solution.py
@@ -127,7 +127,12 @@
     perm = perm_ref[...]
     wire_ref[...] = wire
     self_ref[...] = dot_t(cross[0][...], perm)
-    far_ref[...] = dot_t(cross[2][...], perm).astype(BF16)
+    part = dot_t(cross[2][...], perm).astype(BF16)
+    if len(far_ref.shape) == 2:
+        far_ref[...] = part
+    else:
+        far_ref[0] = part
+        far_ref[1] = wire
     mate_ref[0] = dot_t(cross[1][...], perm).astype(BF16)
     mate_ref[1] = wire
 
@@ -154,6 +159,10 @@
     build(0, sizes, blocks_hbm, row_hbm, col_hbm, *refs[3:], refs[:3])
 
 
+def field_of(ref):
+    return ref[...] if len(ref.shape) == 2 else ref[1]
+
+
 def sent_terms(sent, fields, scratch, other):
     total = 0.0
     for matrix, field in zip(sent, fields):
@@ -167,10 +176,10 @@
     out_ref, scratch, other = refs[-3:]
     straight = dot(mats[0][...], wire_ref[...])
     straight += dot(mats[1][...], mate_ref[1])
-    straight += dot(mats[2][...], field_ref[...])
+    straight += dot(mats[2][...], field_of(field_ref))
     total = dot_t(mats[0][...], perm_ref[...])
     if sent:
-        total += sent_terms(sent, (mate_ref[1], field_ref[...]), scratch, other)
+        total += sent_terms(sent, (mate_ref[1], field_of(field_ref)), scratch, other)
     out_ref[...] = total + restored(straight, scratch)
 
 
@@ -193,7 +202,7 @@
 def update_body(*refs):
     cross, (known_ref, drive_ref, relax_ref, mate_in, field_in), sent = refs[:3], refs[3:8], refs[8:10]
     perm_ref, wire_ref, self_ref, mate_ref, far_ref, scratch, other = refs[10:]
-    late = sent_terms(sent, (mate_in[1], field_in[...]), scratch, other)
+    late = sent_terms(sent, (mate_in[1], field_of(field_in)), scratch, other)
     field = advanced(known_ref[...] + late, drive_ref, relax_ref)
     interleave(field, scratch, perm_ref)
     emit(cross, field.astype(BF16), perm_ref, wire_ref, self_ref, mate_ref, far_ref)
@@ -225,7 +234,7 @@
     work = 2 * rows * rows * channels
     spread = jax.ShapeDtypeStruct((rows, LANES), F32)
     *cross, perm, wire, partial, to_mate, to_far, relax3 = call(
-        functools.partial(first_body, sizes), (*matrices, *emitted, spread), 9 * work,
+        functools.partial(first_body, sizes), (*matrices, *emitted[:4], double, spread), 9 * work,
         [blocks, row2, col2, drive, relax2], [HBM] * 5,
         fetch + [pltpu.VMEM(drive.shape, F32), pltpu.VMEM((1, rows), F32), staging, pltpu.SemaphoreType.DMA((4 + PIECES,))],
     )
@@ -242,13 +251,13 @@
             )
         if sweep == 0:
             from_far, _ = lax.optimization_barrier((from_far, own))
-        got = (partial + from_mate[0].astype(F32) + from_far.astype(F32)).astype(BF16)
+        got = (partial + from_mate[0].astype(F32) + (from_far if sweep else from_far[0]).astype(F32)).astype(BF16)
         received = shifted(got, "ka", 1)
         if sweep == 0:
             gated, down = lax.optimization_barrier((own[1:], down))
             sent = [mate(gated[0]), far(gated[1])]
         nexts = [down, mate(down), far(down)]
-        from_other = far(wire)
+        from_other = far(wire) if sweep else from_far
         args = [*own, wire, perm, from_mate, from_other, *(sent if sweep else [])]
         known = call(own_body, wide, 9 * work, args, scratch=extra)
         known = call(settle_body, wide, HEAVY * work, [known, received])

time: 70.3 us -> 69.4 us (0.987)
  waiting for transfers between devices: 27.8 us -> 22.1 us
  starting transfers between devices: 28 us -> 32.9 us
    ppermute x7 -> x6, waiting for transfers between devices: 7.95 us -> 1.08 us  [far(): lax.ppermute(value, 'rows', [(i, (i + 1 if i & 1 else i - 1) % count) for...]
    ppermute x4, starting transfers between devices: 9.91 us -> 12.6 us  [shifted(): lax.ppermute(value, axis, [(source, (source + steps) % count) for source...]
    ppermute x7 -> x6, starting transfers between devices: 3.5 us -> 4.87 us  [far(): lax.ppermute(value, 'rows', [(i, (i + 1 if i & 1 else i - 1) % count) for...]
    ppermute x4, waiting for transfers between devices: 19.8 us -> 21 us  [shifted(): lax.ppermute(value, axis, [(source, (source + steps) % count) for source...]
    ppermute x5, starting transfers between devices: 14.6 us -> 15.5 us  [mate(): lax.ppermute(value, 'rows', [(i, i ^ 1) for i in range(lax.axis_size('row...]
  transfers between devices with their start and end apart: 16 -> 15, of which waited for: 6 -> 6; matrix products, arithmetic and copies ran while one was open for 0% -> 0% of each run, Pallas kernels for 8% -> 8%
where the time goes in v15:
time: 69.4 us; the launch traced here: 68.5 us
  starting transfers between devices  32.9 us (47%)
  waiting for transfers between devices  22.1 us (32%)
  Pallas kernels  13.1 us (19%)
    ppermute x4, waiting for transfers between devices, shifted(): lax.ppermute(value, axis, [(source, (source + steps) % count) for source...  21 us
    ppermute x5, starting transfers between devices, mate(): lax.ppermute(value, 'rows', [(i, i ^ 1) for i in range(lax.axis_size('row...  15.5 us
    pallas_call x9, Pallas kernels, call(): pl.pallas_call(kernel, out_shape=outs, in_specs=specs or [VMEM] * len(arg...  13.1 us
    ppermute x4, starting transfers between devices, shifted(): lax.ppermute(value, axis, [(source, (source + steps) % count) for source...  12.6 us
    ppermute x6, starting transfers between devices, far(): lax.ppermute(value, 'rows', [(i, (i + 1 if i & 1 else i - 1) % count) for...  4.87 us
  transfers between devices with their start and end apart: 15, of which 6 were waited for; matrix products, arithmetic and copies ran while one was open for 0% of the time, Pallas kernels for 8%

profile of v15, /device:TPU:1, one launch (start us, length us, event | category | flops | bytes accessed | tf_op | source)
XLA Modules:
  0.0 68.5 jit_solution(5236584316575027589)
XLA Ops:
  0.0 3.7 %shard_map.55 = (bf16[512,512]{1,0:T(8,128)(2,1)S(1)}, bf16[512,512]{1,0:T(8,128)(2,1)S(1)}, bf16[512,512]{1,0:T(8,128)(2,1)S(1)}, bf16[512,256]{1,0:T(8,128)(2,...) custom-call(bf16[256,4096]{1,0:T(8,128)(2,1)} %blocks_hbm.3, ...), custom_call_target="tpu_custom_call" | custom-call | flops 1207959552 | bytes 2625536 | tf_op jit(solution)/shard_map/pallas_call | solution.py:43
  3.7 3.1 %collective-permute-start.4 = (bf16[2,512,256]{2,1,0:T(8,128)(2,1)S(1)}, bf16[2,512,256]{2,1,0:T(8,128)(2,1)S(1)}, u32[]{:S(2)}, u32[]{:S(2)}) collective-permute-start(bf16[2,512,256]{2,1,0:T(8,128)(2,1)S(1)} %get-tuple-element.36), channel_id=1, source_target_pairs={{0,31},{1,2},{2,1},{3,4},{4,3},{5,6},{6,5},{7,8},{8,7},{9,10},{10,... | collective-permute-start | bytes 1572872 | tf_op jit(solution)/shard_map/ppermute | solution.py:36
  6.8 4.7 %collective-permute-start.3 = (bf16[2,512,256]{2,1,0:T(8,128)(2,1)S(1)}, bf16[2,512,256]{2,1,0:T(8,128)(2,1)S(1)}, u32[]{:S(2)}, u32[]{:S(2)}) collective-permute-start(bf16[2,512,256]{2,1,0:T(8,128)(2,1)S(1)} %get-tuple-element.35), channel_id=1, source_target_pairs={{0,1},{1,0},{2,3},{3,2},{4,5},{5,4},{6,7},{7,6},{8,9},{9,8},{10,11... | collective-permute-start | bytes 1572872 | tf_op jit(solution)/shard_map/ppermute | solution.py:31
  11.5 4.9 %collective-permute-start = (bf16[512,256]{1,0:T(8,128)(2,1)S(1)}, bf16[512,256]{1,0:T(8,128)(2,1)S(1)}, u32[]{:S(2)}, u32[]{:S(2)}) collective-permute-start(bf16[512,256]{1,0:T(8,128)(2,1)S(1)} %get-tuple-element.31.refs_3_), channel_id=1, source_target_pairs={{0,224},{32,0},{64,32},{96,64},{128,96},{160,128},{192,160},{224,1... | collective-permute-start | bytes 786440 | tf_op jit(solution)/shard_map/ppermute | solution.py:27
  16.4 2.5 %shard_map.56 = (bf16[512,512]{1,0:T(8,128)(2,1)S(1)}, bf16[512,512]{1,0:T(8,128)(2,1)S(1)}, bf16[512,512]{1,0:T(8,128)(2,1)S(1)}) custom-call(bf16[256,4096]{1,0:T(8,128)(2,1)} %blocks_hbm.3, s32[1,256]{1,0:T(1,128)} %bitcast.18, s32[1,256]{1,0:T(1,128)} %bitcast.20), custom_call_target="tpu_custom_call" | custom-call | flops 805306368 | bytes 2099200 | tf_op jit(solution)/shard_map/pallas_call | solution.py:43
  19.0 0.0 collective-permute-done.3.refs_5_.refs_6_
  19.0 0.1 fusion.2
  19.1 0.1 collective-permute-start.5
  19.2 5.9 %collective-permute-done.refs_3_ = bf16[512,256]{1,0:T(8,128)(2,1)S(1)} collective-permute-done((bf16[512,256]{1,0:T(8,128)(2,1)S(1)}, bf16[512,256]{1,0:T(8,128)(2,1)S(1)}, u32[]{:S(2)}, u32[]{:S(2)}) %collective-permute-start) | collective-permute-done | bytes 262176 | tf_op jit(solution)/shard_map/ppermute | solution.py:27
  25.1 0.5 collective-permute-start.1
  25.6 3.2 %collective-permute-start.6 = (bf16[512,512]{1,0:T(8,128)(2,1)S(1)}, bf16[512,512]{1,0:T(8,128)(2,1)S(1)}, u32[]{:S(2)}, u32[]{:S(2)}) collective-permute-start(bf16[512,512]{1,0:T(8,128)(2,1)S(1)} %get-tuple-element.40.refs_1_), channel_id=1, source_target_pairs={{0,1},{1,0},{2,3},{3,2},{4,5},{5,4},{6,7},{7,6},{8,9},{9,8},{10,11... | collective-permute-start | bytes 1572872 | tf_op jit(solution)/shard_map/ppermute | solution.py:31
  28.8 0.8 %shard_map.57.own_ref = f32[512,256]{1,0:T(8,128)S(1)} custom-call(bf16[512,512]{1,0:T(8,128)(2,1)S(1)} %get-tuple-element.33.refs_0_, bf16[512,512]{1,0:T(8,128)(2,1)S(1)} %get-tuple-element.40.refs_1_, bf16[512,512]{1,0:T(8,128)(2,1)S(1)} %get-tuple-element.41.refs_2_, bf16[512,256]{1,0:T(8,128)(2,1)S(1)} %get-tuple-element.31.refs_3_, ...), custom_call_target="tpu_custom_call" | custom-call | flops 1207959552 | bytes 3145728 | tf_op jit(solution)/shard_map/pallas_call | solution.py:43
  29.6 6.4 %collective-permute-done.5.received_ref = bf16[512,256]{1,0:T(8,128)(2,1)S(1)} collective-permute-done((bf16[512,256]{1,0:T(8,128)(2,1)S(1)}, bf16[512,256]{1,0:T(8,128)(2,1)S(1)}, u32[]{:S(2)}, u32[]{:S(2)}) %collective-permute-start.5) | collective-permute-done | bytes 262176 | tf_op jit(solution)/shard_map/ppermute | solution.py:27
  36.1 0.0 collective-permute-done.2.refs_5_
  36.1 0.0 copy-start
  36.1 0.6 shard_map.59.refs_3_
  36.7 0.0 collective-permute-done.6.refs_8_.refs_7_
  36.7 1.0 %collective-permute-done.7.refs_9_.refs_8_ = bf16[512,512]{1,0:T(8,128)(2,1)S(1)} collective-permute-done((bf16[512,512]{1,0:T(8,128)(2,1)S(1)}, bf16[512,512]{1,0:T(8,128)(2,1)S(1)}, u32[]{:S(2)}, u32[]{:S(2)}) %collective-permute-start.7) | collective-permute-done | bytes 524320 | tf_op jit(solution)/shard_map/ppermute | solution.py:36
  37.7 2.2 %shard_map.60 = (bf16[512,256]{1,0:T(8,128)(2,1)S(1)}, bf16[512,256]{1,0:T(8,128)(2,1)S(1)}, f32[512,256]{1,0:T(8,128)S(1)}, bf16[2,512,256]{2,1,0:T(8,128)(2,1)S(1)}, bf16[512,256]{1,0:T(8,128)(2,1)S(1)}) custom-call(bf16[512,512]{1,0:T(8,128)(2,1)S(1)} %get-tuple-element.26.refs_0_, bf16[512,512]{1,0:T(8,128)(2,1)S(1)} %get-tuple-element.27.refs_1_, ...), custom_call_target="tpu_custom_call" | custom-call | flops 1073741824 | bytes 4980736 | tf_op jit(solution)/shard_map/pallas_call | solution.py:43
  39.9 1.9 %collective-permute-start.11 = (bf16[2,512,256]{2,1,0:T(8,128)(2,1)S(1)}, bf16[2,512,256]{2,1,0:T(8,128)(2,1)S(1)}, u32[]{:S(2)}, u32[]{:S(2)}) collective-permute-start(bf16[2,512,256]{2,1,0:T(8,128)(2,1)S(1)} %get-tuple-element.44), channel_id=1, source_target_pairs={{0,1},{1,0},{2,3},{3,2},{4,5},{5,4},{6,7},{7,6},{8,9},{9,8},{10,11... | collective-permute-start | bytes 1572872 | tf_op jit(solution)/shard_map/ppermute | solution.py:31
  41.8 0.0 collective-permute-start.13
  41.8 1.7 %collective-permute-start.12 = (bf16[512,256]{1,0:T(8,128)(2,1)S(1)}, bf16[512,256]{1,0:T(8,128)(2,1)S(1)}, u32[]{:S(2)}, u32[]{:S(2)}) collective-permute-start(bf16[512,256]{1,0:T(8,128)(2,1)S(1)} %get-tuple-element.42.refs_3_), channel_id=1, source_target_pairs={{0,31},{1,2},{2,1},{3,4},{4,3},{5,6},{6,5},{7,8},{8,7},{9,10},{10,... | collective-permute-start | bytes 786440 | tf_op jit(solution)/shard_map/ppermute | solution.py:36
  43.5 4.3 %collective-permute-start.8 = (bf16[512,256]{1,0:T(8,128)(2,1)S(1)}, bf16[512,256]{1,0:T(8,128)(2,1)S(1)}, u32[]{:S(2)}, u32[]{:S(2)}) collective-permute-start(bf16[512,256]{1,0:T(8,128)(2,1)S(1)} %get-tuple-element.42.refs_3_), channel_id=1, source_target_pairs={{0,224},{32,0},{64,32},{96,64},{128,96},{160,128},{192,160},{224,1... | collective-permute-start | bytes 786440 | tf_op jit(solution)/shard_map/ppermute | solution.py:27
  47.8 0.1 collective-permute-done.13
  47.9 0.0 collective-permute-done.11.refs_5_
  47.9 0.1 fusion.1
  48.0 3.3 %collective-permute-start.14 = (bf16[512,256]{1,0:T(8,128)(2,1)S(1)}, bf16[512,256]{1,0:T(8,128)(2,1)S(1)}, u32[]{:S(2)}, u32[]{:S(2)}) collective-permute-start(bf16[512,256]{1,0:T(8,128)(2,1)S(1)} %fusion.1), channel_id=1, source_target_pairs={{0,32},{32,64},{64,96},{96,128},{128,160},{160,192},{192,224},{224... | collective-permute-start | bytes 786440 | tf_op jit(solution)/shard_map/ppermute | solution.py:27
  51.3 6.7 %collective-permute-done.8.refs_3_ = bf16[512,256]{1,0:T(8,128)(2,1)S(1)} collective-permute-done((bf16[512,256]{1,0:T(8,128)(2,1)S(1)}, bf16[512,256]{1,0:T(8,128)(2,1)S(1)}, u32[]{:S(2)}, u32[]{:S(2)}) %collective-permute-start.8) | collective-permute-done | bytes 262176 | tf_op jit(solution)/shard_map/ppermute | solution.py:27
  58.0 5.2 %collective-permute-start.9 = (bf16[512,256]{1,0:T(8,128)(2,1)S(1)}, bf16[512,256]{1,0:T(8,128)(2,1)S(1)}, u32[]{:S(2)}, u32[]{:S(2)}) collective-permute-start(bf16[512,256]{1,0:T(8,128)(2,1)S(1)} %collective-permute-done.8.refs_3_), channel_id=1, source_target_pairs={{0,1},{1,0},{2,3},{3,2},{4,5},{5,4},{6,7},{7,6},{8,9},{9,8},{10,11... | collective-permute-start | bytes 786440 | tf_op jit(solution)/shard_map/ppermute | solution.py:31
  63.1 1.8 %shard_map.61.own_ref = f32[512,256]{1,0:T(8,128)S(1)} custom-call(bf16[512,512]{1,0:T(8,128)(2,1)S(1)} %get-tuple-element.33.refs_0_, bf16[512,512]{1,0:T(8,128)(2,1)S(1)} %get-tuple-element.40.refs_1_, bf16[512,512]{1,0:T(8,128)(2,1)S(1)} %get-tuple-element.41.refs_2_, bf16[512,256]{1,0:T(8,128)(2,1)S(1)} %get-tuple-element.42.refs_3_, ...), custom_call_target="tpu_custom_call" | custom-call | flops 1207959552 | bytes 3932160 | tf_op jit(solution)/shard_map/pallas_call | solution.py:43
  65.0 2.0 %collective-permute-done.14.received_ref = bf16[512,256]{1,0:T(8,128)(2,1)S(1)} collective-permute-done((bf16[512,256]{1,0:T(8,128)(2,1)S(1)}, bf16[512,256]{1,0:T(8,128)(2,1)S(1)}, u32[]{:S(2)}, u32[]{:S(2)}) %collective-permute-start.14) | collective-permute-done | bytes 262176 | tf_op jit(solution)/shard_map/ppermute | solution.py:27
  67.0 1.4 %shard_map.63 = f32[512,256]{1,0:T(8,128)} custom-call(bf16[512,512]{1,0:T(8,128)(2,1)S(1)} %get-tuple-element.26.refs_0_, bf16[512,512]{1,0:T(8,128)(2,1)S(1)} %get-tuple-element.27.refs_1_, bf16[512,512]{1,0:T(8,128)(2,1)S(1)} %get-tuple-element.28.refs_2_, bf16[512,256]{1,0:T(8,128)(2,1)S(1)} %collective-permute-done.8.refs_3_, ...), custom_call_target="tpu_custom_call" | custom-call | flops 402653184 | bytes 3670016 | tf_op jit(solution)/shard_map/pallas_call | solution.py:43
  (11 shorter events, 0.1 us)
Async XLA Ops:
  3.7 15.2 %collective-permute-start.4 = (bf16[2,512,256]{2,1,0:T(8,128)(2,1)S(1)}, bf16[2,512,256]{2,1,0:T(8,128)(2,1)S(1)}, u32[]{:S(2)}, u32[]{:S(2)}) collective-permute-start(bf16[2,512,256]{2,1,0:T(8,128)(2,1)S(1)} %get-tuple-element.36), channel_id=1, source_target_pairs={{0,31},{1,2},{2,1},{3,4},{4,3},{5,6},{6,5},{7,8},{8,7},{9,10},{10,... | collective-permute-start | bytes 1572872 | tf_op jit(solution)/shard_map/ppermute | solution.py:36
  6.8 12.1 %collective-permute-start.3 = (bf16[2,512,256]{2,1,0:T(8,128)(2,1)S(1)}, bf16[2,512,256]{2,1,0:T(8,128)(2,1)S(1)}, u32[]{:S(2)}, u32[]{:S(2)}) collective-permute-start(bf16[2,512,256]{2,1,0:T(8,128)(2,1)S(1)} %get-tuple-element.35), channel_id=1, source_target_pairs={{0,1},{1,0},{2,3},{3,2},{4,5},{5,4},{6,7},{7,6},{8,9},{9,8},{10,11... | collective-permute-start | bytes 1572872 | tf_op jit(solution)/shard_map/ppermute | solution.py:31
  11.5 13.6 %collective-permute-start = (bf16[512,256]{1,0:T(8,128)(2,1)S(1)}, bf16[512,256]{1,0:T(8,128)(2,1)S(1)}, u32[]{:S(2)}, u32[]{:S(2)}) collective-permute-start(bf16[512,256]{1,0:T(8,128)(2,1)S(1)} %get-tuple-element.31.refs_3_), channel_id=1, source_target_pairs={{0,224},{32,0},{64,32},{96,64},{128,96},{160,128},{192,160},{224,1... | collective-permute-start | bytes 786440 | tf_op jit(solution)/shard_map/ppermute | solution.py:27
  19.1 16.9 %collective-permute-start.5 = (bf16[512,256]{1,0:T(8,128)(2,1)S(1)}, bf16[512,256]{1,0:T(8,128)(2,1)S(1)}, u32[]{:S(2)}, u32[]{:S(2)}) collective-permute-start(bf16[512,256]{1,0:T(8,128)(2,1)S(1)} %fusion.2), channel_id=1, source_target_pairs={{0,32},{32,64},{64,96},{96,128},{128,160},{160,192},{192,224},{224... | collective-permute-start | bytes 786440 | tf_op jit(solution)/shard_map/ppermute | solution.py:27
  25.1 10.9 %collective-permute-start.1 = (bf16[512,256]{1,0:T(8,128)(2,1)S(1)}, bf16[512,256]{1,0:T(8,128)(2,1)S(1)}, u32[]{:S(2)}, u32[]{:S(2)}) collective-permute-start(bf16[512,256]{1,0:T(8,128)(2,1)S(1)} %collective-permute-done.refs_3_), channel_id=1, source_target_pairs={{0,1},{1,0},{2,3},{3,2},{4,5},{5,4},{6,7},{7,6},{8,9},{9,8},{10,11... | collective-permute-start | bytes 786440 | tf_op jit(solution)/shard_map/ppermute | solution.py:31
  25.6 10.5 %collective-permute-start.2 = (bf16[512,256]{1,0:T(8,128)(2,1)S(1)}, bf16[512,256]{1,0:T(8,128)(2,1)S(1)}, u32[]{:S(2)}, u32[]{:S(2)}) collective-permute-start(bf16[512,256]{1,0:T(8,128)(2,1)S(1)} %collective-permute-done.refs_3_), channel_id=1, source_target_pairs={{0,31},{1,2},{2,1},{3,4},{4,3},{5,6},{6,5},{7,8},{8,7},{9,10},{10,... | collective-permute-start | bytes 786440 | tf_op jit(solution)/shard_map/ppermute | solution.py:36
  25.6 11.1 %collective-permute-start.6 = (bf16[512,512]{1,0:T(8,128)(2,1)S(1)}, bf16[512,512]{1,0:T(8,128)(2,1)S(1)}, u32[]{:S(2)}, u32[]{:S(2)}) collective-permute-start(bf16[512,512]{1,0:T(8,128)(2,1)S(1)} %get-tuple-element.40.refs_1_), channel_id=1, source_target_pairs={{0,1},{1,0},{2,3},{3,2},{4,5},{5,4},{6,7},{7,6},{8,9},{9,8},{10,11... | collective-permute-start | bytes 1572872 | tf_op jit(solution)/shard_map/ppermute | solution.py:31
  28.8 8.9 %collective-permute-start.7 = (bf16[512,512]{1,0:T(8,128)(2,1)S(1)}, bf16[512,512]{1,0:T(8,128)(2,1)S(1)}, u32[]{:S(2)}, u32[]{:S(2)}) collective-permute-start(bf16[512,512]{1,0:T(8,128)(2,1)S(1)} %get-tuple-element.41.refs_2_), channel_id=1, source_target_pairs={{0,31},{1,2},{2,1},{3,4},{4,3},{5,6},{6,5},{7,8},{8,7},{9,10},{10,... | collective-permute-start | bytes 1572872 | tf_op jit(solution)/shard_map/ppermute | solution.py:36
  36.1 1.6 %copy-start = (f32[512,256]{1,0:T(8,128)S(1)}, f32[512,256]{1,0:T(8,128)}, u32[]{:S(2)}) copy-start(f32[512,256]{1,0:T(8,128)} %refs_7_.1) | copy-start | bytes 1572868
  39.9 8.0 %collective-permute-start.11 = (bf16[2,512,256]{2,1,0:T(8,128)(2,1)S(1)}, bf16[2,512,256]{2,1,0:T(8,128)(2,1)S(1)}, u32[]{:S(2)}, u32[]{:S(2)}) collective-permute-start(bf16[2,512,256]{2,1,0:T(8,128)(2,1)S(1)} %get-tuple-element.44), channel_id=1, source_target_pairs={{0,1},{1,0},{2,3},{3,2},{4,5},{5,4},{6,7},{7,6},{8,9},{9,8},{10,11... | collective-permute-start | bytes 1572872 | tf_op jit(solution)/shard_map/ppermute | solution.py:31
  41.8 6.1 %collective-permute-start.13 = (bf16[512,256]{1,0:T(8,128)(2,1)S(1)}, bf16[512,256]{1,0:T(8,128)(2,1)S(1)}, u32[]{:S(2)}, u32[]{:S(2)}) collective-permute-start(bf16[512,256]{1,0:T(8,128)(2,1)S(1)} %get-tuple-element.46), channel_id=1, source_target_pairs={{0,31},{1,2},{2,1},{3,4},{4,3},{5,6},{6,5},{7,8},{8,7},{9,10},{10,... | collective-permute-start | bytes 786440 | tf_op jit(solution)/shard_map/ppermute | solution.py:36
  41.8 21.3 %collective-permute-start.12 = (bf16[512,256]{1,0:T(8,128)(2,1)S(1)}, bf16[512,256]{1,0:T(8,128)(2,1)S(1)}, u32[]{:S(2)}, u32[]{:S(2)}) collective-permute-start(bf16[512,256]{1,0:T(8,128)(2,1)S(1)} %get-tuple-element.42.refs_3_), channel_id=1, source_target_pairs={{0,31},{1,2},{2,1},{3,4},{4,3},{5,6},{6,5},{7,8},{8,7},{9,10},{10,... | collective-permute-start | bytes 786440 | tf_op jit(solution)/shard_map/ppermute | solution.py:36
  43.5 14.4 %collective-permute-start.8 = (bf16[512,256]{1,0:T(8,128)(2,1)S(1)}, bf16[512,256]{1,0:T(8,128)(2,1)S(1)}, u32[]{:S(2)}, u32[]{:S(2)}) collective-permute-start(bf16[512,256]{1,0:T(8,128)(2,1)S(1)} %get-tuple-element.42.refs_3_), channel_id=1, source_target_pairs={{0,224},{32,0},{64,32},{96,64},{128,96},{160,128},{192,160},{224,1... | collective-permute-start | bytes 786440 | tf_op jit(solution)/shard_map/ppermute | solution.py:27
  48.0 19.0 %collective-permute-start.14 = (bf16[512,256]{1,0:T(8,128)(2,1)S(1)}, bf16[512,256]{1,0:T(8,128)(2,1)S(1)}, u32[]{:S(2)}, u32[]{:S(2)}) collective-permute-start(bf16[512,256]{1,0:T(8,128)(2,1)S(1)} %fusion.1), channel_id=1, source_target_pairs={{0,32},{32,64},{64,96},{96,128},{128,160},{160,192},{192,224},{224... | collective-permute-start | bytes 786440 | tf_op jit(solution)/shard_map/ppermute | solution.py:27
  58.0 9.0 %collective-permute-start.10 = (bf16[512,256]{1,0:T(8,128)(2,1)S(1)}, bf16[512,256]{1,0:T(8,128)(2,1)S(1)}, u32[]{:S(2)}, u32[]{:S(2)}) collective-permute-start(bf16[512,256]{1,0:T(8,128)(2,1)S(1)} %collective-permute-done.8.refs_3_), channel_id=1, source_target_pairs={{0,31},{1,2},{2,1},{3,4},{4,3},{5,6},{6,5},{7,8},{8,7},{9,10},{10,... | collective-permute-start | bytes 786440 | tf_op jit(solution)/shard_map/ppermute | solution.py:36
  58.0 9.1 %collective-permute-start.9 = (bf16[512,256]{1,0:T(8,128)(2,1)S(1)}, bf16[512,256]{1,0:T(8,128)(2,1)S(1)}, u32[]{:S(2)}, u32[]{:S(2)}) collective-permute-start(bf16[512,256]{1,0:T(8,128)(2,1)S(1)} %collective-permute-done.8.refs_3_), channel_id=1, source_target_pairs={{0,1},{1,0},{2,3},{3,2},{4,5},{5,4},{6,7},{7,6},{8,9},{9,8},{10,11... | collective-permute-start | bytes 786440 | tf_op jit(solution)/shard_map/ppermute | solution.py:31

commit v16 on v4

--- a/solution.py
+++ b/solution.py
@@ -78,7 +78,7 @@
     return jnp.concatenate(columns, axis=1)
 
 
-def build(half, sizes, blocks_hbm, row_hbm, col_hbm, blocks, ids, sems, stores):
+def build(half, sizes, blocks_hbm, row_hbm, col_hbm, blocks, ids, sems, stores, meanwhile=lambda: None):
     count, row_devs, ka_devs = sizes
     bits, row_bits = log2(count), log2(row_devs)
     copies = [pltpu.make_async_copy(h, ids.at[k : k + 1], sems.at[k]) for k, h in enumerate((row_hbm, col_hbm))]
@@ -88,6 +88,7 @@
         copies.append(pltpu.make_async_copy(blocks_hbm.at[:, lanes], blocks.at[:, lanes], sems.at[2 + k]))
     for copy in copies:
         copy.start()
+    meanwhile()
     copies[0].wait()
     copies[1].wait()
     row = ids[0:1, :]
@@ -141,13 +142,15 @@
     ]
     for copy in later:
         copy.start()
-    build(1, sizes, blocks_hbm, row_hbm, col_hbm, blocks, ids, sems, cross)
-    for copy in later:
-        copy.wait()
-    spread_ref[...] = jnp.broadcast_to(relax[...], (LANES, relax.shape[1])).T
-    field = drive[...]
-    interleave(field, scratch, perm_ref)
-    emit(cross, field.astype(BF16), perm_ref, wire_ref, self_ref, mate_ref, far_ref)
+
+    def place_field():
+        for copy in later:
+            copy.wait()
+        spread_ref[...] = jnp.broadcast_to(relax[...], (LANES, relax.shape[1])).T
+        interleave(drive[...], scratch, perm_ref)
+
+    build(1, sizes, blocks_hbm, row_hbm, col_hbm, blocks, ids, sems, cross, place_field)
+    emit(cross, drive[...].astype(BF16), perm_ref, wire_ref, self_ref, mate_ref, far_ref)
 
 
 def second_body(sizes, blocks_hbm, row_hbm, col_hbm, *refs):

time: 67.8 us -> 67.7 us (level)
  no operation moved by 1% of the time
where the time goes in v16:
time: 67.7 us; the launch traced here: 67.5 us
  starting transfers between devices  28.2 us (42%)
  waiting for transfers between devices  26 us (38%)
  Pallas kernels  13.1 us (19%)
    ppermute x5, waiting for transfers between devices, far(): lax.ppermute(value, 'rows', [(i, (i + 1 if i & 1 else i - 1) % count) for...  16.5 us
    ppermute x5, starting transfers between devices, far(): lax.ppermute(value, 'rows', [(i, (i + 1 if i & 1 else i - 1) % count) for...  13.9 us
    ppermute x4, starting transfers between devices, shifted(): lax.ppermute(value, axis, [(source, (source + steps) % count) for source...  13.7 us
    pallas_call x9, Pallas kernels, call(): pl.pallas_call(kernel, out_shape=outs, in_specs=specs or [VMEM] * len(arg...  13.1 us
    ppermute x4, waiting for transfers between devices, shifted(): lax.ppermute(value, axis, [(source, (source + steps) % count) for source...  9.43 us
  transfers between devices with their start and end apart: 14, of which 9 were waited for; matrix products, arithmetic and copies ran while one was open for 0% of the time, Pallas kernels for 9%

profile of v16, /device:TPU:24, one launch (start us, length us, event | category | flops | bytes accessed | tf_op | source)
XLA Modules:
  0.0 67.5 jit_solution(6962968276761490077)
XLA Ops:
  0.0 3.7 %shard_map.55 = (bf16[512,512]{1,0:T(8,128)(2,1)S(1)}, bf16[512,512]{1,0:T(8,128)(2,1)S(1)}, bf16[512,512]{1,0:T(8,128)(2,1)S(1)}, bf16[512,256]{1,0:T(8,128)(2,...) custom-call(bf16[256,4096]{1,0:T(8,128)(2,1)} %blocks_hbm.3, ...), custom_call_target="tpu_custom_call" | custom-call | flops 1207959552 | bytes 2625536 | tf_op jit(solution)/shard_map/pallas_call | solution.py:43
  3.7 6.3 %collective-permute-start.4 = (bf16[2,512,256]{2,1,0:T(8,128)(2,1)S(1)}, bf16[2,512,256]{2,1,0:T(8,128)(2,1)S(1)}, u32[]{:S(2)}, u32[]{:S(2)}) collective-permute-start(bf16[2,512,256]{2,1,0:T(8,128)(2,1)S(1)} %get-tuple-element.36), channel_id=1, source_target_pairs={{0,31},{1,2},{2,1},{3,4},{4,3},{5,6},{6,5},{7,8},{8,7},{9,10},{10,... | collective-permute-start | bytes 1572872 | tf_op jit(solution)/shard_map/ppermute | solution.py:36
  10.0 0.0 collective-permute-start.3
  10.0 2.9 %collective-permute-start = (bf16[512,256]{1,0:T(8,128)(2,1)S(1)}, bf16[512,256]{1,0:T(8,128)(2,1)S(1)}, u32[]{:S(2)}, u32[]{:S(2)}) collective-permute-start(bf16[512,256]{1,0:T(8,128)(2,1)S(1)} %get-tuple-element.31.refs_3_), channel_id=1, source_target_pairs={{0,224},{32,0},{64,32},{96,64},{128,96},{160,128},{192,160},{224,1... | collective-permute-start | bytes 786440 | tf_op jit(solution)/shard_map/ppermute | solution.py:27
  12.9 2.5 %shard_map.56 = (bf16[512,512]{1,0:T(8,128)(2,1)S(1)}, bf16[512,512]{1,0:T(8,128)(2,1)S(1)}, bf16[512,512]{1,0:T(8,128)(2,1)S(1)}) custom-call(bf16[256,4096]{1,0:T(8,128)(2,1)} %blocks_hbm.3, s32[1,256]{1,0:T(1,128)} %bitcast.23, s32[1,256]{1,0:T(1,128)} %bitcast.25), custom_call_target="tpu_custom_call" | custom-call | flops 805306368 | bytes 2099200 | tf_op jit(solution)/shard_map/pallas_call | solution.py:43
  15.4 1.5 %collective-permute-done.4.refs_6_.refs_7_ = bf16[2,512,256]{2,1,0:T(8,128)(2,1)S(1)} collective-permute-done((bf16[2,512,256]{2,1,0:T(8,128)(2,1)S(1)}, bf16[2,512,256]{2,1,0:T(8,128)(2,1)S(1)}, u32[]{:S(2)}, u32[]{:S(2)}) %collective-permute-start.4) | collective-permute-done | bytes 524320 | tf_op jit(solution)/shard_map/ppermute | solution.py:36
  16.9 0.0 collective-permute-done.3.refs_5_.refs_6_
  17.0 0.1 fusion.1
  17.0 2.8 %collective-permute-start.5 = (bf16[512,256]{1,0:T(8,128)(2,1)S(1)}, bf16[512,256]{1,0:T(8,128)(2,1)S(1)}, u32[]{:S(2)}, u32[]{:S(2)}) collective-permute-start(bf16[512,256]{1,0:T(8,128)(2,1)S(1)} %fusion.1), channel_id=1, source_target_pairs={{0,32},{32,64},{64,96},{96,128},{128,160},{160,192},{192,224},{224... | collective-permute-start | bytes 786440 | tf_op jit(solution)/shard_map/ppermute | solution.py:27
  19.8 4.2 %collective-permute-done.refs_3_ = bf16[512,256]{1,0:T(8,128)(2,1)S(1)} collective-permute-done((bf16[512,256]{1,0:T(8,128)(2,1)S(1)}, bf16[512,256]{1,0:T(8,128)(2,1)S(1)}, u32[]{:S(2)}, u32[]{:S(2)}) %collective-permute-start) | collective-permute-done | bytes 262176 | tf_op jit(solution)/shard_map/ppermute | solution.py:27
  24.0 2.1 %collective-permute-start.2 = (bf16[512,256]{1,0:T(8,128)(2,1)S(1)}, bf16[512,256]{1,0:T(8,128)(2,1)S(1)}, u32[]{:S(2)}, u32[]{:S(2)}) collective-permute-start(bf16[512,256]{1,0:T(8,128)(2,1)S(1)} %collective-permute-done.refs_3_), channel_id=1, source_target_pairs={{0,31},{1,2},{2,1},{3,4},{4,3},{5,6},{6,5},{7,8},{8,7},{9,10},{10,... | collective-permute-start | bytes 786440 | tf_op jit(solution)/shard_map/ppermute | solution.py:36
  26.2 0.5 collective-permute-start.6
  26.7 1.7 %collective-permute-start.7 = (bf16[512,512]{1,0:T(8,128)(2,1)S(1)}, bf16[512,512]{1,0:T(8,128)(2,1)S(1)}, u32[]{:S(2)}, u32[]{:S(2)}) collective-permute-start(bf16[512,512]{1,0:T(8,128)(2,1)S(1)} %get-tuple-element.41.refs_2_), channel_id=1, source_target_pairs={{0,31},{1,2},{2,1},{3,4},{4,3},{5,6},{6,5},{7,8},{8,7},{9,10},{10,... | collective-permute-start | bytes 1572872 | tf_op jit(solution)/shard_map/ppermute | solution.py:36
  28.4 0.8 %shard_map.57.own_ref = f32[512,256]{1,0:T(8,128)S(1)} custom-call(bf16[512,512]{1,0:T(8,128)(2,1)S(1)} %get-tuple-element.33.refs_0_, bf16[512,512]{1,0:T(8,128)(2,1)S(1)} %get-tuple-element.40.refs_1_, bf16[512,512]{1,0:T(8,128)(2,1)S(1)} %get-tuple-element.41.refs_2_, bf16[512,256]{1,0:T(8,128)(2,1)S(1)} %get-tuple-element.31.refs_3_, ...), custom_call_target="tpu_custom_call" | custom-call | flops 1207959552 | bytes 3145728 | tf_op jit(solution)/shard_map/pallas_call | solution.py:43
  29.2 0.6 collective-permute-done.5.received_ref
  29.8 2.1 %collective-permute-done.2.refs_5_ = bf16[512,256]{1,0:T(8,128)(2,1)S(1)} collective-permute-done((bf16[512,256]{1,0:T(8,128)(2,1)S(1)}, bf16[512,256]{1,0:T(8,128)(2,1)S(1)}, u32[]{:S(2)}, u32[]{:S(2)}) %collective-permute-start.2) | collective-permute-done | bytes 262176 | tf_op jit(solution)/shard_map/ppermute | solution.py:36
  31.9 0.0 collective-permute-done.1.refs_4_
  31.9 0.6 shard_map.59.refs_3_
  32.6 5.0 %collective-permute-done.7.refs_9_.refs_8_ = bf16[512,512]{1,0:T(8,128)(2,1)S(1)} collective-permute-done((bf16[512,512]{1,0:T(8,128)(2,1)S(1)}, bf16[512,512]{1,0:T(8,128)(2,1)S(1)}, u32[]{:S(2)}, u32[]{:S(2)}) %collective-permute-start.7) | collective-permute-done | bytes 524320 | tf_op jit(solution)/shard_map/ppermute | solution.py:36
  37.6 2.2 %shard_map.60 = (bf16[512,256]{1,0:T(8,128)(2,1)S(1)}, bf16[512,256]{1,0:T(8,128)(2,1)S(1)}, f32[512,256]{1,0:T(8,128)S(1)}, bf16[2,512,256]{2,1,0:T(8,128)(2,1)S(1)}, bf16[2,512,256]{2,1,0:T(8,128)(2,1)S(1)}) custom-call(bf16[512,512]{1,0:T(8,128)(2,1)S(1)} %get-tuple-element.26.refs_0_, bf16[512,512]{1,0:T(8,128)(2,1)S(1)} %get-tuple-element.27.refs_1_, ...), custom_call_target="tpu_custom_call" | custom-call | flops 1073741824 | bytes 4980736 | tf_op jit(solution)/shard_map/pallas_call | solution.py:43
  39.8 0.1 collective-permute-start.11
  39.9 2.5 %collective-permute-start.12 = (bf16[2,512,256]{2,1,0:T(8,128)(2,1)S(1)}, bf16[2,512,256]{2,1,0:T(8,128)(2,1)S(1)}, u32[]{:S(2)}, u32[]{:S(2)}) collective-permute-start(bf16[2,512,256]{2,1,0:T(8,128)(2,1)S(1)} %get-tuple-element.45), channel_id=1, source_target_pairs={{0,31},{1,2},{2,1},{3,4},{4,3},{5,6},{6,5},{7,8},{8,7},{9,10},{10,... | collective-permute-start | bytes 1572872 | tf_op jit(solution)/shard_map/ppermute | solution.py:36
  42.4 4.8 %collective-permute-start.8 = (bf16[512,256]{1,0:T(8,128)(2,1)S(1)}, bf16[512,256]{1,0:T(8,128)(2,1)S(1)}, u32[]{:S(2)}, u32[]{:S(2)}) collective-permute-start(bf16[512,256]{1,0:T(8,128)(2,1)S(1)} %get-tuple-element.42.refs_3_), channel_id=1, source_target_pairs={{0,224},{32,0},{64,32},{96,64},{128,96},{160,128},{192,160},{224,1... | collective-permute-start | bytes 786440 | tf_op jit(solution)/shard_map/ppermute | solution.py:27
  47.2 3.8 %collective-permute-done.12.refs_6_ = bf16[2,512,256]{2,1,0:T(8,128)(2,1)S(1)} collective-permute-done((bf16[2,512,256]{2,1,0:T(8,128)(2,1)S(1)}, bf16[2,512,256]{2,1,0:T(8,128)(2,1)S(1)}, u32[]{:S(2)}, u32[]{:S(2)}) %collective-permute-start.12) | collective-permute-done | bytes 524320 | tf_op jit(solution)/shard_map/ppermute | solution.py:36
  50.9 0.1 fusion
  51.0 3.2 %collective-permute-start.13 = (bf16[512,256]{1,0:T(8,128)(2,1)S(1)}, bf16[512,256]{1,0:T(8,128)(2,1)S(1)}, u32[]{:S(2)}, u32[]{:S(2)}) collective-permute-start(bf16[512,256]{1,0:T(8,128)(2,1)S(1)} %fusion), channel_id=1, source_target_pairs={{0,32},{32,64},{64,96},{96,128},{128,160},{160,192},{192,224},{224... | collective-permute-start | bytes 786440 | tf_op jit(solution)/shard_map/ppermute | solution.py:27
  54.2 4.0 %collective-permute-done.8.refs_3_ = bf16[512,256]{1,0:T(8,128)(2,1)S(1)} collective-permute-done((bf16[512,256]{1,0:T(8,128)(2,1)S(1)}, bf16[512,256]{1,0:T(8,128)(2,1)S(1)}, u32[]{:S(2)}, u32[]{:S(2)}) %collective-permute-start.8) | collective-permute-done | bytes 262176 | tf_op jit(solution)/shard_map/ppermute | solution.py:27
  58.2 1.2 %collective-permute-start.10 = (bf16[512,256]{1,0:T(8,128)(2,1)S(1)}, bf16[512,256]{1,0:T(8,128)(2,1)S(1)}, u32[]{:S(2)}, u32[]{:S(2)}) collective-permute-start(bf16[512,256]{1,0:T(8,128)(2,1)S(1)} %collective-permute-done.8.refs_3_), channel_id=1, source_target_pairs={{0,31},{1,2},{2,1},{3,4},{4,3},{5,6},{6,5},{7,8},{8,7},{9,10},{10,... | collective-permute-start | bytes 786440 | tf_op jit(solution)/shard_map/ppermute | solution.py:36
  59.4 1.8 %shard_map.61.own_ref = f32[512,256]{1,0:T(8,128)S(1)} custom-call(bf16[512,512]{1,0:T(8,128)(2,1)S(1)} %get-tuple-element.33.refs_0_, bf16[512,512]{1,0:T(8,128)(2,1)S(1)} %get-tuple-element.40.refs_1_, bf16[512,512]{1,0:T(8,128)(2,1)S(1)} %get-tuple-element.41.refs_2_, bf16[512,256]{1,0:T(8,128)(2,1)S(1)} %get-tuple-element.42.refs_3_, ...), custom_call_target="tpu_custom_call" | custom-call | flops 1207959552 | bytes 4194304 | tf_op jit(solution)/shard_map/pallas_call | solution.py:43
  61.3 0.6 collective-permute-done.13.received_ref
  62.0 4.2 %collective-permute-done.10.refs_5_ = bf16[512,256]{1,0:T(8,128)(2,1)S(1)} collective-permute-done((bf16[512,256]{1,0:T(8,128)(2,1)S(1)}, bf16[512,256]{1,0:T(8,128)(2,1)S(1)}, u32[]{:S(2)}, u32[]{:S(2)}) %collective-permute-start.10) | collective-permute-done | bytes 262176 | tf_op jit(solution)/shard_map/ppermute | solution.py:36
  66.1 1.4 %shard_map.63 = f32[512,256]{1,0:T(8,128)} custom-call(bf16[512,512]{1,0:T(8,128)(2,1)S(1)} %get-tuple-element.26.refs_0_, bf16[512,512]{1,0:T(8,128)(2,1)S(1)} %get-tuple-element.27.refs_1_, bf16[512,512]{1,0:T(8,128)(2,1)S(1)} %get-tuple-element.28.refs_2_, bf16[512,256]{1,0:T(8,128)(2,1)S(1)} %collective-permute-done.8.refs_3_, ...), custom_call_target="tpu_custom_call" | custom-call | flops 402653184 | bytes 3670016 | tf_op jit(solution)/shard_map/pallas_call | solution.py:43
  (9 shorter events, 0.1 us)
Async XLA Ops:
  3.7 13.3 %collective-permute-start.4 = (bf16[2,512,256]{2,1,0:T(8,128)(2,1)S(1)}, bf16[2,512,256]{2,1,0:T(8,128)(2,1)S(1)}, u32[]{:S(2)}, u32[]{:S(2)}) collective-permute-start(bf16[2,512,256]{2,1,0:T(8,128)(2,1)S(1)} %get-tuple-element.36), channel_id=1, source_target_pairs={{0,31},{1,2},{2,1},{3,4},{4,3},{5,6},{6,5},{7,8},{8,7},{9,10},{10,... | collective-permute-start | bytes 1572872 | tf_op jit(solution)/shard_map/ppermute | solution.py:36
  10.0 7.0 %collective-permute-start.3 = (bf16[2,512,256]{2,1,0:T(8,128)(2,1)S(1)}, bf16[2,512,256]{2,1,0:T(8,128)(2,1)S(1)}, u32[]{:S(2)}, u32[]{:S(2)}) collective-permute-start(bf16[2,512,256]{2,1,0:T(8,128)(2,1)S(1)} %get-tuple-element.35), channel_id=1, source_target_pairs={{0,1},{1,0},{2,3},{3,2},{4,5},{5,4},{6,7},{7,6},{8,9},{9,8},{10,11... | collective-permute-start | bytes 1572872 | tf_op jit(solution)/shard_map/ppermute | solution.py:31
  10.0 14.0 %collective-permute-start = (bf16[512,256]{1,0:T(8,128)(2,1)S(1)}, bf16[512,256]{1,0:T(8,128)(2,1)S(1)}, u32[]{:S(2)}, u32[]{:S(2)}) collective-permute-start(bf16[512,256]{1,0:T(8,128)(2,1)S(1)} %get-tuple-element.31.refs_3_), channel_id=1, source_target_pairs={{0,224},{32,0},{64,32},{96,64},{128,96},{160,128},{192,160},{224,1... | collective-permute-start | bytes 786440 | tf_op jit(solution)/shard_map/ppermute | solution.py:27
  17.0 12.8 %collective-permute-start.5 = (bf16[512,256]{1,0:T(8,128)(2,1)S(1)}, bf16[512,256]{1,0:T(8,128)(2,1)S(1)}, u32[]{:S(2)}, u32[]{:S(2)}) collective-permute-start(bf16[512,256]{1,0:T(8,128)(2,1)S(1)} %fusion.1), channel_id=1, source_target_pairs={{0,32},{32,64},{64,96},{96,128},{128,160},{160,192},{192,224},{224... | collective-permute-start | bytes 786440 | tf_op jit(solution)/shard_map/ppermute | solution.py:27
  24.0 7.9 %collective-permute-start.2 = (bf16[512,256]{1,0:T(8,128)(2,1)S(1)}, bf16[512,256]{1,0:T(8,128)(2,1)S(1)}, u32[]{:S(2)}, u32[]{:S(2)}) collective-permute-start(bf16[512,256]{1,0:T(8,128)(2,1)S(1)} %collective-permute-done.refs_3_), channel_id=1, source_target_pairs={{0,31},{1,2},{2,1},{3,4},{4,3},{5,6},{6,5},{7,8},{8,7},{9,10},{10,... | collective-permute-start | bytes 786440 | tf_op jit(solution)/shard_map/ppermute | solution.py:36
  26.2 5.8 %collective-permute-start.1 = (bf16[512,256]{1,0:T(8,128)(2,1)S(1)}, bf16[512,256]{1,0:T(8,128)(2,1)S(1)}, u32[]{:S(2)}, u32[]{:S(2)}) collective-permute-start(bf16[512,256]{1,0:T(8,128)(2,1)S(1)} %collective-permute-done.refs_3_), channel_id=1, source_target_pairs={{0,1},{1,0},{2,3},{3,2},{4,5},{5,4},{6,7},{7,6},{8,9},{9,8},{10,11... | collective-permute-start | bytes 786440 | tf_op jit(solution)/shard_map/ppermute | solution.py:31
  26.2 6.4 %collective-permute-start.6 = (bf16[512,512]{1,0:T(8,128)(2,1)S(1)}, bf16[512,512]{1,0:T(8,128)(2,1)S(1)}, u32[]{:S(2)}, u32[]{:S(2)}) collective-permute-start(bf16[512,512]{1,0:T(8,128)(2,1)S(1)} %get-tuple-element.40.refs_1_), channel_id=1, source_target_pairs={{0,1},{1,0},{2,3},{3,2},{4,5},{5,4},{6,7},{7,6},{8,9},{9,8},{10,11... | collective-permute-start | bytes 1572872 | tf_op jit(solution)/shard_map/ppermute | solution.py:31
  26.7 10.9 %collective-permute-start.7 = (bf16[512,512]{1,0:T(8,128)(2,1)S(1)}, bf16[512,512]{1,0:T(8,128)(2,1)S(1)}, u32[]{:S(2)}, u32[]{:S(2)}) collective-permute-start(bf16[512,512]{1,0:T(8,128)(2,1)S(1)} %get-tuple-element.41.refs_2_), channel_id=1, source_target_pairs={{0,31},{1,2},{2,1},{3,4},{4,3},{5,6},{6,5},{7,8},{8,7},{9,10},{10,... | collective-permute-start | bytes 1572872 | tf_op jit(solution)/shard_map/ppermute | solution.py:36
  31.9 5.6 %copy-start = (f32[512,256]{1,0:T(8,128)S(1)}, f32[512,256]{1,0:T(8,128)}, u32[]{:S(2)}) copy-start(f32[512,256]{1,0:T(8,128)} %refs_7_.1) | copy-start | bytes 1572868
  39.8 7.4 %collective-permute-start.11 = (bf16[2,512,256]{2,1,0:T(8,128)(2,1)S(1)}, bf16[2,512,256]{2,1,0:T(8,128)(2,1)S(1)}, u32[]{:S(2)}, u32[]{:S(2)}) collective-permute-start(bf16[2,512,256]{2,1,0:T(8,128)(2,1)S(1)} %get-tuple-element.44), channel_id=1, source_target_pairs={{0,1},{1,0},{2,3},{3,2},{4,5},{5,4},{6,7},{7,6},{8,9},{9,8},{10,11... | collective-permute-start | bytes 1572872 | tf_op jit(solution)/shard_map/ppermute | solution.py:31
  39.9 11.1 %collective-permute-start.12 = (bf16[2,512,256]{2,1,0:T(8,128)(2,1)S(1)}, bf16[2,512,256]{2,1,0:T(8,128)(2,1)S(1)}, u32[]{:S(2)}, u32[]{:S(2)}) collective-permute-start(bf16[2,512,256]{2,1,0:T(8,128)(2,1)S(1)} %get-tuple-element.45), channel_id=1, source_target_pairs={{0,31},{1,2},{2,1},{3,4},{4,3},{5,6},{6,5},{7,8},{8,7},{9,10},{10,... | collective-permute-start | bytes 1572872 | tf_op jit(solution)/shard_map/ppermute | solution.py:36
  42.4 15.8 %collective-permute-start.8 = (bf16[512,256]{1,0:T(8,128)(2,1)S(1)}, bf16[512,256]{1,0:T(8,128)(2,1)S(1)}, u32[]{:S(2)}, u32[]{:S(2)}) collective-permute-start(bf16[512,256]{1,0:T(8,128)(2,1)S(1)} %get-tuple-element.42.refs_3_), channel_id=1, source_target_pairs={{0,224},{32,0},{64,32},{96,64},{128,96},{160,128},{192,160},{224,1... | collective-permute-start | bytes 786440 | tf_op jit(solution)/shard_map/ppermute | solution.py:27
  51.0 10.9 %collective-permute-start.13 = (bf16[512,256]{1,0:T(8,128)(2,1)S(1)}, bf16[512,256]{1,0:T(8,128)(2,1)S(1)}, u32[]{:S(2)}, u32[]{:S(2)}) collective-permute-start(bf16[512,256]{1,0:T(8,128)(2,1)S(1)} %fusion), channel_id=1, source_target_pairs={{0,32},{32,64},{64,96},{96,128},{128,160},{160,192},{192,224},{224... | collective-permute-start | bytes 786440 | tf_op jit(solution)/shard_map/ppermute | solution.py:27
  58.2 7.9 %collective-permute-start.10 = (bf16[512,256]{1,0:T(8,128)(2,1)S(1)}, bf16[512,256]{1,0:T(8,128)(2,1)S(1)}, u32[]{:S(2)}, u32[]{:S(2)}) collective-permute-start(bf16[512,256]{1,0:T(8,128)(2,1)S(1)} %collective-permute-done.8.refs_3_), channel_id=1, source_target_pairs={{0,31},{1,2},{2,1},{3,4},{4,3},{5,6},{6,5},{7,8},{8,7},{9,10},{10,... | collective-permute-start | bytes 786440 | tf_op jit(solution)/shard_map/ppermute | solution.py:36
  59.4 6.7 %collective-permute-start.9 = (bf16[512,256]{1,0:T(8,128)(2,1)S(1)}, bf16[512,256]{1,0:T(8,128)(2,1)S(1)}, u32[]{:S(2)}, u32[]{:S(2)}) collective-permute-start(bf16[512,256]{1,0:T(8,128)(2,1)S(1)} %collective-permute-done.8.refs_3_), channel_id=1, source_target_pairs={{0,1},{1,0},{2,3},{3,2},{4,5},{5,4},{6,7},{7,6},{8,9},{9,8},{10,11... | collective-permute-start | bytes 786440 | tf_op jit(solution)/shard_map/ppermute | solution.py:31
